TPU v7x, 32 devices: a whole 2x2x4 slice. The times are simulated.
32 devices in a mesh: seq: 16 (over z, y, x), batch: 2 (over core).
Axes of the slice: x: 2, y: 2, z: 4, core: 2. Of those that a mesh axis runs over, the one named last changes fastest.
Arguments:
- inputs: bfloat16 [2, 4096, 512], P('batch', 'seq'), may hold values from -6 to 6
- cotangent: bfloat16 [2, 4096, 512], P('batch', 'seq'), may hold values from -6 to 6
- lengths: int32 [2, 4], P('batch'), may hold values from 1 to 2048, as said below
- master: float32 [2759168], P(('seq', 'batch')), may hold values from -9.2 to 30, as said below
- first_moment: float32 [2759168], P(('seq', 'batch')), may hold values from -0.0014648438 to 0.0014648438
- second_moment: float32 [2759168], P(('seq', 'batch')), may hold values from 1e-10 to 1e-09
Outputs:
- output: bfloat16 [2, 4096, 512], P('batch', 'seq')
- input_grad: float32 [2, 4096, 512], P('batch', 'seq')
- grad: float32 [2759168], P(('seq', 'batch'))
- update: float32 [2759168], P(('seq', 'batch'))
- first_new: float32 [2759168], P(('seq', 'batch'))
- second_new: float32 [2759168], P(('seq', 'batch'))
- grad_norm: float32 [], replicated
Inputs may be any that keep to these rules, and one draw needn't show every extreme that they name: `lengths`: each row sums to 4096; its last entry counts padding tokens at the stream's end, at most max(1, 128); the third entry is exactly 2048. `master`: step_log lies in -9.2 to -2.3, decay_log in -1.5 to 0.5, frequency in 0 to 30, norm_gain and second_gain in 0.7 to 1.3.
All inputs are finite; a program needn't handle non-finite values.
Results may differ from a plain program's by a relative error of at most 0.0064.
Values sent between devices are 32-bit elements; how exact they have to be, the bound alone decides.
No kernel may reach another device: no remote copies, remote signals or barrier semaphores. Data moves between devices by JAX's collectives and lax.ppermute only.
A program may use at most 512 MiB of HBM per device.

v0:
```python
from functools import partial

import jax
import jax.numpy as jnp
from jax import lax
from jax.sharding import PartitionSpec as P

D = 512
NSTATE = 64
G = 1024
FF = 2048
DOCS = 4


highest = lax.Precision.HIGHEST
norm_eps = 1e-05
root_half = 0.7071067811865476
inv_root_two_pi = 0.3989422804014327


def entering(part, axis, combine, identity, reverse):
    count = lax.axis_size(axis)
    place = lax.axis_index(axis)
    ahead = count - 1 - place if reverse else place
    gathered = jax.tree.map(lambda a: lax.all_gather(a, axis), part)
    state = jax.tree.map(lambda a, e: jnp.zeros_like(a) + jnp.asarray(e, a.dtype), part, identity)

    def one(step, state):
        source = count - 1 - step if reverse else step
        return combine(
            state, jax.tree.map(lambda a: lax.dynamic_index_in_dim(a, source, 0, False), gathered)
        )

    return lax.fori_loop(0, ahead, one, state)


def unpack(flat):
    layout = [
        ("norm_gain", (D,)),
        ("norm_bias", (D,)),
        ("step_log", (D,)),
        ("skip_gain", (D,)),
        ("decay_log", (D, NSTATE)),
        ("frequency", (D, NSTATE)),
        ("out_real", (D, NSTATE)),
        ("out_imag", (D, NSTATE)),
        ("gate_weight", (D, G)),
        ("gate_bias", (G,)),
        ("second_gain", (D,)),
        ("second_bias", (D,)),
        ("expand_weight", (D, FF)),
        ("expand_bias", (FF,)),
        ("reduce_weight", (FF, D)),
        ("reduce_bias", (D,)),
    ]
    params = {}
    offset = 0
    for name, shape in layout:
        count = 1
        for extent in shape:
            count = count * extent
        params[name] = flat[offset : offset + count].reshape(shape)
        offset = offset + count
    return params


def gelu(values):
    return 0.5 * values * (1.0 + lax.erf(values * root_half))


def gelu_slope(values):
    return (
        0.5 * (1.0 + lax.erf(values * root_half))
        + values * jnp.exp(-0.5 * values * values) * inv_root_two_pi
    )


def normalize(values):
    center = values - jnp.mean(values, axis=-1, keepdims=True)
    scale = lax.rsqrt(jnp.mean(center * center, axis=-1, keepdims=True) + norm_eps)
    return (center * scale, scale)


def norm_back(d_hat, hat, scale):
    return scale * (
        d_hat
        - jnp.mean(d_hat, axis=-1, keepdims=True)
        - hat * jnp.mean(d_hat * hat, axis=-1, keepdims=True)
    )


def pole_args(step_log, decay_log, frequency):
    delta = jnp.exp(step_log)[:, None]
    return (delta * -jnp.exp(decay_log), delta * frequency)


def powers(arg_re, arg_im, levels):
    magnitude = jnp.exp(arg_re[:, :, None] * levels)
    return (
        magnitude * jnp.cos(arg_im[:, :, None] * levels),
        magnitude * jnp.sin(arg_im[:, :, None] * levels),
    )


def tables_of(step_log, decay_log, frequency, out_real, out_imag, width):
    arg_re, arg_im = pole_args(step_log, decay_log, frequency)
    rate_re = -jnp.exp(decay_log)
    magnitude = jnp.exp(arg_re)
    pole_re = magnitude * jnp.cos(arg_im) - 1.0
    pole_im = magnitude * jnp.sin(arg_im)
    denom = rate_re * rate_re + frequency * frequency
    ratio_re = (pole_re * rate_re + pole_im * frequency) / denom
    ratio_im = (pole_im * rate_re - pole_re * frequency) / denom
    mix_re = out_real * ratio_re - out_imag * ratio_im
    mix_im = out_real * ratio_im + out_imag * ratio_re
    levels = jnp.arange(width, dtype=jnp.float32)
    zero_re, zero_im = powers(arg_re, arg_im, levels)
    up_re, up_im = powers(arg_re, arg_im, levels + 1.0)
    kernel = jnp.sum(mix_re[:, :, None] * zero_re - mix_im[:, :, None] * zero_im, axis=1)
    full_mag = jnp.exp(arg_re * width)
    full_re = full_mag * jnp.cos(arg_im * width)
    full_im = full_mag * jnp.sin(arg_im * width)
    return (
        kernel,
        up_re,
        up_im,
        zero_re[:, :, ::-1],
        zero_im[:, :, ::-1],
        full_re,
        full_im,
        mix_re,
        mix_im,
    )


def block_apply(tables, carry, piece):
    kernel, up_re, up_im, down_re, down_im, full_re, full_im, mix_re, mix_im = tables
    state_re, state_im, prev = carry
    values, labels = piece
    width = labels.shape[0]
    mixed_re = mix_re * state_re - mix_im * state_im
    mixed_im = mix_re * state_im + mix_im * state_re
    carried = jnp.einsum("hnt,hn->th", up_re, mixed_re, precision=highest) - jnp.einsum(
        "hnt,hn->th", up_im, mixed_im, precision=highest
    )
    joined = (labels == prev).astype(jnp.float32)
    result = carried * joined[:, None]
    last = labels[width - 1]
    keep = (last == prev).astype(jnp.float32)
    new_re = keep * (full_re * state_re - full_im * state_im)
    new_im = keep * (full_re * state_im + full_im * state_re)
    if values is not None:
        places = jnp.arange(width, dtype=jnp.int32)
        gap = places[:, None] - places[None, :]
        same = ((labels[:, None] == labels[None, :]) & (gap >= 0)).astype(jnp.float32)
        toeplitz = kernel[:, jnp.clip(gap, 0, width - 1)] * same[None]
        result = result + jnp.einsum("hts,sh->th", toeplitz, values, precision=highest)
        tail = values * (labels == last).astype(jnp.float32)[:, None]
        new_re = new_re + jnp.einsum("hns,sh->hn", down_re, tail, precision=highest)
        new_im = new_im + jnp.einsum("hns,sh->hn", down_im, tail, precision=highest)
    return ((new_re, new_im, last), result)


def group_response(tables, values, labels, prev, state_re, state_im, width):
    count = labels.shape[0] // width
    blocks = labels.reshape(count, width)
    pieces = (None if values is None else values.reshape(count, width, values.shape[-1]), blocks)
    stepper = jax.checkpoint(partial(block_apply, tables))
    finals, out = lax.scan(stepper, (state_re, state_im, prev), pieces)
    return (out.reshape(labels.shape[0], out.shape[-1]), finals[0], finals[1])


def compose(earlier, later):
    lead_re, lead_im, tail_re, tail_im = later
    return (
        lead_re * earlier[0] - lead_im * earlier[1],
        lead_re * earlier[1] + lead_im * earlier[0],
        lead_re * earlier[2] - lead_im * earlier[3] + tail_re,
        lead_re * earlier[3] + lead_im * earlier[2] + tail_im,
    )


def per_device(inputs, cotangent, lengths, master, first_moment, second_moment):
    full = lax.all_gather(master, ("seq", "batch"), axis=0, tiled=True)
    params = unpack(full)
    group = inputs.shape[1]
    width = min(128, group)
    rows = inputs[0].astype(jnp.float32)
    ends = jnp.cumsum(lengths[0])
    offset = lax.axis_index("seq") * group
    where = offset + jnp.arange(group, dtype=jnp.int32)
    labels = jnp.sum((where[:, None] >= ends[None, :]).astype(jnp.int32), axis=1)
    before = jnp.sum((offset - 1 >= ends).astype(jnp.int32))
    prev_label = jnp.where(offset > 0, before, -1)
    valid = (labels < DOCS - 1).astype(jnp.float32)
    zero_state = jnp.zeros((D, NSTATE), jnp.float32)
    one_state = jnp.ones((D, NSTATE), jnp.float32)
    first_hat, first_scale = normalize(rows)
    signal = first_hat * params["norm_gain"] + params["norm_bias"]
    ssm = (
        params["step_log"],
        params["decay_log"],
        params["frequency"],
        params["out_real"],
        params["out_imag"],
    )

    def local_part(step_log, decay_log, frequency, out_real, out_imag, values):
        tables = tables_of(step_log, decay_log, frequency, out_real, out_imag, width)
        return group_response(tables, values, labels, prev_label, zero_state, zero_state, width)

    (local_out, end_re, end_im), local_pull = jax.vjp(local_part, *ssm, signal)
    keep_group = (labels[group - 1] == prev_label).astype(jnp.float32)

    def group_decay(step_log, decay_log, frequency):
        arg_re, arg_im = pole_args(step_log, decay_log, frequency)
        magnitude = jnp.exp(group * arg_re) * keep_group
        return (magnitude * jnp.cos(group * arg_im), magnitude * jnp.sin(group * arg_im))

    (decay_re, decay_im), decay_pull = jax.vjp(group_decay, ssm[0], ssm[1], ssm[2])
    arg_re, arg_im = pole_args(ssm[0], ssm[1], ssm[2])
    prior = entering(
        (decay_re, decay_im, end_re, end_im),
        "seq",
        compose,
        (one_state, zero_state, zero_state, zero_state),
        False,
    )
    state_re, state_im = (prior[2], prior[3])

    def carried_part(step_log, decay_log, frequency, out_real, out_imag, start_re, start_im):
        tables = tables_of(step_log, decay_log, frequency, out_real, out_imag, width)
        out, _, _ = group_response(tables, None, labels, prev_label, start_re, start_im, width)
        return out

    carried_out, carried_pull = jax.vjp(carried_part, *ssm, state_re, state_im)
    response = local_out + carried_out + params["skip_gain"] * signal
    hidden_low = gelu(response).astype(jnp.bfloat16)
    gate_low = params["gate_weight"].astype(jnp.bfloat16)
    opened = jnp.dot(hidden_low, gate_low, preferred_element_type=jnp.float32) + params["gate_bias"]
    linear = opened[:, :D]
    gating = jax.nn.sigmoid(opened[:, D:])
    mid = rows + linear * gating
    second_hat, second_scale = normalize(mid)
    normed_low = (second_hat * params["second_gain"] + params["second_bias"]).astype(jnp.bfloat16)
    expand_low = params["expand_weight"].astype(jnp.bfloat16)
    lifted = (
        jnp.dot(normed_low, expand_low, preferred_element_type=jnp.float32) + params["expand_bias"]
    )
    active_low = gelu(lifted).astype(jnp.bfloat16)
    reduce_low = params["reduce_weight"].astype(jnp.bfloat16)
    result = (
        mid
        + jnp.dot(active_low, reduce_low, preferred_element_type=jnp.float32)
        + params["reduce_bias"]
    )
    output = result.astype(jnp.bfloat16)[None]
    back = cotangent[0].astype(jnp.float32) * valid[:, None]
    back_low = back.astype(jnp.bfloat16)
    g_reduce_w = jnp.einsum("tf,td->fd", active_low, back_low, preferred_element_type=jnp.float32)
    g_reduce_b = jnp.sum(back, axis=0)
    d_active = jnp.einsum("td,fd->tf", back_low, reduce_low, preferred_element_type=jnp.float32)
    d_lifted = (d_active * gelu_slope(lifted)).astype(jnp.bfloat16)
    g_expand_w = jnp.einsum("td,tf->df", normed_low, d_lifted, preferred_element_type=jnp.float32)
    g_expand_b = jnp.sum(d_lifted.astype(jnp.float32), axis=0)
    d_normed = jnp.einsum("tf,df->td", d_lifted, expand_low, preferred_element_type=jnp.float32)
    g_second_gain = jnp.sum(d_normed * second_hat, axis=0)
    g_second_bias = jnp.sum(d_normed, axis=0)
    d_mid = back + norm_back(d_normed * params["second_gain"], second_hat, second_scale)
    d_linear = d_mid * gating
    d_gating = d_mid * linear * gating * (1.0 - gating)
    d_opened = jnp.concatenate([d_linear, d_gating], axis=1).astype(jnp.bfloat16)
    g_gate_w = jnp.einsum("td,tg->dg", hidden_low, d_opened, preferred_element_type=jnp.float32)
    g_gate_b = jnp.sum(d_opened.astype(jnp.float32), axis=0)
    d_hidden = jnp.einsum("tg,dg->td", d_opened, gate_low, preferred_element_type=jnp.float32)
    d_response = d_hidden * gelu_slope(response)
    g_skip = jnp.sum(d_response * signal, axis=0)
    carried_grads = carried_pull(d_response)
    lead_re, lead_im = (carried_grads[5], carried_grads[6])
    later = entering(
        (decay_re, -decay_im, lead_re, lead_im),
        "seq",
        compose,
        (one_state, zero_state, zero_state, zero_state),
        True,
    )
    adjoint_re, adjoint_im = (later[2], later[3])
    local_grads = local_pull((d_response, adjoint_re, adjoint_im))
    decay_grads = decay_pull(
        (
            adjoint_re * state_re + adjoint_im * state_im,
            adjoint_im * state_re - adjoint_re * state_im,
        )
    )
    g_step = carried_grads[0] + local_grads[0] + decay_grads[0]
    g_decay = carried_grads[1] + local_grads[1] + decay_grads[1]
    g_frequency = carried_grads[2] + local_grads[2] + decay_grads[2]
    g_out_real = carried_grads[3] + local_grads[3]
    g_out_imag = carried_grads[4] + local_grads[4]
    d_signal = d_response * params["skip_gain"] + local_grads[5]
    g_norm_gain = jnp.sum(d_signal * first_hat, axis=0)
    g_norm_bias = jnp.sum(d_signal, axis=0)
    d_rows = d_mid + norm_back(d_signal * params["norm_gain"], first_hat, first_scale)
    parts = [
        g_norm_gain,
        g_norm_bias,
        g_step,
        g_skip,
        g_decay,
        g_frequency,
        g_out_real,
        g_out_imag,
        g_gate_w,
        g_gate_b,
        g_second_gain,
        g_second_bias,
        g_expand_w,
        g_expand_b,
        g_reduce_w,
        g_reduce_b,
    ]
    packed = jnp.concatenate([item.reshape(-1) for item in parts])
    packed = jnp.concatenate([packed, jnp.zeros((full.shape[0] - packed.shape[0],), jnp.float32)])
    shard = lax.psum_scatter(packed, ("seq", "batch"), scatter_dimension=0, tiled=True)
    total = lax.psum(jnp.sum(shard * shard), ("seq", "batch"))
    grad_norm = jnp.sqrt(total)
    factor = jnp.minimum(1.0, 1.0 / (grad_norm + 1e-06))
    clipped = shard * factor
    first_new = 0.9 * first_moment + 0.1 * clipped
    second_new = 0.999 * second_moment + 0.001 * clipped * clipped
    first_hat_new = first_new / (1.0 - 0.9**10)
    second_hat_new = second_new / (1.0 - 0.999**10)
    update = -0.05 * (first_hat_new / (jnp.sqrt(second_hat_new) + 1e-08) + 0.1 * master)
    return (output, d_rows[None], shard, update, first_new, second_new, grad_norm)


def solution(mesh):
    placed = (
        P("batch", "seq", None),
        P("batch", "seq", None),
        P("batch", None),
        P(("seq", "batch")),
        P(("seq", "batch")),
        P(("seq", "batch")),
    )
    return jax.shard_map(
        per_device,
        mesh=mesh,
        in_specs=placed,
        out_specs=(
            P("batch", "seq", None),
            P("batch", "seq", None),
            P(("seq", "batch")),
            P(("seq", "batch")),
            P(("seq", "batch")),
            P(("seq", "batch")),
            P(),
        ),
        check_vma=False,
    )
```

profile of v0, /device:TPU:0, one launch (start us, length us, event | category | flops | bytes accessed | tf_op | source)
XLA Modules:
  0.0 3322.4 jit_solution(15731368219948396358)
XLA Ops:
  18.7 216.9 %all-reduce.5.cloned.1.call-done = f32[2759168]{0:T(1024)} async-done(((f32[2759168]{0:T(1024)}), f32[2759168]{0:T(1024)}) %all-reduce.5.cloned.1.call-update) | async-done | bytes 11036688
  244.6 71.0 %subtract_reduce_fusion = (f32[512,128]{1,0:T(8,128)S(1)}, f32[512,64,128]{2,1,0:T(8,128)}, f32[512,64,128]{2,1,0:T(8,128)}) fusion(f32[512,64]{1,0:T(8,128)} %get-tuple-element.3876, f32[512,64]{1,0:T(8,128)} %get-tuple-element.3875, f32[512,64]{1,0:T(8,128)} %get-tuple-element.3884, f32[512,64]{1,0:T(8,128)} %get-tuple-element.3882), kind=kLoop, calls=%fused_computation.189 | loop fusion | flops 33488896 | bytes 34340864 | tf_op jit(solution)/shard_map/jvp()/reduce_sum | solution.py:119
  468.4 467.5 %while.154 = (s32[]{:T(128)}, f32[512,64]{1,0:T(8,128)S(1)}, f32[512,64]{1,0:T(8,128)S(1)}, s32[]{:T(128)}, f32[2,128,512]{2,1,0:T(8,128)S(1)}, /*index=5*/f32[2...) while((s32[]{:T(128)}, f32[512,64]{1,0:T(8,128)S(1)}, ...), condition=%wide.region_7.8_spmd.clone.clone.clone, body=%wide.region_6.7_spmd.clone.clone.clone.sunk | while | flops 252592640 | bytes 76944664 | solution.py:169
  548.9 76.4 %fusion.259 = f32[512,1,128]{2,1,0:T(1,128)S(1)} fusion(f32[512,64,1]{1,2,0:T(1,128)S(1)} %bitcast.504, f32[512,64]{1,0:T(8,128)} %get-tuple-element.3664, f32[128]{0:T(128)S(1)} %get-tuple-element.3663, f32[512,64]{1,0:T(8,128)} %get-tuple-element.3662), kind=kOutput, calls=%fused_computation.86.clone.1 | convolution fusion | flops 62914560 | bytes 655872 | tf_op jit(solution)/shard_map/jvp()/while/body/eval_jaxpr/hnt,hn->th/dot_general | solution.py:143
  625.4 75.9 %fusion.260 = f32[512,1,128]{2,1,0:T(1,128)S(1)} fusion(f32[512,64,1]{1,2,0:T(1,128)S(1)} %bitcast.503, f32[512,64]{1,0:T(8,128)} %get-tuple-element.3664, f32[128]{0:T(128)S(1)} %get-tuple-element.3663, f32[512,64]{1,0:T(8,128)} %get-tuple-element.3662), kind=kOutput, calls=%fused_computation.84.clone.1 | convolution fusion | flops 62914560 | bytes 655872 | tf_op jit(solution)/shard_map/jvp()/while/body/eval_jaxpr/hnt,hn->th/dot_general | solution.py:143
  782.3 76.4 %fusion.259 = f32[512,1,128]{2,1,0:T(1,128)S(1)} fusion(f32[512,64,1]{1,2,0:T(1,128)S(1)} %bitcast.504, f32[512,64]{1,0:T(8,128)} %get-tuple-element.3664, f32[128]{0:T(128)S(1)} %get-tuple-element.3663, f32[512,64]{1,0:T(8,128)} %get-tuple-element.3662), kind=kOutput, calls=%fused_computation.86.clone.1 | convolution fusion | flops 62914560 | bytes 655872 | tf_op jit(solution)/shard_map/jvp()/while/body/eval_jaxpr/hnt,hn->th/dot_general | solution.py:143
  858.8 75.9 %fusion.260 = f32[512,1,128]{2,1,0:T(1,128)S(1)} fusion(f32[512,64,1]{1,2,0:T(1,128)S(1)} %bitcast.503, f32[512,64]{1,0:T(8,128)} %get-tuple-element.3664, f32[128]{0:T(128)S(1)} %get-tuple-element.3663, f32[512,64]{1,0:T(8,128)} %get-tuple-element.3662), kind=kOutput, calls=%fused_computation.84.clone.1 | convolution fusion | flops 62914560 | bytes 655872 | tf_op jit(solution)/shard_map/jvp()/while/body/eval_jaxpr/hnt,hn->th/dot_general | solution.py:143
  1012.1 77.3 %all-gather.20.cloned.1.call-done = f32[8192,64]{1,0:T(8,128)} async-done(((f32[512,64]{1,0:T(8,128)}), f32[8192,64]{1,0:T(8,128)}) %all-gather.20.cloned.1.call-update) | async-done | bytes 2097168 | tf_op jit(solution)/shard_map/all_gather | solution.py:25
  1092.3 318.3 %while.153 = (s32[]{:T(128)}, f32[512,64]{1,0:T(8,128)S(1)}, f32[512,64]{1,0:T(8,128)S(1)}, s32[]{:T(128)}, f32[2,128,512]{2,1,0:T(8,128)}, /*index=5*/f32[2,512...) while((s32[]{:T(128)}, f32[512,64]{1,0:T(8,128)S(1)}, ...), condition=%wide.region_11.12_spmd.clone.clone, body=%wide.region_10.11_spmd.clone.clone.sunk | while | flops 126419200 | bytes 9440539 | solution.py:169
  1096.5 76.4 %fusion.245 = f32[512,1,128]{2,1,0:T(1,128)S(1)} fusion(f32[512,64,1]{1,2,0:T(1,128)S(1)} %bitcast.506, f32[512,64]{1,0:T(8,128)} %get-tuple-element.3749, f32[128]{0:T(128)S(1)} %get-tuple-element.3748, f32[512,64]{1,0:T(8,128)} %get-tuple-element.3747), kind=kOutput, calls=%fused_computation.35.clone.2 | convolution fusion | flops 62914560 | bytes 655872 | tf_op jit(solution)/shard_map/jvp()/while/body/eval_jaxpr/hnt,hn->th/dot_general | solution.py:143
  1173.1 76.6 %fusion.246 = f32[512,1,128]{2,1,0:T(1,128)S(1)} fusion(f32[512,64,1]{1,2,0:T(1,128)} %bitcast.505, f32[512,64]{1,0:T(8,128)} %get-tuple-element.3749, f32[128]{0:T(128)S(1)} %get-tuple-element.3748, f32[512,64]{1,0:T(8,128)} %get-tuple-element.3747), kind=kOutput, calls=%fused_computation.33.clone.2 | convolution fusion | flops 62914560 | bytes 655872 | tf_op jit(solution)/shard_map/jvp()/while/body/eval_jaxpr/hnt,hn->th/dot_general | solution.py:143
  1255.7 76.4 %fusion.245 = f32[512,1,128]{2,1,0:T(1,128)S(1)} fusion(f32[512,64,1]{1,2,0:T(1,128)S(1)} %bitcast.506, f32[512,64]{1,0:T(8,128)} %get-tuple-element.3749, f32[128]{0:T(128)S(1)} %get-tuple-element.3748, f32[512,64]{1,0:T(8,128)} %get-tuple-element.3747), kind=kOutput, calls=%fused_computation.35.clone.2 | convolution fusion | flops 62914560 | bytes 655872 | tf_op jit(solution)/shard_map/jvp()/while/body/eval_jaxpr/hnt,hn->th/dot_general | solution.py:143
  1332.2 76.6 %fusion.246 = f32[512,1,128]{2,1,0:T(1,128)S(1)} fusion(f32[512,64,1]{1,2,0:T(1,128)} %bitcast.505, f32[512,64]{1,0:T(8,128)} %get-tuple-element.3749, f32[128]{0:T(128)S(1)} %get-tuple-element.3748, f32[512,64]{1,0:T(8,128)} %get-tuple-element.3747), kind=kOutput, calls=%fused_computation.33.clone.2 | convolution fusion | flops 62914560 | bytes 655872 | tf_op jit(solution)/shard_map/jvp()/while/body/eval_jaxpr/hnt,hn->th/dot_general | solution.py:143
  1425.5 295.4 %while.155 = (s32[]{:T(128)}, f32[512,64]{1,0:T(8,128)S(1)}, f32[512,64]{1,0:T(8,128)S(1)}, f32[512,64,128]{2,1,0:T(8,128)}, f32[512,64,128]{2,1,0:T(8,128)}, /*...) while((s32[]{:T(128)}, f32[512,64]{1,0:T(8,128)S(1)}, ...), condition=%wide.region_17.18_spmd.clone.clone.clone, body=%wide.region_16.17_spmd.clone.clone.clone.sunk | while | flops 144310528 | bytes 209980784 | solution.py:169
  1425.7 65.7 %fusion.265 = (f32[512,64,128]{2,1,0:T(8,128)}, f32[512,64,128]{2,1,0:T(8,128)}) fusion(f32[512,64]{1,0:T(8,128)} %get-tuple-element.3817, f32[128]{0:T(128)S(1)} %get-tuple-element.3816, f32[512,64]{1,0:T(8,128)} %get-tuple-element.3815), kind=kLoop, calls=%fused_computation.58.clone.1 | loop fusion | flops 16777216 | bytes 33817088 | tf_op jit(solution)/shard_map/jvp()/mul | solution.py:101
  1735.9 97.2 %all-gather.22.cloned.1.call-done = f32[8192,64]{1,0:T(8,128)} async-done(((f32[512,64]{1,0:T(8,128)}), f32[8192,64]{1,0:T(8,128)}) %all-gather.22.cloned.1.call-update) | async-done | bytes 2097168 | tf_op jit(solution)/shard_map/all_gather | solution.py:25
  1833.0 77.5 %all-gather.24.cloned.1.call-done = f32[8192,64]{1,0:T(8,128)} async-done(((f32[512,64]{1,0:T(8,128)}), f32[8192,64]{1,0:T(8,128)}) %all-gather.24.cloned.1.call-update) | async-done | bytes 2097168 | tf_op jit(solution)/shard_map/all_gather | solution.py:25
  1950.3 811.8 %while.156 = (s32[]{:T(128)}, f32[512,64]{1,0:T(8,128)}, f32[512,64]{1,0:T(8,128)}, f32[512,64,128]{2,1,0:T(8,128)}, f32[512,64,128]{2,1,0:T(8,128)}, /*index=5*...) while((s32[]{:T(128)}, f32[512,64]{1,0:T(8,128)}, ...), condition=%wide.region_22.23_spmd.clone.clone.clone, body=%wide.region_20.22_spmd.clone.clone.clone.sunk | while | flops 320799232 | bytes 501897216 | solution.py:169
  1950.6 65.8 %fusion.277 = (f32[512,64,128]{2,1,0:T(8,128)}, f32[512,64,128]{2,1,0:T(8,128)}) fusion(f32[512,64]{1,0:T(8,128)} %get-tuple-element.3946, f32[128]{0:T(128)S(1)} %get-tuple-element.3945, f32[512,64]{1,0:T(8,128)} %get-tuple-element.3944), kind=kLoop, calls=%fused_computation.119.clone.1 | loop fusion | flops 16777216 | bytes 33817088 | tf_op jit(solution)/shard_map/jvp()/mul | solution.py:101
  2236.2 104.3 %scatter_fusion = f32[512,128]{0,1:T(8,128)S(1)} fusion(f32[512,128]{0,1:T(8,128)S(1)} %copy-done.3, s32[16384]{0:T(1024)S(1)} %fusion.281, f32[16384,512]{1,0:T(8,128)} %bitcast.478), kind=kCustom, calls=%fused_computation.2.clone.clone.clone.clone.1 | custom fusion | flops 8388608 | bytes 100728832 | tf_op jit(solution)/shard_map/transpose(jvp())/while/body/eval_jaxpr/checkpoint/scatter-add | solution.py:156
  2341.8 65.8 %fusion.277 = (f32[512,64,128]{2,1,0:T(8,128)}, f32[512,64,128]{2,1,0:T(8,128)}) fusion(f32[512,64]{1,0:T(8,128)} %get-tuple-element.3946, f32[128]{0:T(128)S(1)} %get-tuple-element.3945, f32[512,64]{1,0:T(8,128)} %get-tuple-element.3944), kind=kLoop, calls=%fused_computation.119.clone.1 | loop fusion | flops 16777216 | bytes 33817088 | tf_op jit(solution)/shard_map/jvp()/mul | solution.py:101
  2648.0 104.3 %scatter_fusion = f32[512,128]{0,1:T(8,128)S(1)} fusion(f32[512,128]{0,1:T(8,128)S(1)} %copy-done.3, s32[16384]{0:T(1024)S(1)} %fusion.281, f32[16384,512]{1,0:T(8,128)} %bitcast.478), kind=kCustom, calls=%fused_computation.2.clone.clone.clone.clone.1 | custom fusion | flops 8388608 | bytes 100728832 | tf_op jit(solution)/shard_map/transpose(jvp())/while/body/eval_jaxpr/checkpoint/scatter-add | solution.py:156
  2817.4 189.3 %fusion.82 = (f32[512,64]{1,0:T(8,128)S(1)}, f32[512,64]{1,0:T(8,128)S(1)}, f32[512,64]{1,0:T(8,128)S(1)}, f32[512,64]{1,0:T(8,128)S(1)}, f32[512,64]{1,0:T(8,12...) fusion(f32[512,64,128]{2,1,0:T(8,128)} %get-tuple-element.1388,, ...), kind=kLoop, calls=%fused_computation.175 | loop fusion | flops 247103488 | bytes 103154176 | tf_op jit(solution)/shard_map/transpose(jvp())/reduce_sum | solution.py:98
  3061.8 208.4 %all-reduce.7.cloned.1.call-done = f32[2759168]{0:T(1024)} async-done(((f32[2759168]{0:T(1024)}), f32[2759168]{0:T(1024)}) %all-reduce.7.cloned.1.call-update) | async-done | bytes 11036688
  (636 shorter events, 1363.9 us)
Async XLA Ops:
  7.2 228.4 %all-reduce.5.cloned.1.call-start = ((), (), s32[]{:S(2)}) async-start(), calls=%async_computation.7 | async-start | bytes 22077440
  15.9 940.9 %all-gather.12.cloned.1.call-start = ((), (), s32[]{:S(2)}) async-start(), calls=%async_computation | async-start | bytes 2228224 | tf_op jit(solution)/shard_map/all_gather | solution.py:25
  239.9 720.8 %all-gather.14.cloned.1.call-start = ((), (), s32[]{:S(2)}) async-start(), calls=%async_computation.1 | async-start | bytes 2228224 | tf_op jit(solution)/shard_map/all_gather | solution.py:25
  465.6 546.5 %all-gather.18.cloned.1.call-start = ((), (), s32[]{:S(2)}) async-start(), calls=%async_computation.3 | async-start | bytes 4456448 | tf_op jit(solution)/shard_map/all_gather | solution.py:25
  936.7 152.8 %all-gather.20.cloned.1.call-start = ((), (), s32[]{:S(2)}) async-start(), calls=%async_computation.4 | async-start | bytes 4456448 | tf_op jit(solution)/shard_map/all_gather | solution.py:25
  936.8 486.4 %copy-start.106 = (f32[256]{0:T(256)}, f32[256]{0:T(256)S(1)}, u32[]{:S(2)}) copy-start(f32[256]{0:T(256)S(1)} %compare_convert_fusion.6) | copy-start | bytes 3076
  937.2 798.6 %all-gather.16.cloned.1.call-start = ((), (), s32[]{:S(2)}) async-start(), calls=%async_computation.2 | async-start | bytes 2228224 | tf_op jit(solution)/shard_map/all_gather | solution.py:25
  956.7 876.3 %all-gather.22.cloned.1.call-start = ((), (), s32[]{:S(2)}) async-start(), calls=%async_computation.5 | async-start | bytes 4456448 | tf_op jit(solution)/shard_map/all_gather | solution.py:25
  1092.1 318.4 %copy-start.91 = (f32[512]{0:T(512)S(1)}, f32[512]{0:T(512)}, u32[]{:S(2)}) copy-start(f32[512]{0:T(512)} %get-tuple-element.2774) | copy-start | bytes 6148
  1092.2 318.4 %copy-start.103 = (f32[2,128]{1,0:T(2,128)S(1)}, f32[2,128]{1,0:T(2,128)}, u32[]{:S(2)}) copy-start(f32[2,128]{1,0:T(2,128)} %copy-done.102) | copy-start | bytes 3076
  1092.2 318.4 %copy-start.105 = (f32[2,128]{1,0:T(2,128)S(1)}, f32[2,128]{1,0:T(2,128)}, u32[]{:S(2)}) copy-start(f32[2,128]{1,0:T(2,128)} %copy-done.104) | copy-start | bytes 3076
  1092.2 320.1 %slice-start.3 = ((f32[2759168]{0:T(1024)}), f32[1024]{0:T(1024)S(1)}, s32[]{:S(2)}) async-start(f32[2759168]{0:T(1024)} %all-reduce.5.cloned.1.call-done), calls=%async_computation.12 | async-start | bytes 8192 | tf_op jit(solution)/shard_map/slice | solution.py:62
  1092.2 321.8 %copy-start.96 = (f32[256]{0:T(256)S(1)}, f32[256]{0:T(256)}, u32[]{:S(2)}) copy-start(f32[256]{0:T(256)} %copy-done.95) | copy-start | bytes 3076
  1092.2 321.8 %copy-start.100 = (f32[256]{0:T(256)S(1)}, f32[256]{0:T(256)}, u32[]{:S(2)}) copy-start(f32[256]{0:T(256)} %get-tuple-element.2798) | copy-start | bytes 3076
  1092.2 322.4 %slice-start.4 = ((f32[2759168]{0:T(1024)}), f32[2048]{0:T(1024)S(1)}, s32[]{:S(2)}) async-start(f32[2759168]{0:T(1024)} %all-reduce.5.cloned.1.call-done), calls=%async_computation.13 | async-start | bytes 16384 | tf_op jit(solution)/shard_map/slice | solution.py:62
  1092.2 322.4 %copy-start.77 = (f32[512]{0:T(512)S(1)}, f32[512]{0:T(512)}, u32[]{:S(2)}) copy-start(f32[512]{0:T(512)} %get-tuple-element.2773) | copy-start | bytes 6148
  1092.2 322.4 %copy-start.84 = (f32[512]{0:T(512)S(1)}, f32[512]{0:T(512)}, u32[]{:S(2)}) copy-start(f32[512]{0:T(512)} %get-tuple-element.2772) | copy-start | bytes 6148
  1721.6 188.9 %all-gather.24.cloned.1.call-start = ((), (), s32[]{:S(2)}) async-start(), calls=%async_computation.6 | async-start | bytes 4456448 | tf_op jit(solution)/shard_map/all_gather | solution.py:25
  1722.4 1547.8 %all-reduce.7.cloned.1.call-start = ((), (), s32[]{:S(2)}) async-start(), calls=%async_computation.8 | async-start | bytes 22077440
  1950.3 814.0 %copy-start.81 = (f32[512]{0:T(512)S(1)}, f32[512]{0:T(512)}, u32[]{:S(2)}) copy-start(f32[512]{0:T(512)} %copy-done.79) | copy-start | bytes 6148
  1950.3 814.0 %copy-start.88 = (f32[512]{0:T(512)S(1)}, f32[512]{0:T(512)}, u32[]{:S(2)}) copy-start(f32[512]{0:T(512)} %copy-done.86) | copy-start | bytes 6148
  1950.3 814.0 %copy-start.92 = (f32[512]{0:T(512)S(1)}, f32[512]{0:T(512)}, u32[]{:S(2)}) copy-start(f32[512]{0:T(512)} %get-tuple-element.2774) | copy-start | bytes 6148
  1950.3 814.0 %copy-start.97 = (f32[256]{0:T(256)S(1)}, f32[256]{0:T(256)}, u32[]{:S(2)}) copy-start(f32[256]{0:T(256)} %copy-done.95) | copy-start | bytes 3076
  1950.3 814.0 %copy-start.101 = (f32[256]{0:T(256)S(1)}, f32[256]{0:T(256)}, u32[]{:S(2)}) copy-start(f32[256]{0:T(256)} %get-tuple-element.2798) | copy-start | bytes 3076
  (129 other events, 11171.3 us)
Sparse Core Ops, SparseCore 0:
  16.0 219.5 all-reduce.4
  240.0 59.9 all-gather.11
  465.7 60.0 all-gather.13
  936.8 75.2 all-gather.17
  1014.7 74.6 all-gather.19
  1092.1 59.4 all-gather.15
  1721.8 111.2 all-gather.21
  1835.8 74.6 all-gather.23
  3057.6 212.6 all-reduce.6
where the time goes:
time: 3330 us; the launch traced here: 3320 us
  matrix products  1040 us (31%)
  other arithmetic  1020 us (31%)
  waiting for transfers between devices  730 us (22%)
  local copies, waits for them, and re-layouts  450 us (14%)
  blocking collectives  39.6 us (1%)
    unnamed x11, waiting for transfers between devices  426 us
    dot_general x8, matrix products, block_apply(): jnp.einsum('hnt,hn->th', up_im, mixed_im, precision=highest)  422 us
    dot_general x8, matrix products, block_apply(): jnp.einsum('hnt,hn->th', up_re, mixed_re, precision=highest)  416 us
    all_gather x7, waiting for transfers between devices, entering(): gathered = jax.tree.map(lambda a: lax.all_gather(a, axis), part)  303 us
    mul x4, other arithmetic, powers(): magnitude * jnp.sin(arg_im[:, :, None] * levels)  263 us
    gather x4, local copies, waits for them, and re-layouts, block_apply(): toeplitz = kernel[:, jnp.clip(gap, 0, width - 1)] * same[None]  229 us
    scatter-add x2, other arithmetic, block_apply(): toeplitz = kernel[:, jnp.clip(gap, 0, width - 1)] * same[None]  209 us
    reduce_sum x1, other arithmetic, powers(): magnitude = jnp.exp(arg_re[:, :, None] * levels)  189 us
  transfers between devices with their start and end apart: 9, of which 6 were waited for; matrix products, arithmetic and copies ran while one was open for 41% of the time, Pallas kernels for 0%

commit v1 on v0

v1 whole, which is shorter than its diff:
```python
from functools import partial
import jax, jax.numpy as jnp
from jax import lax
from jax.experimental import pallas as pl
from jax.experimental.pallas import tpu as pltpu
from jax.sharding import PartitionSpec as P

D = 512
NSTATE = 64
CH = 128
DOCS = 4
G = 1024
FF = 2048


norm_eps = 1e-05
root_half = 0.7071067811865476
inv_root_two_pi = 0.3989422804014327


f32 = jnp.float32
bf16 = jnp.bfloat16

def split(v):
    hi = v.astype(bf16)
    return hi, (v - hi.astype(f32)).astype(bf16)

def dot3(a, b, ca, cb):
    ah, al = a
    bh, bl = b
    lhs = jnp.concatenate([ah, ah, al], axis=ca)
    rhs = jnp.concatenate([bh, bl, bh], axis=cb)
    return lax.dot_general(lhs, rhs, (((ca,), (cb,)), ((), ())), preferred_element_type=f32)

def swap(v):
    return pltpu.roll(v, NSTATE, 1)

def twist(table, re, im):
    return re * table + im * swap(table)

def ladder(prm, order):
    sub = lax.broadcasted_iota(jnp.int32, (8, 2 * NSTATE), 0)
    lane = lax.broadcasted_iota(jnp.int32, (8, 2 * NSTATE), 1)
    power = sub if order == 1 else 7 - sub
    table = jnp.where(lane < NSTATE, 1.0, 0.0).astype(f32)
    for bit in range(3):
        table = jnp.where((power >> bit) & 1 == 1, twist(table, prm[2 * bit:2 * bit + 1], prm[2 * bit + 1:2 * bit + 2]), table)
    for bit in range(3, 7):
        more = twist(table, prm[2 * bit:2 * bit + 1], prm[2 * bit + 1:2 * bit + 2])
        table = jnp.concatenate([table, more] if order == 1 else [more, table], axis=0)
    return table

def toeplitz(prm, table):
    wrow = jnp.broadcast_to(prm[16:17], (8, 2 * NSTATE))
    taps = dot3(split(wrow), split(table), 1, 1)
    wide = jnp.broadcast_to(taps[0:1], (CH, CH))
    wide = pltpu.roll(wide, 0, 1, stride=1, stride_axis=0)
    row = lax.broadcasted_iota(jnp.int32, (CH, CH), 0)
    col = lax.broadcasted_iota(jnp.int32, (CH, CH), 1)
    return jnp.where(col >= row, wide, 0.0)

def label_at(ends, pos):
    total = jnp.zeros_like(pos)
    for k in range(DOCS):
        total = total + (pos >= ends[k]).astype(jnp.int32)
    return total

def make_masks(ends_ref, masks_ref, nck):
    ends = [ends_ref[k] for k in range(DOCS)]
    row = lax.broadcasted_iota(jnp.int32, (nck, CH), 0)
    lane = lax.broadcasted_iota(jnp.int32, (nck, CH), 1)
    base = row * CH
    label = label_at(ends, base + lane)
    prev = jnp.where(base == 0, -1, label_at(ends, base - 1))
    last = label_at(ends, base + CH - 1)
    for k in range(DOCS):
        masks_ref[k] = (label == k).astype(f32)
    masks_ref[DOCS] = (label == prev).astype(f32)
    masks_ref[DOCS + 1] = (label == last).astype(f32)

def keep_of(ends_ref, c):
    first = jnp.int32(0)
    second = jnp.int32(0)
    for k in range(DOCS):
        first = first + (c * CH - 1 >= ends_ref[k]).astype(jnp.int32)
        second = second + (c * CH + CH - 1 >= ends_ref[k]).astype(jnp.int32)
    return jnp.where((c > 0) & (first == second), 1.0, 0.0).astype(f32)

def masked_rows(v, masks_ref):
    return jnp.concatenate([v * masks_ref[k] for k in range(DOCS)], axis=0)

def fold_rows(v, masks_ref, nck):
    total = v[:nck] * masks_ref[0]
    for k in range(1, DOCS):
        total = total + v[k * nck:(k + 1) * nck] * masks_ref[k]
    return total

def fwd_body(nck, nch, ends_ref, prm_ref, x_ref, y_ref, prior_ref, masks_ref, end_ref, gt_ref):
    make_masks(ends_ref, masks_ref, nck)

    def one(h, _):
        prm = prm_ref[h]
        u = x_ref[pl.ds(h, nck, stride=nch), :] * prm[19:20] + prm[20:21]
        table = ladder(prm, 1)
        down = ladder(prm, -1)
        gt_ref[h] = twist(table, prm[17:18], prm[18:19])
        local = dot3(split(masked_rows(u, masks_ref)), split(toeplitz(prm, table)), 1, 0)
        y_ref[pl.ds(h, nck, stride=nch), :] = fold_rows(local, masks_ref, nck) + prm[21:22] * u
        end_ref[pl.ds(h, nck, stride=nch), :] = dot3(split(u * masks_ref[DOCS + 1]), split(down), 1, 0)
        return 0

    lax.fori_loop(0, nch, one, 0)
    full_re = prm_ref[:, 14, :]
    full_im = prm_ref[:, 15, :]

    def step(c, state):
        at = pl.ds(pl.multiple_of(c * nch, 8), nch)
        prior_ref[at, :] = state
        return keep_of(ends_ref, c) * twist(state, full_re, full_im) + end_ref[at, :]

    lax.fori_loop(0, nck, step, jnp.zeros((nch, 2 * NSTATE), f32))

    def two(h, _):
        prior = prior_ref[pl.ds(h, nck, stride=nch), :]
        carried = dot3(split(prior), split(gt_ref[h]), 1, 1) * masks_ref[DOCS]
        y_ref[pl.ds(h, nck, stride=nch), :] += carried
        return 0

    lax.fori_loop(0, nch, two, 0)

def ssm_forward(ends, prm, x, nck, nch):
    vm = pl.BlockSpec(memory_space=pltpu.VMEM)
    return pl.pallas_call(
        partial(fwd_body, nck, nch),
        out_shape=(jax.ShapeDtypeStruct((nck * nch, CH), f32), jax.ShapeDtypeStruct((nck * nch, 2 * NSTATE), f32)),
        in_specs=[pl.BlockSpec(memory_space=pltpu.SMEM), vm, vm],
        out_specs=(vm, vm),
        scratch_shapes=[
            pltpu.VMEM((DOCS + 2, nck, CH), f32),
            pltpu.VMEM((nck * nch, 2 * NSTATE), f32),
            pltpu.VMEM((nch, CH, 2 * NSTATE), f32),
        ],
        name="state_forward",
    )(ends, prm, x)

def bwd_body(nck, nch, ends_ref, prm_ref, x_ref, g_ref, prior_ref, dx_ref, rows_ref, masks_ref, lead_ref, adj_ref, table_ref):
    make_masks(ends_ref, masks_ref, nck)

    def one(h, _):
        prm = prm_ref[h]
        g = g_ref[pl.ds(h, nck, stride=nch), :]
        table = ladder(prm, 1)
        table_ref[h] = table
        gt = twist(table, prm[17:18], prm[18:19])
        lead_ref[pl.ds(h, nck, stride=nch), :] = dot3(split(g * masks_ref[DOCS]), split(gt), 1, 0)
        return 0

    lax.fori_loop(0, nch, one, 0)
    full_re = prm_ref[:, 14, :]
    full_im = prm_ref[:, 15, :]
    zero = jnp.zeros((nch, 2 * NSTATE), f32)

    def step(k, carry):
        adjoint, same, cross = carry
        c = nck - 1 - k
        at = pl.ds(pl.multiple_of(c * nch, 8), nch)
        adj_ref[at, :] = adjoint
        keep = keep_of(ends_ref, c)
        prior = prior_ref[at, :]
        same = same + keep * adjoint * prior
        cross = cross + keep * adjoint * swap(prior)
        adjoint = lead_ref[at, :] + keep * (full_re * adjoint - full_im * swap(adjoint))
        return adjoint, same, cross

    _, same, cross = lax.fori_loop(0, nck, step, (zero, zero, zero))
    rows_ref[8] = same
    rows_ref[9] = cross
    for k in range(13, 16):
        rows_ref[k] = zero
    row = lax.broadcasted_iota(jnp.int32, (CH, CH), 0)
    col = lax.broadcasted_iota(jnp.int32, (CH, CH), 1)
    flip = (row + col == CH - 1).astype(f32).astype(bf16)

    def two(h, _):
        prm = prm_ref[h]
        x = x_ref[pl.ds(h, nck, stride=nch), :]
        u = x * prm[19:20] + prm[20:21]
        g = g_ref[pl.ds(h, nck, stride=nch), :]
        table = table_ref[h]
        down = ladder(prm, -1)
        mat = split(toeplitz(prm, table))
        gm = split(masked_rows(g, masks_ref))
        um = split(masked_rows(u, masks_ref))
        adjoint = split(adj_ref[pl.ds(h, nck, stride=nch), :])
        prior = split(prior_ref[pl.ds(h, nck, stride=nch), :])
        du = fold_rows(dot3(gm, mat, 1, 1), masks_ref, nck)
        du = du + dot3(adjoint, split(down), 1, 1) * masks_ref[DOCS + 1]
        du = du + prm[21:22] * g
        dx_ref[pl.ds(h, nck, stride=nch), :] = du
        flipped = [jnp.dot(v, flip, preferred_element_type=f32).astype(bf16) for v in um]
        square = dot3(flipped, gm, 0, 0)
        square = jnp.where(row + col >= CH - 1, square, 0.0)
        square = pltpu.roll(square, 1, 1, stride=1, stride_axis=0)
        taps = jnp.sum(square, axis=0, keepdims=True)
        place = lax.broadcasted_iota(jnp.int32, (8, CH), 1).astype(f32)
        sub = lax.broadcasted_iota(jnp.int32, (8, CH), 0)
        both = jnp.where(sub == 0, 1.0, jnp.where(sub == 1, place, 0.0)) * taps
        both = dot3(split(both), split(table), 1, 0)
        rows_ref[0, pl.ds(h, 1), :] = both[0:1]
        rows_ref[1, pl.ds(h, 1), :] = both[1:2]
        late = row.astype(f32)
        dgt = dot3(split(g * masks_ref[DOCS]), prior, 0, 0)
        one = dgt * table
        two = dgt * swap(table)
        rows_ref[2, pl.ds(h, 1), :] = jnp.sum(one, axis=0, keepdims=True)
        rows_ref[3, pl.ds(h, 1), :] = jnp.sum(two, axis=0, keepdims=True)
        rows_ref[4, pl.ds(h, 1), :] = jnp.sum(one * late, axis=0, keepdims=True)
        rows_ref[5, pl.ds(h, 1), :] = jnp.sum(two * late, axis=0, keepdims=True)
        ddown = dot3(split(u * masks_ref[DOCS + 1]), adjoint, 0, 0) * ((CH - 1) - late)
        rows_ref[6, pl.ds(h, 1), :] = jnp.sum(ddown * down, axis=0, keepdims=True)
        rows_ref[7, pl.ds(h, 1), :] = jnp.sum(ddown * swap(down), axis=0, keepdims=True)
        rows_ref[10, pl.ds(h, 1), :] = jnp.sum(g * u, axis=0, keepdims=True)
        rows_ref[11, pl.ds(h, 1), :] = jnp.sum(du * x, axis=0, keepdims=True)
        rows_ref[12, pl.ds(h, 1), :] = jnp.sum(du, axis=0, keepdims=True)
        return 0

    lax.fori_loop(0, nch, two, 0)

def ssm_backward(ends, prm, x, g, prior, nck, nch):
    vm = pl.BlockSpec(memory_space=pltpu.VMEM)
    return pl.pallas_call(
        partial(bwd_body, nck, nch),
        out_shape=(jax.ShapeDtypeStruct((nck * nch, CH), f32), jax.ShapeDtypeStruct((16, nch, 2 * NSTATE), f32)),
        in_specs=[pl.BlockSpec(memory_space=pltpu.SMEM), vm, vm, vm, vm],
        out_specs=(vm, vm),
        scratch_shapes=[
            pltpu.VMEM((DOCS + 2, nck, CH), f32),
            pltpu.VMEM((nck * nch, 2 * NSTATE), f32),
            pltpu.VMEM((nck * nch, 2 * NSTATE), f32),
            pltpu.VMEM((nch, CH, 2 * NSTATE), f32),
        ],
        name="state_backward",
    )(ends, prm, x, g, prior)

def mixing(step_log, decay_log, frequency, out_real, out_imag):
    delta = jnp.exp(step_log)[:, None]
    rate_re = -jnp.exp(decay_log)
    arg_re, arg_im = delta * rate_re, delta * frequency
    magnitude = jnp.exp(arg_re)
    pole_re = magnitude * jnp.cos(arg_im) - 1.0
    pole_im = magnitude * jnp.sin(arg_im)
    denom = rate_re * rate_re + frequency * frequency
    ratio_re = (pole_re * rate_re + pole_im * frequency) / denom
    ratio_im = (pole_im * rate_re - pole_re * frequency) / denom
    mix_re = out_real * ratio_re - out_imag * ratio_im
    mix_im = out_real * ratio_im + out_imag * ratio_re
    return arg_re, arg_im, mix_re, mix_im

def pair(left, right):
    return jnp.concatenate([left, right], axis=-1)

def mode_rows(arg_re, arg_im, mix_re, mix_im, gain, bias, skip):
    nch = arg_re.shape[0]
    scale = jnp.asarray([2.0**b for b in range(8)], f32)[None, :, None]
    magnitude = jnp.exp(arg_re[:, None] * scale)
    p_re = magnitude * jnp.cos(arg_im[:, None] * scale)
    p_im = magnitude * jnp.sin(arg_im[:, None] * scale)
    powers = jnp.stack([pair(p_re, p_re), pair(-p_im, p_im)], axis=2).reshape(nch, 16, 2 * NSTATE)
    c_re = mix_re * p_re[:, 0] - mix_im * p_im[:, 0]
    c_im = mix_re * p_im[:, 0] + mix_im * p_re[:, 0]
    flat = lambda v: jnp.broadcast_to(v[:, None], (nch, 2 * NSTATE))
    rest = jnp.stack([pair(mix_re, -mix_im), pair(c_re, -c_re), pair(-c_im, -c_im), flat(gain), flat(bias), flat(skip), flat(0 * gain), flat(0 * gain)], axis=1)
    return jnp.concatenate([powers, rest], axis=1)

def mode_grads(rows, arg_re, arg_im, mix_re, mix_im):
    lo, hi = rows[:, :, :NSTATE], rows[:, :, NSTATE:]
    magnitude = jnp.exp(arg_re)
    p_re, p_im = magnitude * jnp.cos(arg_im), magnitude * jnp.sin(arg_im)
    magnitude = jnp.exp(arg_re * CH)
    f_re, f_im = magnitude * jnp.cos(arg_im * CH), magnitude * jnp.sin(arg_im * CH)
    a_re, a_im = lo[2] - hi[2], -(hi[3] + lo[3])
    b_re, b_im = lo[4] - hi[4], -(hi[5] + lo[5])
    b_re, b_im = b_re + a_re, b_im + a_im
    w_re = lo[0] + p_re * a_re + p_im * a_im
    w_im = -hi[0] + p_re * a_im - p_im * a_re
    v_re = lo[1] + p_re * b_re + p_im * b_im
    v_im = -hi[1] + p_re * b_im - p_im * b_re
    g_re = mix_re * v_re + mix_im * v_im
    g_im = mix_re * v_im - mix_im * v_re
    g_re = g_re + lo[6] + hi[6]
    g_im = g_im + hi[7] - lo[7]
    d_re, d_im = lo[8] + hi[8], hi[9] - lo[9]
    g_re = g_re + CH * (f_re * d_re + f_im * d_im)
    g_im = g_im + CH * (f_re * d_im - f_im * d_re)
    return g_re, g_im, w_re, w_im


def unpack(flat):
    layout = [
        ("norm_gain", (D,)),
        ("norm_bias", (D,)),
        ("step_log", (D,)),
        ("skip_gain", (D,)),
        ("decay_log", (D, NSTATE)),
        ("frequency", (D, NSTATE)),
        ("out_real", (D, NSTATE)),
        ("out_imag", (D, NSTATE)),
        ("gate_weight", (D, G)),
        ("gate_bias", (G,)),
        ("second_gain", (D,)),
        ("second_bias", (D,)),
        ("expand_weight", (D, FF)),
        ("expand_bias", (FF,)),
        ("reduce_weight", (FF, D)),
        ("reduce_bias", (D,)),
    ]
    params = {}
    offset = 0
    for name, shape in layout:
        count = 1
        for extent in shape:
            count = count * extent
        params[name] = flat[offset : offset + count].reshape(shape)
        offset = offset + count
    return params


def gelu(values):
    return 0.5 * values * (1.0 + lax.erf(values * root_half))


def gelu_slope(values):
    return (
        0.5 * (1.0 + lax.erf(values * root_half))
        + values * jnp.exp(-0.5 * values * values) * inv_root_two_pi
    )


def normalize(values):
    center = values - jnp.mean(values, axis=-1, keepdims=True)
    scale = lax.rsqrt(jnp.mean(center * center, axis=-1, keepdims=True) + norm_eps)
    return (center * scale, scale)


def norm_back(d_hat, hat, scale):
    return scale * (
        d_hat
        - jnp.mean(d_hat, axis=-1, keepdims=True)
        - hat * jnp.mean(d_hat * hat, axis=-1, keepdims=True)
    )


def to_channels(rows):
    seq = lax.axis_size("seq")
    parts = rows.shape[0] // CH
    turned = rows.reshape(parts, CH, seq, D // seq).transpose(2, 0, 3, 1)
    return lax.all_to_all(turned, "seq", 0, 0).reshape(-1, CH)


def to_tokens(rows, group):
    seq = lax.axis_size("seq")
    turned = lax.all_to_all(rows.reshape(seq, group // CH, D // seq, CH), "seq", 0, 0)
    return turned.transpose(1, 3, 0, 2).reshape(group, D)


def per_device(inputs, cotangent, lengths, master, first_moment, second_moment):
    seq, batch = lax.axis_size("seq"), lax.axis_size("batch")
    devices = seq * batch
    share = master.shape[0]
    padded = -(-share // 1024) * 1024
    full = lax.all_gather(jnp.pad(master, (0, padded - share)), ("seq", "batch"), axis=0, tiled=True)
    full = full.reshape(devices, padded)[:, :share].reshape(-1)
    params = unpack(full)
    group = inputs.shape[1]
    nch, nck = D // seq, seq * group // CH
    rows = inputs[0].astype(jnp.float32)
    ends = jnp.cumsum(lengths[0])
    offset = lax.axis_index("seq") * group
    where = offset + jnp.arange(group, dtype=jnp.int32)
    labels = jnp.sum((where[:, None] >= ends[None, :]).astype(jnp.int32), axis=1)
    valid = (labels < DOCS - 1).astype(jnp.float32)
    first_hat, first_scale = normalize(rows)
    mine = lambda v: lax.dynamic_slice_in_dim(v, lax.axis_index("seq") * nch, nch, 0)
    names = ("step_log", "decay_log", "frequency", "out_real", "out_imag")
    modes, modes_pull = jax.vjp(mixing, *(mine(params[name]) for name in names))
    prm = mode_rows(*modes, *(mine(params[name]) for name in ("norm_gain", "norm_bias", "skip_gain")))
    hats = to_channels(first_hat)
    outs, prior = ssm_forward(ends, prm, hats, nck, nch)
    response = to_tokens(outs, group)
    hidden_low = gelu(response).astype(jnp.bfloat16)
    gate_low = params["gate_weight"].astype(jnp.bfloat16)
    opened = jnp.dot(hidden_low, gate_low, preferred_element_type=jnp.float32) + params["gate_bias"]
    linear = opened[:, :D]
    gating = jax.nn.sigmoid(opened[:, D:])
    mid = rows + linear * gating
    second_hat, second_scale = normalize(mid)
    normed_low = (second_hat * params["second_gain"] + params["second_bias"]).astype(jnp.bfloat16)
    expand_low = params["expand_weight"].astype(jnp.bfloat16)
    lifted = (
        jnp.dot(normed_low, expand_low, preferred_element_type=jnp.float32) + params["expand_bias"]
    )
    active_low = gelu(lifted).astype(jnp.bfloat16)
    reduce_low = params["reduce_weight"].astype(jnp.bfloat16)
    result = (
        mid
        + jnp.dot(active_low, reduce_low, preferred_element_type=jnp.float32)
        + params["reduce_bias"]
    )
    output = result.astype(jnp.bfloat16)[None]
    back = cotangent[0].astype(jnp.float32) * valid[:, None]
    back_low = back.astype(jnp.bfloat16)
    g_reduce_w = jnp.einsum("tf,td->fd", active_low, back_low, preferred_element_type=jnp.float32)
    g_reduce_b = jnp.sum(back, axis=0)
    d_active = jnp.einsum("td,fd->tf", back_low, reduce_low, preferred_element_type=jnp.float32)
    d_lifted = (d_active * gelu_slope(lifted)).astype(jnp.bfloat16)
    g_expand_w = jnp.einsum("td,tf->df", normed_low, d_lifted, preferred_element_type=jnp.float32)
    g_expand_b = jnp.sum(d_lifted.astype(jnp.float32), axis=0)
    d_normed = jnp.einsum("tf,df->td", d_lifted, expand_low, preferred_element_type=jnp.float32)
    g_second_gain = jnp.sum(d_normed * second_hat, axis=0)
    g_second_bias = jnp.sum(d_normed, axis=0)
    d_mid = back + norm_back(d_normed * params["second_gain"], second_hat, second_scale)
    d_linear = d_mid * gating
    d_gating = d_mid * linear * gating * (1.0 - gating)
    d_opened = jnp.concatenate([d_linear, d_gating], axis=1).astype(jnp.bfloat16)
    g_gate_w = jnp.einsum("td,tg->dg", hidden_low, d_opened, preferred_element_type=jnp.float32)
    g_gate_b = jnp.sum(d_opened.astype(jnp.float32), axis=0)
    d_hidden = jnp.einsum("tg,dg->td", d_opened, gate_low, preferred_element_type=jnp.float32)
    d_response = d_hidden * gelu_slope(response)
    d_outs = to_channels(d_response)
    d_signals, sums = ssm_backward(ends, prm, hats, d_outs, prior, nck, nch)
    d_signal = to_tokens(d_signals, group)
    d_modes = modes_pull(mode_grads(sums, *modes))
    d_rows = d_mid + norm_back(d_signal * params["norm_gain"], first_hat, first_scale)
    lane_sums = jnp.sum(sums[10:13], axis=-1)

    def spread(v):
        whole = jnp.zeros((D,) + v.shape[1:], jnp.float32)
        return lax.dynamic_update_slice_in_dim(whole, v, lax.axis_index("seq") * nch, 0)

    parts = [
        spread(lane_sums[1]),
        spread(lane_sums[2]),
        spread(d_modes[0]),
        spread(lane_sums[0]),
        spread(d_modes[1]),
        spread(d_modes[2]),
        spread(d_modes[3]),
        spread(d_modes[4]),
        g_gate_w,
        g_gate_b,
        g_second_gain,
        g_second_bias,
        g_expand_w,
        g_expand_b,
        g_reduce_w,
        g_reduce_b,
    ]
    packed = jnp.concatenate([item.reshape(-1) for item in parts])
    packed = jnp.pad(packed, (0, full.shape[0] - packed.shape[0]))
    packed = jnp.pad(packed.reshape(devices, share), ((0, 0), (0, padded - share)))
    shard = lax.psum_scatter(packed.reshape(devices, padded // 128, 128), ("seq", "batch"), scatter_dimension=0)
    shard = shard.reshape(-1)[:share]
    total = lax.psum(jnp.sum(shard * shard), ("seq", "batch"))
    grad_norm = jnp.sqrt(total)
    factor = jnp.minimum(1.0, 1.0 / (grad_norm + 1e-06))
    clipped = shard * factor
    first_new = 0.9 * first_moment + 0.1 * clipped
    second_new = 0.999 * second_moment + 0.001 * clipped * clipped
    first_hat_new = first_new / (1.0 - 0.9**10)
    second_hat_new = second_new / (1.0 - 0.999**10)
    update = -0.05 * (first_hat_new / (jnp.sqrt(second_hat_new) + 1e-08) + 0.1 * master)
    return (output, d_rows[None], shard, update, first_new, second_new, grad_norm)


def solution(mesh):
    placed = (
        P("batch", "seq", None),
        P("batch", "seq", None),
        P("batch", None),
        P(("seq", "batch")),
        P(("seq", "batch")),
        P(("seq", "batch")),
    )
    return jax.shard_map(
        per_device,
        mesh=mesh,
        in_specs=placed,
        out_specs=(
            P("batch", "seq", None),
            P("batch", "seq", None),
            P(("seq", "batch")),
            P(("seq", "batch")),
            P(("seq", "batch")),
            P(("seq", "batch")),
            P(),
        ),
        check_vma=False,
    )
```

time: 3330 us -> 629 us (0.19)
  the two profiles are of different devices: /device:TPU:0 before, /device:TPU:12 now
where the time goes in v1:
time: 629 us; the launch traced here: 617 us
  local copies, waits for them, and re-layouts  206 us (33%)
  waiting for transfers between devices  160 us (25%)
  Pallas kernels  104 us (17%)
  blocking collectives  64.2 us (10%)
  starting transfers between devices  24.3 us (4%)
  other arithmetic  21.8 us (3%)
  matrix products  20.1 us (3%)
  between operations  17.2 us (3%)
    slice x12, local copies, waits for them, and re-layouts, unpack(): params[name] = flat[offset:offset + count].reshape(shape)  79.2 us
    unnamed x3, waiting for transfers between devices  73.6 us
    psum x1, blocking collectives, per_device(): total = lax.psum(jnp.sum(shard * shard), ('seq', 'batch'))  64.2 us
    all_gather x1, waiting for transfers between devices, per_device(): lax.all_gather(jnp.pad(master, (0, padded - share)), ('seq', 'batch'), ax...  63.8 us
    pallas_call x1, Pallas kernels, ssm_backward(): pl.pallas_call(partial(bwd_body, nck, nch), out_shape=(jax.ShapeDtypeStru...  63.6 us
    unnamed x111, local copies, waits for them, and re-layouts  53.2 us
    pallas_call x1, Pallas kernels, ssm_forward(): pl.pallas_call(partial(fwd_body, nck, nch), out_shape=(jax.ShapeDtypeStru...  39.9 us
    reshape x2, local copies, waits for them, and re-layouts, per_device(): full = full.reshape(devices, padded)[:, :share].reshape(-1)  24.5 us
  transfers between devices with their start and end apart: 6, of which 4 were waited for; matrix products, arithmetic and copies ran while one was open for 18% of the time, Pallas kernels for 0%

profile of v1, /device:TPU:12, one launch (start us, length us, event | category | flops | bytes accessed | tf_op | source)
XLA Modules:
  0.0 617.2 jit_solution(11562582831171363566)
XLA Ops:
  15.4 7.2 %all-to-all-start = ((f32[16,2,32,128]{3,1,2,0:T(2,128)}), f32[16,2,32,128]{3,1,2,0:T(2,128)S(1)}, u32[]{:S(2)}, u32[]{:S(2)}) async-start(f32[16,2,32,128]{3,1,2,0:T(2,128)} %fusion.36), calls=%async_computation | async-start | bytes 1048576 | tf_op jit(solution)/shard_map/all_to_all | solution.py:357
  23.9 19.8 %all-to-all-done = f32[16,2,32,128]{3,1,2,0:T(2,128)S(1)} async-done(((f32[16,2,32,128]{3,1,2,0:T(2,128)}), f32[16,2,32,128]{3,1,2,0:T(2,128)S(1)}, u32[]{:S(2)}, u32[]{:S(2)}) %all-to-all-start) | async-done | bytes 524320 | tf_op jit(solution)/shard_map/all_to_all | solution.py:357
  44.6 63.8 %all-gather.2.cloned.1.call-done = f32[2785280]{0:T(1024)} async-done(((f32[87040]{0:T(1024)}), f32[2785280]{0:T(1024)}) %all-gather.2.cloned.1.call-update) | async-done | bytes 11141136 | tf_op jit(solution)/shard_map/all_gather | solution.py:371
  108.4 8.9 %reshape.258 = f32[32,87040]{1,0:T(8,128)} reshape(f32[2785280]{0:T(1024)} %all-gather.2.cloned.1.call-done) | data formatting | bytes 22282240 | tf_op jit(solution)/shard_map/reshape | solution.py:372
  117.2 8.9 %slice.228 = f32[32,86224]{1,0:T(8,128)} slice(f32[32,87040]{1,0:T(8,128)} %reshape.258), slice={[0:32], [0:86224]} | slice | bytes 22073344 | tf_op jit(solution)/shard_map/slice | solution.py:372
  126.1 15.6 %reshape.259 = f32[2759168]{0:T(1024)} reshape(f32[32,86224]{1,0:T(8,128)} %slice.228) | data formatting | bytes 22073344 | tf_op jit(solution)/shard_map/reshape | solution.py:372
  143.1 16.5 %slice.180 = f32[43112,64]{1,0:T(8,128)} reshape(f32[2759168]{0:T(1024)} %reshape.259) | data formatting | bytes 22073344 | tf_op jit(solution)/shard_map/slice | solution.py:323
  165.4 39.9 %state_forward.1 = (f32[1024,128]{1,0:T(8,128)}, f32[1024,128]{1,0:T(8,128)}) custom-call(s32[4]{0:T(128)} %bitcast.287, f32[32,24,128]{2,1,0:T(8,128)} %concatenate.30.prm_ref, f32[1024,128]{1,0:T(8,128)} %bitcast.271), custom_call_target="tpu_custom_call" | custom-call | tf_op jit(solution)/shard_map/state_forward/pallas_call | solution.py:133
  205.4 5.0 all-to-all-start.1
  211.1 7.0 %slice.354 = bf16[32,86224]{1,0:T(8,128)(2,1)} slice(f32[32,87040]{1,0:T(8,128)} %reshape.258), slice={[0:32], [0:86224]} | slice | bytes 11036672 | tf_op jit(solution)/shard_map/slice | solution.py:372
  223.2 13.3 %reshape.281 = bf16[2759168]{0:T(1024)(128)(2,1)} reshape(bf16[32,86224]{1,0:T(8,128)(2,1)} %slice.354) | data formatting | bytes 11036672
  236.5 9.9 %slice.198 = bf16[5389,512]{1,0:T(8,128)(2,1)} reshape(bf16[2759168]{0:T(1024)(128)(2,1)} %reshape.281) | data formatting | bytes 11036672 | tf_op jit(solution)/shard_map/slice | solution.py:323
  254.7 3.9 multiply_convert_fusion
  258.6 4.0 convert_reduce_fusion
  268.8 6.9 %all-to-all-start.2 = ((f32[16,2,32,128]{3,1,2,0:T(2,128)}), f32[16,2,32,128]{3,1,2,0:T(2,128)}, u32[]{:S(2)}, u32[]{:S(2)}) async-start(f32[16,2,32,128]{3,1,2,0:T(2,128)} %bitcast.22), calls=%async_computation.2 | async-start | bytes 1048576 | tf_op jit(solution)/shard_map/all_to_all | solution.py:357
  291.5 63.6 %state_backward.1 = (f32[1024,128]{1,0:T(8,128)}, f32[16,32,128]{2,1,0:T(8,128)}) custom-call(s32[4]{0:T(128)} %bitcast.288, f32[32,24,128]{2,1,0:T(8,128)} %concatenate.30.prm_ref, f32[1024,128]{1,0:T(8,128)} %bitcast.272, f32[1024,128]{1,0:T(8,128)} %bitcast.275, f32[1024,128]{1,0:T(8,128)} %get-tuple-element.12.prior_ref), custom_call_target="tpu_custom_call" | custom-call | tf_op jit(solution)/shard_map/state_backward/pallas_call | solution.py:231
  375.3 4.4 constant_dynamic-update-slice_fusion.3
  383.3 14.5 %reshape.275 = f32[32,86224]{1,0:T(8,128)} reshape(f32[2759168]{0:T(1024)} %constant_dynamic-update-slice_fusion) | data formatting | bytes 22073344 | tf_op jit(solution)/shard_map/reshape | solution.py:460
  397.7 4.9 pad_bitcast_fusion
  402.6 6.1 copy.111
  410.9 5.1 all-to-all-start.3
  416.1 44.3 %slice.201 = f32[86224,32]{1,0:T(8,128)} reshape(f32[32,86224]{1,0:T(8,128)} %slice.228) | data formatting | bytes 22073344 | tf_op jit(solution)/shard_map/slice | solution.py:323
  466.3 73.5 %reduce-scatter.5.cloned.1.call-done = f32[1,680,128]{2,1,0:T(8,128)} async-done(((f32[32,680,128]{2,1,0:T(8,128)}), f32[1,680,128]{2,1,0:T(8,128)}) %reduce-scatter.5.cloned.1.call-update) | async-done | bytes 348176
  541.5 64.2 %psum.7 = f32[]{:T(128)} all-reduce(f32[]{:T(128)} %get-tuple-element.24), channel_id=1, replica_groups=mesh['seq'=16,'batch'=2] {'seq','batch'}, use_global_device_ids=true, to_apply=%region_20.21 | all-reduce | flops 1 | bytes 8 | tf_op jit(solution)/shard_map/psum | solution.py:463
  (214 shorter events, 88.9 us)
Async XLA Ops:
  7.2 101.2 %all-gather.2.cloned.1.call-start = ((), (), s32[]{:S(2)}) async-start(), calls=%async_computation.5 | async-start | bytes 11489280 | tf_op jit(solution)/shard_map/all_gather | solution.py:371
  10.3 106.9 %copy-start.6 = (f32[2,128,16,32]{1,0,3,2:T(2,128)}, f32[2,128,16,32]{1,0,3,2:T(2,128)S(1)}, u32[]{:S(2)}) copy-start(f32[2,128,16,32]{1,0,3,2:T(2,128)S(1)} %reshape.277) | copy-start | bytes 1572868
  15.4 28.3 %all-to-all-start = ((f32[16,2,32,128]{3,1,2,0:T(2,128)}), f32[16,2,32,128]{3,1,2,0:T(2,128)S(1)}, u32[]{:S(2)}, u32[]{:S(2)}) async-start(f32[16,2,32,128]{3,1,2,0:T(2,128)} %fusion.36), calls=%async_computation | async-start | bytes 1048576 | tf_op jit(solution)/shard_map/all_to_all | solution.py:357
  143.1 18.4 %copy-start.43 = (f32[8]{0:T(128)S(1)}, f32[8]{0:T(128)}, u32[]{:S(2)}) copy-start(f32[8]{0:T(128)} %constant.80.clone) | copy-start | bytes 100
  143.1 67.3 %copy-start.37 = (s32[4,1]{0,1:T(1,128)S(1)}, s32[4,1]{0,1:T(1,128)}, u32[]{:S(2)}) copy-start(s32[4,1]{0,1:T(1,128)} %reduce-window.8) | copy-start | bytes 52
  161.3 56.9 %copy-start.17 = (f32[512,64]{1,0:T(8,128)}, f32[512,64]{1,0:T(8,128)S(1)}, u32[]{:S(2)}) copy-start(f32[512,64]{1,0:T(8,128)S(1)} %get-tuple-element.58) | copy-start | bytes 393220
  161.3 56.9 %copy-start.18 = (f32[512,64]{1,0:T(8,128)}, f32[512,64]{1,0:T(8,128)S(1)}, u32[]{:S(2)}) copy-start(f32[512,64]{1,0:T(8,128)S(1)} %get-tuple-element.59) | copy-start | bytes 393220
  205.4 46.0 %all-to-all-start.1 = ((f32[16,2,32,128]{3,2,1,0:T(8,128)}), f32[16,2,32,128]{3,2,1,0:T(8,128)S(1)}, u32[]{:S(2)}, u32[]{:S(2)}) async-start(f32[16,2,32,128]{3,2,1,0:T(8,128)} %bitcast.282), calls=%async_computation.1 | async-start | bytes 1048576 | tf_op jit(solution)/shard_map/all_to_all | solution.py:362
  236.5 18.1 %slice-start.1 = ((f32[2759168]{0:T(1024)}), f32[2048]{0:T(1024)S(1)}, s32[]{:S(2)}) async-start(f32[2759168]{0:T(1024)} %reshape.259), calls=%async_computation.8 | async-start | bytes 16384 | tf_op jit(solution)/shard_map/slice | solution.py:323
  254.4 22.3 %copy-start.1 = (f32[256,512]{1,0:T(8,128)}, f32[256,512]{1,0:T(8,128)S(1)}, u32[]{:S(2)}) copy-start(f32[256,512]{1,0:T(8,128)S(1)} %get-tuple-element.43) | copy-start | bytes 1572868
  268.8 20.8 %all-to-all-start.2 = ((f32[16,2,32,128]{3,1,2,0:T(2,128)}), f32[16,2,32,128]{3,1,2,0:T(2,128)}, u32[]{:S(2)}, u32[]{:S(2)}) async-start(f32[16,2,32,128]{3,1,2,0:T(2,128)} %bitcast.22), calls=%async_computation.2 | async-start | bytes 1048576 | tf_op jit(solution)/shard_map/all_to_all | solution.py:357
  275.7 264.1 %reduce-scatter.5.cloned.1.call-start = ((), (), s32[]{:S(2)}) async-start(), calls=%async_computation.6 | async-start | bytes 11489280
  281.8 74.5 %copy-start.19 = (f32[32,64]{1,0:T(8,128)S(1)}, f32[32,64]{1,0:T(8,128)}, u32[]{:S(2)}) copy-start(f32[32,64]{1,0:T(8,128)} %get-tuple-element.49) | copy-start | bytes 24580
  281.8 74.6 %copy-start.20 = (f32[32,64]{1,0:T(8,128)S(1)}, f32[32,64]{1,0:T(8,128)}, u32[]{:S(2)}) copy-start(f32[32,64]{1,0:T(8,128)} %get-tuple-element.50) | copy-start | bytes 24580
  281.8 76.5 %copy-start.39 = (f32[32]{0:T(128)S(1)}, f32[32]{0:T(128)}, u32[]{:S(2)}) copy-start(f32[32]{0:T(128)} %copy-done.38) | copy-start | bytes 388
  287.0 92.7 %copy-start.36 = (f32[2048]{0:T(1024)S(1)}, f32[2048]{0:T(1024)}, u32[]{:S(2)}) copy-start(f32[2048]{0:T(1024)} %get-tuple-element.82) | copy-start | bytes 24580
  360.7 19.7 %copy-start = (f32[256,4,8,128]{3,1,2,0:T(4,128)S(1)}, f32[256,4,8,128]{3,1,2,0:T(4,128)}, u32[]{:S(2)}) copy-start(f32[256,4,8,128]{3,1,2,0:T(4,128)} %copy.110) | copy-start | bytes 12582916
  410.9 53.3 %all-to-all-start.3 = ((f32[16,2,32,128]{3,1,2,0:T(2,128)}), f32[16,2,32,128]{3,1,2,0:T(2,128)S(1)}, u32[]{:S(2)}, u32[]{:S(2)}) async-start(f32[16,2,32,128]{3,1,2,0:T(2,128)} %copy.101), calls=%async_computation.3 | async-start | bytes 1048576 | tf_op jit(solution)/shard_map/all_to_all | solution.py:362
  416.0 45.2 %copy-start.2 = (f32[256,512]{1,0:T(8,128)S(1)}, f32[256,512]{1,0:T(8,128)}, u32[]{:S(2)}) copy-start(f32[256,512]{1,0:T(8,128)} %copy-done.1) | copy-start | bytes 1572868
  416.0 45.2 %copy-start.9 = (bf16[256,2048]{1,0:T(8,128)(2,1)S(1)}, bf16[256,2048]{1,0:T(8,128)(2,1)}, u32[]{:S(2)}) copy-start(bf16[256,2048]{1,0:T(8,128)(2,1)} %get-tuple-element.79) | copy-start | bytes 3145732
  416.0 45.2 %copy-start.42 = (f32[512]{0:T(512)S(1)}, f32[512]{0:T(512)}, u32[]{:S(2)}) copy-start(f32[512]{0:T(512)} %get-tuple-element.62) | copy-start | bytes 6148
  416.0 48.5 %copy-start.31 = (f32[2,128]{1,0:T(2,128)S(1)}, f32[2,128]{1,0:T(2,128)}, u32[]{:S(2)}) copy-start(f32[2,128]{1,0:T(2,128)} %copy-done.30) | copy-start | bytes 3076
  416.0 48.5 %copy-start.33 = (f32[2,128]{1,0:T(2,128)S(1)}, f32[2,128]{1,0:T(2,128)}, u32[]{:S(2)}) copy-start(f32[2,128]{1,0:T(2,128)} %copy-done.32) | copy-start | bytes 3076
  541.5 67.2 %copy-start.11 = (f32[86224]{0:T(1024)}, f32[86224]{0:T(1024)S(1)}, u32[]{:S(2)}) copy-start(f32[86224]{0:T(1024)S(1)} %get-tuple-element.25) | copy-start | bytes 1034692
  (28 other events, 223.8 us)
Sparse Core Ops, SparseCore 0:
  11.4 96.8 all-gather.1
  408.8 130.9 reduce-scatter.4

commit v2 on v1

--- a/solution.py
+++ b/solution.py
@@ -11,6 +11,8 @@
 DOCS = 4
 G = 1024
 FF = 2048
+GATHER_PART = 0.45
+SCATTER_PART = 0.35
 
 
 norm_eps = 1e-05
@@ -295,34 +297,301 @@
     return g_re, g_im, w_re, w_im
 
 
-def unpack(flat):
-    layout = [
-        ("norm_gain", (D,)),
-        ("norm_bias", (D,)),
-        ("step_log", (D,)),
-        ("skip_gain", (D,)),
-        ("decay_log", (D, NSTATE)),
-        ("frequency", (D, NSTATE)),
-        ("out_real", (D, NSTATE)),
-        ("out_imag", (D, NSTATE)),
-        ("gate_weight", (D, G)),
-        ("gate_bias", (G,)),
-        ("second_gain", (D,)),
-        ("second_bias", (D,)),
-        ("expand_weight", (D, FF)),
-        ("expand_bias", (FF,)),
-        ("reduce_weight", (FF, D)),
-        ("reduce_bias", (D,)),
-    ]
-    params = {}
-    offset = 0
-    for name, shape in layout:
-        count = 1
-        for extent in shape:
-            count = count * extent
-        params[name] = flat[offset : offset + count].reshape(shape)
-        offset = offset + count
-    return params
+TILE = 1024
+GATE_AT, EXPAND_AT, REDUCE_AT = 130, 644, 1670
+SMALL_AT = (642, 643, 1668, 1669, 2694)
+MODE_TILES = 130
+
+
+def lay(share, devices):
+    base = share // TILE
+    return base, base + 2, (devices - 1) * share // TILE + base + 2
+
+
+def strips():
+    return ((GATE_AT, D, G // CH), (EXPAND_AT, D, FF // CH), (REDUCE_AT, FF, D // CH))
+
+
+def unpack_body(streams, base, tiles, devices, *refs):
+    n = len(streams)
+    dest = refs[0]
+    sources = refs[1:1 + n]
+    gate_ref, expand_ref, reduce_ref, small_ref, modes_ref, flat, side, sem, side_sem = refs[1 + n:]
+
+    def clear(j, _):
+        at = pl.multiple_of(dest[j], 8)
+        for tile in (0, base, base + 1):
+            flat[pl.ds(at + tile * 8, 8), :] = jnp.zeros((8, CH), f32)
+        return 0
+
+    lax.fori_loop(0, devices, clear, 0)
+    inside = 0
+    for k, (first, last, order, slot, count) in enumerate(streams):
+        lo, hi = max(first, 1), min(last, base)
+        rows = (last - first) * 8
+
+        def send(b, _, k=k, first=first, last=last, lo=lo, hi=hi, rows=rows, order=order, slot=slot):
+            at = pl.multiple_of(dest[order + b], 8)
+            begin = pl.multiple_of(b * rows, 8)
+            pltpu.make_async_copy(sources[k].at[pl.ds(begin + (lo - first) * 8, (hi - lo) * 8), :], flat.at[pl.ds(at + lo * 8, (hi - lo) * 8), :], sem).start()
+            for s, tile in enumerate((0, base, base + 1)):
+                if first <= tile < last:
+                    pltpu.make_async_copy(sources[k].at[pl.ds(begin + (tile - first) * 8, 8), :], side.at[s, pl.ds(pl.multiple_of((slot + b) * 8, 8), 8), :], side_sem).start()
+            return 0
+
+        lax.fori_loop(0, count, send, 0)
+        inside += (hi - lo) * count
+    pltpu.make_async_copy(flat.at[pl.ds(0, inside * 8), :], flat.at[pl.ds(0, inside * 8), :], sem).wait()
+    pltpu.make_async_copy(side, side, side_sem).wait()
+    for s, tile in enumerate((0, base, base + 1)):
+        for first, last, order, slot, count in streams:
+            if not first <= tile < last:
+                continue
+
+            def join(b, _, s=s, tile=tile, order=order, slot=slot):
+                at = pl.multiple_of(dest[order + b], 8)
+                flat[pl.ds(at + tile * 8, 8), :] += side[s, pl.ds(pl.multiple_of((slot + b) * 8, 8), 8), :]
+                return 0
+
+            lax.fori_loop(0, count, join, 0)
+    for (first, rows, per), out in zip(strips(), (gate_ref, expand_ref, reduce_ref)):
+        def narrow(i, _, first=first, per=per, out=out):
+            for k in range(per):
+                v = flat[pl.ds(first * 8 + i * 16 * per + k, 16, stride=per), :]
+                out[pl.ds(pl.multiple_of(i * 16, 16), 16), k * CH:(k + 1) * CH] = v.astype(bf16)
+            return 0
+
+        lax.fori_loop(0, rows // 16, narrow, 0)
+    for k, tile in enumerate(SMALL_AT):
+        small_ref[k * 8:(k + 1) * 8, :] = flat[tile * 8:(tile + 1) * 8, :]
+    modes_ref[...] = flat[:MODE_TILES * 8, :]
+
+
+def unpack_kernel(streams, arrays, dest, share, devices):
+    base, _, tiles = lay(share, devices)
+    hbm = pl.BlockSpec(memory_space=pl.ANY)
+    vm = pl.BlockSpec(memory_space=pltpu.VMEM)
+    shapes = ((D, G), (D, FF), (FF, D))
+    return pl.pallas_call(
+        partial(unpack_body, streams, base, tiles, devices),
+        out_shape=tuple(jax.ShapeDtypeStruct(s, bf16) for s in shapes)
+        + (jax.ShapeDtypeStruct((len(SMALL_AT) * 8, CH), f32), jax.ShapeDtypeStruct((MODE_TILES * 8, CH), f32)),
+        in_specs=[pl.BlockSpec(memory_space=pltpu.SMEM)] + [hbm] * len(arrays),
+        out_specs=(vm,) * 5,
+        scratch_shapes=[
+            pltpu.VMEM((tiles * 8, CH), f32),
+            pltpu.VMEM((3, devices * 8, CH), f32),
+            pltpu.SemaphoreType.DMA,
+            pltpu.SemaphoreType.DMA,
+        ],
+        name="unpack_weights",
+    )(dest, *arrays)
+
+
+def pack_body(streams, tiles, devices, has_modes, *refs):
+    n = len(streams)
+    dest, gate_ref, expand_ref, reduce_ref, small_ref = refs[:5]
+    modes_ref = refs[5] if has_modes else None
+    outs = refs[5 + has_modes:5 + has_modes + n]
+    flat, sem = refs[5 + has_modes + n:]
+    if has_modes:
+        flat[:MODE_TILES * 8, :] = modes_ref[...]
+    else:
+        flat[:MODE_TILES * 8, :] = jnp.zeros((MODE_TILES * 8, CH), f32)
+    for k, tile in enumerate(SMALL_AT):
+        flat[tile * 8:(tile + 1) * 8, :] = small_ref[k * 8:(k + 1) * 8, :]
+    flat[(SMALL_AT[-1] + 1) * 8:, :] = jnp.zeros(((tiles - SMALL_AT[-1] - 1) * 8, CH), f32)
+    for (first, rows, per), src in zip(strips(), (gate_ref, expand_ref, reduce_ref)):
+        def spread(i, _, first=first, per=per, src=src):
+            for k in range(per):
+                v = src[pl.ds(pl.multiple_of(i * 16, 16), 16), k * CH:(k + 1) * CH]
+                flat[pl.ds(first * 8 + i * 16 * per + k, 16, stride=per), :] = v
+            return 0
+
+        lax.fori_loop(0, rows // 16, spread, 0)
+    for k, (first, last, order) in enumerate(streams):
+        rows = (last - first) * 8
+
+        def send(b, _, k=k, first=first, rows=rows, order=order):
+            at = pl.multiple_of(dest[order + b], 8)
+            pltpu.make_async_copy(flat.at[pl.ds(at + first * 8, rows), :], outs[k].at[pl.ds(pl.multiple_of(b * rows, 8), rows), :], sem.at[k]).start()
+            return 0
+
+        lax.fori_loop(0, outs[k].shape[0] // rows, send, 0)
+    for k, out in enumerate(outs):
+        pltpu.make_async_copy(out, out, sem.at[k]).wait()
+
+
+def pack_kernel(streams, dest, grads, small, modes, share, devices):
+    _, _, tiles = lay(share, devices)
+    hbm = pl.BlockSpec(memory_space=pl.ANY)
+    vm = pl.BlockSpec(memory_space=pltpu.VMEM)
+    has = int(modes is not None)
+    return pl.pallas_call(
+        partial(pack_body, tuple(s[:3] for s in streams), tiles, devices, has),
+        out_shape=tuple(jax.ShapeDtypeStruct((blocks * (last - first) * 8, CH), f32) for first, last, _, blocks in streams),
+        in_specs=[pl.BlockSpec(memory_space=pltpu.SMEM)] + [vm] * (4 + has),
+        out_specs=(hbm,) * len(streams),
+        scratch_shapes=[pltpu.VMEM((tiles * 8, CH), f32), pltpu.SemaphoreType.DMA((len(streams),))],
+        name="pack_gradients",
+    )(dest, *grads, small, *((modes,) if has else ()))
+
+
+AXES = ("seq", "batch")
+PAIR = [(0, 1), (1, 0)]
+
+
+def columns(seq):
+    return seq // 4, 4
+
+
+def across(v, step):
+    return lax.ppermute(v, "seq", [(i, i ^ step) for i in range(16)])
+
+
+def along(v, step):
+    return lax.ppermute(v, "seq", [(i, (i + 4 * step) % 16) for i in range(16)])
+
+
+def swap_cores(v):
+    return lax.ppermute(v, "batch", PAIR)
+
+
+def direct():
+    return lax.axis_size("seq") == 16 and lax.axis_size("batch") == 2
+
+
+def first_rows(share, devices, ids):
+    return ids * share // TILE * 8
+
+
+def place_of(step_z, step_p, other):
+    seq, batch = lax.axis_index("seq"), lax.axis_index("batch")
+    z = (seq // 4 + 4 + step_z) % 4
+    return 2 * (z * 4 + (seq % 4 ^ step_p)) + (batch ^ other)
+
+
+def cuts_of(tiles, part):
+    one = round(tiles * part)
+    two = one + round((tiles - one) * 2 / 3)
+    return one, two
+
+
+def gather_weights(master, share, devices):
+    base, tiles, _ = lay(share, devices)
+    me = 2 * lax.axis_index("seq") + lax.axis_index("batch") if direct() else lax.axis_index("seq") * lax.axis_size("batch") + lax.axis_index("batch")
+    box = lax.dynamic_update_slice(jnp.zeros((tiles * TILE,), f32), master, (me * share % TILE,)).reshape(tiles * 8, CH)
+    natural = first_rows(share, devices, jnp.arange(devices, dtype=jnp.int32))
+    if not direct():
+        return (((0, tiles, 0, 0, devices),), [lax.all_gather(box, AXES, axis=0, tiled=True)], natural)
+    one, two = cuts_of(tiles, GATHER_PART)
+    lone, ltwo = box[one * 8:two * 8], box[two * 8:]
+    streams, arrays, dest = [], [], []
+    if one:
+        arrays.append(lax.all_gather(box[:one * 8], AXES, axis=0, tiled=True))
+        streams.append((0, one, 0, 0, devices))
+        dest.append(natural)
+    near_z = jnp.concatenate([lone] + [along(lone, k) for k in range(1, 4)])
+    near_p = jnp.concatenate([ltwo] + [across(ltwo, p) for p in range(1, 4)])
+    sets_z = [near_z] + [across(near_z, p) for p in range(1, 4)]
+    sets_p = [near_p] + [along(near_p, k) for k in range(1, 4)]
+    for lo, hi, sets, ids in (
+        (one, two, sets_z, lambda s, b, o: place_of(-b, s, o)),
+        (two, tiles, sets_p, lambda s, b, o: place_of(-s, b, o)),
+    ):
+        slot = 0
+        for other in range(2):
+            for s in range(4):
+                arrays.append(swap_cores(sets[s]) if other else sets[s])
+                streams.append((lo, hi, devices * bool(one) + 32 * (lo == two) + slot, slot, 4))
+                dest.append(first_rows(share, devices, jnp.stack([ids(s, b, other) for b in range(4)])))
+                slot += 4
+    return tuple(streams), arrays, jnp.concatenate(dest).astype(jnp.int32)
+
+
+def scatter_plan(share, devices):
+    _, tiles, _ = lay(share, devices)
+    natural = first_rows(share, devices, jnp.arange(devices, dtype=jnp.int32))
+    if not direct():
+        return ((0, tiles, 0, devices),), natural
+    one, two = cuts_of(tiles, SCATTER_PART)
+    streams, dest = [], []
+    if one:
+        streams.append((0, one, 0, devices))
+        dest.append(natural)
+    for lo, hi, ids in (
+        (one, two, lambda s, b, o: place_of(b, s, o)),
+        (two, tiles, lambda s, b, o: place_of(s, b, o)),
+    ):
+        for other in range(2):
+            for s in range(4):
+                streams.append((lo, hi, sum(d.shape[0] for d in dest), 4))
+                dest.append(first_rows(share, devices, jnp.stack([ids(s, b, other) for b in range(4)])))
+    return tuple(streams), jnp.concatenate(dest).astype(jnp.int32)
+
+
+def scatter_gradients(arrays, share, devices):
+    _, tiles, _ = lay(share, devices)
+    if not direct():
+        return lax.psum_scatter(arrays[0].reshape(devices, tiles * 8, CH), AXES, scatter_dimension=0)
+    one, two = cuts_of(tiles, SCATTER_PART)
+    pieces = []
+    if one:
+        pieces.append(lax.psum_scatter(arrays[0].reshape(devices, one * 8, CH), AXES, scatter_dimension=0))
+        arrays = arrays[1:]
+    both = [a + swap_cores(b) for a, b in zip(arrays[:4] + arrays[8:12], arrays[4:8] + arrays[12:16])]
+    by_p, by_z = both[:4], both[4:]
+    part_p = by_p[0] + across(by_p[1], 1) + across(by_p[2], 2) + across(by_p[3], 3)
+    part_z = by_z[0] + along(by_z[1], 1) + along(by_z[2], 2) + along(by_z[3], 3)
+    part_p, part_z = part_p.reshape(4, -1, CH), part_z.reshape(4, -1, CH)
+    pieces.append(part_p[0] + along(part_p[1], 1) + along(part_p[2], 2) + along(part_p[3], 3))
+    pieces.append(part_z[0] + across(part_z[1], 1) + across(part_z[2], 2) + across(part_z[3], 3))
+    return jnp.concatenate(pieces)
+
+
+MODE_ROWS = 65
+
+
+def scatter_modes(master):
+    other = swap_cores(master)
+    even = lax.axis_index("batch") == 0
+    lead = jnp.concatenate([jnp.where(even, master, other), jnp.where(even, other, master)])[:MODE_TILES * TILE]
+    small = lead[:4 * D].reshape(4, 16, 32).transpose(1, 0, 2).reshape(16, 1, CH)
+    rest = lead[4 * D:].reshape(4, 16, 16, CH).transpose(1, 0, 2, 3).reshape(16, 64, CH)
+    blocks = jnp.concatenate([small, rest], axis=1)
+    seq = lax.axis_index("seq")
+    far = [lax.ppermute(blocks[4 * k:4 * k + 4], "seq", [(0, 4 * k)]) for k in range(1, 4)]
+    plane = jnp.where(seq == 0, blocks[:4], far[0] + far[1] + far[2])
+    near = [lax.ppermute(plane[p], "seq", [(4 * z, 4 * z + p) for z in range(4)]) for p in range(1, 4)]
+    return jnp.where(seq % 4 == 0, plane[0], near[0] + near[1] + near[2])
+
+
+def read_modes(block):
+    nch = D // 16
+    small = block[0].reshape(4, nch)
+    rest = block[1:].reshape(4, nch, NSTATE)
+    return small, rest
+
+
+def gather_modes(small, rest):
+    block = jnp.concatenate([small.reshape(1, CH), rest.reshape(64, CH)])
+    near = [lax.ppermute(block, "seq", [(4 * z + p, 4 * z) for z in range(4)]) for p in range(1, 4)]
+    plane = jnp.stack([block] + near)
+    far = [lax.ppermute(plane, "seq", [(4 * k, 0)]) for k in range(1, 4)]
+    blocks = jnp.concatenate([plane] + far)
+    lead = blocks[:, 0].reshape(16, 4, 32).transpose(1, 0, 2).reshape(-1)
+    tail = blocks[:, 1:].reshape(16, 4, 16, CH).transpose(1, 0, 2, 3).reshape(-1)
+    return jnp.concatenate([lead, tail])
+
+
+def total_of(v):
+    if not direct():
+        return lax.psum(v, AXES)
+    v = jnp.broadcast_to(v, (8, CH))
+    v = v + swap_cores(v)
+    v = v + (across(v, 1) + across(v, 2) + across(v, 3))
+    v = v + (along(v, 1) + along(v, 2) + along(v, 3))
+    return v[0, 0]
 
 
 def gelu(values):
@@ -367,10 +636,7 @@
     seq, batch = lax.axis_size("seq"), lax.axis_size("batch")
     devices = seq * batch
     share = master.shape[0]
-    padded = -(-share // 1024) * 1024
-    full = lax.all_gather(jnp.pad(master, (0, padded - share)), ("seq", "batch"), axis=0, tiled=True)
-    full = full.reshape(devices, padded)[:, :share].reshape(-1)
-    params = unpack(full)
+    streams, arrays, dest = gather_weights(master, share, devices)
     group = inputs.shape[1]
     nch, nck = D // seq, seq * group // CH
     rows = inputs[0].astype(jnp.float32)
@@ -380,27 +646,41 @@
     labels = jnp.sum((where[:, None] >= ends[None, :]).astype(jnp.int32), axis=1)
     valid = (labels < DOCS - 1).astype(jnp.float32)
     first_hat, first_scale = normalize(rows)
+    hats = to_channels(first_hat)
     mine = lambda v: lax.dynamic_slice_in_dim(v, lax.axis_index("seq") * nch, nch, 0)
-    names = ("step_log", "decay_log", "frequency", "out_real", "out_imag")
-    modes, modes_pull = jax.vjp(mixing, *(mine(params[name]) for name in names))
-    prm = mode_rows(*modes, *(mine(params[name]) for name in ("norm_gain", "norm_bias", "skip_gain")))
-    hats = to_channels(first_hat)
+    if direct():
+        few, many = read_modes(scatter_modes(master))
+        gate_low, expand_low, reduce_low, small, lead = unpack_kernel(streams, arrays, dest, share, devices)
+        lead = lead.reshape(-1)
+    else:
+        gate_low, expand_low, reduce_low, small, lead = unpack_kernel(streams, arrays, dest, share, devices)
+        lead = lead.reshape(-1)
+        few = jnp.stack([mine(lead[k * D:(k + 1) * D]) for k in range(4)])
+        many = jnp.stack([mine(v) for v in lead[4 * D:].reshape(4, D, NSTATE)])
+    modes, modes_pull = jax.vjp(mixing, few[2], many[0], many[1], many[2], many[3])
+    prm = mode_rows(*modes, few[0], few[1], few[3])
     outs, prior = ssm_forward(ends, prm, hats, nck, nch)
+    small = small.reshape(-1)
+    params = {
+        "norm_gain": lead[:D],
+        "gate_bias": small[:G],
+        "second_gain": small[G:G + D],
+        "second_bias": small[G + D:G + 2 * D],
+        "expand_bias": small[2 * G:2 * G + FF],
+        "reduce_bias": small[2 * G + FF:2 * G + FF + D],
+    }
     response = to_tokens(outs, group)
     hidden_low = gelu(response).astype(jnp.bfloat16)
-    gate_low = params["gate_weight"].astype(jnp.bfloat16)
     opened = jnp.dot(hidden_low, gate_low, preferred_element_type=jnp.float32) + params["gate_bias"]
     linear = opened[:, :D]
     gating = jax.nn.sigmoid(opened[:, D:])
     mid = rows + linear * gating
     second_hat, second_scale = normalize(mid)
     normed_low = (second_hat * params["second_gain"] + params["second_bias"]).astype(jnp.bfloat16)
-    expand_low = params["expand_weight"].astype(jnp.bfloat16)
     lifted = (
         jnp.dot(normed_low, expand_low, preferred_element_type=jnp.float32) + params["expand_bias"]
     )
     active_low = gelu(lifted).astype(jnp.bfloat16)
-    reduce_low = params["reduce_weight"].astype(jnp.bfloat16)
     result = (
         mid
         + jnp.dot(active_low, reduce_low, preferred_element_type=jnp.float32)
@@ -427,40 +707,39 @@
     d_hidden = jnp.einsum("tg,dg->td", d_opened, gate_low, preferred_element_type=jnp.float32)
     d_response = d_hidden * gelu_slope(response)
     d_outs = to_channels(d_response)
+    flat_small = jnp.concatenate([g_gate_b, g_second_gain, g_second_bias, g_expand_b, g_reduce_b, jnp.zeros((D,), f32)]).reshape(-1, CH)
+    plan, places = scatter_plan(share, devices)
     d_signals, sums = ssm_backward(ends, prm, hats, d_outs, prior, nck, nch)
     d_signal = to_tokens(d_signals, group)
-    d_modes = modes_pull(mode_grads(sums, *modes))
     d_rows = d_mid + norm_back(d_signal * params["norm_gain"], first_hat, first_scale)
     lane_sums = jnp.sum(sums[10:13], axis=-1)
-
-    def spread(v):
-        whole = jnp.zeros((D,) + v.shape[1:], jnp.float32)
-        return lax.dynamic_update_slice_in_dim(whole, v, lax.axis_index("seq") * nch, 0)
-
-    parts = [
-        spread(lane_sums[1]),
-        spread(lane_sums[2]),
-        spread(d_modes[0]),
-        spread(lane_sums[0]),
-        spread(d_modes[1]),
-        spread(d_modes[2]),
-        spread(d_modes[3]),
-        spread(d_modes[4]),
-        g_gate_w,
-        g_gate_b,
-        g_second_gain,
-        g_second_bias,
-        g_expand_w,
-        g_expand_b,
-        g_reduce_w,
-        g_reduce_b,
-    ]
-    packed = jnp.concatenate([item.reshape(-1) for item in parts])
-    packed = jnp.pad(packed, (0, full.shape[0] - packed.shape[0]))
-    packed = jnp.pad(packed.reshape(devices, share), ((0, 0), (0, padded - share)))
-    shard = lax.psum_scatter(packed.reshape(devices, padded // 128, 128), ("seq", "batch"), scatter_dimension=0)
-    shard = shard.reshape(-1)[:share]
-    total = lax.psum(jnp.sum(shard * shard), ("seq", "batch"))
+    d_modes = modes_pull(mode_grads(sums, *modes))
+    few = jnp.stack([lane_sums[1], lane_sums[2], d_modes[0], lane_sums[0]])
+    many = jnp.stack(d_modes[1:])
+    if direct():
+        packed = pack_kernel(plan, places, (g_gate_w, g_expand_w, g_reduce_w), flat_small, None, share, devices)
+    else:
+
+        def spread(v):
+            whole = jnp.zeros((v.shape[0], D) + v.shape[2:], f32)
+            return lax.dynamic_update_slice_in_dim(whole, v, lax.axis_index("seq") * nch, 1)
+
+        lead = jnp.concatenate([spread(few).reshape(-1), spread(many).reshape(-1)]).reshape(-1, CH)
+        packed = pack_kernel(plan, places, (g_gate_w, g_expand_w, g_reduce_w), flat_small, lead, share, devices)
+    me = lax.axis_index("seq") * batch + lax.axis_index("batch")
+    box = scatter_gradients(packed, share, devices)
+    shard = lax.dynamic_slice(box.reshape(-1), (me * share % TILE,), (share,))
+    if direct():
+        few, many = few + swap_cores(few), many + swap_cores(many)
+        lead = gather_modes(few, many)
+        lead = jnp.pad(lead, (0, 2 * share - lead.shape[0]))
+        mark = me * share + jnp.arange(share, dtype=jnp.int32) < MODE_TILES * TILE
+        squares = jnp.sum(jnp.where(mark, 0.0, shard * shard))
+        squares = squares + 0.5 * (jnp.sum(few * few) + jnp.sum(many * many))
+        shard = jnp.where(mark, lax.dynamic_slice(lead, (jnp.minimum(me, 1) * share,), (share,)), shard)
+    else:
+        squares = jnp.sum(shard * shard)
+    total = total_of(squares)
     grad_norm = jnp.sqrt(total)
     factor = jnp.minimum(1.0, 1.0 / (grad_norm + 1e-06))
     clipped = shard * factor

time: 629 us -> 420 us (0.67)
  the two profiles are of different devices: /device:TPU:12 before, /device:TPU:0 now
where the time goes in v2:
time: 420 us; the launch traced here: 418 us
  Pallas kernels  127 us (30%)
  starting transfers between devices  89.2 us (21%)
  waiting for transfers between devices  80.3 us (19%)
  other arithmetic  46.5 us (11%)
  local copies, waits for them, and re-layouts  38.2 us (9%)
  between operations  19.5 us (5%)
  matrix products  17.1 us (4%)
    pallas_call x1, Pallas kernels, ssm_backward(): pl.pallas_call(partial(bwd_body, nck, nch), out_shape=(jax.ShapeDtypeStru...  63.9 us
    ppermute x15, waiting for transfers between devices, along(): return lax.ppermute(v, 'seq', [(i, (i + 4 * step) % 16) for i in range(16)])  56 us
    pallas_call x1, Pallas kernels, ssm_forward(): pl.pallas_call(partial(fwd_body, nck, nch), out_shape=(jax.ShapeDtypeStru...  40 us
    ppermute x15, starting transfers between devices, along(): return lax.ppermute(v, 'seq', [(i, (i + 4 * step) % 16) for i in range(16)])  22.1 us
    ppermute x15, starting transfers between devices, across(): return lax.ppermute(v, 'seq', [(i, i ^ step) for i in range(16)])  21.7 us
    add x6, other arithmetic, scatter_gradients(): a + swap_cores(b)  11.8 us
    pallas_call x1, Pallas kernels, unpack_kernel(): pl.pallas_call(partial(unpack_body, streams, base, tiles, devices), out_s...  11.6 us
    pallas_call x1, Pallas kernels, pack_kernel(): pl.pallas_call(partial(pack_body, tuple((s[:3] for s in streams)), tiles,...  11.3 us
  transfers between devices with their start and end apart: 68, of which 21 were waited for; matrix products, arithmetic and copies ran while one was open for 18% of the time, Pallas kernels for 25%

profile of v2, /device:TPU:0, one launch (start us, length us, event | category | flops | bytes accessed | tf_op | source)
XLA Modules:
  0.0 417.6 jit_solution(9736287347293891627)
XLA Ops:
  7.3 3.7 dynamic_update_slice.3
  11.0 4.0 collective-permute-start.19
  19.6 7.3 %all-to-all-start = ((f32[16,2,32,128]{3,1,2,0:T(2,128)}), f32[16,2,32,128]{3,1,2,0:T(2,128)S(1)}, u32[]{:S(2)}, u32[]{:S(2)}) async-start(f32[16,2,32,128]{3,1,2,0:T(2,128)} %fusion.24), calls=%async_computation | async-start | bytes 1048576 | tf_op jit(solution)/shard_map/all_to_all | solution.py:626
  34.1 5.4 %collective-permute-start.3 = (f32[4,65,128]{2,1,0:T(8,128)S(1)}, f32[4,65,128]{2,1,0:T(8,128)S(1)}, u32[]{:S(2)}, u32[]{:S(2)}) collective-permute-start(f32[4,65,128]{2,1,0:T(8,128)S(1)} %get-tuple-element.101), channel_id=1, source_target_pairs={{0,24},{1,25}} | collective-permute-start | bytes 399368 | tf_op jit(solution)/shard_map/ppermute | solution.py:563
  51.8 3.4 collective-permute-start.21
  56.7 17.4 %collective-permute-done.8 = f32[248,128]{1,0:T(8,128)S(1)} collective-permute-done((f32[248,128]{1,0:T(8,128)S(1)}, f32[248,128]{1,0:T(8,128)S(1)}, u32[]{:S(2)}, u32[]{:S(2)}) %collective-permute-start.8) | collective-permute-done | bytes 127008 | tf_op jit(solution)/shard_map/ppermute | solution.py:453
  74.1 3.9 collective-permute-start.4
  89.1 40.0 %state_forward.1 = (f32[1024,128]{1,0:T(8,128)}, f32[1024,128]{1,0:T(8,128)}) custom-call(s32[4]{0:T(128)} %bitcast.387, f32[32,24,128]{2,1,0:T(8,128)} %concatenate.63.prm_ref, f32[1024,128]{1,0:T(8,128)} %bitcast.358), custom_call_target="tpu_custom_call" | custom-call | tf_op jit(solution)/shard_map/state_forward/pallas_call | solution.py:135
  131.3 4.3 %all-to-all-start.1 = ((f32[16,2,32,128]{3,1,2,0:T(2,128)}), f32[16,2,32,128]{3,1,2,0:T(2,128)S(1)}, u32[]{:S(2)}, u32[]{:S(2)}) async-start(f32[16,2,32,128]{3,1,2,0:T(2,128)} %copy.66), calls=%async_computation.1 | async-start | bytes 1048576 | tf_op jit(solution)/shard_map/all_to_all | solution.py:631
  142.6 6.0 %all-to-all-done.1 = f32[16,2,32,128]{3,1,2,0:T(2,128)S(1)} async-done(((f32[16,2,32,128]{3,1,2,0:T(2,128)}), f32[16,2,32,128]{3,1,2,0:T(2,128)S(1)}, u32[]{:S(2)}, u32[]{:S(2)}) %all-to-all-start.1) | async-done | bytes 524320 | tf_op jit(solution)/shard_map/all_to_all | solution.py:631
  149.7 11.6 %unpack_weights.1 = (bf16[512,1024]{1,0:T(8,128)(2,1)}, bf16[512,2048]{1,0:T(8,128)(2,1)}, bf16[2048,512]{1,0:T(8,128)(2,1)}, f32[40,128]{1,0:T(8,128)}, f32[1040,128]{1,0:T(8,128)}) custom-call(s32[96]{0:T(128)} %concatenate.64.refs_0_, f32[9984,128]{1,0:T(8,128)} %all-gather.2.cloned.1.call-done.refs_1_, f32[992,128]{1,0:T(8,128)} %copy-done.5, ...), custom_call_target="tpu_custom_call" | custom-call | tf_op jit(solution)/shard_map/unpack_weights/pallas_call | solution.py:375
  170.1 2.9 fusion.112.refs_2_
  179.0 11.3 %pack_gradients.1 = (f32[7680,128]{1,0:T(8,128)}, f32[1184,128]{1,0:T(8,128)}, f32[1184,128]{1,0:T(8,128)}, f32[1184,128]{1,0:T(8,128)}, f32[1184,128]{1,0:T(8,1...) custom-call(s32[96]{0:T(128)} %concatenate.71.refs_0_, ...), custom_call_target="tpu_custom_call" | custom-call | tf_op jit(solution)/shard_map/pack_gradients/pallas_call | solution.py:430
  198.7 3.8 all-to-all-start.2
  205.0 3.7 collective-permute-start.51
  215.1 5.5 %collective-permute-done.51 = f32[608,128]{1,0:T(8,128)} collective-permute-done((f32[608,128]{1,0:T(8,128)}, f32[608,128]{1,0:T(8,128)}, u32[]{:S(2)}, u32[]{:S(2)}) %collective-permute-start.51) | collective-permute-done | bytes 311328 | tf_op jit(solution)/shard_map/ppermute | solution.py:453
  220.6 23.7 %collective-permute-done.49 = f32[608,128]{1,0:T(8,128)} collective-permute-done((f32[608,128]{1,0:T(8,128)}, f32[608,128]{1,0:T(8,128)}, u32[]{:S(2)}, u32[]{:S(2)}) %collective-permute-start.49) | collective-permute-done | bytes 311328 | tf_op jit(solution)/shard_map/ppermute | solution.py:453
  263.3 63.9 %state_backward.1 = (f32[1024,128]{1,0:T(8,128)}, f32[16,32,128]{2,1,0:T(8,128)}) custom-call(s32[4]{0:T(128)} %bitcast.388, f32[32,24,128]{2,1,0:T(8,128)} %concatenate.63.prm_ref, f32[1024,128]{1,0:T(8,128)} %bitcast.359, f32[1024,128]{1,0:T(8,128)} %bitcast.365, f32[1024,128]{1,0:T(8,128)} %get-tuple-element.38.prior_ref), custom_call_target="tpu_custom_call" | custom-call | tf_op jit(solution)/shard_map/state_backward/pallas_call | solution.py:233
  331.6 3.6 all-to-all-start.3
  356.2 4.5 %collective-permute-done.32 = f32[4,65,128]{2,1,0:T(8,128)S(1)} collective-permute-done((f32[4,65,128]{2,1,0:T(8,128)S(1)}, f32[4,65,128]{2,1,0:T(8,128)S(1)}, u32[]{:S(2)}, u32[]{:S(2)}) %collective-permute-start.32) | collective-permute-done | bytes 133152 | tf_op jit(solution)/shard_map/ppermute | solution.py:580
  363.3 5.3 %collective-permute-done.33 = f32[4,65,128]{2,1,0:T(8,128)S(1)} collective-permute-done((f32[4,65,128]{2,1,0:T(8,128)S(1)}, f32[4,65,128]{2,1,0:T(8,128)S(1)}, u32[]{:S(2)}, u32[]{:S(2)}) %collective-permute-start.33) | collective-permute-done | bytes 133152 | tf_op jit(solution)/shard_map/ppermute | solution.py:580
  373.2 4.5 %collective-permute-start.44 = (f32[296,128]{1,0:T(8,128)S(1)}, f32[296,128]{1,0:T(8,128)}, u32[]{:S(2)}, u32[]{:S(2)}) collective-permute-start(f32[296,128]{1,0:T(8,128)S(1)} %get-tuple-element.95), channel_id=1, source_target_pairs={{0,24},{2,26},{4,28},{6,30},{8,0},{10,2},{12,4},{14,6},{16,8},{18,... | collective-permute-start | bytes 454664 | tf_op jit(solution)/shard_map/ppermute | solution.py:453
  381.5 7.1 %collective-permute-done.43 = f32[296,128]{1,0:T(8,128)} collective-permute-done((f32[296,128]{1,0:T(8,128)S(1)}, f32[296,128]{1,0:T(8,128)}, u32[]{:S(2)}, u32[]{:S(2)}) %collective-permute-start.43) | collective-permute-done | bytes 151584 | tf_op jit(solution)/shard_map/ppermute | solution.py:453
  394.1 3.5 collective-permute-start.57
  (388 shorter events, 147.8 us)
Async XLA Ops:
  7.2 141.8 %all-gather.2.cloned.1.call-start = ((), (), s32[]{:S(2)}) async-start(), calls=%async_computation.5 | async-start | bytes 5271552 | tf_op jit(solution)/shard_map/all_gather | solution.py:491
  11.0 29.8 %collective-permute-start.19 = (f32[128,128]{1,0:T(8,128)S(1)}, f32[128,128]{1,0:T(8,128)S(1)}, u32[]{:S(2)}, u32[]{:S(2)}) collective-permute-start(f32[128,128]{1,0:T(8,128)S(1)} %slice_bitcast_fusion.2), channel_id=1, source_target_pairs={{0,6},{2,4},{4,2},{6,0},{8,14},{10,12},{12,10},{14,8},{16,22},{18,... | collective-permute-start | bytes 196616 | tf_op jit(solution)/shard_map/ppermute | solution.py:449
  15.0 28.6 %collective-permute-start.18 = (f32[128,128]{1,0:T(8,128)S(1)}, f32[128,128]{1,0:T(8,128)S(1)}, u32[]{:S(2)}, u32[]{:S(2)}) collective-permute-start(f32[128,128]{1,0:T(8,128)S(1)} %slice_bitcast_fusion.2), channel_id=1, source_target_pairs={{0,4},{2,6},{4,0},{6,2},{8,12},{10,14},{12,8},{14,10},{16,20},{18,... | collective-permute-start | bytes 196616 | tf_op jit(solution)/shard_map/ppermute | solution.py:449
  15.5 28.1 %collective-permute-start.17 = (f32[128,128]{1,0:T(8,128)S(1)}, f32[128,128]{1,0:T(8,128)S(1)}, u32[]{:S(2)}, u32[]{:S(2)}) collective-permute-start(f32[128,128]{1,0:T(8,128)S(1)} %slice_bitcast_fusion.2), channel_id=1, source_target_pairs={{0,2},{2,0},{4,6},{6,4},{8,10},{10,8},{12,14},{14,12},{16,18},{18,... | collective-permute-start | bytes 196616 | tf_op jit(solution)/shard_map/ppermute | solution.py:449
  19.6 68.6 %all-to-all-start = ((f32[16,2,32,128]{3,1,2,0:T(2,128)}), f32[16,2,32,128]{3,1,2,0:T(2,128)S(1)}, u32[]{:S(2)}, u32[]{:S(2)}) async-start(f32[16,2,32,128]{3,1,2,0:T(2,128)} %fusion.24), calls=%async_computation | async-start | bytes 1048576 | tf_op jit(solution)/shard_map/all_to_all | solution.py:626
  43.6 30.5 %collective-permute-start.8 = (f32[248,128]{1,0:T(8,128)S(1)}, f32[248,128]{1,0:T(8,128)S(1)}, u32[]{:S(2)}, u32[]{:S(2)}) collective-permute-start(f32[248,128]{1,0:T(8,128)S(1)} %slice_bitcast_fusion.1), channel_id=1, source_target_pairs={{0,16},{2,18},{4,20},{6,22},{8,24},{10,26},{12,28},{14,30},{16,0},... | collective-permute-start | bytes 380936 | tf_op jit(solution)/shard_map/ppermute | solution.py:453
  43.7 34.2 %collective-permute-start.7 = (f32[248,128]{1,0:T(8,128)S(1)}, f32[248,128]{1,0:T(8,128)S(1)}, u32[]{:S(2)}, u32[]{:S(2)}) collective-permute-start(f32[248,128]{1,0:T(8,128)S(1)} %slice_bitcast_fusion.1), channel_id=1, source_target_pairs={{0,8},{2,10},{4,12},{6,14},{8,16},{10,18},{12,20},{14,22},{16,24},... | collective-permute-start | bytes 380936 | tf_op jit(solution)/shard_map/ppermute | solution.py:453
  46.9 39.1 %collective-permute-start.20 = (f32[512,128]{1,0:T(8,128)S(1)}, f32[512,128]{1,0:T(8,128)S(1)}, u32[]{:S(2)}, u32[]{:S(2)}) collective-permute-start(f32[512,128]{1,0:T(8,128)S(1)} %pad_maximum_fusion.4.refs_10_), channel_id=1, source_target_pairs={{0,8},{2,10},{4,12},{6,14},{8,16},{10,18},{12,20},{14,22},{16,24},... | collective-permute-start | bytes 786440 | tf_op jit(solution)/shard_map/ppermute | solution.py:453
  51.8 83.9 %collective-permute-start.21 = (f32[512,128]{1,0:T(8,128)S(1)}, f32[512,128]{1,0:T(8,128)S(1)}, u32[]{:S(2)}, u32[]{:S(2)}) collective-permute-start(f32[512,128]{1,0:T(8,128)S(1)} %pad_maximum_fusion.4.refs_10_), channel_id=1, source_target_pairs={{0,16},{2,18},{4,20},{6,22},{8,24},{10,26},{12,28},{14,30},{16,0},... | collective-permute-start | bytes 786440 | tf_op jit(solution)/shard_map/ppermute | solution.py:453
  55.4 24.0 %collective-permute-start.6 = (f32[65,128]{1,0:T(8,128)S(1)}, f32[65,128]{1,0:T(8,128)S(1)}, u32[]{:S(2)}, u32[]{:S(2)}) collective-permute-start(f32[65,128]{1,0:T(8,128)S(1)} %get-tuple-element.107), channel_id=1, source_target_pairs={{0,6},{8,14},{16,22},{24,30},{1,7},{9,15},{17,23},{25,31}} | collective-permute-start | bytes 99848 | tf_op jit(solution)/shard_map/ppermute | solution.py:565
  79.3 56.5 %collective-permute-start.22 = (f32[512,128]{1,0:T(8,128)S(1)}, f32[512,128]{1,0:T(8,128)}, u32[]{:S(2)}, u32[]{:S(2)}) collective-permute-start(f32[512,128]{1,0:T(8,128)S(1)} %pad_maximum_fusion.4.refs_10_), channel_id=1, source_target_pairs={{0,24},{2,26},{4,28},{6,30},{8,0},{10,2},{12,4},{14,6},{16,8},{18,... | collective-permute-start | bytes 786440 | tf_op jit(solution)/shard_map/ppermute | solution.py:453
  79.6 58.4 %collective-permute-start.10 = (f32[992,128]{1,0:T(8,128)S(1)}, f32[992,128]{1,0:T(8,128)}, u32[]{:S(2)}, u32[]{:S(2)}) collective-permute-start(f32[992,128]{1,0:T(8,128)S(1)} %pad_maximum_fusion.2.refs_2_), channel_id=1, source_target_pairs={{0,2},{2,0},{4,6},{6,4},{8,10},{10,8},{12,14},{14,12},{16,18},{18,... | collective-permute-start | bytes 1523720 | tf_op jit(solution)/shard_map/ppermute | solution.py:449
  81.9 56.3 %collective-permute-start.11 = (f32[992,128]{1,0:T(8,128)S(1)}, f32[992,128]{1,0:T(8,128)}, u32[]{:S(2)}, u32[]{:S(2)}) collective-permute-start(f32[992,128]{1,0:T(8,128)S(1)} %pad_maximum_fusion.2.refs_2_), channel_id=1, source_target_pairs={{0,4},{2,6},{4,0},{6,2},{8,12},{10,14},{12,8},{14,10},{16,20},{18,... | collective-permute-start | bytes 1523720 | tf_op jit(solution)/shard_map/ppermute | solution.py:449
  86.0 52.5 %collective-permute-start.12 = (f32[992,128]{1,0:T(8,128)S(1)}, f32[992,128]{1,0:T(8,128)}, u32[]{:S(2)}, u32[]{:S(2)}) collective-permute-start(f32[992,128]{1,0:T(8,128)S(1)} %pad_maximum_fusion.2.refs_2_), channel_id=1, source_target_pairs={{0,6},{2,4},{4,2},{6,0},{8,14},{10,12},{12,10},{14,8},{16,22},{18,... | collective-permute-start | bytes 1523720 | tf_op jit(solution)/shard_map/ppermute | solution.py:449
  198.7 63.7 %all-to-all-start.2 = ((f32[16,2,32,128]{3,1,2,0:T(2,128)}), f32[16,2,32,128]{3,1,2,0:T(2,128)S(1)}, u32[]{:S(2)}, u32[]{:S(2)}) async-start(f32[16,2,32,128]{3,1,2,0:T(2,128)} %bitcast.368), calls=%async_computation.2 | async-start | bytes 1048576 | tf_op jit(solution)/shard_map/all_to_all | solution.py:626
  202.6 187.9 %reduce-scatter.2.cloned.1.call-start = ((), (), s32[]{:S(2)}) async-start(), calls=%async_computation.6 | async-start | bytes 4055040 | tf_op jit(solution)/shard_map/reduce_scatter | solution.py:540
  202.8 46.6 %collective-permute-start.40 = (f32[1184,128]{1,0:T(8,128)}, f32[1184,128]{1,0:T(8,128)}, u32[]{:S(2)}, u32[]{:S(2)}) collective-permute-start(f32[1184,128]{1,0:T(8,128)} %get-tuple-element.50), channel_id=1, source_target_pairs={{0,1},{1,0},{2,3},{3,2},{4,5},{5,4},{6,7},{7,6},{8,9},{9,8},{10,11... | collective-permute-start | bytes 1818632 | tf_op jit(solution)/shard_map/ppermute | solution.py:457
  210.6 33.7 %collective-permute-start.49 = (f32[608,128]{1,0:T(8,128)}, f32[608,128]{1,0:T(8,128)}, u32[]{:S(2)}, u32[]{:S(2)}) collective-permute-start(f32[608,128]{1,0:T(8,128)} %add.1640), channel_id=1, source_target_pairs={{0,16},{2,18},{4,20},{6,22},{8,24},{10,26},{12,28},{14,30},{16,0},... | collective-permute-start | bytes 933896 | tf_op jit(solution)/shard_map/ppermute | solution.py:453
  212.4 31.9 %collective-permute-start.47 = (f32[608,128]{1,0:T(8,128)}, f32[608,128]{1,0:T(8,128)}, u32[]{:S(2)}, u32[]{:S(2)}) collective-permute-start(f32[608,128]{1,0:T(8,128)} %add.1638), channel_id=1, source_target_pairs={{0,8},{2,10},{4,12},{6,14},{8,16},{10,18},{12,20},{14,22},{16,24},... | collective-permute-start | bytes 933896 | tf_op jit(solution)/shard_map/ppermute | solution.py:453
  215.0 38.9 %collective-permute-start.38 = (f32[1184,128]{1,0:T(8,128)}, f32[1184,128]{1,0:T(8,128)S(1)}, u32[]{:S(2)}, u32[]{:S(2)}) collective-permute-start(f32[1184,128]{1,0:T(8,128)} %get-tuple-element.48), channel_id=1, source_target_pairs={{0,1},{1,0},{2,3},{3,2},{4,5},{5,4},{6,7},{7,6},{8,9},{9,8},{10,11... | collective-permute-start | bytes 1818632 | tf_op jit(solution)/shard_map/ppermute | solution.py:457
  220.6 36.3 %collective-permute-start.36 = (f32[1184,128]{1,0:T(8,128)}, f32[1184,128]{1,0:T(8,128)}, u32[]{:S(2)}, u32[]{:S(2)}) collective-permute-start(f32[1184,128]{1,0:T(8,128)} %get-tuple-element.46), channel_id=1, source_target_pairs={{0,1},{1,0},{2,3},{3,2},{4,5},{5,4},{6,7},{7,6},{8,9},{9,8},{10,11... | collective-permute-start | bytes 1818632 | tf_op jit(solution)/shard_map/ppermute | solution.py:457
  254.7 115.9 %collective-permute-start.35 = (f32[1184,128]{1,0:T(8,128)}, f32[1184,128]{1,0:T(8,128)S(1)}, u32[]{:S(2)}, u32[]{:S(2)}) collective-permute-start(f32[1184,128]{1,0:T(8,128)} %get-tuple-element.44), channel_id=1, source_target_pairs={{0,1},{1,0},{2,3},{3,2},{4,5},{5,4},{6,7},{7,6},{8,9},{9,8},{10,11... | collective-permute-start | bytes 1818632 | tf_op jit(solution)/shard_map/ppermute | solution.py:457
  256.9 113.7 %collective-permute-start.41 = (f32[1184,128]{1,0:T(8,128)}, f32[1184,128]{1,0:T(8,128)}, u32[]{:S(2)}, u32[]{:S(2)}) collective-permute-start(f32[1184,128]{1,0:T(8,128)} %add.1632), channel_id=1, source_target_pairs={{0,6},{2,4},{4,2},{6,0},{8,14},{10,12},{12,10},{14,8},{16,22},{18,... | collective-permute-start | bytes 1818632 | tf_op jit(solution)/shard_map/ppermute | solution.py:449
  331.6 58.1 %all-to-all-start.3 = ((f32[16,2,32,128]{3,1,2,0:T(2,128)}), f32[16,2,32,128]{3,1,2,0:T(2,128)S(1)}, u32[]{:S(2)}, u32[]{:S(2)}) async-start(f32[16,2,32,128]{3,1,2,0:T(2,128)} %copy.74), calls=%async_computation.3 | async-start | bytes 1048576 | tf_op jit(solution)/shard_map/all_to_all | solution.py:631
  (96 other events, 1457.0 us)
Sparse Core Ops, SparseCore 0:
  16.4 103.4 all-gather.1
  215.1 110.8 reduce-scatter.1

commit v3 on v2

--- a/solution.py
+++ b/solution.py
@@ -11,8 +11,7 @@
 DOCS = 4
 G = 1024
 FF = 2048
-GATHER_PART = 0.45
-SCATTER_PART = 0.35
+SCATTER_PART = 1
 
 
 norm_eps = 1e-05
@@ -111,7 +110,7 @@
         end_ref[pl.ds(h, nck, stride=nch), :] = dot3(split(u * masks_ref[DOCS + 1]), split(down), 1, 0)
         return 0
 
-    lax.fori_loop(0, nch, one, 0)
+    lax.fori_loop(0, nch, one, 0, unroll=8)
     full_re = prm_ref[:, 14, :]
     full_im = prm_ref[:, 15, :]
 
@@ -128,7 +127,7 @@
         y_ref[pl.ds(h, nck, stride=nch), :] += carried
         return 0
 
-    lax.fori_loop(0, nch, two, 0)
+    lax.fori_loop(0, nch, two, 0, unroll=8)
 
 def ssm_forward(ends, prm, x, nck, nch):
     vm = pl.BlockSpec(memory_space=pltpu.VMEM)
@@ -157,7 +156,7 @@
         lead_ref[pl.ds(h, nck, stride=nch), :] = dot3(split(g * masks_ref[DOCS]), split(gt), 1, 0)
         return 0
 
-    lax.fori_loop(0, nch, one, 0)
+    lax.fori_loop(0, nch, one, 0, unroll=8)
     full_re = prm_ref[:, 14, :]
     full_im = prm_ref[:, 15, :]
     zero = jnp.zeros((nch, 2 * NSTATE), f32)
@@ -226,7 +225,7 @@
         rows_ref[12, pl.ds(h, 1), :] = jnp.sum(du, axis=0, keepdims=True)
         return 0
 
-    lax.fori_loop(0, nch, two, 0)
+    lax.fori_loop(0, nch, two, 0, unroll=8)
 
 def ssm_backward(ends, prm, x, g, prior, nck, nch):
     vm = pl.BlockSpec(memory_space=pltpu.VMEM)
@@ -297,10 +296,36 @@
     return g_re, g_im, w_re, w_im
 
 
+def gelu(values):
+    return 0.5 * values * (1.0 + lax.erf(values * root_half))
+
+
+def gelu_slope(values):
+    return (
+        0.5 * (1.0 + lax.erf(values * root_half))
+        + values * jnp.exp(-0.5 * values * values) * inv_root_two_pi
+    )
+
+
+def normalize(values):
+    center = values - jnp.mean(values, axis=-1, keepdims=True)
+    scale = lax.rsqrt(jnp.mean(center * center, axis=-1, keepdims=True) + norm_eps)
+    return (center * scale, scale)
+
+
+def norm_back(d_hat, hat, scale):
+    return scale * (
+        d_hat
+        - jnp.mean(d_hat, axis=-1, keepdims=True)
+        - hat * jnp.mean(d_hat * hat, axis=-1, keepdims=True)
+    )
+
+
 TILE = 1024
 GATE_AT, EXPAND_AT, REDUCE_AT = 130, 644, 1670
 SMALL_AT = (642, 643, 1668, 1669, 2694)
 MODE_TILES = 130
+BLOCK = 512
 
 
 def lay(share, devices):
@@ -308,107 +333,204 @@
     return base, base + 2, (devices - 1) * share // TILE + base + 2
 
 
-def strips():
-    return ((GATE_AT, D, G // CH), (EXPAND_AT, D, FF // CH), (REDUCE_AT, FF, D // CH))
-
-
-def unpack_body(streams, base, tiles, devices, *refs):
-    n = len(streams)
-    dest = refs[0]
-    sources = refs[1:1 + n]
-    gate_ref, expand_ref, reduce_ref, small_ref, modes_ref, flat, side, sem, side_sem = refs[1 + n:]
-
-    def clear(j, _):
-        at = pl.multiple_of(dest[j], 8)
-        for tile in (0, base, base + 1):
-            flat[pl.ds(at + tile * 8, 8), :] = jnp.zeros((8, CH), f32)
+def product(a, b, ca, cb):
+    return lax.dot_general(a, b, (((ca,), (cb,)), ((), ())), preferred_element_type=f32)
+
+
+def narrow(flat, out, first, rows, per):
+    def one(i, _):
+        for k in range(per):
+            v = flat[pl.ds(first * 8 + i * 16 * per + k, 16, stride=per), :]
+            out[pl.ds(pl.multiple_of(i * 16, 16), 16), k * CH:(k + 1) * CH] = v.astype(bf16)
         return 0
 
-    lax.fori_loop(0, devices, clear, 0)
-    inside = 0
-    for k, (first, last, order, slot, count) in enumerate(streams):
-        lo, hi = max(first, 1), min(last, base)
-        rows = (last - first) * 8
-
-        def send(b, _, k=k, first=first, last=last, lo=lo, hi=hi, rows=rows, order=order, slot=slot):
-            at = pl.multiple_of(dest[order + b], 8)
-            begin = pl.multiple_of(b * rows, 8)
-            pltpu.make_async_copy(sources[k].at[pl.ds(begin + (lo - first) * 8, (hi - lo) * 8), :], flat.at[pl.ds(at + lo * 8, (hi - lo) * 8), :], sem).start()
-            for s, tile in enumerate((0, base, base + 1)):
-                if first <= tile < last:
-                    pltpu.make_async_copy(sources[k].at[pl.ds(begin + (tile - first) * 8, 8), :], side.at[s, pl.ds(pl.multiple_of((slot + b) * 8, 8), 8), :], side_sem).start()
+    lax.fori_loop(0, rows // 16, one, 0, unroll=max(1, 16 // per))
+
+
+def small_row(flat, tile, begin, count):
+    return jnp.concatenate([flat[tile * 8 + (begin + k) // CH:tile * 8 + (begin + k) // CH + 1, :] for k in range(0, count, CH)], axis=1)
+
+
+def put_small(small_ref, begin, row):
+    for k in range(row.shape[1] // CH):
+        small_ref[begin // CH + k:begin // CH + k + 1, :] = row[:, k * CH:(k + 1) * CH]
+
+
+def column_sum(v):
+    return jnp.sum(v, axis=0, keepdims=True)
+
+
+def mlp_body(share, devices, nseq, place_ref, boxes, resp_ref, x_ref, cot_ref, out_ref, dmid_ref, dresp_ref, small_ref, lead_ref, hidden_ref, active_ref, normed_ref, back_ref, dopen_ref, dlift_ref, flat, side, gate, expand, reduce, acc, dnorm, sems):
+    base, box, _ = lay(share, devices)
+    nch = D // nseq
+    group = x_ref.shape[0]
+    start_of = lambda j: (j * share) // TILE
+    edges = [0] + [min(devices, tile * TILE // share + 1) for tile in (EXPAND_AT, REDUCE_AT)] + [devices]
+
+    def copy_side(j, _):
+        for s, tile in enumerate((0, base, base + 1)):
+            pltpu.make_async_copy(boxes.at[pl.ds(pl.multiple_of((j * box + tile) * 8, 8), 8), :], side.at[s, pl.ds(pl.multiple_of(j * 8, 8), 8), :], sems.at[3]).start()
+        return 0
+
+    lax.fori_loop(0, devices, copy_side, 0)
+    for g in range(3):
+
+        def copy_box(j, _, g=g):
+            pltpu.make_async_copy(
+                boxes.at[pl.ds(pl.multiple_of((j * box + 1) * 8, 8), (base - 1) * 8), :],
+                flat.at[pl.ds(pl.multiple_of((start_of(j) + 1) * 8, 8), (base - 1) * 8), :],
+                sems.at[g],
+            ).start()
             return 0
 
-        lax.fori_loop(0, count, send, 0)
-        inside += (hi - lo) * count
-    pltpu.make_async_copy(flat.at[pl.ds(0, inside * 8), :], flat.at[pl.ds(0, inside * 8), :], sem).wait()
-    pltpu.make_async_copy(side, side, side_sem).wait()
-    for s, tile in enumerate((0, base, base + 1)):
-        for first, last, order, slot, count in streams:
-            if not first <= tile < last:
-                continue
-
-            def join(b, _, s=s, tile=tile, order=order, slot=slot):
-                at = pl.multiple_of(dest[order + b], 8)
-                flat[pl.ds(at + tile * 8, 8), :] += side[s, pl.ds(pl.multiple_of((slot + b) * 8, 8), 8), :]
-                return 0
-
-            lax.fori_loop(0, count, join, 0)
-    for (first, rows, per), out in zip(strips(), (gate_ref, expand_ref, reduce_ref)):
-        def narrow(i, _, first=first, per=per, out=out):
-            for k in range(per):
-                v = flat[pl.ds(first * 8 + i * 16 * per + k, 16, stride=per), :]
-                out[pl.ds(pl.multiple_of(i * 16, 16), 16), k * CH:(k + 1) * CH] = v.astype(bf16)
-            return 0
-
-        lax.fori_loop(0, rows // 16, narrow, 0)
-    for k, tile in enumerate(SMALL_AT):
-        small_ref[k * 8:(k + 1) * 8, :] = flat[tile * 8:(tile + 1) * 8, :]
-    modes_ref[...] = flat[:MODE_TILES * 8, :]
-
-
-def unpack_kernel(streams, arrays, dest, share, devices):
-    base, _, tiles = lay(share, devices)
-    hbm = pl.BlockSpec(memory_space=pl.ANY)
+        lax.fori_loop(edges[g], edges[g + 1], copy_box, 0)
+    parts = group // CH
+    turned = [
+        jnp.concatenate([resp_ref[pl.ds((d * parts + k) * nch, nch), :] for d in range(nseq)], axis=0).T
+        for k in range(parts)
+    ]
+    response = jnp.concatenate(turned, axis=0)
+    hidden_ref[...] = gelu(response).astype(bf16)
+    pos = place_ref[DOCS] + lax.broadcasted_iota(jnp.int32, (group, D), 0)
+    total = jnp.zeros((group, D), jnp.int32)
+    for k in range(DOCS):
+        total = total + (pos >= place_ref[k]).astype(jnp.int32)
+    back = jnp.where(total < DOCS - 1, cot_ref[...].astype(f32), 0.0)
+    back_ref[...] = back.astype(bf16)
+    acc[...] = back
+    put_small(small_ref, 2 * G + FF, column_sum(back))
+    small_ref[36:40, :] = jnp.zeros((4, CH), f32)
+    inner = side.at[:, pl.ds(0, devices * 8), :]
+    pltpu.make_async_copy(inner, inner, sems.at[3]).wait()
+    side[0, devices * 8:, :] = jnp.zeros((8, CH), f32)
+    flat[:8, :] = side[0, :8, :]
+
+    def join(j, _):
+        at = start_of(j)
+        step = start_of(j + 1) - at
+        far = jnp.broadcast_to(step, (8, CH)) > base
+        here = pl.ds(pl.multiple_of(j * 8, 8), 8)
+        one, two, then = side[1, here, :], side[2, here, :], side[0, pl.ds(pl.multiple_of(j * 8 + 8, 8), 8), :]
+        flat[pl.ds(pl.multiple_of((at + base) * 8, 8), 8), :] = one + jnp.where(far, 0.0, then)
+        flat[pl.ds(pl.multiple_of((at + step) * 8, 8), 8), :] = jnp.where(far, two, one) + then
+        return 0
+
+    lax.fori_loop(0, devices, join, 0)
+
+    def arrived(g):
+        rows = (edges[g + 1] - edges[g]) * (base - 1) * 8
+        some = flat.at[pl.ds(0, rows), :]
+        pltpu.make_async_copy(some, some, sems.at[g]).wait()
+
+    arrived(0)
+    lead_ref[...] = flat[:MODE_TILES * 8, :]
+    narrow(flat, gate, GATE_AT, D, G // CH)
+    gate_bias = small_row(flat, SMALL_AT[0], 0, G)
+    second_gain = small_row(flat, SMALL_AT[1], 0, D)
+    second_bias = small_row(flat, SMALL_AT[1], D, D)
+    hidden = hidden_ref[...]
+    linear = product(hidden, gate[:, :D], 1, 0) + gate_bias[:, :D]
+    gating = jax.nn.sigmoid(product(hidden, gate[:, D:], 1, 0) + gate_bias[:, D:])
+    mid = x_ref[...].astype(f32) + linear * gating
+    hat, scale = normalize(mid)
+    normed_ref[...] = (hat * second_gain + second_bias).astype(bf16)
+    out_acc = mid
+    arrived(1)
+    narrow(flat, expand, EXPAND_AT, D, FF // CH)
+    arrived(2)
+    narrow(flat, reduce, REDUCE_AT, FF, D // CH)
+    dnorm[...] = jnp.zeros((group, D), f32)
+    acc[...] = mid + small_row(flat, SMALL_AT[4], 0, D)
+    for b in range(FF // BLOCK):
+        at = slice(b * BLOCK, (b + 1) * BLOCK)
+        bias = small_row(flat, SMALL_AT[2] + b * BLOCK // TILE, b * BLOCK % TILE, BLOCK)
+        lifted = product(normed_ref[...], expand[:, at], 1, 0) + bias
+        half = 0.5 * (1.0 + lax.erf(lifted * root_half))
+        active = (lifted * half).astype(bf16)
+        active_ref[:, at] = active
+        slope = half + lifted * jnp.exp(-0.5 * lifted * lifted) * inv_root_two_pi
+        d_lifted = (product(back_ref[...], reduce[at, :], 1, 1) * slope).astype(bf16)
+        dlift_ref[:, at] = d_lifted
+        put_small(small_ref, 2 * G + b * BLOCK, column_sum(d_lifted.astype(f32)))
+        acc[...] += product(active, reduce[at, :], 1, 0)
+        dnorm[...] += product(d_lifted, expand[:, at], 1, 1)
+    out_ref[...] = acc[...].astype(bf16)
+    d_normed = dnorm[...]
+    put_small(small_ref, G, column_sum(d_normed * hat))
+    put_small(small_ref, G + D, column_sum(d_normed))
+    d_mid = back_ref[...].astype(f32) + norm_back(d_normed * second_gain, hat, scale)
+    dmid_ref[...] = d_mid
+    d_linear = (d_mid * gating).astype(bf16)
+    d_gating = (d_mid * linear * gating * (1.0 - gating)).astype(bf16)
+    dopen_ref[:, :D] = d_linear
+    dopen_ref[:, D:] = d_gating
+    put_small(small_ref, 0, column_sum(d_linear.astype(f32)))
+    put_small(small_ref, D, column_sum(d_gating.astype(f32)))
+    d_hidden = product(d_linear, gate[:, :D], 1, 1) + product(d_gating, gate[:, D:], 1, 1)
+    for k in range(parts):
+        rows = resp_ref
+        again = jnp.concatenate([resp_ref[pl.ds((d * parts + k) * nch, nch), :] for d in range(nseq)], axis=0)
+        back_turned = d_hidden[k * CH:(k + 1) * CH].T * gelu_slope(again)
+        for d in range(nseq):
+            dresp_ref[pl.ds((d * parts + k) * nch, nch), :] = back_turned[d * nch:(d + 1) * nch]
+
+
+def mlp_kernel(place, boxes, response, rows, cotangent, share, devices, nseq):
+    base, box, tiles = lay(share, devices)
+    group = rows.shape[0]
     vm = pl.BlockSpec(memory_space=pltpu.VMEM)
-    shapes = ((D, G), (D, FF), (FF, D))
+    shape = lambda r, c, t: jax.ShapeDtypeStruct((r, c), t)
     return pl.pallas_call(
-        partial(unpack_body, streams, base, tiles, devices),
-        out_shape=tuple(jax.ShapeDtypeStruct(s, bf16) for s in shapes)
-        + (jax.ShapeDtypeStruct((len(SMALL_AT) * 8, CH), f32), jax.ShapeDtypeStruct((MODE_TILES * 8, CH), f32)),
-        in_specs=[pl.BlockSpec(memory_space=pltpu.SMEM)] + [hbm] * len(arrays),
-        out_specs=(vm,) * 5,
+        partial(mlp_body, share, devices, nseq),
+        out_shape=(
+            shape(group, D, bf16),
+            shape(group, D, f32),
+            jax.ShapeDtypeStruct(response.shape, f32),
+            shape(len(SMALL_AT) * 8, CH, f32),
+            shape(MODE_TILES * 8, CH, f32),
+            shape(group, D, bf16),
+            shape(group, FF, bf16),
+            shape(group, D, bf16),
+            shape(group, D, bf16),
+            shape(group, G, bf16),
+            shape(group, FF, bf16),
+        ),
+        in_specs=[pl.BlockSpec(memory_space=pltpu.SMEM), pl.BlockSpec(memory_space=pl.ANY)] + [vm] * 3,
+        out_specs=(vm,) * 11,
         scratch_shapes=[
             pltpu.VMEM((tiles * 8, CH), f32),
-            pltpu.VMEM((3, devices * 8, CH), f32),
-            pltpu.SemaphoreType.DMA,
-            pltpu.SemaphoreType.DMA,
+            pltpu.VMEM((3, devices * 8 + 8, CH), f32),
+            pltpu.VMEM((D, G), bf16),
+            pltpu.VMEM((D, FF), bf16),
+            pltpu.VMEM((FF, D), bf16),
+            pltpu.VMEM((group, D), f32),
+            pltpu.VMEM((group, D), f32),
+            pltpu.SemaphoreType.DMA((4,)),
         ],
-        name="unpack_weights",
-    )(dest, *arrays)
-
-
-def pack_body(streams, tiles, devices, has_modes, *refs):
+        name="feed_forward",
+    )(place, boxes, response, rows, cotangent)
+
+
+def pack_body(streams, tiles, has_lead, *refs):
     n = len(streams)
-    dest, gate_ref, expand_ref, reduce_ref, small_ref = refs[:5]
-    modes_ref = refs[5] if has_modes else None
-    outs = refs[5 + has_modes:5 + has_modes + n]
-    flat, sem = refs[5 + has_modes + n:]
-    if has_modes:
-        flat[:MODE_TILES * 8, :] = modes_ref[...]
+    dest, hidden, active, normed, back, dopen, dlift, small_ref = refs[:8]
+    outs = refs[8 + has_lead:8 + has_lead + n]
+    flat, sem = refs[8 + has_lead + n:]
+    if has_lead:
+        flat[:MODE_TILES * 8, :] = refs[8][...]
     else:
         flat[:MODE_TILES * 8, :] = jnp.zeros((MODE_TILES * 8, CH), f32)
     for k, tile in enumerate(SMALL_AT):
         flat[tile * 8:(tile + 1) * 8, :] = small_ref[k * 8:(k + 1) * 8, :]
     flat[(SMALL_AT[-1] + 1) * 8:, :] = jnp.zeros(((tiles - SMALL_AT[-1] - 1) * 8, CH), f32)
-    for (first, rows, per), src in zip(strips(), (gate_ref, expand_ref, reduce_ref)):
-        def spread(i, _, first=first, per=per, src=src):
-            for k in range(per):
-                v = src[pl.ds(pl.multiple_of(i * 16, 16), 16), k * CH:(k + 1) * CH]
-                flat[pl.ds(first * 8 + i * 16 * per + k, 16, stride=per), :] = v
-            return 0
-
-        lax.fori_loop(0, rows // 16, spread, 0)
+    for first, left, right, per in ((GATE_AT, hidden, dopen, G // CH), (EXPAND_AT, normed, dlift, FF // CH), (REDUCE_AT, active, back, D // CH)):
+        wide = 128
+        flip = left[...].T
+
+        for k in range(left.shape[1] // wide):
+            v = product(flip[k * wide:(k + 1) * wide], right[...], 1, 0)
+            for c in range(per):
+                flat[pl.ds(first * 8 + k * wide * per + c, wide, stride=per), :] = v[:, c * CH:(c + 1) * CH]
     for k, (first, last, order) in enumerate(streams):
         rows = (last - first) * 8
 
@@ -422,19 +544,19 @@
         pltpu.make_async_copy(out, out, sem.at[k]).wait()
 
 
-def pack_kernel(streams, dest, grads, small, modes, share, devices):
+def pack_kernel(streams, dest, values, small, lead, share, devices):
     _, _, tiles = lay(share, devices)
     hbm = pl.BlockSpec(memory_space=pl.ANY)
     vm = pl.BlockSpec(memory_space=pltpu.VMEM)
-    has = int(modes is not None)
+    has = int(lead is not None)
     return pl.pallas_call(
-        partial(pack_body, tuple(s[:3] for s in streams), tiles, devices, has),
+        partial(pack_body, tuple(s[:3] for s in streams), tiles, has),
         out_shape=tuple(jax.ShapeDtypeStruct((blocks * (last - first) * 8, CH), f32) for first, last, _, blocks in streams),
-        in_specs=[pl.BlockSpec(memory_space=pltpu.SMEM)] + [vm] * (4 + has),
+        in_specs=[pl.BlockSpec(memory_space=pltpu.SMEM)] + [vm] * (7 + has),
         out_specs=(hbm,) * len(streams),
         scratch_shapes=[pltpu.VMEM((tiles * 8, CH), f32), pltpu.SemaphoreType.DMA((len(streams),))],
-        name="pack_gradients",
-    )(dest, *grads, small, *((modes,) if has else ()))
+        name="weight_gradients",
+    )(dest, *values, small, *((lead,) if has else ()))
 
 
 AXES = ("seq", "batch")
@@ -477,42 +599,20 @@
     return one, two
 
 
+def device_index():
+    return lax.axis_index("seq") * lax.axis_size("batch") + lax.axis_index("batch")
+
+
 def gather_weights(master, share, devices):
-    base, tiles, _ = lay(share, devices)
-    me = 2 * lax.axis_index("seq") + lax.axis_index("batch") if direct() else lax.axis_index("seq") * lax.axis_size("batch") + lax.axis_index("batch")
-    box = lax.dynamic_update_slice(jnp.zeros((tiles * TILE,), f32), master, (me * share % TILE,)).reshape(tiles * 8, CH)
-    natural = first_rows(share, devices, jnp.arange(devices, dtype=jnp.int32))
-    if not direct():
-        return (((0, tiles, 0, 0, devices),), [lax.all_gather(box, AXES, axis=0, tiled=True)], natural)
-    one, two = cuts_of(tiles, GATHER_PART)
-    lone, ltwo = box[one * 8:two * 8], box[two * 8:]
-    streams, arrays, dest = [], [], []
-    if one:
-        arrays.append(lax.all_gather(box[:one * 8], AXES, axis=0, tiled=True))
-        streams.append((0, one, 0, 0, devices))
-        dest.append(natural)
-    near_z = jnp.concatenate([lone] + [along(lone, k) for k in range(1, 4)])
-    near_p = jnp.concatenate([ltwo] + [across(ltwo, p) for p in range(1, 4)])
-    sets_z = [near_z] + [across(near_z, p) for p in range(1, 4)]
-    sets_p = [near_p] + [along(near_p, k) for k in range(1, 4)]
-    for lo, hi, sets, ids in (
-        (one, two, sets_z, lambda s, b, o: place_of(-b, s, o)),
-        (two, tiles, sets_p, lambda s, b, o: place_of(-s, b, o)),
-    ):
-        slot = 0
-        for other in range(2):
-            for s in range(4):
-                arrays.append(swap_cores(sets[s]) if other else sets[s])
-                streams.append((lo, hi, devices * bool(one) + 32 * (lo == two) + slot, slot, 4))
-                dest.append(first_rows(share, devices, jnp.stack([ids(s, b, other) for b in range(4)])))
-                slot += 4
-    return tuple(streams), arrays, jnp.concatenate(dest).astype(jnp.int32)
+    _, tiles, _ = lay(share, devices)
+    box = lax.dynamic_update_slice(jnp.zeros((tiles * TILE,), f32), master, (device_index() * share % TILE,))
+    return lax.all_gather(box.reshape(tiles * 8, CH), AXES, axis=0, tiled=True)
 
 
 def scatter_plan(share, devices):
     _, tiles, _ = lay(share, devices)
     natural = first_rows(share, devices, jnp.arange(devices, dtype=jnp.int32))
-    if not direct():
+    if not direct() or SCATTER_PART == 1:
         return ((0, tiles, 0, devices),), natural
     one, two = cuts_of(tiles, SCATTER_PART)
     streams, dest = [], []
@@ -532,7 +632,7 @@
 
 def scatter_gradients(arrays, share, devices):
     _, tiles, _ = lay(share, devices)
-    if not direct():
+    if not direct() or SCATTER_PART == 1:
         return lax.psum_scatter(arrays[0].reshape(devices, tiles * 8, CH), AXES, scatter_dimension=0)
     one, two = cuts_of(tiles, SCATTER_PART)
     pieces = []
@@ -594,31 +694,6 @@
     return v[0, 0]
 
 
-def gelu(values):
-    return 0.5 * values * (1.0 + lax.erf(values * root_half))
-
-
-def gelu_slope(values):
-    return (
-        0.5 * (1.0 + lax.erf(values * root_half))
-        + values * jnp.exp(-0.5 * values * values) * inv_root_two_pi
-    )
-
-
-def normalize(values):
-    center = values - jnp.mean(values, axis=-1, keepdims=True)
-    scale = lax.rsqrt(jnp.mean(center * center, axis=-1, keepdims=True) + norm_eps)
-    return (center * scale, scale)
-
-
-def norm_back(d_hat, hat, scale):
-    return scale * (
-        d_hat
-        - jnp.mean(d_hat, axis=-1, keepdims=True)
-        - hat * jnp.mean(d_hat * hat, axis=-1, keepdims=True)
-    )
-
-
 def to_channels(rows):
     seq = lax.axis_size("seq")
     parts = rows.shape[0] // CH
@@ -636,88 +711,42 @@
     seq, batch = lax.axis_size("seq"), lax.axis_size("batch")
     devices = seq * batch
     share = master.shape[0]
-    streams, arrays, dest = gather_weights(master, share, devices)
+    boxes = gather_weights(master, share, devices)
     group = inputs.shape[1]
     nch, nck = D // seq, seq * group // CH
     rows = inputs[0].astype(jnp.float32)
-    ends = jnp.cumsum(lengths[0])
-    offset = lax.axis_index("seq") * group
-    where = offset + jnp.arange(group, dtype=jnp.int32)
-    labels = jnp.sum((where[:, None] >= ends[None, :]).astype(jnp.int32), axis=1)
-    valid = (labels < DOCS - 1).astype(jnp.float32)
+    ends = jnp.cumsum(lengths[0]).astype(jnp.int32)
+    place = jnp.concatenate([ends, lax.axis_index("seq")[None] * group]).astype(jnp.int32)
     first_hat, first_scale = normalize(rows)
     hats = to_channels(first_hat)
-    mine = lambda v: lax.dynamic_slice_in_dim(v, lax.axis_index("seq") * nch, nch, 0)
+
+    def feed_forward(outs):
+        response = lax.all_to_all(outs.reshape(seq, -1, nch, CH), "seq", 0, 0).reshape(-1, CH)
+        return mlp_kernel(place, boxes, response, inputs[0], cotangent[0], share, devices, seq)
+
     if direct():
         few, many = read_modes(scatter_modes(master))
-        gate_low, expand_low, reduce_low, small, lead = unpack_kernel(streams, arrays, dest, share, devices)
-        lead = lead.reshape(-1)
     else:
-        gate_low, expand_low, reduce_low, small, lead = unpack_kernel(streams, arrays, dest, share, devices)
-        lead = lead.reshape(-1)
-        few = jnp.stack([mine(lead[k * D:(k + 1) * D]) for k in range(4)])
-        many = jnp.stack([mine(v) for v in lead[4 * D:].reshape(4, D, NSTATE)])
+        lead = jnp.concatenate([lax.dynamic_slice(boxes[j * (boxes.shape[0] // devices):(j + 1) * (boxes.shape[0] // devices)].reshape(-1), (j * share % TILE,), (share,)) for j in range(MODE_TILES * TILE // share + 1)])
+        mine = lambda v: lax.dynamic_slice_in_dim(v, lax.axis_index("seq") * nch, nch, 1)
+        few = mine(lead[:4 * D].reshape(4, D))
+        many = mine(lead[4 * D:MODE_TILES * TILE].reshape(4, D, NSTATE))
     modes, modes_pull = jax.vjp(mixing, few[2], many[0], many[1], many[2], many[3])
     prm = mode_rows(*modes, few[0], few[1], few[3])
     outs, prior = ssm_forward(ends, prm, hats, nck, nch)
-    small = small.reshape(-1)
-    params = {
-        "norm_gain": lead[:D],
-        "gate_bias": small[:G],
-        "second_gain": small[G:G + D],
-        "second_bias": small[G + D:G + 2 * D],
-        "expand_bias": small[2 * G:2 * G + FF],
-        "reduce_bias": small[2 * G + FF:2 * G + FF + D],
-    }
-    response = to_tokens(outs, group)
-    hidden_low = gelu(response).astype(jnp.bfloat16)
-    opened = jnp.dot(hidden_low, gate_low, preferred_element_type=jnp.float32) + params["gate_bias"]
-    linear = opened[:, :D]
-    gating = jax.nn.sigmoid(opened[:, D:])
-    mid = rows + linear * gating
-    second_hat, second_scale = normalize(mid)
-    normed_low = (second_hat * params["second_gain"] + params["second_bias"]).astype(jnp.bfloat16)
-    lifted = (
-        jnp.dot(normed_low, expand_low, preferred_element_type=jnp.float32) + params["expand_bias"]
-    )
-    active_low = gelu(lifted).astype(jnp.bfloat16)
-    result = (
-        mid
-        + jnp.dot(active_low, reduce_low, preferred_element_type=jnp.float32)
-        + params["reduce_bias"]
-    )
-    output = result.astype(jnp.bfloat16)[None]
-    back = cotangent[0].astype(jnp.float32) * valid[:, None]
-    back_low = back.astype(jnp.bfloat16)
-    g_reduce_w = jnp.einsum("tf,td->fd", active_low, back_low, preferred_element_type=jnp.float32)
-    g_reduce_b = jnp.sum(back, axis=0)
-    d_active = jnp.einsum("td,fd->tf", back_low, reduce_low, preferred_element_type=jnp.float32)
-    d_lifted = (d_active * gelu_slope(lifted)).astype(jnp.bfloat16)
-    g_expand_w = jnp.einsum("td,tf->df", normed_low, d_lifted, preferred_element_type=jnp.float32)
-    g_expand_b = jnp.sum(d_lifted.astype(jnp.float32), axis=0)
-    d_normed = jnp.einsum("tf,df->td", d_lifted, expand_low, preferred_element_type=jnp.float32)
-    g_second_gain = jnp.sum(d_normed * second_hat, axis=0)
-    g_second_bias = jnp.sum(d_normed, axis=0)
-    d_mid = back + norm_back(d_normed * params["second_gain"], second_hat, second_scale)
-    d_linear = d_mid * gating
-    d_gating = d_mid * linear * gating * (1.0 - gating)
-    d_opened = jnp.concatenate([d_linear, d_gating], axis=1).astype(jnp.bfloat16)
-    g_gate_w = jnp.einsum("td,tg->dg", hidden_low, d_opened, preferred_element_type=jnp.float32)
-    g_gate_b = jnp.sum(d_opened.astype(jnp.float32), axis=0)
-    d_hidden = jnp.einsum("tg,dg->td", d_opened, gate_low, preferred_element_type=jnp.float32)
-    d_response = d_hidden * gelu_slope(response)
-    d_outs = to_channels(d_response)
-    flat_small = jnp.concatenate([g_gate_b, g_second_gain, g_second_bias, g_expand_b, g_reduce_b, jnp.zeros((D,), f32)]).reshape(-1, CH)
+    output, d_mid, d_response, small, lead, *values = feed_forward(outs)
+    d_outs = lax.all_to_all(d_response.reshape(seq, -1, nch, CH), "seq", 0, 0).reshape(-1, CH)
     plan, places = scatter_plan(share, devices)
     d_signals, sums = ssm_backward(ends, prm, hats, d_outs, prior, nck, nch)
     d_signal = to_tokens(d_signals, group)
-    d_rows = d_mid + norm_back(d_signal * params["norm_gain"], first_hat, first_scale)
+    norm_gain = lead[:D // CH].reshape(D)
+    d_rows = d_mid + norm_back(d_signal * norm_gain, first_hat, first_scale)
     lane_sums = jnp.sum(sums[10:13], axis=-1)
     d_modes = modes_pull(mode_grads(sums, *modes))
     few = jnp.stack([lane_sums[1], lane_sums[2], d_modes[0], lane_sums[0]])
     many = jnp.stack(d_modes[1:])
     if direct():
-        packed = pack_kernel(plan, places, (g_gate_w, g_expand_w, g_reduce_w), flat_small, None, share, devices)
+        packed = pack_kernel(plan, places, values, small, None, share, devices)
     else:
 
         def spread(v):
@@ -725,8 +754,8 @@
             return lax.dynamic_update_slice_in_dim(whole, v, lax.axis_index("seq") * nch, 1)
 
         lead = jnp.concatenate([spread(few).reshape(-1), spread(many).reshape(-1)]).reshape(-1, CH)
-        packed = pack_kernel(plan, places, (g_gate_w, g_expand_w, g_reduce_w), flat_small, lead, share, devices)
-    me = lax.axis_index("seq") * batch + lax.axis_index("batch")
+        packed = pack_kernel(plan, places, values, small, lead, share, devices)
+    me = device_index()
     box = scatter_gradients(packed, share, devices)
     shard = lax.dynamic_slice(box.reshape(-1), (me * share % TILE,), (share,))
     if direct():
@@ -748,7 +777,7 @@
     first_hat_new = first_new / (1.0 - 0.9**10)
     second_hat_new = second_new / (1.0 - 0.999**10)
     update = -0.05 * (first_hat_new / (jnp.sqrt(second_hat_new) + 1e-08) + 0.1 * master)
-    return (output, d_rows[None], shard, update, first_new, second_new, grad_norm)
+    return (output[None], d_rows[None], shard, update, first_new, second_new, grad_norm)
 
 
 def solution(mesh):

time: 420 us -> 335 us (0.80)
  waiting for transfers between devices: 80.3 us -> 152 us
  Pallas kernels: 127 us -> 79.3 us
  starting transfers between devices: 89.2 us -> 47.4 us
  other arithmetic: 46.5 us -> 21.3 us
  local copies, waits for them, and re-layouts: 38.2 us -> 14.8 us
  matrix products: 17.1 us -> 0 us
    ppermute x15 -> x3, waiting for transfers between devices: 56 us -> 2.46 us  [along(): return lax.ppermute(v, 'seq', [(i, (i + 4 * step) % 16) for i in range(16)])]
    reduce_scatter x1, waiting for transfers between devices: 0.02 us -> 52.1 us  [scatter_gradients(): lax.psum_scatter(arrays[0].reshape(devices, tiles * 8, CH), AXES, scatter...]
    all_to_all x0 -> x2, waiting for transfers between devices: none -> 40.2 us  [the longest x1 20.3 us: feed_forward(): lax.all_to_all(outs.reshape(seq, -1, nch, CH), 'seq', 0, 0).reshape(-1, CH)]
    pallas_call x1, Pallas kernels: 63.9 us -> 36.4 us  [ssm_backward(): pl.pallas_call(partial(bwd_body, nck, nch), out_shape=(jax.ShapeDtypeStru...]
    ppermute x15 -> x3, starting transfers between devices: 22.1 us -> 3.83 us  [along(): return lax.ppermute(v, 'seq', [(i, (i + 4 * step) % 16) for i in range(16)])]
    ppermute x15 -> x3, starting transfers between devices: 21.7 us -> 3.48 us  [across(): return lax.ppermute(v, 'seq', [(i, i ^ step) for i in range(16)])]
    pallas_call x1, Pallas kernels: 40 us -> 21.9 us  [ssm_forward(): pl.pallas_call(partial(fwd_body, nck, nch), out_shape=(jax.ShapeDtypeStru...]
    all_to_all x2 -> x1, waiting for transfers between devices: 0.01 us -> 17.8 us  [to_channels(): return lax.all_to_all(turned, 'seq', 0, 0).reshape(-1, CH)]
  transfers between devices with their start and end apart: 68 -> 28, of which waited for: 21 -> 15; matrix products, arithmetic and copies ran while one was open for 18% -> 8% of each run, Pallas kernels for 25% -> 17%
where the time goes in v3:
time: 335 us; the launch traced here: 333 us
  waiting for transfers between devices  152 us (45%)
  Pallas kernels  79.3 us (24%)
  starting transfers between devices  47.4 us (14%)
  other arithmetic  21.3 us (6%)
  between operations  18.5 us (6%)
  local copies, waits for them, and re-layouts  14.8 us (4%)
    reduce_scatter x1, waiting for transfers between devices, scatter_gradients(): lax.psum_scatter(arrays[0].reshape(devices, tiles * 8, CH), AXES, scatter...  52.1 us
    pallas_call x1, Pallas kernels, ssm_backward(): pl.pallas_call(partial(bwd_body, nck, nch), out_shape=(jax.ShapeDtypeStru...  36.4 us
    pallas_call x1, Pallas kernels, ssm_forward(): pl.pallas_call(partial(fwd_body, nck, nch), out_shape=(jax.ShapeDtypeStru...  21.9 us
    all_to_all x1, waiting for transfers between devices, feed_forward(): lax.all_to_all(outs.reshape(seq, -1, nch, CH), 'seq', 0, 0).reshape(-1, CH)  20.3 us
    all_to_all x1, waiting for transfers between devices, per_device(): lax.all_to_all(d_response.reshape(seq, -1, nch, CH), 'seq', 0, 0)  19.8 us
    all_to_all x1, waiting for transfers between devices, to_channels(): return lax.all_to_all(turned, 'seq', 0, 0).reshape(-1, CH)  17.8 us
    ppermute x3, waiting for transfers between devices, scatter_modes(): lax.ppermute(blocks[4 * k:4 * k + 4], 'seq', [(0, 4 * k)])  14.2 us
    pallas_call x1, Pallas kernels, mlp_kernel(): pl.pallas_call(partial(mlp_body, share, devices, nseq), out_shape=(shape(...  12.2 us
  transfers between devices with their start and end apart: 28, of which 15 were waited for; matrix products, arithmetic and copies ran while one was open for 8% of the time, Pallas kernels for 17%

profile of v3, /device:TPU:0, one launch (start us, length us, event | category | flops | bytes accessed | tf_op | source)
XLA Modules:
  0.0 333.4 jit_solution(3889043191181104180)
XLA Ops:
  7.3 3.7 %dynamic_update_slice.3 = f32[88064]{0:T(1024)S(1)} dynamic-update-slice(f32[88064]{0:T(1024)S(1)} %broadcast_in_dim.11, f32[86224]{0:T(1024)} %param.10, s32[]{:T(128)S(6)} %select_n.62) | dynamic-update-slice | bytes 689796 | tf_op jit(solution)/shard_map/dynamic_update_slice | solution.py:608
  17.4 4.5 %collective-permute-start.1 = (f32[4,65,128]{2,1,0:T(8,128)S(1)}, f32[4,65,128]{2,1,0:T(8,128)S(1)}, u32[]{:S(2)}, u32[]{:S(2)}) collective-permute-start(f32[4,65,128]{2,1,0:T(8,128)S(1)} %get-tuple-element.67), channel_id=1, source_target_pairs={{0,8},{1,9}} | collective-permute-start | bytes 399368 | tf_op jit(solution)/shard_map/ppermute | solution.py:663
  25.3 2.8 collective-permute-done.1
  28.1 6.3 %collective-permute-done.2 = f32[4,65,128]{2,1,0:T(8,128)S(1)} collective-permute-done((f32[4,65,128]{2,1,0:T(8,128)S(1)}, f32[4,65,128]{2,1,0:T(8,128)S(1)}, u32[]{:S(2)}, u32[]{:S(2)}) %collective-permute-start.2) | collective-permute-done | bytes 133152 | tf_op jit(solution)/shard_map/ppermute | solution.py:663
  34.4 5.0 %collective-permute-done.3 = f32[4,65,128]{2,1,0:T(8,128)S(1)} collective-permute-done((f32[4,65,128]{2,1,0:T(8,128)S(1)}, f32[4,65,128]{2,1,0:T(8,128)S(1)}, u32[]{:S(2)}, u32[]{:S(2)}) %collective-permute-start.3) | collective-permute-done | bytes 133152 | tf_op jit(solution)/shard_map/ppermute | solution.py:663
  44.4 5.7 %all-to-all-start = ((f32[16,2,32,128]{3,1,2,0:T(2,128)}), f32[16,2,32,128]{3,1,2,0:T(2,128)S(1)}, u32[]{:S(2)}, u32[]{:S(2)}) async-start(f32[16,2,32,128]{3,1,2,0:T(2,128)} %fusion.14), calls=%async_computation | async-start | bytes 1048576 | tf_op jit(solution)/shard_map/all_to_all | solution.py:701
  54.7 17.8 %all-to-all-done = f32[16,2,32,128]{3,1,2,0:T(2,128)S(1)} async-done(((f32[16,2,32,128]{3,1,2,0:T(2,128)}), f32[16,2,32,128]{3,1,2,0:T(2,128)S(1)}, u32[]{:S(2)}, u32[]{:S(2)}) %all-to-all-start) | async-done | bytes 524320 | tf_op jit(solution)/shard_map/all_to_all | solution.py:701
  73.3 21.9 %state_forward.1 = (f32[1024,128]{1,0:T(8,128)}, f32[1024,128]{1,0:T(8,128)}) custom-call(s32[4]{0:T(128)} %bitcast.282, f32[32,24,128]{2,1,0:T(8,128)} %concatenate.45.prm_ref, f32[1024,128]{1,0:T(8,128)} %bitcast.254), custom_call_target="tpu_custom_call" | custom-call | tf_op jit(solution)/shard_map/state_forward/pallas_call | solution.py:134
  95.2 5.2 %all-to-all-start.1 = ((f32[16,2,32,128]{3,2,1,0:T(8,128)}), f32[16,2,32,128]{3,2,1,0:T(8,128)S(1)}, u32[]{:S(2)}, u32[]{:S(2)}) async-start(f32[16,2,32,128]{3,2,1,0:T(8,128)} %bitcast.270), calls=%async_computation.1 | async-start | bytes 1048576 | tf_op jit(solution)/shard_map/all_to_all | solution.py:724
  102.4 20.3 %all-to-all-done.1 = f32[16,2,32,128]{3,2,1,0:T(8,128)S(1)} async-done(((f32[16,2,32,128]{3,2,1,0:T(8,128)}), f32[16,2,32,128]{3,2,1,0:T(8,128)S(1)}, u32[]{:S(2)}, u32[]{:S(2)}) %all-to-all-start.1) | async-done | bytes 524320 | tf_op jit(solution)/shard_map/all_to_all | solution.py:724
  122.7 2.6 all-gather.2.cloned.1.call-done.boxes
  125.4 12.2 %feed_forward.1 = (bf16[256,512]{1,0:T(8,128)(2,1)}, f32[256,512]{1,0:T(8,128)}, f32[1024,128]{1,0:T(8,128)}, f32[40,128]{1,0:T(8,128)}, f32[1040,128]{1,0:T(8,1...) custom-call(s32[5]{0:T(128)} %pad_add_fusion.place_ref, ...), custom_call_target="tpu_custom_call" | custom-call | tf_op jit(solution)/shard_map/feed_forward/pallas_call | solution.py:483
  137.6 8.8 %weight_gradients.1 = f32[22016,128]{1,0:T(8,128)} custom-call(s32[32]{0:T(128)} %fusion.51.refs_0_, bf16[256,512]{1,0:T(8,128)(2,1)} %get-tuple-element.30.refs_1_, bf16[256,2048]{1,0:T(8,128)(2,1)} %get-tuple-element.31.refs_2_, bf16[256,512]{1,0:T(8,128)(2,1)} %get-tuple-element.32.refs_3_, bf16[256,512]{1,0:T(8,128)(2,1)} %get-tuple-element.33.refs_4_, ...), custom_call_target="tpu_custom_call" | custom-call | tf_op jit(solution)/shard_map/weight_gradients/pallas_call | solution.py:552
  146.5 4.0 %all-to-all-start.2 = ((f32[16,2,32,128]{3,2,1,0:T(8,128)}), f32[16,2,32,128]{3,2,1,0:T(8,128)S(1)}, u32[]{:S(2)}, u32[]{:S(2)}) async-start(f32[16,2,32,128]{3,2,1,0:T(8,128)} %bitcast.36), calls=%async_computation.2 | async-start | bytes 1048576 | tf_op jit(solution)/shard_map/all_to_all | solution.py:738
  151.5 19.8 %all-to-all-done.2 = f32[16,2,32,128]{3,2,1,0:T(8,128)S(1)} async-done(((f32[16,2,32,128]{3,2,1,0:T(8,128)}), f32[16,2,32,128]{3,2,1,0:T(8,128)S(1)}, u32[]{:S(2)}, u32[]{:S(2)}) %all-to-all-start.2) | async-done | bytes 524320 | tf_op jit(solution)/shard_map/all_to_all | solution.py:738
  172.1 36.4 %state_backward.1 = (f32[1024,128]{1,0:T(8,128)}, f32[16,32,128]{2,1,0:T(8,128)}) custom-call(s32[4]{0:T(128)} %bitcast.284, f32[32,24,128]{2,1,0:T(8,128)} %concatenate.45.prm_ref, f32[1024,128]{1,0:T(8,128)} %bitcast.255, f32[1024,128]{1,0:T(8,128)} %bitcast.260, f32[1024,128]{1,0:T(8,128)} %get-tuple-element.26.prior_ref), custom_call_target="tpu_custom_call" | custom-call | tf_op jit(solution)/shard_map/state_backward/pallas_call | solution.py:232
  217.0 4.3 %all-to-all-start.3 = ((f32[16,2,32,128]{3,1,2,0:T(2,128)}), f32[16,2,32,128]{3,1,2,0:T(2,128)S(1)}, u32[]{:S(2)}, u32[]{:S(2)}) async-start(f32[16,2,32,128]{3,1,2,0:T(2,128)} %copy.35), calls=%async_computation.3 | async-start | bytes 1048576 | tf_op jit(solution)/shard_map/all_to_all | solution.py:706
  227.9 3.1 collective-permute-done.9
  231.0 5.5 %collective-permute-done.11 = f32[65,128]{1,0:T(8,128)S(1)} collective-permute-done((f32[65,128]{1,0:T(8,128)S(1)}, f32[65,128]{1,0:T(8,128)S(1)}, u32[]{:S(2)}, u32[]{:S(2)}) %collective-permute-start.11) | collective-permute-done | bytes 33312 | tf_op jit(solution)/shard_map/ppermute | solution.py:678
  240.4 11.8 %collective-permute-done.12 = f32[4,65,128]{2,1,0:T(8,128)S(1)} collective-permute-done((f32[4,65,128]{2,1,0:T(8,128)S(1)}, f32[4,65,128]{2,1,0:T(8,128)S(1)}, u32[]{:S(2)}, u32[]{:S(2)}) %collective-permute-start.12) | collective-permute-done | bytes 133152 | tf_op jit(solution)/shard_map/ppermute | solution.py:680
  253.3 52.1 %reduce-scatter.2.cloned.1.call-done = f32[1,688,128]{2,1,0:T(8,128)} async-done(((f32[32,688,128]{2,1,0:T(8,128)}), f32[1,688,128]{2,1,0:T(8,128)}) %reduce-scatter.2.cloned.1.call-update) | async-done | bytes 352272 | tf_op jit(solution)/shard_map/reduce_scatter | solution.py:636
  309.0 3.5 %collective-permute-start.18 = (f32[8,128]{1,0:T(8,128)S(1)}, f32[8,128]{1,0:T(8,128)S(1)}, u32[]{:S(2)}, u32[]{:S(2)}) collective-permute-start(f32[8,128]{1,0:T(8,128)S(1)} %broadcast_add_fusion), channel_id=1, source_target_pairs={{0,6},{2,4},{4,2},{6,0},{8,14},{10,12},{12,10},{14,8},{16,22},{18,... | collective-permute-start | bytes 12296 | tf_op jit(solution)/shard_map/ppermute | solution.py:571
  314.1 3.7 %collective-permute-start.20 = (f32[8,128]{1,0:T(8,128)S(1)}, f32[8,128]{1,0:T(8,128)S(1)}, u32[]{:S(2)}, u32[]{:S(2)}) collective-permute-start(f32[8,128]{1,0:T(8,128)S(1)} %add_add_fusion.3), channel_id=1, source_target_pairs={{0,16},{2,18},{4,20},{6,22},{8,24},{10,26},{12,28},{14,30},{16,0},... | collective-permute-start | bytes 12296 | tf_op jit(solution)/shard_map/ppermute | solution.py:575
  322.7 2.8 add_multiply_fusion
  (150 shorter events, 51.2 us)
Async XLA Ops:
  7.2 118.2 %all-gather.2.cloned.1.call-start = ((), (), s32[]{:S(2)}) async-start(), calls=%async_computation.5 | async-start | bytes 11624448 | tf_op jit(solution)/shard_map/all_gather | solution.py:609
  11.8 4.1 %collective-permute-start = (f32[86224]{0:T(1024)}, f32[86224]{0:T(1024)S(1)}, u32[]{:S(2)}, u32[]{:S(2)}) collective-permute-start(f32[86224]{0:T(1024)} %param.10), channel_id=1, source_target_pairs={{0,1},{1,0},{2,3},{3,2},{4,5},{5,4},{6,7},{7,6},{8,9},{9,8},{10,11... | collective-permute-start | bytes 1034696 | tf_op jit(solution)/shard_map/ppermute | solution.py:579
  17.4 10.7 %collective-permute-start.1 = (f32[4,65,128]{2,1,0:T(8,128)S(1)}, f32[4,65,128]{2,1,0:T(8,128)S(1)}, u32[]{:S(2)}, u32[]{:S(2)}) collective-permute-start(f32[4,65,128]{2,1,0:T(8,128)S(1)} %get-tuple-element.67), channel_id=1, source_target_pairs={{0,8},{1,9}} | collective-permute-start | bytes 399368 | tf_op jit(solution)/shard_map/ppermute | solution.py:663
  21.9 12.5 %collective-permute-start.2 = (f32[4,65,128]{2,1,0:T(8,128)S(1)}, f32[4,65,128]{2,1,0:T(8,128)S(1)}, u32[]{:S(2)}, u32[]{:S(2)}) collective-permute-start(f32[4,65,128]{2,1,0:T(8,128)S(1)} %get-tuple-element.66), channel_id=1, source_target_pairs={{0,16},{1,17}} | collective-permute-start | bytes 399368 | tf_op jit(solution)/shard_map/ppermute | solution.py:663
  23.6 15.9 %collective-permute-start.3 = (f32[4,65,128]{2,1,0:T(8,128)S(1)}, f32[4,65,128]{2,1,0:T(8,128)S(1)}, u32[]{:S(2)}, u32[]{:S(2)}) collective-permute-start(f32[4,65,128]{2,1,0:T(8,128)S(1)} %get-tuple-element.68), channel_id=1, source_target_pairs={{0,24},{1,25}} | collective-permute-start | bytes 399368 | tf_op jit(solution)/shard_map/ppermute | solution.py:663
  39.5 11.4 %collective-permute-start.4 = (f32[65,128]{1,0:T(8,128)S(1)}, f32[65,128]{1,0:T(8,128)S(1)}, u32[]{:S(2)}, u32[]{:S(2)}) collective-permute-start(f32[65,128]{1,0:T(8,128)S(1)} %get-tuple-element.71), channel_id=1, source_target_pairs={{0,2},{8,10},{16,18},{24,26},{1,3},{9,11},{17,19},{25,27}} | collective-permute-start | bytes 99848 | tf_op jit(solution)/shard_map/ppermute | solution.py:665
  40.8 10.1 %collective-permute-start.5 = (f32[65,128]{1,0:T(8,128)S(1)}, f32[65,128]{1,0:T(8,128)S(1)}, u32[]{:S(2)}, u32[]{:S(2)}) collective-permute-start(f32[65,128]{1,0:T(8,128)S(1)} %get-tuple-element.69), channel_id=1, source_target_pairs={{0,4},{8,12},{16,20},{24,28},{1,5},{9,13},{17,21},{25,29}} | collective-permute-start | bytes 99848 | tf_op jit(solution)/shard_map/ppermute | solution.py:665
  42.1 8.8 %collective-permute-start.6 = (f32[65,128]{1,0:T(8,128)S(1)}, f32[65,128]{1,0:T(8,128)S(1)}, u32[]{:S(2)}, u32[]{:S(2)}) collective-permute-start(f32[65,128]{1,0:T(8,128)S(1)} %get-tuple-element.70), channel_id=1, source_target_pairs={{0,6},{8,14},{16,22},{24,30},{1,7},{9,15},{17,23},{25,31}} | collective-permute-start | bytes 99848 | tf_op jit(solution)/shard_map/ppermute | solution.py:665
  44.4 28.0 %all-to-all-start = ((f32[16,2,32,128]{3,1,2,0:T(2,128)}), f32[16,2,32,128]{3,1,2,0:T(2,128)S(1)}, u32[]{:S(2)}, u32[]{:S(2)}) async-start(f32[16,2,32,128]{3,1,2,0:T(2,128)} %fusion.14), calls=%async_computation | async-start | bytes 1048576 | tf_op jit(solution)/shard_map/all_to_all | solution.py:701
  95.2 27.5 %all-to-all-start.1 = ((f32[16,2,32,128]{3,2,1,0:T(8,128)}), f32[16,2,32,128]{3,2,1,0:T(8,128)S(1)}, u32[]{:S(2)}, u32[]{:S(2)}) async-start(f32[16,2,32,128]{3,2,1,0:T(8,128)} %bitcast.270), calls=%async_computation.1 | async-start | bytes 1048576 | tf_op jit(solution)/shard_map/all_to_all | solution.py:724
  100.4 205.0 %reduce-scatter.2.cloned.1.call-start = ((), (), s32[]{:S(2)}) async-start(), calls=%async_computation.6 | async-start | bytes 11624448 | tf_op jit(solution)/shard_map/reduce_scatter | solution.py:636
  146.5 24.9 %all-to-all-start.2 = ((f32[16,2,32,128]{3,2,1,0:T(8,128)}), f32[16,2,32,128]{3,2,1,0:T(8,128)S(1)}, u32[]{:S(2)}, u32[]{:S(2)}) async-start(f32[16,2,32,128]{3,2,1,0:T(8,128)} %bitcast.36), calls=%async_computation.2 | async-start | bytes 1048576 | tf_op jit(solution)/shard_map/all_to_all | solution.py:738
  212.0 9.3 %collective-permute-start.7 = (f32[4,32]{1,0:T(4,128)S(1)}, f32[4,32]{1,0:T(4,128)S(1)}, u32[]{:S(2)}, u32[]{:S(2)}) collective-permute-start(f32[4,32]{1,0:T(4,128)S(1)} %pad_maximum_fusion.9), channel_id=1, source_target_pairs={{0,1},{1,0},{2,3},{3,2},{4,5},{5,4},{6,7},{7,6},{8,9},{9,8},{10,11... | collective-permute-start | bytes 1544 | tf_op jit(solution)/shard_map/ppermute | solution.py:579
  214.2 7.8 %collective-permute-start.8 = (f32[4,32,64]{2,1,0:T(8,128)S(1)}, f32[4,32,64]{2,1,0:T(8,128)S(1)}, u32[]{:S(2)}, u32[]{:S(2)}) collective-permute-start(f32[4,32,64]{2,1,0:T(8,128)S(1)} %pad_maximum_fusion.4), channel_id=1, source_target_pairs={{0,1},{1,0},{2,3},{3,2},{4,5},{5,4},{6,7},{7,6},{8,9},{9,8},{10,11... | collective-permute-start | bytes 98312 | tf_op jit(solution)/shard_map/ppermute | solution.py:579
  217.0 35.6 %all-to-all-start.3 = ((f32[16,2,32,128]{3,1,2,0:T(2,128)}), f32[16,2,32,128]{3,1,2,0:T(2,128)S(1)}, u32[]{:S(2)}, u32[]{:S(2)}) async-start(f32[16,2,32,128]{3,1,2,0:T(2,128)} %copy.35), calls=%async_computation.3 | async-start | bytes 1048576 | tf_op jit(solution)/shard_map/all_to_all | solution.py:706
  222.7 8.3 %collective-permute-start.9 = (f32[65,128]{1,0:T(8,128)S(1)}, f32[65,128]{1,0:T(8,128)S(1)}, u32[]{:S(2)}, u32[]{:S(2)}) collective-permute-start(f32[65,128]{1,0:T(8,128)S(1)} %get-tuple-element.86), channel_id=1, source_target_pairs={{2,0},{10,8},{18,16},{26,24},{3,1},{11,9},{19,17},{27,25}} | collective-permute-start | bytes 99848 | tf_op jit(solution)/shard_map/ppermute | solution.py:678
  224.0 7.0 %collective-permute-start.10 = (f32[65,128]{1,0:T(8,128)S(1)}, f32[65,128]{1,0:T(8,128)S(1)}, u32[]{:S(2)}, u32[]{:S(2)}) collective-permute-start(f32[65,128]{1,0:T(8,128)S(1)} %get-tuple-element.86), channel_id=1, source_target_pairs={{4,0},{12,8},{20,16},{28,24},{5,1},{13,9},{21,17},{29,25}} | collective-permute-start | bytes 99848 | tf_op jit(solution)/shard_map/ppermute | solution.py:678
  225.3 11.1 %collective-permute-start.11 = (f32[65,128]{1,0:T(8,128)S(1)}, f32[65,128]{1,0:T(8,128)S(1)}, u32[]{:S(2)}, u32[]{:S(2)}) collective-permute-start(f32[65,128]{1,0:T(8,128)S(1)} %get-tuple-element.86), channel_id=1, source_target_pairs={{6,0},{14,8},{22,16},{30,24},{7,1},{15,9},{23,17},{31,25}} | collective-permute-start | bytes 99848 | tf_op jit(solution)/shard_map/ppermute | solution.py:678
  236.5 15.7 %collective-permute-start.12 = (f32[4,65,128]{2,1,0:T(8,128)S(1)}, f32[4,65,128]{2,1,0:T(8,128)S(1)}, u32[]{:S(2)}, u32[]{:S(2)}) collective-permute-start(f32[4,65,128]{2,1,0:T(8,128)S(1)} %pad_maximum_fusion.3), channel_id=1, source_target_pairs={{8,0},{9,1}} | collective-permute-start | bytes 399368 | tf_op jit(solution)/shard_map/ppermute | solution.py:680
  237.8 14.4 %collective-permute-start.13 = (f32[4,65,128]{2,1,0:T(8,128)S(1)}, f32[4,65,128]{2,1,0:T(8,128)S(1)}, u32[]{:S(2)}, u32[]{:S(2)}) collective-permute-start(f32[4,65,128]{2,1,0:T(8,128)S(1)} %pad_maximum_fusion.3), channel_id=1, source_target_pairs={{16,0},{17,1}} | collective-permute-start | bytes 399368 | tf_op jit(solution)/shard_map/ppermute | solution.py:680
  239.1 13.2 %collective-permute-start.14 = (f32[4,65,128]{2,1,0:T(8,128)S(1)}, f32[4,65,128]{2,1,0:T(8,128)S(1)}, u32[]{:S(2)}, u32[]{:S(2)}) collective-permute-start(f32[4,65,128]{2,1,0:T(8,128)S(1)} %pad_maximum_fusion.3), channel_id=1, source_target_pairs={{24,0},{25,1}} | collective-permute-start | bytes 399368 | tf_op jit(solution)/shard_map/ppermute | solution.py:680
  309.0 5.1 %collective-permute-start.18 = (f32[8,128]{1,0:T(8,128)S(1)}, f32[8,128]{1,0:T(8,128)S(1)}, u32[]{:S(2)}, u32[]{:S(2)}) collective-permute-start(f32[8,128]{1,0:T(8,128)S(1)} %broadcast_add_fusion), channel_id=1, source_target_pairs={{0,6},{2,4},{4,2},{6,0},{8,14},{10,12},{12,10},{14,8},{16,22},{18,... | collective-permute-start | bytes 12296 | tf_op jit(solution)/shard_map/ppermute | solution.py:571
  314.1 5.4 %collective-permute-start.19 = (f32[8,128]{1,0:T(8,128)S(1)}, f32[8,128]{1,0:T(8,128)S(1)}, u32[]{:S(2)}, u32[]{:S(2)}) collective-permute-start(f32[8,128]{1,0:T(8,128)S(1)} %add_add_fusion.3), channel_id=1, source_target_pairs={{0,8},{2,10},{4,12},{6,14},{8,16},{10,18},{12,20},{14,22},{16,24},... | collective-permute-start | bytes 12296 | tf_op jit(solution)/shard_map/ppermute | solution.py:575
  314.1 5.4 %collective-permute-start.20 = (f32[8,128]{1,0:T(8,128)S(1)}, f32[8,128]{1,0:T(8,128)S(1)}, u32[]{:S(2)}, u32[]{:S(2)}) collective-permute-start(f32[8,128]{1,0:T(8,128)S(1)} %add_add_fusion.3), channel_id=1, source_target_pairs={{0,16},{2,18},{4,20},{6,22},{8,24},{10,26},{12,28},{14,30},{16,0},... | collective-permute-start | bytes 12296 | tf_op jit(solution)/shard_map/ppermute | solution.py:575
  (12 other events, 623.0 us)
Sparse Core Ops, SparseCore 0:
  11.9 113.4 all-gather.1
  146.6 158.7 reduce-scatter.1

commit v4 on v3

--- a/solution.py
+++ b/solution.py
@@ -1,5 +1,7 @@
 from functools import partial
-import jax, jax.numpy as jnp
+import jax
+import jax.numpy as jnp
+import numpy as np
 from jax import lax
 from jax.experimental import pallas as pl
 from jax.experimental.pallas import tpu as pltpu
@@ -11,7 +13,7 @@
 DOCS = 4
 G = 1024
 FF = 2048
-SCATTER_PART = 1
+ALONG_PART = 0.75
 
 
 norm_eps = 1e-05
@@ -96,12 +98,12 @@
         total = total + v[k * nck:(k + 1) * nck] * masks_ref[k]
     return total
 
-def fwd_body(nck, nch, ends_ref, prm_ref, x_ref, y_ref, prior_ref, masks_ref, end_ref, gt_ref):
+def fwd_body(nck, nch, apart, ends_ref, prm_ref, x_ref, y_ref, prior_ref, masks_ref, end_ref, gt_ref):
     make_masks(ends_ref, masks_ref, nck)
 
     def one(h, _):
         prm = prm_ref[h]
-        u = x_ref[pl.ds(h, nck, stride=nch), :] * prm[19:20] + prm[20:21]
+        u = x_ref[pl.ds(h, nck, stride=apart), :] * prm[19:20] + prm[20:21]
         table = ladder(prm, 1)
         down = ladder(prm, -1)
         gt_ref[h] = twist(table, prm[17:18], prm[18:19])
@@ -132,7 +134,7 @@
 def ssm_forward(ends, prm, x, nck, nch):
     vm = pl.BlockSpec(memory_space=pltpu.VMEM)
     return pl.pallas_call(
-        partial(fwd_body, nck, nch),
+        partial(fwd_body, nck, nch, x.shape[0] // nck),
         out_shape=(jax.ShapeDtypeStruct((nck * nch, CH), f32), jax.ShapeDtypeStruct((nck * nch, 2 * NSTATE), f32)),
         in_specs=[pl.BlockSpec(memory_space=pltpu.SMEM), vm, vm],
         out_specs=(vm, vm),
@@ -141,10 +143,11 @@
             pltpu.VMEM((nck * nch, 2 * NSTATE), f32),
             pltpu.VMEM((nch, CH, 2 * NSTATE), f32),
         ],
+        cost_estimate=pl.CostEstimate(flops=int(2.0e10), bytes_accessed=3 * 2**20, transcendentals=0),
         name="state_forward",
     )(ends, prm, x)
 
-def bwd_body(nck, nch, ends_ref, prm_ref, x_ref, g_ref, prior_ref, dx_ref, rows_ref, masks_ref, lead_ref, adj_ref, table_ref):
+def bwd_body(nck, nch, apart, ends_ref, prm_ref, x_ref, g_ref, prior_ref, dx_ref, rows_ref, masks_ref, lead_ref, adj_ref, table_ref):
     make_masks(ends_ref, masks_ref, nck)
 
     def one(h, _):
@@ -184,7 +187,7 @@
 
     def two(h, _):
         prm = prm_ref[h]
-        x = x_ref[pl.ds(h, nck, stride=nch), :]
+        x = x_ref[pl.ds(h, nck, stride=apart), :]
         u = x * prm[19:20] + prm[20:21]
         g = g_ref[pl.ds(h, nck, stride=nch), :]
         table = table_ref[h]
@@ -197,7 +200,7 @@
         du = fold_rows(dot3(gm, mat, 1, 1), masks_ref, nck)
         du = du + dot3(adjoint, split(down), 1, 1) * masks_ref[DOCS + 1]
         du = du + prm[21:22] * g
-        dx_ref[pl.ds(h, nck, stride=nch), :] = du
+        dx_ref[pl.ds(h, nck, stride=apart), :] = du
         flipped = [jnp.dot(v, flip, preferred_element_type=f32).astype(bf16) for v in um]
         square = dot3(flipped, gm, 0, 0)
         square = jnp.where(row + col >= CH - 1, square, 0.0)
@@ -230,7 +233,7 @@
 def ssm_backward(ends, prm, x, g, prior, nck, nch):
     vm = pl.BlockSpec(memory_space=pltpu.VMEM)
     return pl.pallas_call(
-        partial(bwd_body, nck, nch),
+        partial(bwd_body, nck, nch, x.shape[0] // nck),
         out_shape=(jax.ShapeDtypeStruct((nck * nch, CH), f32), jax.ShapeDtypeStruct((16, nch, 2 * NSTATE), f32)),
         in_specs=[pl.BlockSpec(memory_space=pltpu.SMEM), vm, vm, vm, vm],
         out_specs=(vm, vm),
@@ -240,6 +243,7 @@
             pltpu.VMEM((nck * nch, 2 * NSTATE), f32),
             pltpu.VMEM((nch, CH, 2 * NSTATE), f32),
         ],
+        cost_estimate=pl.CostEstimate(flops=int(3.5e10), bytes_accessed=4 * 2**20, transcendentals=0),
         name="state_backward",
     )(ends, prm, x, g, prior)
 
@@ -360,30 +364,32 @@
     return jnp.sum(v, axis=0, keepdims=True)
 
 
-def mlp_body(share, devices, nseq, place_ref, boxes, resp_ref, x_ref, cot_ref, out_ref, dmid_ref, dresp_ref, small_ref, lead_ref, hidden_ref, active_ref, normed_ref, back_ref, dopen_ref, dlift_ref, flat, side, gate, expand, reduce, acc, dnorm, sems):
+def mlp_body(share, devices, nseq, streams, place_ref, ids, *refs):
+    boxes = refs[:len(streams)]
+    resp_ref, x_ref, cot_ref, out_ref, dmid_ref, dresp_ref, small_ref, lead_ref, hidden_ref, active_ref, normed_ref, back_ref, dopen_ref, dlift_ref, flat, side, gate, expand, reduce, acc, dnorm, sems = refs[len(streams):]
     base, box, _ = lay(share, devices)
     nch = D // nseq
     group = x_ref.shape[0]
     start_of = lambda j: (j * share) // TILE
-    edges = [0] + [min(devices, tile * TILE // share + 1) for tile in (EXPAND_AT, REDUCE_AT)] + [devices]
-
-    def copy_side(j, _):
-        for s, tile in enumerate((0, base, base + 1)):
-            pltpu.make_async_copy(boxes.at[pl.ds(pl.multiple_of((j * box + tile) * 8, 8), 8), :], side.at[s, pl.ds(pl.multiple_of(j * 8, 8), 8), :], sems.at[3]).start()
-        return 0
-
-    lax.fori_loop(0, devices, copy_side, 0)
-    for g in range(3):
-
-        def copy_box(j, _, g=g):
+    inside = 0
+    for k, (first, last, off, count) in enumerate(streams):
+        lo, hi = max(first, 1), min(last, base)
+
+        def copy_box(i, _, k=k, first=first, last=last, lo=lo, hi=hi, off=off):
+            j = ids[off + i]
+            begin = (i * (last - first) - first) * 8
+            for s, tile in enumerate((0, base, base + 1)):
+                if first <= tile < last:
+                    pltpu.make_async_copy(boxes[k].at[pl.ds(pl.multiple_of(begin + tile * 8, 8), 8), :], side.at[s, pl.ds(pl.multiple_of(j * 8, 8), 8), :], sems.at[1]).start()
             pltpu.make_async_copy(
-                boxes.at[pl.ds(pl.multiple_of((j * box + 1) * 8, 8), (base - 1) * 8), :],
-                flat.at[pl.ds(pl.multiple_of((start_of(j) + 1) * 8, 8), (base - 1) * 8), :],
-                sems.at[g],
+                boxes[k].at[pl.ds(pl.multiple_of(begin + lo * 8, 8), (hi - lo) * 8), :],
+                flat.at[pl.ds(pl.multiple_of((start_of(j) + lo) * 8, 8), (hi - lo) * 8), :],
+                sems.at[0],
             ).start()
             return 0
 
-        lax.fori_loop(edges[g], edges[g + 1], copy_box, 0)
+        lax.fori_loop(0, count, copy_box, 0)
+        inside += (hi - lo) * count
     parts = group // CH
     turned = [
         jnp.concatenate([resp_ref[pl.ds((d * parts + k) * nch, nch), :] for d in range(nseq)], axis=0).T
@@ -397,11 +403,10 @@
         total = total + (pos >= place_ref[k]).astype(jnp.int32)
     back = jnp.where(total < DOCS - 1, cot_ref[...].astype(f32), 0.0)
     back_ref[...] = back.astype(bf16)
-    acc[...] = back
     put_small(small_ref, 2 * G + FF, column_sum(back))
     small_ref[36:40, :] = jnp.zeros((4, CH), f32)
     inner = side.at[:, pl.ds(0, devices * 8), :]
-    pltpu.make_async_copy(inner, inner, sems.at[3]).wait()
+    pltpu.make_async_copy(inner, inner, sems.at[1]).wait()
     side[0, devices * 8:, :] = jnp.zeros((8, CH), f32)
     flat[:8, :] = side[0, :8, :]
 
@@ -417,12 +422,8 @@
 
     lax.fori_loop(0, devices, join, 0)
 
-    def arrived(g):
-        rows = (edges[g + 1] - edges[g]) * (base - 1) * 8
-        some = flat.at[pl.ds(0, rows), :]
-        pltpu.make_async_copy(some, some, sems.at[g]).wait()
-
-    arrived(0)
+    some = flat.at[pl.ds(0, inside * 8), :]
+    pltpu.make_async_copy(some, some, sems.at[0]).wait()
     lead_ref[...] = flat[:MODE_TILES * 8, :]
     narrow(flat, gate, GATE_AT, D, G // CH)
     gate_bias = small_row(flat, SMALL_AT[0], 0, G)
@@ -434,10 +435,7 @@
     mid = x_ref[...].astype(f32) + linear * gating
     hat, scale = normalize(mid)
     normed_ref[...] = (hat * second_gain + second_bias).astype(bf16)
-    out_acc = mid
-    arrived(1)
     narrow(flat, expand, EXPAND_AT, D, FF // CH)
-    arrived(2)
     narrow(flat, reduce, REDUCE_AT, FF, D // CH)
     dnorm[...] = jnp.zeros((group, D), f32)
     acc[...] = mid + small_row(flat, SMALL_AT[4], 0, D)
@@ -468,20 +466,19 @@
     put_small(small_ref, D, column_sum(d_gating.astype(f32)))
     d_hidden = product(d_linear, gate[:, :D], 1, 1) + product(d_gating, gate[:, D:], 1, 1)
     for k in range(parts):
-        rows = resp_ref
         again = jnp.concatenate([resp_ref[pl.ds((d * parts + k) * nch, nch), :] for d in range(nseq)], axis=0)
         back_turned = d_hidden[k * CH:(k + 1) * CH].T * gelu_slope(again)
         for d in range(nseq):
             dresp_ref[pl.ds((d * parts + k) * nch, nch), :] = back_turned[d * nch:(d + 1) * nch]
 
 
-def mlp_kernel(place, boxes, response, rows, cotangent, share, devices, nseq):
+def mlp_kernel(place, streams, ids, boxes, response, rows, cotangent, share, devices, nseq):
     base, box, tiles = lay(share, devices)
     group = rows.shape[0]
     vm = pl.BlockSpec(memory_space=pltpu.VMEM)
     shape = lambda r, c, t: jax.ShapeDtypeStruct((r, c), t)
     return pl.pallas_call(
-        partial(mlp_body, share, devices, nseq),
+        partial(mlp_body, share, devices, nseq, streams),
         out_shape=(
             shape(group, D, bf16),
             shape(group, D, f32),
@@ -495,7 +492,7 @@
             shape(group, G, bf16),
             shape(group, FF, bf16),
         ),
-        in_specs=[pl.BlockSpec(memory_space=pltpu.SMEM), pl.BlockSpec(memory_space=pl.ANY)] + [vm] * 3,
+        in_specs=[pl.BlockSpec(memory_space=pltpu.SMEM)] * 2 + [pl.BlockSpec(memory_space=pl.ANY)] * len(boxes) + [vm] * 3,
         out_specs=(vm,) * 11,
         scratch_shapes=[
             pltpu.VMEM((tiles * 8, CH), f32),
@@ -505,10 +502,11 @@
             pltpu.VMEM((FF, D), bf16),
             pltpu.VMEM((group, D), f32),
             pltpu.VMEM((group, D), f32),
-            pltpu.SemaphoreType.DMA((4,)),
+            pltpu.SemaphoreType.DMA((2,)),
         ],
+        cost_estimate=pl.CostEstimate(flops=int(1.0e10), bytes_accessed=20 * 2**20, transcendentals=0),
         name="feed_forward",
-    )(place, boxes, response, rows, cotangent)
+    )(place, ids, *boxes, response, rows, cotangent)
 
 
 def pack_body(streams, tiles, has_lead, *refs):
@@ -555,6 +553,7 @@
         in_specs=[pl.BlockSpec(memory_space=pltpu.SMEM)] + [vm] * (7 + has),
         out_specs=(hbm,) * len(streams),
         scratch_shapes=[pltpu.VMEM((tiles * 8, CH), f32), pltpu.SemaphoreType.DMA((len(streams),))],
+        cost_estimate=pl.CostEstimate(flops=int(0.8e10), bytes_accessed=16 * 2**20, transcendentals=0),
         name="weight_gradients",
     )(dest, *values, small, *((lead,) if has else ()))
 
@@ -563,16 +562,8 @@
 PAIR = [(0, 1), (1, 0)]
 
 
-def columns(seq):
-    return seq // 4, 4
-
-
-def across(v, step):
+def hop(v, step):
     return lax.ppermute(v, "seq", [(i, i ^ step) for i in range(16)])
-
-
-def along(v, step):
-    return lax.ppermute(v, "seq", [(i, (i + 4 * step) % 16) for i in range(16)])
 
 
 def swap_cores(v):
@@ -583,70 +574,65 @@
     return lax.axis_size("seq") == 16 and lax.axis_size("batch") == 2
 
 
-def first_rows(share, devices, ids):
-    return ids * share // TILE * 8
-
-
-def place_of(step_z, step_p, other):
-    seq, batch = lax.axis_index("seq"), lax.axis_index("batch")
-    z = (seq // 4 + 4 + step_z) % 4
-    return 2 * (z * 4 + (seq % 4 ^ step_p)) + (batch ^ other)
-
-
-def cuts_of(tiles, part):
-    one = round(tiles * part)
-    two = one + round((tiles - one) * 2 / 3)
-    return one, two
-
-
 def device_index():
     return lax.axis_index("seq") * lax.axis_size("batch") + lax.axis_index("batch")
 
 
-def gather_weights(master, share, devices):
+def places_of(steps, other):
+    seq, batch = lax.axis_index("seq"), lax.axis_index("batch")
+    return 2 * (seq ^ np.asarray(steps, np.int32)) + (batch ^ other)
+
+
+def cut_of(tiles):
+    return round(tiles * ALONG_PART)
+
+
+def container(master, share, devices):
     _, tiles, _ = lay(share, devices)
     box = lax.dynamic_update_slice(jnp.zeros((tiles * TILE,), f32), master, (device_index() * share % TILE,))
-    return lax.all_gather(box.reshape(tiles * 8, CH), AXES, axis=0, tiled=True)
+    return box.reshape(tiles * 8, CH)
+
+
+def gather_weights(box, share, devices):
+    _, tiles, _ = lay(share, devices)
+    ids = jnp.arange(devices, dtype=jnp.int32)
+    return ((0, tiles, 0, devices),), ids, [lax.all_gather(box, AXES, axis=0, tiled=True)]
 
 
 def scatter_plan(share, devices):
     _, tiles, _ = lay(share, devices)
-    natural = first_rows(share, devices, jnp.arange(devices, dtype=jnp.int32))
-    if not direct() or SCATTER_PART == 1:
-        return ((0, tiles, 0, devices),), natural
-    one, two = cuts_of(tiles, SCATTER_PART)
-    streams, dest = [], []
-    if one:
-        streams.append((0, one, 0, devices))
-        dest.append(natural)
-    for lo, hi, ids in (
-        (one, two, lambda s, b, o: place_of(b, s, o)),
-        (two, tiles, lambda s, b, o: place_of(s, b, o)),
-    ):
-        for other in range(2):
-            for s in range(4):
-                streams.append((lo, hi, sum(d.shape[0] for d in dest), 4))
-                dest.append(first_rows(share, devices, jnp.stack([ids(s, b, other) for b in range(4)])))
-    return tuple(streams), jnp.concatenate(dest).astype(jnp.int32)
-
-
-def scatter_gradients(arrays, share, devices):
-    _, tiles, _ = lay(share, devices)
-    if not direct() or SCATTER_PART == 1:
-        return lax.psum_scatter(arrays[0].reshape(devices, tiles * 8, CH), AXES, scatter_dimension=0)
-    one, two = cuts_of(tiles, SCATTER_PART)
-    pieces = []
-    if one:
-        pieces.append(lax.psum_scatter(arrays[0].reshape(devices, one * 8, CH), AXES, scatter_dimension=0))
-        arrays = arrays[1:]
-    both = [a + swap_cores(b) for a, b in zip(arrays[:4] + arrays[8:12], arrays[4:8] + arrays[12:16])]
-    by_p, by_z = both[:4], both[4:]
-    part_p = by_p[0] + across(by_p[1], 1) + across(by_p[2], 2) + across(by_p[3], 3)
-    part_z = by_z[0] + along(by_z[1], 1) + along(by_z[2], 2) + along(by_z[3], 3)
-    part_p, part_z = part_p.reshape(4, -1, CH), part_z.reshape(4, -1, CH)
-    pieces.append(part_p[0] + along(part_p[1], 1) + along(part_p[2], 2) + along(part_p[3], 3))
-    pieces.append(part_z[0] + across(part_z[1], 1) + across(part_z[2], 2) + across(part_z[3], 3))
-    return jnp.concatenate(pieces)
+    if not direct():
+        return ((0, tiles, 0, devices),), jnp.arange(devices, dtype=jnp.int32) * share // TILE * 8
+    cut = cut_of(tiles)
+    by_p = [4 * z + p for p in range(4) for z in range(4)]
+    by_z = [4 * z + p for z in range(4) for p in range(4)]
+    ids = jnp.concatenate([places_of(steps, other) for steps in (by_p, by_z) for other in range(2)])
+    streams = ((0, cut, 0, 16), (0, cut, 16, 16), (cut, tiles, 32, 16), (cut, tiles, 48, 16))
+    return streams, (ids * share // TILE * 8).astype(jnp.int32)
+
+
+def pieces(v, count):
+    return v.reshape(count, -1, CH)
+
+
+def join_cores(arrays):
+    own_p, far_p, own_z, far_z = arrays
+    far_p, far_z = pieces(swap_cores(far_p), 4), pieces(swap_cores(far_z), 2)
+    own_p, own_z = pieces(own_p, 4), pieces(own_z, 2)
+    return [own_p[k] + far_p[k] for k in range(4)], [own_z[k] + far_z[k] for k in range(2)]
+
+
+def join_first(by_p, by_z):
+    part_p = by_p[0] + hop(by_p[1], 1) + hop(by_p[2], 2) + hop(by_p[3], 3)
+    part_z = by_z[0] + hop(by_z[1], 8)
+    return pieces(part_p, 4), pieces(part_z, 2)
+
+
+def join_last(part_p, part_z):
+    one = part_p[0] + hop(part_p[1], 4) + hop(part_p[2], 8) + hop(part_p[3], 12)
+    part_z = pieces(part_z[0] + hop(part_z[1], 4), 4)
+    two = part_z[0] + hop(part_z[1], 1) + hop(part_z[2], 2) + hop(part_z[3], 3)
+    return jnp.concatenate([one, two])
 
 
 MODE_ROWS = 65
@@ -673,12 +659,11 @@
     return small, rest
 
 
-def gather_modes(small, rest):
-    block = jnp.concatenate([small.reshape(1, CH), rest.reshape(64, CH)])
-    near = [lax.ppermute(block, "seq", [(4 * z + p, 4 * z) for z in range(4)]) for p in range(1, 4)]
-    plane = jnp.stack([block] + near)
-    far = [lax.ppermute(plane, "seq", [(4 * k, 0)]) for k in range(1, 4)]
-    blocks = jnp.concatenate([plane] + far)
+def gather_modes(block):
+    for step in (1, 2, 4, 8):
+        pairs = [(i, i - step) for i in range(16) if i % (2 * step) == step]
+        block = jnp.concatenate([block, lax.ppermute(block, "seq", pairs)])
+    blocks = block.reshape(16, MODE_ROWS, CH)
     lead = blocks[:, 0].reshape(16, 4, 32).transpose(1, 0, 2).reshape(-1)
     tail = blocks[:, 1:].reshape(16, 4, 16, CH).transpose(1, 0, 2, 3).reshape(-1)
     return jnp.concatenate([lead, tail])
@@ -689,8 +674,8 @@
         return lax.psum(v, AXES)
     v = jnp.broadcast_to(v, (8, CH))
     v = v + swap_cores(v)
-    v = v + (across(v, 1) + across(v, 2) + across(v, 3))
-    v = v + (along(v, 1) + along(v, 2) + along(v, 3))
+    v = v + (hop(v, 1) + hop(v, 2) + hop(v, 3))
+    v = v + (hop(v, 4) + hop(v, 8) + hop(v, 12))
     return v[0, 0]
 
 
@@ -711,7 +696,8 @@
     seq, batch = lax.axis_size("seq"), lax.axis_size("batch")
     devices = seq * batch
     share = master.shape[0]
-    boxes = gather_weights(master, share, devices)
+    box = container(master, share, devices)
+    streams, ids, boxes = gather_weights(box, share, devices)
     group = inputs.shape[1]
     nch, nck = D // seq, seq * group // CH
     rows = inputs[0].astype(jnp.float32)
@@ -722,12 +708,12 @@
 
     def feed_forward(outs):
         response = lax.all_to_all(outs.reshape(seq, -1, nch, CH), "seq", 0, 0).reshape(-1, CH)
-        return mlp_kernel(place, boxes, response, inputs[0], cotangent[0], share, devices, seq)
+        return mlp_kernel(place, streams, ids, boxes, response, inputs[0], cotangent[0], share, devices, seq)
 
     if direct():
         few, many = read_modes(scatter_modes(master))
     else:
-        lead = jnp.concatenate([lax.dynamic_slice(boxes[j * (boxes.shape[0] // devices):(j + 1) * (boxes.shape[0] // devices)].reshape(-1), (j * share % TILE,), (share,)) for j in range(MODE_TILES * TILE // share + 1)])
+        lead = jnp.concatenate([lax.dynamic_slice(boxes[0][j * box.shape[0]:(j + 1) * box.shape[0]].reshape(-1), (j * share % TILE,), (share,)) for j in range(MODE_TILES * TILE // share + 1)])
         mine = lambda v: lax.dynamic_slice_in_dim(v, lax.axis_index("seq") * nch, nch, 1)
         few = mine(lead[:4 * D].reshape(4, D))
         many = mine(lead[4 * D:MODE_TILES * TILE].reshape(4, D, NSTATE))
@@ -737,17 +723,19 @@
     output, d_mid, d_response, small, lead, *values = feed_forward(outs)
     d_outs = lax.all_to_all(d_response.reshape(seq, -1, nch, CH), "seq", 0, 0).reshape(-1, CH)
     plan, places = scatter_plan(share, devices)
+    if direct():
+        packed = join_cores(pack_kernel(plan, places, values, small, None, share, devices))
+        d_outs, packed = lax.optimization_barrier((d_outs, packed))
     d_signals, sums = ssm_backward(ends, prm, hats, d_outs, prior, nck, nch)
+    if direct():
+        d_signals, sums, packed = lax.optimization_barrier((d_signals, sums, join_first(*packed)))
     d_signal = to_tokens(d_signals, group)
     norm_gain = lead[:D // CH].reshape(D)
-    d_rows = d_mid + norm_back(d_signal * norm_gain, first_hat, first_scale)
     lane_sums = jnp.sum(sums[10:13], axis=-1)
     d_modes = modes_pull(mode_grads(sums, *modes))
     few = jnp.stack([lane_sums[1], lane_sums[2], d_modes[0], lane_sums[0]])
     many = jnp.stack(d_modes[1:])
-    if direct():
-        packed = pack_kernel(plan, places, values, small, None, share, devices)
-    else:
+    if not direct():
 
         def spread(v):
             whole = jnp.zeros((v.shape[0], D) + v.shape[2:], f32)
@@ -756,15 +744,20 @@
         lead = jnp.concatenate([spread(few).reshape(-1), spread(many).reshape(-1)]).reshape(-1, CH)
         packed = pack_kernel(plan, places, values, small, lead, share, devices)
     me = device_index()
-    box = scatter_gradients(packed, share, devices)
+    if direct():
+        box, d_signal = lax.optimization_barrier((join_last(*packed), d_signal))
+    else:
+        box = lax.psum_scatter(packed[0].reshape(devices, -1, CH), AXES, scatter_dimension=0)
+    d_rows = d_mid + norm_back(d_signal * norm_gain, first_hat, first_scale)
     shard = lax.dynamic_slice(box.reshape(-1), (me * share % TILE,), (share,))
     if direct():
-        few, many = few + swap_cores(few), many + swap_cores(many)
-        lead = gather_modes(few, many)
+        block = jnp.concatenate([few.reshape(1, CH), many.reshape(64, CH)])
+        block = block + swap_cores(block)
+        lead = gather_modes(block)
         lead = jnp.pad(lead, (0, 2 * share - lead.shape[0]))
         mark = me * share + jnp.arange(share, dtype=jnp.int32) < MODE_TILES * TILE
         squares = jnp.sum(jnp.where(mark, 0.0, shard * shard))
-        squares = squares + 0.5 * (jnp.sum(few * few) + jnp.sum(many * many))
+        squares = squares + 0.5 * jnp.sum(block * block)
         shard = jnp.where(mark, lax.dynamic_slice(lead, (jnp.minimum(me, 1) * share,), (share,)), shard)
     else:
         squares = jnp.sum(shard * shard)

time: 335 us -> 305 us (0.910)
  waiting for transfers between devices: 152 us -> 101 us
  starting transfers between devices: 47.4 us -> 60.9 us
  other arithmetic: 21.3 us -> 25.3 us
    reduce_scatter x1 -> x0, waiting for transfers between devices: 52.1 us -> none  [scatter_gradients(): lax.psum_scatter(arrays[0].reshape(devices, tiles * 8, CH), AXES, scatter...]
    all_to_all x1, waiting for transfers between devices: 19.8 us -> 5.95 us  [per_device(): lax.all_to_all(d_response.reshape(seq, -1, nch, CH), 'seq', 0, 0)]
    ppermute x12 -> x21, starting transfers between devices: 15.1 us -> 26.5 us  [the longest x17 21.3 us: hop(): return lax.ppermute(v, 'seq', [(i, i ^ step) for i in range(16)])]
    ppermute x12 -> x21, waiting for transfers between devices: 24.1 us -> 35.3 us  [the longest x17 22.2 us: hop(): return lax.ppermute(v, 'seq', [(i, i ^ step) for i in range(16)])]
    add x2 -> x11, other arithmetic: 0.01 us -> 11 us  [the longest x1 4.08 us: join_cores(): own_p[k] + far_p[k]]
  transfers between devices with their start and end apart: 28 -> 37, of which waited for: 15 -> 19; matrix products, arithmetic and copies ran while one was open for 8% -> 9% of each run, Pallas kernels for 17% -> 19%
where the time goes in v4:
time: 305 us; the launch traced here: 303 us
  waiting for transfers between devices  101 us (33%)
  Pallas kernels  81.7 us (27%)
  starting transfers between devices  60.9 us (20%)
  other arithmetic  25.3 us (8%)
  between operations  17.9 us (6%)
  local copies, waits for them, and re-layouts  16.6 us (5%)
    pallas_call x1, Pallas kernels, ssm_backward(): pl.pallas_call(partial(bwd_body, nck, nch, x.shape[0] // nck), out_shape=...  36.4 us
    ppermute x17, waiting for transfers between devices, hop(): return lax.ppermute(v, 'seq', [(i, i ^ step) for i in range(16)])  22.2 us
    pallas_call x1, Pallas kernels, ssm_forward(): pl.pallas_call(partial(fwd_body, nck, nch, x.shape[0] // nck), out_shape=...  21.9 us
    ppermute x17, starting transfers between devices, hop(): return lax.ppermute(v, 'seq', [(i, i ^ step) for i in range(16)])  21.3 us
    all_to_all x1, waiting for transfers between devices, feed_forward(): lax.all_to_all(outs.reshape(seq, -1, nch, CH), 'seq', 0, 0).reshape(-1, CH)  20.9 us
    all_to_all x1, waiting for transfers between devices, to_channels(): return lax.all_to_all(turned, 'seq', 0, 0).reshape(-1, CH)  17.8 us
    pallas_call x1, Pallas kernels, mlp_kernel(): pl.pallas_call(partial(mlp_body, share, devices, nseq, streams), out_shap...  14.7 us
    ppermute x3, waiting for transfers between devices, scatter_modes(): lax.ppermute(blocks[4 * k:4 * k + 4], 'seq', [(0, 4 * k)])  14.2 us
  transfers between devices with their start and end apart: 37, of which 19 were waited for; matrix products, arithmetic and copies ran while one was open for 9% of the time, Pallas kernels for 19%

profile of v4, /device:TPU:0, one launch (start us, length us, event | category | flops | bytes accessed | tf_op | source)
XLA Modules:
  0.0 303.3 jit_solution(14702190923729100940)
XLA Ops:
  7.3 3.7 %dynamic_update_slice.3 = f32[88064]{0:T(1024)S(1)} dynamic-update-slice(f32[88064]{0:T(1024)S(1)} %broadcast_in_dim.11, f32[86224]{0:T(1024)} %param.14, s32[]{:T(128)S(6)} %select_n.62) | dynamic-update-slice | bytes 689796 | tf_op jit(solution)/shard_map/dynamic_update_slice | solution.py:592
  17.3 4.5 %collective-permute-start.1 = (f32[4,65,128]{2,1,0:T(8,128)S(1)}, f32[4,65,128]{2,1,0:T(8,128)S(1)}, u32[]{:S(2)}, u32[]{:S(2)}) collective-permute-start(f32[4,65,128]{2,1,0:T(8,128)S(1)} %get-tuple-element.106), channel_id=1, source_target_pairs={{0,8},{1,9}} | collective-permute-start | bytes 399368 | tf_op jit(solution)/shard_map/ppermute | solution.py:649
  25.2 2.9 collective-permute-done.1
  28.1 6.3 %collective-permute-done.2 = f32[4,65,128]{2,1,0:T(8,128)S(1)} collective-permute-done((f32[4,65,128]{2,1,0:T(8,128)S(1)}, f32[4,65,128]{2,1,0:T(8,128)S(1)}, u32[]{:S(2)}, u32[]{:S(2)}) %collective-permute-start.2) | collective-permute-done | bytes 133152 | tf_op jit(solution)/shard_map/ppermute | solution.py:649
  34.4 5.0 %collective-permute-done.3 = f32[4,65,128]{2,1,0:T(8,128)S(1)} collective-permute-done((f32[4,65,128]{2,1,0:T(8,128)S(1)}, f32[4,65,128]{2,1,0:T(8,128)S(1)}, u32[]{:S(2)}, u32[]{:S(2)}) %collective-permute-start.3) | collective-permute-done | bytes 133152 | tf_op jit(solution)/shard_map/ppermute | solution.py:649
  44.4 5.7 %all-to-all-start = ((f32[16,2,32,128]{3,1,2,0:T(2,128)}), f32[16,2,32,128]{3,1,2,0:T(2,128)S(1)}, u32[]{:S(2)}, u32[]{:S(2)}) async-start(f32[16,2,32,128]{3,1,2,0:T(2,128)} %multiply_bitcast_fusion), calls=%async_computation | async-start | bytes 1048576 | tf_op jit(solution)/shard_map/all_to_all | solution.py:686
  54.7 17.8 %all-to-all-done = f32[16,2,32,128]{3,1,2,0:T(2,128)S(1)} async-done(((f32[16,2,32,128]{3,1,2,0:T(2,128)}), f32[16,2,32,128]{3,1,2,0:T(2,128)S(1)}, u32[]{:S(2)}, u32[]{:S(2)}) %all-to-all-start) | async-done | bytes 524320 | tf_op jit(solution)/shard_map/all_to_all | solution.py:686
  73.3 21.9 %state_forward.1 = (f32[1024,128]{1,0:T(8,128)}, f32[1024,128]{1,0:T(8,128)}) custom-call(s32[4]{0:T(128)} %bitcast.285, f32[32,24,128]{2,1,0:T(8,128)} %concatenate.62.prm_ref, f32[1024,128]{1,0:T(8,128)} %bitcast.270), custom_call_target="tpu_custom_call" | custom-call | flops 20000000000 | bytes 3145728 | tf_op jit(solution)/shard_map/state_forward/pallas_call | solution.py:136
  95.2 5.1 %all-to-all-start.1 = ((f32[16,2,32,128]{3,2,1,0:T(8,128)}), f32[16,2,32,128]{3,2,1,0:T(8,128)S(1)}, u32[]{:S(2)}, u32[]{:S(2)}) async-start(f32[16,2,32,128]{3,2,1,0:T(8,128)} %bitcast.274), calls=%async_computation.1 | async-start | bytes 1048576 | tf_op jit(solution)/shard_map/all_to_all | solution.py:710
  101.6 20.9 %all-to-all-done.1 = f32[16,2,32,128]{3,2,1,0:T(8,128)S(1)} async-done(((f32[16,2,32,128]{3,2,1,0:T(8,128)}), f32[16,2,32,128]{3,2,1,0:T(8,128)S(1)}, u32[]{:S(2)}, u32[]{:S(2)}) %all-to-all-start.1) | async-done | bytes 524320 | tf_op jit(solution)/shard_map/all_to_all | solution.py:710
  125.7 14.7 %feed_forward.1 = (bf16[256,512]{1,0:T(8,128)(2,1)}, f32[256,512]{1,0:T(8,128)}, f32[1024,128]{1,0:T(8,128)}, f32[40,128]{1,0:T(8,128)}, f32[1040,128]{1,0:T(8,1...) custom-call(s32[5]{0:T(128)} %pad_add_fusion.place_ref, ...), custom_call_target="tpu_custom_call" | custom-call | flops 10000000000 | bytes 20971520 | tf_op jit(solution)/shard_map/feed_forward/pallas_call | solution.py:480
  140.4 8.8 %weight_gradients.1 = (f32[8192,128]{1,0:T(8,128)}, f32[8192,128]{1,0:T(8,128)}, f32[2816,128]{1,0:T(8,128)}, f32[2816,128]{1,0:T(8,128)}) custom-call(s32[64]{0:T(128)} %fusion.55.refs_0_, bf16[256,512]{1,0:T(8,128)(2,1)} %get-tuple-element.43.refs_1_, bf16[256,2048]{1,0:T(8,128)(2,1)} %get-tuple-element.44.refs_2_, ...), custom_call_target="tpu_custom_call" | custom-call | flops 8000000000 | bytes 16777216 | tf_op jit(solution)/shard_map/weight_gradients/pallas_call | solution.py:550
  150.1 4.5 %all-to-all-start.2 = ((f32[16,2,32,128]{3,2,1,0:T(8,128)}), f32[16,2,32,128]{3,2,1,0:T(8,128)}, u32[]{:S(2)}, u32[]{:S(2)}) async-start(f32[16,2,32,128]{3,2,1,0:T(8,128)} %bitcast.36), calls=%async_computation.2 | async-start | bytes 1048576 | tf_op jit(solution)/shard_map/all_to_all | solution.py:724
  159.7 4.1 %slice_add_fusion = (f32[2048,128]{1,0:T(8,128)}, f32[2048,128]{1,0:T(8,128)}, f32[2048,128]{1,0:T(8,128)}, f32[2048,128]{1,0:T(8,128)S(1)}) fusion(f32[8192,128]{1,0:T(8,128)} %collective-permute-done.7, f32[8192,128]{1,0:T(8,128)S(1)} %copy-done.1), kind=kLoop, calls=%fused_computation.3 | loop fusion | flops 1048576 | bytes 12582912 | tf_op jit(solution)/shard_map/add | solution.py:622
  163.8 6.0 %all-to-all-done.2 = f32[16,2,32,128]{3,2,1,0:T(8,128)} async-done(((f32[16,2,32,128]{3,2,1,0:T(8,128)}), f32[16,2,32,128]{3,2,1,0:T(8,128)}, u32[]{:S(2)}, u32[]{:S(2)}) %all-to-all-start.2) | async-done | bytes 524320 | tf_op jit(solution)/shard_map/all_to_all | solution.py:724
  174.3 36.4 %state_backward.1 = (f32[1024,128]{1,0:T(8,128)}, f32[16,32,128]{2,1,0:T(8,128)}) custom-call(s32[4]{0:T(128)} %bitcast.286, f32[32,24,128]{2,1,0:T(8,128)} %concatenate.62.prm_ref, f32[1024,128]{1,0:T(8,128)} %bitcast.271, f32[1024,128]{1,0:T(8,128)} %bitcast.37.g_ref, f32[1024,128]{1,0:T(8,128)} %get-tuple-element.55.prior_ref), custom_call_target="tpu_custom_call" | custom-call | flops 35000000512 | bytes 4194304 | tf_op jit(solution)/shard_map/state_backward/pallas_call | solution.py:235
  211.9 5.9 %collective-permute-done.10 = f32[2048,128]{1,0:T(8,128)} collective-permute-done((f32[2048,128]{1,0:T(8,128)}, f32[2048,128]{1,0:T(8,128)}, u32[]{:S(2)}, u32[]{:S(2)}) %collective-permute-start.10) | collective-permute-done | bytes 1048608 | tf_op jit(solution)/shard_map/ppermute | solution.py:566
  235.1 6.2 %all-to-all-start.3 = ((f32[16,2,32,128]{3,1,2,0:T(2,128)}), f32[16,2,32,128]{3,1,2,0:T(2,128)S(1)}, u32[]{:S(2)}, u32[]{:S(2)}) async-start(f32[16,2,32,128]{3,1,2,0:T(2,128)} %copy.41), calls=%async_computation.3 | async-start | bytes 1048576 | tf_op jit(solution)/shard_map/all_to_all | solution.py:691
  243.3 6.2 %collective-permute-done.14 = f32[512,128]{1,0:T(8,128)} collective-permute-done((f32[512,128]{1,0:T(8,128)}, f32[512,128]{1,0:T(8,128)}, u32[]{:S(2)}, u32[]{:S(2)}) %collective-permute-start.14) | collective-permute-done | bytes 262176 | tf_op jit(solution)/shard_map/ppermute | solution.py:566
  250.6 6.7 %collective-permute-done.16 = f32[704,128]{1,0:T(8,128)S(1)} collective-permute-done((f32[704,128]{1,0:T(8,128)S(1)}, f32[704,128]{1,0:T(8,128)S(1)}, u32[]{:S(2)}, u32[]{:S(2)}) %collective-permute-start.16) | collective-permute-done | bytes 360480 | tf_op jit(solution)/shard_map/ppermute | solution.py:566
  261.6 4.1 %collective-permute-done.23 = f32[260,128]{1,0:T(8,128)S(1)} collective-permute-done((f32[260,128]{1,0:T(8,128)S(1)}, f32[260,128]{1,0:T(8,128)S(1)}, u32[]{:S(2)}, u32[]{:S(2)}) %collective-permute-start.23) | collective-permute-done | bytes 133152 | tf_op jit(solution)/shard_map/ppermute | solution.py:665
  267.1 9.0 %collective-permute-done.24 = f32[520,128]{1,0:T(8,128)S(1)} collective-permute-done((f32[520,128]{1,0:T(8,128)S(1)}, f32[520,128]{1,0:T(8,128)S(1)}, u32[]{:S(2)}, u32[]{:S(2)}) %collective-permute-start.24) | collective-permute-done | bytes 266272 | tf_op jit(solution)/shard_map/ppermute | solution.py:665
  280.4 3.5 %collective-permute-start.28 = (f32[8,128]{1,0:T(8,128)S(1)}, f32[8,128]{1,0:T(8,128)S(1)}, u32[]{:S(2)}, u32[]{:S(2)}) collective-permute-start(f32[8,128]{1,0:T(8,128)S(1)} %broadcast_add_fusion), channel_id=1, source_target_pairs={{0,6},{2,4},{4,2},{6,0},{8,14},{10,12},{12,10},{14,8},{16,22},{18,... | collective-permute-start | bytes 12296 | tf_op jit(solution)/shard_map/ppermute | solution.py:566
  285.5 4.3 %collective-permute-start.31 = (f32[8,128]{1,0:T(8,128)S(1)}, f32[8,128]{1,0:T(8,128)S(1)}, u32[]{:S(2)}, u32[]{:S(2)}) collective-permute-start(f32[8,128]{1,0:T(8,128)S(1)} %add_add_fusion.4), channel_id=1, source_target_pairs={{0,24},{2,26},{4,28},{6,30},{8,16},{10,18},{12,20},{14,22},{16,8},... | collective-permute-start | bytes 12296 | tf_op jit(solution)/shard_map/ppermute | solution.py:566
  (186 shorter events, 71.5 us)
Async XLA Ops:
  7.2 118.1 %all-gather.2.cloned.1.call-start = ((), (), s32[]{:S(2)}) async-start(), calls=%async_computation.4 | async-start | bytes 11624448 | tf_op jit(solution)/shard_map/all_gather | solution.py:599
  17.3 10.8 %collective-permute-start.1 = (f32[4,65,128]{2,1,0:T(8,128)S(1)}, f32[4,65,128]{2,1,0:T(8,128)S(1)}, u32[]{:S(2)}, u32[]{:S(2)}) collective-permute-start(f32[4,65,128]{2,1,0:T(8,128)S(1)} %get-tuple-element.106), channel_id=1, source_target_pairs={{0,8},{1,9}} | collective-permute-start | bytes 399368 | tf_op jit(solution)/shard_map/ppermute | solution.py:649
  21.9 12.6 %collective-permute-start.2 = (f32[4,65,128]{2,1,0:T(8,128)S(1)}, f32[4,65,128]{2,1,0:T(8,128)S(1)}, u32[]{:S(2)}, u32[]{:S(2)}) collective-permute-start(f32[4,65,128]{2,1,0:T(8,128)S(1)} %get-tuple-element.105), channel_id=1, source_target_pairs={{0,16},{1,17}} | collective-permute-start | bytes 399368 | tf_op jit(solution)/shard_map/ppermute | solution.py:649
  23.5 15.9 %collective-permute-start.3 = (f32[4,65,128]{2,1,0:T(8,128)S(1)}, f32[4,65,128]{2,1,0:T(8,128)S(1)}, u32[]{:S(2)}, u32[]{:S(2)}) collective-permute-start(f32[4,65,128]{2,1,0:T(8,128)S(1)} %get-tuple-element.107), channel_id=1, source_target_pairs={{0,24},{1,25}} | collective-permute-start | bytes 399368 | tf_op jit(solution)/shard_map/ppermute | solution.py:649
  39.5 11.3 %collective-permute-start.4 = (f32[65,128]{1,0:T(8,128)S(1)}, f32[65,128]{1,0:T(8,128)S(1)}, u32[]{:S(2)}, u32[]{:S(2)}) collective-permute-start(f32[65,128]{1,0:T(8,128)S(1)} %get-tuple-element.113), channel_id=1, source_target_pairs={{0,2},{8,10},{16,18},{24,26},{1,3},{9,11},{17,19},{25,27}} | collective-permute-start | bytes 99848 | tf_op jit(solution)/shard_map/ppermute | solution.py:651
  40.8 10.0 %collective-permute-start.5 = (f32[65,128]{1,0:T(8,128)S(1)}, f32[65,128]{1,0:T(8,128)S(1)}, u32[]{:S(2)}, u32[]{:S(2)}) collective-permute-start(f32[65,128]{1,0:T(8,128)S(1)} %get-tuple-element.111), channel_id=1, source_target_pairs={{0,4},{8,12},{16,20},{24,28},{1,5},{9,13},{17,21},{25,29}} | collective-permute-start | bytes 99848 | tf_op jit(solution)/shard_map/ppermute | solution.py:651
  42.1 8.7 %collective-permute-start.6 = (f32[65,128]{1,0:T(8,128)S(1)}, f32[65,128]{1,0:T(8,128)S(1)}, u32[]{:S(2)}, u32[]{:S(2)}) collective-permute-start(f32[65,128]{1,0:T(8,128)S(1)} %get-tuple-element.112), channel_id=1, source_target_pairs={{0,6},{8,14},{16,22},{24,30},{1,7},{9,15},{17,23},{25,31}} | collective-permute-start | bytes 99848 | tf_op jit(solution)/shard_map/ppermute | solution.py:651
  44.4 28.0 %all-to-all-start = ((f32[16,2,32,128]{3,1,2,0:T(2,128)}), f32[16,2,32,128]{3,1,2,0:T(2,128)S(1)}, u32[]{:S(2)}, u32[]{:S(2)}) async-start(f32[16,2,32,128]{3,1,2,0:T(2,128)} %multiply_bitcast_fusion), calls=%async_computation | async-start | bytes 1048576 | tf_op jit(solution)/shard_map/all_to_all | solution.py:686
  95.2 27.3 %all-to-all-start.1 = ((f32[16,2,32,128]{3,2,1,0:T(8,128)}), f32[16,2,32,128]{3,2,1,0:T(8,128)S(1)}, u32[]{:S(2)}, u32[]{:S(2)}) async-start(f32[16,2,32,128]{3,2,1,0:T(8,128)} %bitcast.274), calls=%async_computation.1 | async-start | bytes 1048576 | tf_op jit(solution)/shard_map/all_to_all | solution.py:710
  149.2 10.5 %collective-permute-start.7 = (f32[8192,128]{1,0:T(8,128)}, f32[8192,128]{1,0:T(8,128)}, u32[]{:S(2)}, u32[]{:S(2)}) collective-permute-start(f32[8192,128]{1,0:T(8,128)} %get-tuple-element.51), channel_id=1, source_target_pairs={{0,1},{1,0},{2,3},{3,2},{4,5},{5,4},{6,7},{7,6},{8,9},{9,8},{10,11... | collective-permute-start | bytes 12582920 | tf_op jit(solution)/shard_map/ppermute | solution.py:570
  150.1 19.7 %all-to-all-start.2 = ((f32[16,2,32,128]{3,2,1,0:T(8,128)}), f32[16,2,32,128]{3,2,1,0:T(8,128)}, u32[]{:S(2)}, u32[]{:S(2)}) async-start(f32[16,2,32,128]{3,2,1,0:T(8,128)} %bitcast.36), calls=%async_computation.2 | async-start | bytes 1048576 | tf_op jit(solution)/shard_map/all_to_all | solution.py:724
  169.7 40.9 %collective-permute-start.12 = (f32[1408,128]{1,0:T(8,128)S(1)}, f32[1408,128]{1,0:T(8,128)}, u32[]{:S(2)}, u32[]{:S(2)}) collective-permute-start(f32[1408,128]{1,0:T(8,128)S(1)} %copy-done.5), channel_id=1, source_target_pairs={{0,16},{2,18},{4,20},{6,22},{8,24},{10,26},{12,28},{14,30},{16,0},... | collective-permute-start | bytes 2162696 | tf_op jit(solution)/shard_map/ppermute | solution.py:566
  170.8 47.0 %collective-permute-start.10 = (f32[2048,128]{1,0:T(8,128)}, f32[2048,128]{1,0:T(8,128)}, u32[]{:S(2)}, u32[]{:S(2)}) collective-permute-start(f32[2048,128]{1,0:T(8,128)} %get-tuple-element.60), channel_id=1, source_target_pairs={{0,4},{2,6},{4,0},{6,2},{8,12},{10,14},{12,8},{14,10},{16,20},{18,... | collective-permute-start | bytes 3145736 | tf_op jit(solution)/shard_map/ppermute | solution.py:566
  171.5 46.3 %collective-permute-start.11 = (f32[2048,128]{1,0:T(8,128)}, f32[2048,128]{1,0:T(8,128)}, u32[]{:S(2)}, u32[]{:S(2)}) collective-permute-start(f32[2048,128]{1,0:T(8,128)} %get-tuple-element.61), channel_id=1, source_target_pairs={{0,6},{2,4},{4,2},{6,0},{8,14},{10,12},{12,10},{14,8},{16,22},{18,... | collective-permute-start | bytes 3145736 | tf_op jit(solution)/shard_map/ppermute | solution.py:566
  173.8 45.3 %collective-permute-start.9 = (f32[2048,128]{1,0:T(8,128)}, f32[2048,128]{1,0:T(8,128)}, u32[]{:S(2)}, u32[]{:S(2)}) collective-permute-start(f32[2048,128]{1,0:T(8,128)} %get-tuple-element.59), channel_id=1, source_target_pairs={{0,2},{2,0},{4,6},{6,4},{8,10},{10,8},{12,14},{14,12},{16,18},{18,... | collective-permute-start | bytes 3145736 | tf_op jit(solution)/shard_map/ppermute | solution.py:566
  226.8 16.4 %collective-permute-start.13 = (f32[512,128]{1,0:T(8,128)}, f32[512,128]{1,0:T(8,128)}, u32[]{:S(2)}, u32[]{:S(2)}) collective-permute-start(f32[512,128]{1,0:T(8,128)} %get-tuple-element.100), channel_id=1, source_target_pairs={{0,8},{2,10},{4,12},{6,14},{8,0},{10,2},{12,4},{14,6},{16,24},{18,... | collective-permute-start | bytes 786440 | tf_op jit(solution)/shard_map/ppermute | solution.py:566
  227.8 21.7 %collective-permute-start.14 = (f32[512,128]{1,0:T(8,128)}, f32[512,128]{1,0:T(8,128)}, u32[]{:S(2)}, u32[]{:S(2)}) collective-permute-start(f32[512,128]{1,0:T(8,128)} %get-tuple-element.102), channel_id=1, source_target_pairs={{0,16},{2,18},{4,20},{6,22},{8,24},{10,26},{12,28},{14,30},{16,0},... | collective-permute-start | bytes 786440 | tf_op jit(solution)/shard_map/ppermute | solution.py:566
  229.7 19.8 %collective-permute-start.15 = (f32[512,128]{1,0:T(8,128)}, f32[512,128]{1,0:T(8,128)}, u32[]{:S(2)}, u32[]{:S(2)}) collective-permute-start(f32[512,128]{1,0:T(8,128)} %get-tuple-element.101), channel_id=1, source_target_pairs={{0,24},{2,26},{4,28},{6,30},{8,16},{10,18},{12,20},{14,22},{16,8},... | collective-permute-start | bytes 786440 | tf_op jit(solution)/shard_map/ppermute | solution.py:566
  231.2 10.7 %collective-permute-start.22 = (f32[130,128]{1,0:T(8,128)S(1)}, f32[130,128]{1,0:T(8,128)S(1)}, u32[]{:S(2)}, u32[]{:S(2)}) collective-permute-start(f32[130,128]{1,0:T(8,128)S(1)} %pad_maximum_fusion.6), channel_id=1, source_target_pairs={{4,0},{12,8},{20,16},{28,24},{5,1},{13,9},{21,17},{29,25}} | collective-permute-start | bytes 199688 | tf_op jit(solution)/shard_map/ppermute | solution.py:665
  232.5 24.8 %collective-permute-start.16 = (f32[704,128]{1,0:T(8,128)S(1)}, f32[704,128]{1,0:T(8,128)S(1)}, u32[]{:S(2)}, u32[]{:S(2)}) collective-permute-start(f32[704,128]{1,0:T(8,128)S(1)} %slice_bitcast_fusion), channel_id=1, source_target_pairs={{0,8},{2,10},{4,12},{6,14},{8,0},{10,2},{12,4},{14,6},{16,24},{18,... | collective-permute-start | bytes 1081352 | tf_op jit(solution)/shard_map/ppermute | solution.py:566
  235.1 42.6 %all-to-all-start.3 = ((f32[16,2,32,128]{3,1,2,0:T(2,128)}), f32[16,2,32,128]{3,1,2,0:T(2,128)S(1)}, u32[]{:S(2)}, u32[]{:S(2)}) async-start(f32[16,2,32,128]{3,1,2,0:T(2,128)} %copy.41), calls=%async_computation.3 | async-start | bytes 1048576 | tf_op jit(solution)/shard_map/all_to_all | solution.py:691
  241.9 23.7 %collective-permute-start.23 = (f32[260,128]{1,0:T(8,128)S(1)}, f32[260,128]{1,0:T(8,128)S(1)}, u32[]{:S(2)}, u32[]{:S(2)}) collective-permute-start(f32[260,128]{1,0:T(8,128)S(1)} %pad_maximum_fusion.5), channel_id=1, source_target_pairs={{8,0},{24,16},{9,1},{25,17}} | collective-permute-start | bytes 399368 | tf_op jit(solution)/shard_map/ppermute | solution.py:665
  257.4 9.6 %collective-permute-start.17 = (f32[176,128]{1,0:T(8,128)S(1)}, f32[176,128]{1,0:T(8,128)S(1)}, u32[]{:S(2)}, u32[]{:S(2)}) collective-permute-start(f32[176,128]{1,0:T(8,128)S(1)} %get-tuple-element.108), channel_id=1, source_target_pairs={{0,2},{2,0},{4,6},{6,4},{8,10},{10,8},{12,14},{14,12},{16,18},{18,... | collective-permute-start | bytes 270344 | tf_op jit(solution)/shard_map/ppermute | solution.py:566
  265.7 10.4 %collective-permute-start.24 = (f32[520,128]{1,0:T(8,128)S(1)}, f32[520,128]{1,0:T(8,128)S(1)}, u32[]{:S(2)}, u32[]{:S(2)}) collective-permute-start(f32[520,128]{1,0:T(8,128)S(1)} %pad_maximum_fusion.2), channel_id=1, source_target_pairs={{16,0},{17,1}} | collective-permute-start | bytes 798728 | tf_op jit(solution)/shard_map/ppermute | solution.py:665
  (26 other events, 291.0 us)
Sparse Core Ops, SparseCore 0:
  11.8 113.3 all-gather.1

commit v5 on v4

--- a/solution.py
+++ b/solution.py
@@ -13,7 +13,7 @@
 DOCS = 4
 G = 1024
 FF = 2048
-ALONG_PART = 0.75
+Z_FIRST = 0.2
 
 
 norm_eps = 1e-05
@@ -34,6 +34,12 @@
     lhs = jnp.concatenate([ah, ah, al], axis=ca)
     rhs = jnp.concatenate([bh, bl, bh], axis=cb)
     return lax.dot_general(lhs, rhs, (((ca,), (cb,)), ((), ())), preferred_element_type=f32)
+
+def dot2(data, table, ct):
+    hi, lo = data
+    both = jnp.concatenate([hi, lo], axis=0)
+    out = lax.dot_general(both, table, (((1,), (ct,)), ((), ())), preferred_element_type=f32)
+    return out[:hi.shape[0]] + out[hi.shape[0]:]
 
 def swap(v):
     return pltpu.roll(v, NSTATE, 1)
@@ -53,14 +59,11 @@
         table = jnp.concatenate([table, more] if order == 1 else [more, table], axis=0)
     return table
 
-def toeplitz(prm, table):
-    wrow = jnp.broadcast_to(prm[16:17], (8, 2 * NSTATE))
-    taps = dot3(split(wrow), split(table), 1, 1)
-    wide = jnp.broadcast_to(taps[0:1], (CH, CH))
-    wide = pltpu.roll(wide, 0, 1, stride=1, stride_axis=0)
+def toeplitz(taps):
+    wide = pltpu.roll(jnp.broadcast_to(taps, (CH, CH)), 0, 1, stride=1, stride_axis=0)
     row = lax.broadcasted_iota(jnp.int32, (CH, CH), 0)
     col = lax.broadcasted_iota(jnp.int32, (CH, CH), 1)
-    return jnp.where(col >= row, wide, 0.0)
+    return jnp.where(col >= row, wide, 0.0).astype(bf16)
 
 def label_at(ends, pos):
     total = jnp.zeros_like(pos)
@@ -68,7 +71,7 @@
         total = total + (pos >= ends[k]).astype(jnp.int32)
     return total
 
-def make_masks(ends_ref, masks_ref, nck):
+def make_masks(ends_ref, masks_ref, low_ref, nck):
     ends = [ends_ref[k] for k in range(DOCS)]
     row = lax.broadcasted_iota(jnp.int32, (nck, CH), 0)
     lane = lax.broadcasted_iota(jnp.int32, (nck, CH), 1)
@@ -80,6 +83,11 @@
         masks_ref[k] = (label == k).astype(f32)
     masks_ref[DOCS] = (label == prev).astype(f32)
     masks_ref[DOCS + 1] = (label == last).astype(f32)
+    low_ref[:DOCS + 2] = masks_ref[...].astype(bf16)
+    if low_ref.shape[0] > DOCS + 2:
+        label = label_at(ends, base + (CH - 1 - lane))
+        for k in range(DOCS):
+            low_ref[DOCS + 2 + k] = (label == k).astype(f32).astype(bf16)
 
 def keep_of(ends_ref, c):
     first = jnp.int32(0)
@@ -89,8 +97,11 @@
         second = second + (c * CH + CH - 1 >= ends_ref[k]).astype(jnp.int32)
     return jnp.where((c > 0) & (first == second), 1.0, 0.0).astype(f32)
 
-def masked_rows(v, masks_ref):
-    return jnp.concatenate([v * masks_ref[k] for k in range(DOCS)], axis=0)
+def masked_rows(v, low_ref):
+    return [jnp.concatenate([part * low_ref[k] for k in range(DOCS)], axis=0) for part in v]
+
+def masked(v, low_ref, k):
+    return [part * low_ref[k] for part in v]
 
 def fold_rows(v, masks_ref, nck):
     total = v[:nck] * masks_ref[0]
@@ -98,21 +109,35 @@
         total = total + v[k * nck:(k + 1) * nck] * masks_ref[k]
     return total
 
-def fwd_body(nck, nch, apart, ends_ref, prm_ref, x_ref, y_ref, prior_ref, masks_ref, end_ref, gt_ref):
-    make_masks(ends_ref, masks_ref, nck)
-
-    def one(h, _):
+def for_channels(nch, body):
+    lax.fori_loop(0, nch, lambda h, _: body(h) or 0, 0, unroll=min(nch, 16))
+
+def fwd_body(nck, nch, apart, ends_ref, prm_ref, x_ref, y_ref, prior_ref, table_ref, down_ref, out_ref, mat_ref, masks_ref, low_ref, end_ref):
+    make_masks(ends_ref, masks_ref, low_ref, nck)
+
+    def tables(h):
         prm = prm_ref[h]
-        u = x_ref[pl.ds(h, nck, stride=apart), :] * prm[19:20] + prm[20:21]
         table = ladder(prm, 1)
-        down = ladder(prm, -1)
-        gt_ref[h] = twist(table, prm[17:18], prm[18:19])
-        local = dot3(split(masked_rows(u, masks_ref)), split(toeplitz(prm, table)), 1, 0)
-        y_ref[pl.ds(h, nck, stride=nch), :] = fold_rows(local, masks_ref, nck) + prm[21:22] * u
-        end_ref[pl.ds(h, nck, stride=nch), :] = dot3(split(u * masks_ref[DOCS + 1]), split(down), 1, 0)
-        return 0
-
-    lax.fori_loop(0, nch, one, 0, unroll=8)
+        table_ref[h] = table.astype(bf16)
+        out_ref[h] = twist(table, prm[17:18], prm[18:19]).astype(bf16)
+
+    def falling(h):
+        down_ref[h] = ladder(prm_ref[h], -1).astype(bf16)
+
+    def taps(h):
+        wrow = jnp.broadcast_to(prm_ref[h, 16:17, :], (16, 2 * NSTATE))
+        mat_ref[h] = toeplitz(dot2(split(wrow), table_ref[h], 1)[0:1])
+
+    def local(h):
+        prm = prm_ref[h, 16:24, :]
+        u = x_ref[pl.ds(h, nck, stride=apart), :] * prm[3:4] + prm[4:5]
+        parts = split(u)
+        local = dot2(masked_rows(parts, low_ref), mat_ref[h], 0)
+        y_ref[pl.ds(h, nck, stride=nch), :] = fold_rows(local, masks_ref, nck) + prm[5:6] * u
+        end_ref[pl.ds(h, nck, stride=nch), :] = dot2(masked(parts, low_ref, DOCS + 1), down_ref[h], 0)
+
+    for body in (tables, falling, taps, local):
+        for_channels(nch, body)
     full_re = prm_ref[:, 14, :]
     full_im = prm_ref[:, 15, :]
 
@@ -123,43 +148,37 @@
 
     lax.fori_loop(0, nck, step, jnp.zeros((nch, 2 * NSTATE), f32))
 
-    def two(h, _):
-        prior = prior_ref[pl.ds(h, nck, stride=nch), :]
-        carried = dot3(split(prior), split(gt_ref[h]), 1, 1) * masks_ref[DOCS]
-        y_ref[pl.ds(h, nck, stride=nch), :] += carried
-        return 0
-
-    lax.fori_loop(0, nch, two, 0, unroll=8)
+    def carried(h):
+        prior = split(prior_ref[pl.ds(h, nck, stride=nch), :])
+        y_ref[pl.ds(h, nck, stride=nch), :] += dot2(prior, out_ref[h], 1) * masks_ref[DOCS]
+
+    for_channels(nch, carried)
 
 def ssm_forward(ends, prm, x, nck, nch):
     vm = pl.BlockSpec(memory_space=pltpu.VMEM)
+    table = jax.ShapeDtypeStruct((nch, CH, 2 * NSTATE), bf16)
     return pl.pallas_call(
         partial(fwd_body, nck, nch, x.shape[0] // nck),
-        out_shape=(jax.ShapeDtypeStruct((nck * nch, CH), f32), jax.ShapeDtypeStruct((nck * nch, 2 * NSTATE), f32)),
+        out_shape=(jax.ShapeDtypeStruct((nck * nch, CH), f32), jax.ShapeDtypeStruct((nck * nch, 2 * NSTATE), f32)) + (table,) * 4,
         in_specs=[pl.BlockSpec(memory_space=pltpu.SMEM), vm, vm],
-        out_specs=(vm, vm),
+        out_specs=(vm,) * 6,
         scratch_shapes=[
             pltpu.VMEM((DOCS + 2, nck, CH), f32),
+            pltpu.VMEM((DOCS + 2, nck, CH), bf16),
             pltpu.VMEM((nck * nch, 2 * NSTATE), f32),
-            pltpu.VMEM((nch, CH, 2 * NSTATE), f32),
         ],
         cost_estimate=pl.CostEstimate(flops=int(2.0e10), bytes_accessed=3 * 2**20, transcendentals=0),
         name="state_forward",
     )(ends, prm, x)
 
-def bwd_body(nck, nch, apart, ends_ref, prm_ref, x_ref, g_ref, prior_ref, dx_ref, rows_ref, masks_ref, lead_ref, adj_ref, table_ref):
-    make_masks(ends_ref, masks_ref, nck)
-
-    def one(h, _):
-        prm = prm_ref[h]
-        g = g_ref[pl.ds(h, nck, stride=nch), :]
-        table = ladder(prm, 1)
-        table_ref[h] = table
-        gt = twist(table, prm[17:18], prm[18:19])
-        lead_ref[pl.ds(h, nck, stride=nch), :] = dot3(split(g * masks_ref[DOCS]), split(gt), 1, 0)
-        return 0
-
-    lax.fori_loop(0, nch, one, 0, unroll=8)
+def bwd_body(nck, nch, apart, ends_ref, prm_ref, x_ref, g_ref, prior_ref, table_ref, down_ref, out_ref, mat_ref, dx_ref, rows_ref, masks_ref, low_ref, lead_ref, adj_ref, taps_ref):
+    make_masks(ends_ref, masks_ref, low_ref, nck)
+    at_channel = lambda h: pl.ds(h, nck, stride=nch)
+
+    def lead(h):
+        lead_ref[at_channel(h), :] = dot2(masked(split(g_ref[at_channel(h), :]), low_ref, DOCS), out_ref[h], 0)
+
+    for_channels(nch, lead)
     full_re = prm_ref[:, 14, :]
     full_im = prm_ref[:, 15, :]
     zero = jnp.zeros((nch, 2 * NSTATE), f32)
@@ -184,68 +203,79 @@
     row = lax.broadcasted_iota(jnp.int32, (CH, CH), 0)
     col = lax.broadcasted_iota(jnp.int32, (CH, CH), 1)
     flip = (row + col == CH - 1).astype(f32).astype(bf16)
-
-    def two(h, _):
-        prm = prm_ref[h]
+    put = lambda k, h, v: rows_ref.__setitem__((k, pl.ds(h, 1), slice(None)), jnp.sum(v, axis=0, keepdims=True))
+
+    def signal(h):
+        prm = prm_ref[h, 16:24, :]
         x = x_ref[pl.ds(h, nck, stride=apart), :]
-        u = x * prm[19:20] + prm[20:21]
-        g = g_ref[pl.ds(h, nck, stride=nch), :]
-        table = table_ref[h]
-        down = ladder(prm, -1)
-        mat = split(toeplitz(prm, table))
-        gm = split(masked_rows(g, masks_ref))
-        um = split(masked_rows(u, masks_ref))
-        adjoint = split(adj_ref[pl.ds(h, nck, stride=nch), :])
-        prior = split(prior_ref[pl.ds(h, nck, stride=nch), :])
-        du = fold_rows(dot3(gm, mat, 1, 1), masks_ref, nck)
-        du = du + dot3(adjoint, split(down), 1, 1) * masks_ref[DOCS + 1]
-        du = du + prm[21:22] * g
-        dx_ref[pl.ds(h, nck, stride=apart), :] = du
-        flipped = [jnp.dot(v, flip, preferred_element_type=f32).astype(bf16) for v in um]
-        square = dot3(flipped, gm, 0, 0)
+        g = g_ref[at_channel(h), :]
+        du = fold_rows(dot2(masked_rows(split(g), low_ref), mat_ref[h], 1), masks_ref, nck)
+        du = du + dot2(split(adj_ref[at_channel(h), :]), down_ref[h], 1) * masks_ref[DOCS + 1]
+        du = du + prm[5:6] * g
+        dx_ref[at_channel(h), :] = du
+        put(10, h, g * (x * prm[3:4] + prm[4:5]))
+        put(11, h, du * x)
+        put(12, h, du)
+
+    def taps(h):
+        prm = prm_ref[h, 16:24, :]
+        u = split(x_ref[pl.ds(h, nck, stride=apart), :] * prm[3:4] + prm[4:5])
+        both = jnp.dot(jnp.concatenate(u, axis=0), flip, preferred_element_type=f32).astype(bf16)
+        um = []
+        for part in (both[:nck], both[nck:]):
+            um.append(jnp.concatenate([part * low_ref[DOCS + 2 + k] for k in range(DOCS)], axis=0))
+        square = dot3(um, masked_rows(split(g_ref[at_channel(h), :]), low_ref), 0, 0)
         square = jnp.where(row + col >= CH - 1, square, 0.0)
         square = pltpu.roll(square, 1, 1, stride=1, stride_axis=0)
-        taps = jnp.sum(square, axis=0, keepdims=True)
-        place = lax.broadcasted_iota(jnp.int32, (8, CH), 1).astype(f32)
-        sub = lax.broadcasted_iota(jnp.int32, (8, CH), 0)
-        both = jnp.where(sub == 0, 1.0, jnp.where(sub == 1, place, 0.0)) * taps
-        both = dot3(split(both), split(table), 1, 0)
+        taps_ref[pl.ds(h, 1), :] = jnp.sum(square, axis=0, keepdims=True)
+
+    def kernel(h):
+        place = lax.broadcasted_iota(jnp.int32, (16, CH), 1).astype(f32)
+        sub = lax.broadcasted_iota(jnp.int32, (16, CH), 0)
+        both = jnp.where(sub == 0, 1.0, jnp.where(sub == 1, place, 0.0)) * taps_ref[pl.ds(h, 1), :]
+        both = dot2(split(both), table_ref[h], 0)
         rows_ref[0, pl.ds(h, 1), :] = both[0:1]
         rows_ref[1, pl.ds(h, 1), :] = both[1:2]
-        late = row.astype(f32)
-        dgt = dot3(split(g * masks_ref[DOCS]), prior, 0, 0)
-        one = dgt * table
-        two = dgt * swap(table)
-        rows_ref[2, pl.ds(h, 1), :] = jnp.sum(one, axis=0, keepdims=True)
-        rows_ref[3, pl.ds(h, 1), :] = jnp.sum(two, axis=0, keepdims=True)
-        rows_ref[4, pl.ds(h, 1), :] = jnp.sum(one * late, axis=0, keepdims=True)
-        rows_ref[5, pl.ds(h, 1), :] = jnp.sum(two * late, axis=0, keepdims=True)
-        ddown = dot3(split(u * masks_ref[DOCS + 1]), adjoint, 0, 0) * ((CH - 1) - late)
-        rows_ref[6, pl.ds(h, 1), :] = jnp.sum(ddown * down, axis=0, keepdims=True)
-        rows_ref[7, pl.ds(h, 1), :] = jnp.sum(ddown * swap(down), axis=0, keepdims=True)
-        rows_ref[10, pl.ds(h, 1), :] = jnp.sum(g * u, axis=0, keepdims=True)
-        rows_ref[11, pl.ds(h, 1), :] = jnp.sum(du * x, axis=0, keepdims=True)
-        rows_ref[12, pl.ds(h, 1), :] = jnp.sum(du, axis=0, keepdims=True)
-        return 0
-
-    lax.fori_loop(0, nch, two, 0, unroll=8)
-
-def ssm_backward(ends, prm, x, g, prior, nck, nch):
+
+    late = row.astype(f32)
+
+    def carried(h):
+        dgt = dot3(masked(split(g_ref[at_channel(h), :]), low_ref, DOCS), split(prior_ref[at_channel(h), :]), 0, 0)
+        table = table_ref[h].astype(f32)
+        same, cross = dgt * table, dgt * swap(table)
+        put(2, h, same)
+        put(3, h, cross)
+        put(4, h, same * late)
+        put(5, h, cross * late)
+
+    def ending(h):
+        prm = prm_ref[h, 16:24, :]
+        u = split(x_ref[pl.ds(h, nck, stride=apart), :] * prm[3:4] + prm[4:5])
+        ddown = dot3(masked(u, low_ref, DOCS + 1), split(adj_ref[at_channel(h), :]), 0, 0) * ((CH - 1) - late)
+        down = down_ref[h].astype(f32)
+        put(6, h, ddown * down)
+        put(7, h, ddown * swap(down))
+
+    for body in (signal, taps, kernel, carried, ending):
+        for_channels(nch, body)
+
+def ssm_backward(ends, prm, x, g, prior, tables, nck, nch):
     vm = pl.BlockSpec(memory_space=pltpu.VMEM)
     return pl.pallas_call(
         partial(bwd_body, nck, nch, x.shape[0] // nck),
         out_shape=(jax.ShapeDtypeStruct((nck * nch, CH), f32), jax.ShapeDtypeStruct((16, nch, 2 * NSTATE), f32)),
-        in_specs=[pl.BlockSpec(memory_space=pltpu.SMEM), vm, vm, vm, vm],
+        in_specs=[pl.BlockSpec(memory_space=pltpu.SMEM)] + [vm] * 8,
         out_specs=(vm, vm),
         scratch_shapes=[
             pltpu.VMEM((DOCS + 2, nck, CH), f32),
+            pltpu.VMEM((2 * DOCS + 2, nck, CH), bf16),
             pltpu.VMEM((nck * nch, 2 * NSTATE), f32),
             pltpu.VMEM((nck * nch, 2 * NSTATE), f32),
-            pltpu.VMEM((nch, CH, 2 * NSTATE), f32),
+            pltpu.VMEM((nch, CH), f32),
         ],
         cost_estimate=pl.CostEstimate(flops=int(3.5e10), bytes_accessed=4 * 2**20, transcendentals=0),
         name="state_backward",
-    )(ends, prm, x, g, prior)
+    )(ends, prm, x, g, prior, *tables)
 
 def mixing(step_log, decay_log, frequency, out_real, out_imag):
     delta = jnp.exp(step_log)[:, None]
@@ -583,8 +613,9 @@
     return 2 * (seq ^ np.asarray(steps, np.int32)) + (batch ^ other)
 
 
-def cut_of(tiles):
-    return round(tiles * ALONG_PART)
+def cuts_of(tiles):
+    one = round(tiles * (1.0 - Z_FIRST) / 2)
+    return one, 2 * one
 
 
 def container(master, share, devices):
@@ -593,46 +624,73 @@
     return box.reshape(tiles * 8, CH)
 
 
-def gather_weights(box, share, devices):
-    _, tiles, _ = lay(share, devices)
-    ids = jnp.arange(devices, dtype=jnp.int32)
-    return ((0, tiles, 0, devices),), ids, [lax.all_gather(box, AXES, axis=0, tiled=True)]
+def gather_near(box):
+    half = box.shape[0] // 16 * 8
+    sets = [box] + [hop(box, step) for step in (4, 8, 12)]
+    return [jnp.concatenate([v[at] for v in sets]) for at in (slice(0, half), slice(half, None))]
+
+
+def gather_plane(near):
+    return [jnp.concatenate([near[0], hop(near[0], 1)]), jnp.concatenate([near[1], hop(near[1], 2)])]
+
+
+def gather_cores(plane, far, tiles):
+    half = tiles // 2
+    arrays, streams, ids = [], [], []
+    for v, first, second in ((plane[0], 0, 1), (plane[1], 0, 2), (far[0], 2, 3), (far[1], 1, 3)):
+        for other in range(2):
+            arrays.append(swap_cores(v) if other else v)
+            streams.append(((0, half) if len(arrays) % 4 in (1, 2) else (half, tiles)) + (8 * len(ids), 8))
+            ids.append(places_of([4 * z + p for p in (first, second) for z in range(4)], other))
+    return tuple(streams), jnp.concatenate(ids).astype(jnp.int32), arrays
 
 
 def scatter_plan(share, devices):
     _, tiles, _ = lay(share, devices)
     if not direct():
         return ((0, tiles, 0, devices),), jnp.arange(devices, dtype=jnp.int32) * share // TILE * 8
-    cut = cut_of(tiles)
-    by_p = [4 * z + p for p in range(4) for z in range(4)]
-    by_z = [4 * z + p for z in range(4) for p in range(4)]
-    ids = jnp.concatenate([places_of(steps, other) for steps in (by_p, by_z) for other in range(2)])
-    streams = ((0, cut, 0, 16), (0, cut, 16, 16), (cut, tiles, 32, 16), (cut, tiles, 48, 16))
-    return streams, (ids * share // TILE * 8).astype(jnp.int32)
+    one, two = cuts_of(tiles)
+    streams, ids = [], []
+    for first, last, bits in ((0, one, (1, 2, 8, 4)), (one, two, (2, 1, 8, 4)), (two, tiles, (8, 4, 2, 1))):
+        steps = [0]
+        for bit in bits[::-1]:
+            steps = steps + [bit + step for step in steps]
+        for other in range(2):
+            streams.append((first, last, 16 * len(ids), 16))
+            ids.append(places_of(steps, other))
+    return tuple(streams), (jnp.concatenate(ids) * share // TILE * 8).astype(jnp.int32)
 
 
 def pieces(v, count):
     return v.reshape(count, -1, CH)
 
 
+def halve(two, step):
+    return pieces(two[0] + hop(two[1], step), 2)
+
+
 def join_cores(arrays):
-    own_p, far_p, own_z, far_z = arrays
-    far_p, far_z = pieces(swap_cores(far_p), 4), pieces(swap_cores(far_z), 2)
-    own_p, own_z = pieces(own_p, 4), pieces(own_z, 2)
-    return [own_p[k] + far_p[k] for k in range(4)], [own_z[k] + far_z[k] for k in range(2)]
-
-
-def join_first(by_p, by_z):
-    part_p = by_p[0] + hop(by_p[1], 1) + hop(by_p[2], 2) + hop(by_p[3], 3)
-    part_z = by_z[0] + hop(by_z[1], 8)
-    return pieces(part_p, 4), pieces(part_z, 2)
-
-
-def join_last(part_p, part_z):
-    one = part_p[0] + hop(part_p[1], 4) + hop(part_p[2], 8) + hop(part_p[3], 12)
-    part_z = pieces(part_z[0] + hop(part_z[1], 4), 4)
-    two = part_z[0] + hop(part_z[1], 1) + hop(part_z[2], 2) + hop(part_z[3], 3)
-    return jnp.concatenate([one, two])
+    sums = []
+    for own, far in zip(arrays[::2], arrays[1::2]):
+        own, far = pieces(own, 2), pieces(swap_cores(far), 2)
+        sums.append([own[k] + far[k] for k in range(2)])
+    return sums
+
+
+def join_first(sums):
+    return [halve(v, step) for v, step in zip(sums, (1, 2, 8))]
+
+
+def join_second(sums):
+    return [halve(v, step) for v, step in zip(sums, (2, 1, 4))]
+
+
+def join_last(sums):
+    rows = [pieces(v.reshape(-1, CH), 4) for v in sums[:2]]
+    four = [jnp.concatenate([v[k] for v in rows]) for k in range(4)]
+    near = halve(sums[2], 2)
+    one = four[0] + hop(four[1], 4) + hop(four[2], 8) + hop(four[3], 12)
+    return jnp.concatenate([one, near[0] + hop(near[1], 1)])
 
 
 MODE_ROWS = 65
@@ -646,10 +704,11 @@
     rest = lead[4 * D:].reshape(4, 16, 16, CH).transpose(1, 0, 2, 3).reshape(16, 64, CH)
     blocks = jnp.concatenate([small, rest], axis=1)
     seq = lax.axis_index("seq")
-    far = [lax.ppermute(blocks[4 * k:4 * k + 4], "seq", [(0, 4 * k)]) for k in range(1, 4)]
-    plane = jnp.where(seq == 0, blocks[:4], far[0] + far[1] + far[2])
-    near = [lax.ppermute(plane[p], "seq", [(4 * z, 4 * z + p) for z in range(4)]) for p in range(1, 4)]
-    return jnp.where(seq % 4 == 0, plane[0], near[0] + near[1] + near[2])
+    blocks = blocks.reshape(2, 2, 2, 2, MODE_ROWS, CH).transpose(3, 2, 1, 0, 4, 5)
+    for step in (1, 2, 4, 8):
+        come = lax.ppermute(blocks[1], "seq", [(i, i + step) for i in range(step)])
+        blocks = jnp.where(seq & step == 0, blocks[0], come)
+    return blocks
 
 
 def read_modes(block):
@@ -659,11 +718,15 @@
     return small, rest
 
 
-def gather_modes(block):
-    for step in (1, 2, 4, 8):
-        pairs = [(i, i - step) for i in range(16) if i % (2 * step) == step]
+def gather_modes(block, steps):
+    for step in steps:
+        pairs = [(i, i - step) for i in range(2 * step) if i >= step]
         block = jnp.concatenate([block, lax.ppermute(block, "seq", pairs)])
-    blocks = block.reshape(16, MODE_ROWS, CH)
+    return block
+
+
+def mode_vector(block):
+    blocks = block.reshape(2, 2, 2, 2, MODE_ROWS, CH).transpose(3, 2, 1, 0, 4, 5).reshape(16, MODE_ROWS, CH)
     lead = blocks[:, 0].reshape(16, 4, 32).transpose(1, 0, 2).reshape(-1)
     tail = blocks[:, 1:].reshape(16, 4, 16, CH).transpose(1, 0, 2, 3).reshape(-1)
     return jnp.concatenate([lead, tail])
@@ -697,7 +760,11 @@
     devices = seq * batch
     share = master.shape[0]
     box = container(master, share, devices)
-    streams, ids, boxes = gather_weights(box, share, devices)
+    if direct():
+        near = gather_near(box)
+    else:
+        streams, ids = ((0, box.shape[0] // 8, 0, devices),), jnp.arange(devices, dtype=jnp.int32)
+        boxes = [lax.all_gather(box, AXES, axis=0, tiled=True)]
     group = inputs.shape[1]
     nch, nck = D // seq, seq * group // CH
     rows = inputs[0].astype(jnp.float32)
@@ -706,8 +773,7 @@
     first_hat, first_scale = normalize(rows)
     hats = to_channels(first_hat)
 
-    def feed_forward(outs):
-        response = lax.all_to_all(outs.reshape(seq, -1, nch, CH), "seq", 0, 0).reshape(-1, CH)
+    def feed_forward(response):
         return mlp_kernel(place, streams, ids, boxes, response, inputs[0], cotangent[0], share, devices, seq)
 
     if direct():
@@ -717,18 +783,27 @@
         mine = lambda v: lax.dynamic_slice_in_dim(v, lax.axis_index("seq") * nch, nch, 1)
         few = mine(lead[:4 * D].reshape(4, D))
         many = mine(lead[4 * D:MODE_TILES * TILE].reshape(4, D, NSTATE))
+    if direct():
+        plane = gather_plane(near)
     modes, modes_pull = jax.vjp(mixing, few[2], many[0], many[1], many[2], many[3])
     prm = mode_rows(*modes, few[0], few[1], few[3])
-    outs, prior = ssm_forward(ends, prm, hats, nck, nch)
-    output, d_mid, d_response, small, lead, *values = feed_forward(outs)
+    outs, prior, *tables = ssm_forward(ends, prm, hats, nck, nch)
+    if direct():
+        outs, plane = lax.optimization_barrier((outs, plane))
+    response = lax.all_to_all(outs.reshape(seq, -1, nch, CH), "seq", 0, 0).reshape(-1, CH)
+    if direct():
+        far = [hop(plane[0], 2), hop(plane[1], 1)]
+        response, far = lax.optimization_barrier((response, far))
+        streams, ids, boxes = gather_cores(plane, far, box.shape[0] // 8)
+    output, d_mid, d_response, small, lead, *values = feed_forward(response)
     d_outs = lax.all_to_all(d_response.reshape(seq, -1, nch, CH), "seq", 0, 0).reshape(-1, CH)
     plan, places = scatter_plan(share, devices)
     if direct():
         packed = join_cores(pack_kernel(plan, places, values, small, None, share, devices))
         d_outs, packed = lax.optimization_barrier((d_outs, packed))
-    d_signals, sums = ssm_backward(ends, prm, hats, d_outs, prior, nck, nch)
+    d_signals, sums = ssm_backward(ends, prm, hats, d_outs, prior, tables, nck, nch)
     if direct():
-        d_signals, sums, packed = lax.optimization_barrier((d_signals, sums, join_first(*packed)))
+        d_signals, sums, packed = lax.optimization_barrier((d_signals, sums, join_first(packed)))
     d_signal = to_tokens(d_signals, group)
     norm_gain = lead[:D // CH].reshape(D)
     lane_sums = jnp.sum(sums[10:13], axis=-1)
@@ -745,19 +820,19 @@
         packed = pack_kernel(plan, places, values, small, lead, share, devices)
     me = device_index()
     if direct():
-        box, d_signal = lax.optimization_barrier((join_last(*packed), d_signal))
+        own = jnp.concatenate([few.reshape(1, CH), many.reshape(64, CH)])
+        own, packed = lax.optimization_barrier((own + swap_cores(own), join_second(packed)))
+        box, block, d_signal = lax.optimization_barrier((join_last(packed), gather_modes(own, (8, 4)), d_signal))
     else:
         box = lax.psum_scatter(packed[0].reshape(devices, -1, CH), AXES, scatter_dimension=0)
     d_rows = d_mid + norm_back(d_signal * norm_gain, first_hat, first_scale)
     shard = lax.dynamic_slice(box.reshape(-1), (me * share % TILE,), (share,))
     if direct():
-        block = jnp.concatenate([few.reshape(1, CH), many.reshape(64, CH)])
-        block = block + swap_cores(block)
-        lead = gather_modes(block)
+        lead = mode_vector(gather_modes(block, (2, 1)))
         lead = jnp.pad(lead, (0, 2 * share - lead.shape[0]))
         mark = me * share + jnp.arange(share, dtype=jnp.int32) < MODE_TILES * TILE
         squares = jnp.sum(jnp.where(mark, 0.0, shard * shard))
-        squares = squares + 0.5 * jnp.sum(block * block)
+        squares = squares + 0.5 * jnp.sum(own * own)
         shard = jnp.where(mark, lax.dynamic_slice(lead, (jnp.minimum(me, 1) * share,), (share,)), shard)
     else:
         squares = jnp.sum(shard * shard)

time: 305 us -> 283 us (0.928)
  Pallas kernels: 81.7 us -> 54.8 us
  starting transfers between devices: 60.9 us -> 80.3 us
  waiting for transfers between devices: 101 us -> 87.1 us
  between operations: 17.9 us -> 4.82 us
  local copies, waits for them, and re-layouts: 16.6 us -> 24.3 us
  other arithmetic: 25.3 us -> 30.1 us
    ppermute x17 -> x24, waiting for transfers between devices: 22.2 us -> 43.6 us  [hop(): return lax.ppermute(v, 'seq', [(i, i ^ step) for i in range(16)])]
    all_to_all x1, waiting for transfers between devices: 17.8 us -> 0.01 us  [to_channels(): return lax.all_to_all(turned, 'seq', 0, 0).reshape(-1, CH)]
    pallas_call x1, Pallas kernels: 36.4 us -> 19.5 us  [ssm_backward(): pl.pallas_call(partial(bwd_body, nck, nch, x.shape[0] // nck), out_shape=...]
    ppermute x6 -> x4, waiting for transfers between devices: 14.2 us -> 2.54 us  [scatter_modes(): come = lax.ppermute(blocks[1], 'seq', [(i, i + step) for i in range(step)])]
    ppermute x17 -> x24, starting transfers between devices: 21.3 us -> 32.9 us  [hop(): return lax.ppermute(v, 'seq', [(i, i ^ step) for i in range(16)])]
    pallas_call x1, Pallas kernels: 21.9 us -> 11.7 us  [ssm_forward(): pl.pallas_call(partial(fwd_body, nck, nch, x.shape[0] // nck), out_shape=...]
    ppermute x4, waiting for transfers between devices: 13.1 us -> 6.47 us  [gather_modes(): block = jnp.concatenate([block, lax.ppermute(block, 'seq', pairs)])]
    add x7 -> x13, other arithmetic: 10.9 us -> 16.9 us  [the longest x3 8.54 us: join_cores(): sums.append([own[k] + far[k] for k in range(2)])]
  transfers between devices with their start and end apart: 37 -> 46, of which waited for: 19 -> 19; matrix products, arithmetic and copies ran while one was open for 9% -> 14% of each run, Pallas kernels for 19% -> 11%
where the time goes in v5:
time: 283 us; the launch traced here: 281 us
  waiting for transfers between devices  87.1 us (31%)
  starting transfers between devices  80.3 us (28%)
  Pallas kernels  54.8 us (19%)
  other arithmetic  30.1 us (11%)
  local copies, waits for them, and re-layouts  24.3 us (9%)
  between operations  4.82 us (2%)
    ppermute x24, waiting for transfers between devices, hop(): return lax.ppermute(v, 'seq', [(i, i ^ step) for i in range(16)])  43.6 us
    ppermute x24, starting transfers between devices, hop(): return lax.ppermute(v, 'seq', [(i, i ^ step) for i in range(16)])  32.9 us
    all_to_all x1, waiting for transfers between devices, per_device(): lax.all_to_all(outs.reshape(seq, -1, nch, CH), 'seq', 0, 0).reshape(-1, CH)  25.8 us
    pallas_call x1, Pallas kernels, ssm_backward(): pl.pallas_call(partial(bwd_body, nck, nch, x.shape[0] // nck), out_shape=...  19.5 us
    pallas_call x1, Pallas kernels, mlp_kernel(): pl.pallas_call(partial(mlp_body, share, devices, nseq, streams), out_shap...  14.8 us
    ppermute x4, starting transfers between devices, scatter_modes(): come = lax.ppermute(blocks[1], 'seq', [(i, i + step) for i in range(step)])  13.1 us
    pallas_call x1, Pallas kernels, ssm_forward(): pl.pallas_call(partial(fwd_body, nck, nch, x.shape[0] // nck), out_shape=...  11.7 us
    pallas_call x1, Pallas kernels, pack_kernel(): pl.pallas_call(partial(pack_body, tuple((s[:3] for s in streams)), tiles,...  8.74 us
  transfers between devices with their start and end apart: 46, of which 19 were waited for; matrix products, arithmetic and copies ran while one was open for 14% of the time, Pallas kernels for 11%

profile of v5, /device:TPU:0, one launch (start us, length us, event | category | flops | bytes accessed | tf_op | source)
XLA Modules:
  0.0 281.3 jit_solution(3556988856266696159)
XLA Ops:
  0.7 3.7 %dynamic_update_slice.3 = f32[88064]{0:T(1024)S(1)} dynamic-update-slice(f32[88064]{0:T(1024)S(1)} %broadcast_in_dim.11, f32[86224]{0:T(1024)} %param.24, s32[]{:T(128)S(6)} %select_n.85) | dynamic-update-slice | bytes 689796 | tf_op jit(solution)/shard_map/dynamic_update_slice | solution.py:623
  4.4 3.1 %collective-permute-start.5 = (f32[688,128]{1,0:T(8,128)S(1)}, f32[688,128]{1,0:T(8,128)S(1)}, u32[]{:S(2)}, u32[]{:S(2)}) collective-permute-start(f32[688,128]{1,0:T(8,128)S(1)} %bitcast.315), channel_id=1, source_target_pairs={{0,8},{2,10},{4,12},{6,14},{8,0},{10,2},{12,4},{14,6},{16,24},{18,... | collective-permute-start | bytes 1056776 | tf_op jit(solution)/shard_map/ppermute | solution.py:596
  12.9 7.2 %all-to-all-start = ((f32[16,2,32,128]{3,1,2,0:T(2,128)}), f32[16,2,32,128]{3,1,2,0:T(2,128)S(1)}, u32[]{:S(2)}, u32[]{:S(2)}) async-start(f32[16,2,32,128]{3,1,2,0:T(2,128)} %multiply_bitcast_fusion), calls=%async_computation | async-start | bytes 1048576 | tf_op jit(solution)/shard_map/all_to_all | solution.py:749
  23.2 3.8 %collective-permute-start.1 = (f32[2,2,2,65,128]{4,3,0,1,2:T(8,128)S(1)}, f32[2,2,2,65,128]{4,3,0,1,2:T(8,128)S(1)}, u32[]{:S(2)}, u32[]{:S(2)}) collective-permute-start(f32[2,2,2,65,128]{4,3,0,1,2:T(8,128)S(1)} %slice_bitcast_fusion.2), channel_id=1, source_target_pairs={{0,2},{1,3}} | collective-permute-start | bytes 798728 | tf_op jit(solution)/shard_map/ppermute | solution.py:709
  27.8 11.5 %collective-permute-done.6 = f32[688,128]{1,0:T(8,128)S(1)} collective-permute-done((f32[688,128]{1,0:T(8,128)S(1)}, f32[688,128]{1,0:T(8,128)S(1)}, u32[]{:S(2)}, u32[]{:S(2)}) %collective-permute-start.6) | collective-permute-done | bytes 352288 | tf_op jit(solution)/shard_map/ppermute | solution.py:596
  46.0 5.2 %collective-permute-start.3 = (f32[2,65,128]{2,1,0:T(8,128)S(1)}, f32[2,65,128]{2,1,0:T(8,128)S(1)}, u32[]{:S(2)}, u32[]{:S(2)}) collective-permute-start(f32[2,65,128]{2,1,0:T(8,128)S(1)} %slice_bitcast_fusion.18), channel_id=1, source_target_pairs={{0,8},{2,10},{4,12},{6,14},{1,9},{3,11},{5,13},{7,15}} | collective-permute-start | bytes 199688 | tf_op jit(solution)/shard_map/ppermute | solution.py:709
  60.9 11.7 %state_forward.1 = (f32[1024,128]{1,0:T(8,128)}, f32[1024,128]{1,0:T(8,128)}, bf16[32,128,128]{2,1,0:T(8,128)(2,1)}, bf16[32,128,128]{2,1,0:T(8,128)(2,1)}, bf16...) custom-call(s32[4]{0:T(128)} %bitcast.349, f32[32,24,128]{2,1,0:T(8,128)} %concatenate.98.prm_ref, ...), custom_call_target="tpu_custom_call" | custom-call | flops 20000000000 | bytes 3145728 | tf_op jit(solution)/shard_map/state_forward/pallas_call | solution.py:160
  78.6 6.4 %all-to-all-start.1 = ((f32[16,2,32,128]{3,2,1,0:T(8,128)}), f32[16,2,32,128]{3,2,1,0:T(8,128)S(1)}, u32[]{:S(2)}, u32[]{:S(2)}) async-start(f32[16,2,32,128]{3,2,1,0:T(8,128)} %bitcast.39), calls=%async_computation.1 | async-start | bytes 1048576 | tf_op jit(solution)/shard_map/all_to_all | solution.py:793
  85.6 25.8 %all-to-all-done.1 = f32[16,2,32,128]{3,2,1,0:T(8,128)S(1)} async-done(((f32[16,2,32,128]{3,2,1,0:T(8,128)}), f32[16,2,32,128]{3,2,1,0:T(8,128)S(1)}, u32[]{:S(2)}, u32[]{:S(2)}) %all-to-all-start.1) | async-done | bytes 524320 | tf_op jit(solution)/shard_map/all_to_all | solution.py:793
  117.0 14.8 %feed_forward.1 = (bf16[256,512]{1,0:T(8,128)(2,1)}, f32[256,512]{1,0:T(8,128)}, f32[1024,128]{1,0:T(8,128)}, f32[40,128]{1,0:T(8,128)}, f32[1040,128]{1,0:T(8,1...) custom-call(s32[5]{0:T(128)} %pad_add_fusion.place_ref, ...), custom_call_target="tpu_custom_call" | custom-call | flops 10000000000 | bytes 20971520 | tf_op jit(solution)/shard_map/feed_forward/pallas_call | solution.py:510
  131.8 8.7 %weight_gradients.1 = (f32[4352,128]{1,0:T(8,128)}, f32[4352,128]{1,0:T(8,128)}, f32[4352,128]{1,0:T(8,128)}, f32[4352,128]{1,0:T(8,128)}, f32[2304,128]{1,0:T(8,128)}, /*index=5*/f32[2304,128]{1,0:T(8,128)}) custom-call(s32[96]{0:T(128)} %fusion.52.refs_0_, bf16[256,512]{1,0:T(8,128)(2,1)} %get-tuple-element.67.refs_1_, ...), custom_call_target="tpu_custom_call" | custom-call | flops 8000000000 | bytes 16777216 | tf_op jit(solution)/shard_map/weight_gradients/pallas_call | solution.py:580
  141.6 7.7 %all-to-all-start.2 = ((f32[16,2,32,128]{3,2,1,0:T(8,128)}), f32[16,2,32,128]{3,2,1,0:T(8,128)}, u32[]{:S(2)}, u32[]{:S(2)}) async-start(f32[16,2,32,128]{3,2,1,0:T(8,128)} %bitcast.43), calls=%async_computation.2 | async-start | bytes 1048576 | tf_op jit(solution)/shard_map/all_to_all | solution.py:799
  154.1 3.0 %slice_add_fusion = (f32[2176,128]{1,0:T(8,128)}, f32[2176,128]{1,0:T(8,128)S(1)}) fusion(f32[4352,128]{1,0:T(8,128)} %copy-done.8, f32[4352,128]{1,0:T(8,128)S(1)} %copy-done.7), kind=kLoop, calls=%fused_computation | loop fusion | flops 557056 | bytes 6684672 | tf_op jit(solution)/shard_map/add | solution.py:676
  160.0 4.8 %all-to-all-done.2 = f32[16,2,32,128]{3,2,1,0:T(8,128)} async-done(((f32[16,2,32,128]{3,2,1,0:T(8,128)}), f32[16,2,32,128]{3,2,1,0:T(8,128)}, u32[]{:S(2)}, u32[]{:S(2)}) %all-to-all-start.2) | async-done | bytes 524320 | tf_op jit(solution)/shard_map/all_to_all | solution.py:799
  167.2 19.5 %state_backward.1 = (f32[1024,128]{1,0:T(8,128)}, f32[16,32,128]{2,1,0:T(8,128)}) custom-call(s32[4]{0:T(128)} %bitcast.350, f32[32,24,128]{2,1,0:T(8,128)} %concatenate.98.prm_ref, f32[1024,128]{1,0:T(8,128)} %bitcast.337, f32[1024,128]{1,0:T(8,128)} %bitcast.44.g_ref, f32[1024,128]{1,0:T(8,128)} %get-tuple-element.81.prior_ref, ...), custom_call_target="tpu_custom_call" | custom-call | flops 35000000512 | bytes 4194304 | tf_op jit(solution)/shard_map/state_backward/pallas_call | solution.py:264
  186.7 4.9 %collective-permute-done.21 = f32[1152,128]{1,0:T(8,128)} collective-permute-done((f32[1152,128]{1,0:T(8,128)}, f32[1152,128]{1,0:T(8,128)}, u32[]{:S(2)}, u32[]{:S(2)}) %collective-permute-start.21) | collective-permute-done | bytes 589856 | tf_op jit(solution)/shard_map/ppermute | solution.py:596
  204.0 5.6 %all-to-all-start.3 = ((f32[16,2,32,128]{3,1,2,0:T(2,128)}), f32[16,2,32,128]{3,1,2,0:T(2,128)S(1)}, u32[]{:S(2)}, u32[]{:S(2)}) async-start(f32[16,2,32,128]{3,1,2,0:T(2,128)} %copy.59), calls=%async_computation.3 | async-start | bytes 1048576 | tf_op jit(solution)/shard_map/all_to_all | solution.py:754
  213.1 8.4 %collective-permute-done.23 = f32[1088,128]{1,0:T(8,128)} collective-permute-done((f32[1088,128]{1,0:T(8,128)}, f32[1088,128]{1,0:T(8,128)}, u32[]{:S(2)}, u32[]{:S(2)}) %collective-permute-start.23) | collective-permute-done | bytes 557088 | tf_op jit(solution)/shard_map/ppermute | solution.py:596
  227.2 3.6 %collective-permute-start.27 = (f32[544,128]{1,0:T(8,128)S(1)}, f32[544,128]{1,0:T(8,128)S(1)}, u32[]{:S(2)}, u32[]{:S(2)}) collective-permute-start(f32[544,128]{1,0:T(8,128)S(1)} %pad_maximum_fusion.5), channel_id=1, source_target_pairs={{0,16},{2,18},{4,20},{6,22},{8,24},{10,26},{12,28},{14,30},{16,0},... | collective-permute-start | bytes 835592 | tf_op jit(solution)/shard_map/ppermute | solution.py:596
  233.1 3.0 %collective-permute-done.29 = f32[288,128]{1,0:T(8,128)S(1)} collective-permute-done((f32[288,128]{1,0:T(8,128)S(1)}, f32[288,128]{1,0:T(8,128)S(1)}, u32[]{:S(2)}, u32[]{:S(2)}) %collective-permute-start.29) | collective-permute-done | bytes 147488 | tf_op jit(solution)/shard_map/ppermute | solution.py:596
  241.4 8.9 %collective-permute-done.27 = f32[544,128]{1,0:T(8,128)S(1)} collective-permute-done((f32[544,128]{1,0:T(8,128)S(1)}, f32[544,128]{1,0:T(8,128)S(1)}, u32[]{:S(2)}, u32[]{:S(2)}) %collective-permute-start.27) | collective-permute-done | bytes 278560 | tf_op jit(solution)/shard_map/ppermute | solution.py:596
  259.4 2.9 %collective-permute-done.38 = f32[8,128]{1,0:T(8,128)S(1)} collective-permute-done((f32[8,128]{1,0:T(8,128)S(1)}, f32[8,128]{1,0:T(8,128)S(1)}, u32[]{:S(2)}, u32[]{:S(2)}) %collective-permute-start.38) | collective-permute-done | bytes 4128 | tf_op jit(solution)/shard_map/ppermute | solution.py:596
  262.3 3.0 %collective-permute-start.39 = (f32[8,128]{1,0:T(8,128)S(1)}, f32[8,128]{1,0:T(8,128)S(1)}, u32[]{:S(2)}, u32[]{:S(2)}) collective-permute-start(f32[8,128]{1,0:T(8,128)S(1)} %add_add_fusion.3), channel_id=1, source_target_pairs={{0,8},{2,10},{4,12},{6,14},{8,0},{10,2},{12,4},{14,6},{16,24},{18,... | collective-permute-start | bytes 12296 | tf_op jit(solution)/shard_map/ppermute | solution.py:596
  272.3 3.8 %collective-permute-done.34 = f32[520,128]{1,0:T(8,128)S(1)} collective-permute-done((f32[520,128]{1,0:T(8,128)S(1)}, f32[520,128]{1,0:T(8,128)S(1)}, u32[]{:S(2)}, u32[]{:S(2)}) %collective-permute-start.34) | collective-permute-done | bytes 266272 | tf_op jit(solution)/shard_map/ppermute | solution.py:724
  (264 shorter events, 95.3 us)
Async XLA Ops:
  4.4 22.6 %collective-permute-start.5 = (f32[688,128]{1,0:T(8,128)S(1)}, f32[688,128]{1,0:T(8,128)S(1)}, u32[]{:S(2)}, u32[]{:S(2)}) collective-permute-start(f32[688,128]{1,0:T(8,128)S(1)} %bitcast.315), channel_id=1, source_target_pairs={{0,8},{2,10},{4,12},{6,14},{8,0},{10,2},{12,4},{14,6},{16,24},{18,... | collective-permute-start | bytes 1056776 | tf_op jit(solution)/shard_map/ppermute | solution.py:596
  7.5 31.9 %collective-permute-start.6 = (f32[688,128]{1,0:T(8,128)S(1)}, f32[688,128]{1,0:T(8,128)S(1)}, u32[]{:S(2)}, u32[]{:S(2)}) collective-permute-start(f32[688,128]{1,0:T(8,128)S(1)} %bitcast.316), channel_id=1, source_target_pairs={{0,16},{2,18},{4,20},{6,22},{8,24},{10,26},{12,28},{14,30},{16,0},... | collective-permute-start | bytes 1056776 | tf_op jit(solution)/shard_map/ppermute | solution.py:596
  10.1 32.9 %collective-permute-start.7 = (f32[688,128]{1,0:T(8,128)S(1)}, f32[688,128]{1,0:T(8,128)S(1)}, u32[]{:S(2)}, u32[]{:S(2)}) collective-permute-start(f32[688,128]{1,0:T(8,128)S(1)} %bitcast.317), channel_id=1, source_target_pairs={{0,24},{2,26},{4,28},{6,30},{8,16},{10,18},{12,20},{14,22},{16,8},... | collective-permute-start | bytes 1056776 | tf_op jit(solution)/shard_map/ppermute | solution.py:596
  12.9 47.1 %all-to-all-start = ((f32[16,2,32,128]{3,1,2,0:T(2,128)}), f32[16,2,32,128]{3,1,2,0:T(2,128)S(1)}, u32[]{:S(2)}, u32[]{:S(2)}) async-start(f32[16,2,32,128]{3,1,2,0:T(2,128)} %multiply_bitcast_fusion), calls=%async_computation | async-start | bytes 1048576 | tf_op jit(solution)/shard_map/all_to_all | solution.py:749
  23.2 17.0 %collective-permute-start.1 = (f32[2,2,2,65,128]{4,3,0,1,2:T(8,128)S(1)}, f32[2,2,2,65,128]{4,3,0,1,2:T(8,128)S(1)}, u32[]{:S(2)}, u32[]{:S(2)}) collective-permute-start(f32[2,2,2,65,128]{4,3,0,1,2:T(8,128)S(1)} %slice_bitcast_fusion.2), channel_id=1, source_target_pairs={{0,2},{1,3}} | collective-permute-start | bytes 798728 | tf_op jit(solution)/shard_map/ppermute | solution.py:709
  51.2 21.4 %collective-permute-start.9 = (f32[1376,128]{1,0:T(8,128)S(1)}, f32[1376,128]{1,0:T(8,128)S(1)}, u32[]{:S(2)}, u32[]{:S(2)}) collective-permute-start(f32[1376,128]{1,0:T(8,128)S(1)} %pad_maximum_fusion.1), channel_id=1, source_target_pairs={{0,4},{2,6},{4,0},{6,2},{8,12},{10,14},{12,8},{14,10},{16,20},{18,... | collective-permute-start | bytes 2113544 | tf_op jit(solution)/shard_map/ppermute | solution.py:596
  54.6 19.0 %collective-permute-start.8 = (f32[1376,128]{1,0:T(8,128)S(1)}, f32[1376,128]{1,0:T(8,128)}, u32[]{:S(2)}, u32[]{:S(2)}) collective-permute-start(f32[1376,128]{1,0:T(8,128)S(1)} %pad_maximum_fusion), channel_id=1, source_target_pairs={{0,2},{2,0},{4,6},{6,4},{8,10},{10,8},{12,14},{14,12},{16,18},{18,... | collective-permute-start | bytes 2113544 | tf_op jit(solution)/shard_map/ppermute | solution.py:596
  75.7 35.7 %collective-permute-start.12 = (f32[2752,128]{1,0:T(8,128)}, f32[2752,128]{1,0:T(8,128)}, u32[]{:S(2)}, u32[]{:S(2)}) collective-permute-start(f32[2752,128]{1,0:T(8,128)} %constant_dynamic-update-slice_fusion.refs_0_), channel_id=1, source_target_pairs={{0,4},{2,6},{4,0},{6,2},{8,12},{10,14},{12,8},{14,10},{16,20},{18,... | collective-permute-start | bytes 4227080 | tf_op jit(solution)/shard_map/ppermute | solution.py:596
  77.1 34.3 %collective-permute-start.13 = (f32[2752,128]{1,0:T(8,128)S(1)}, f32[2752,128]{1,0:T(8,128)}, u32[]{:S(2)}, u32[]{:S(2)}) collective-permute-start(f32[2752,128]{1,0:T(8,128)S(1)} %copy-done.18), channel_id=1, source_target_pairs={{0,2},{2,0},{4,6},{6,4},{8,10},{10,8},{12,14},{14,12},{16,18},{18,... | collective-permute-start | bytes 4227080 | tf_op jit(solution)/shard_map/ppermute | solution.py:596
  78.6 32.8 %all-to-all-start.1 = ((f32[16,2,32,128]{3,2,1,0:T(8,128)}), f32[16,2,32,128]{3,2,1,0:T(8,128)S(1)}, u32[]{:S(2)}, u32[]{:S(2)}) async-start(f32[16,2,32,128]{3,2,1,0:T(8,128)} %bitcast.39), calls=%async_computation.1 | async-start | bytes 1048576 | tf_op jit(solution)/shard_map/all_to_all | solution.py:793
  85.0 28.8 %collective-permute-start.10 = (f32[2752,128]{1,0:T(8,128)}, f32[2752,128]{1,0:T(8,128)}, u32[]{:S(2)}, u32[]{:S(2)}) collective-permute-start(f32[2752,128]{1,0:T(8,128)} %constant_dynamic-update-slice_fusion.refs_0_), channel_id=1, source_target_pairs={{0,1},{1,0},{2,3},{3,2},{4,5},{5,4},{6,7},{7,6},{8,9},{9,8},{10,11... | collective-permute-start | bytes 4227080 | tf_op jit(solution)/shard_map/ppermute | solution.py:600
  85.1 28.7 %collective-permute-start.11 = (f32[2752,128]{1,0:T(8,128)S(1)}, f32[2752,128]{1,0:T(8,128)}, u32[]{:S(2)}, u32[]{:S(2)}) collective-permute-start(f32[2752,128]{1,0:T(8,128)S(1)} %copy-done.18), channel_id=1, source_target_pairs={{0,1},{1,0},{2,3},{3,2},{4,5},{5,4},{6,7},{7,6},{8,9},{9,8},{10,11... | collective-permute-start | bytes 4227080 | tf_op jit(solution)/shard_map/ppermute | solution.py:600
  141.1 16.0 %collective-permute-start.16 = (f32[4352,128]{1,0:T(8,128)}, f32[4352,128]{1,0:T(8,128)}, u32[]{:S(2)}, u32[]{:S(2)}) collective-permute-start(f32[4352,128]{1,0:T(8,128)} %get-tuple-element.75), channel_id=1, source_target_pairs={{0,1},{1,0},{2,3},{3,2},{4,5},{5,4},{6,7},{7,6},{8,9},{9,8},{10,11... | collective-permute-start | bytes 6684680 | tf_op jit(solution)/shard_map/ppermute | solution.py:600
  141.6 23.2 %all-to-all-start.2 = ((f32[16,2,32,128]{3,2,1,0:T(8,128)}), f32[16,2,32,128]{3,2,1,0:T(8,128)}, u32[]{:S(2)}, u32[]{:S(2)}) async-start(f32[16,2,32,128]{3,2,1,0:T(8,128)} %bitcast.43), calls=%async_computation.2 | async-start | bytes 1048576 | tf_op jit(solution)/shard_map/all_to_all | solution.py:799
  164.8 26.7 %collective-permute-start.21 = (f32[1152,128]{1,0:T(8,128)}, f32[1152,128]{1,0:T(8,128)}, u32[]{:S(2)}, u32[]{:S(2)}) collective-permute-start(f32[1152,128]{1,0:T(8,128)} %get-tuple-element.93), channel_id=1, source_target_pairs={{0,16},{2,18},{4,20},{6,22},{8,24},{10,26},{12,28},{14,30},{16,0},... | collective-permute-start | bytes 1769480 | tf_op jit(solution)/shard_map/ppermute | solution.py:596
  165.7 27.0 %collective-permute-start.20 = (f32[2176,128]{1,0:T(8,128)}, f32[2176,128]{1,0:T(8,128)}, u32[]{:S(2)}, u32[]{:S(2)}) collective-permute-start(f32[2176,128]{1,0:T(8,128)} %get-tuple-element.91), channel_id=1, source_target_pairs={{0,4},{2,6},{4,0},{6,2},{8,12},{10,14},{12,8},{14,10},{16,20},{18,... | collective-permute-start | bytes 3342344 | tf_op jit(solution)/shard_map/ppermute | solution.py:596
  166.5 27.8 %collective-permute-start.19 = (f32[2176,128]{1,0:T(8,128)}, f32[2176,128]{1,0:T(8,128)}, u32[]{:S(2)}, u32[]{:S(2)}) collective-permute-start(f32[2176,128]{1,0:T(8,128)} %get-tuple-element.89), channel_id=1, source_target_pairs={{0,2},{2,0},{4,6},{6,4},{8,10},{10,8},{12,14},{14,12},{16,18},{18,... | collective-permute-start | bytes 3342344 | tf_op jit(solution)/shard_map/ppermute | solution.py:596
  198.0 14.0 %collective-permute-start.24 = (f32[1088,128]{1,0:T(8,128)}, f32[1088,128]{1,0:T(8,128)}, u32[]{:S(2)}, u32[]{:S(2)}) collective-permute-start(f32[1088,128]{1,0:T(8,128)} %slice_bitcast_fusion), channel_id=1, source_target_pairs={{0,2},{2,0},{4,6},{6,4},{8,10},{10,8},{12,14},{14,12},{16,18},{18,... | collective-permute-start | bytes 1671176 | tf_op jit(solution)/shard_map/ppermute | solution.py:596
  202.0 19.5 %collective-permute-start.23 = (f32[1088,128]{1,0:T(8,128)}, f32[1088,128]{1,0:T(8,128)}, u32[]{:S(2)}, u32[]{:S(2)}) collective-permute-start(f32[1088,128]{1,0:T(8,128)} %slice_bitcast_fusion.1), channel_id=1, source_target_pairs={{0,4},{2,6},{4,0},{6,2},{8,12},{10,14},{12,8},{14,10},{16,20},{18,... | collective-permute-start | bytes 1671176 | tf_op jit(solution)/shard_map/ppermute | solution.py:596
  204.0 46.4 %all-to-all-start.3 = ((f32[16,2,32,128]{3,1,2,0:T(2,128)}), f32[16,2,32,128]{3,1,2,0:T(2,128)S(1)}, u32[]{:S(2)}, u32[]{:S(2)}) async-start(f32[16,2,32,128]{3,1,2,0:T(2,128)} %copy.59), calls=%async_computation.3 | async-start | bytes 1048576 | tf_op jit(solution)/shard_map/all_to_all | solution.py:754
  224.7 16.7 %collective-permute-start.26 = (f32[544,128]{1,0:T(8,128)S(1)}, f32[544,128]{1,0:T(8,128)S(1)}, u32[]{:S(2)}, u32[]{:S(2)}) collective-permute-start(f32[544,128]{1,0:T(8,128)S(1)} %pad_maximum_fusion.4), channel_id=1, source_target_pairs={{0,8},{2,10},{4,12},{6,14},{8,0},{10,2},{12,4},{14,6},{16,24},{18,... | collective-permute-start | bytes 835592 | tf_op jit(solution)/shard_map/ppermute | solution.py:596
  227.2 23.1 %collective-permute-start.27 = (f32[544,128]{1,0:T(8,128)S(1)}, f32[544,128]{1,0:T(8,128)S(1)}, u32[]{:S(2)}, u32[]{:S(2)}) collective-permute-start(f32[544,128]{1,0:T(8,128)S(1)} %pad_maximum_fusion.5), channel_id=1, source_target_pairs={{0,16},{2,18},{4,20},{6,22},{8,24},{10,26},{12,28},{14,30},{16,0},... | collective-permute-start | bytes 835592 | tf_op jit(solution)/shard_map/ppermute | solution.py:596
  231.0 19.3 %collective-permute-start.28 = (f32[544,128]{1,0:T(8,128)S(1)}, f32[544,128]{1,0:T(8,128)S(1)}, u32[]{:S(2)}, u32[]{:S(2)}) collective-permute-start(f32[544,128]{1,0:T(8,128)S(1)} %pad_maximum_fusion.6), channel_id=1, source_target_pairs={{0,24},{2,26},{4,28},{6,30},{8,16},{10,18},{12,20},{14,22},{16,8},... | collective-permute-start | bytes 835592 | tf_op jit(solution)/shard_map/ppermute | solution.py:596
  250.5 17.3 %collective-permute-start.33 = (f32[260,128]{1,0:T(8,128)S(1)}, f32[260,128]{1,0:T(8,128)S(1)}, u32[]{:S(2)}, u32[]{:S(2)}) collective-permute-start(f32[260,128]{1,0:T(8,128)S(1)} %pad_maximum_fusion.9), channel_id=1, source_target_pairs={{4,0},{6,2},{5,1},{7,3}} | collective-permute-start | bytes 399368 | tf_op jit(solution)/shard_map/ppermute | solution.py:724
  (50 other events, 539.1 us)

commit v6 on v5

--- a/solution.py
+++ b/solution.py
@@ -36,10 +36,7 @@
     return lax.dot_general(lhs, rhs, (((ca,), (cb,)), ((), ())), preferred_element_type=f32)
 
 def dot2(data, table, ct):
-    hi, lo = data
-    both = jnp.concatenate([hi, lo], axis=0)
-    out = lax.dot_general(both, table, (((1,), (ct,)), ((), ())), preferred_element_type=f32)
-    return out[:hi.shape[0]] + out[hi.shape[0]:]
+    return dot3(data, (table[0], table[1]), 1, ct)
 
 def swap(v):
     return pltpu.roll(v, NSTATE, 1)
@@ -63,7 +60,7 @@
     wide = pltpu.roll(jnp.broadcast_to(taps, (CH, CH)), 0, 1, stride=1, stride_axis=0)
     row = lax.broadcasted_iota(jnp.int32, (CH, CH), 0)
     col = lax.broadcasted_iota(jnp.int32, (CH, CH), 1)
-    return jnp.where(col >= row, wide, 0.0).astype(bf16)
+    return jnp.where(col >= row, wide, 0.0)
 
 def label_at(ends, pos):
     total = jnp.zeros_like(pos)
@@ -109,6 +106,9 @@
         total = total + v[k * nck:(k + 1) * nck] * masks_ref[k]
     return total
 
+def keep(ref, h, v):
+    ref[h, 0], ref[h, 1] = split(v)
+
 def for_channels(nch, body):
     lax.fori_loop(0, nch, lambda h, _: body(h) or 0, 0, unroll=min(nch, 16))
 
@@ -118,15 +118,15 @@
     def tables(h):
         prm = prm_ref[h]
         table = ladder(prm, 1)
-        table_ref[h] = table.astype(bf16)
-        out_ref[h] = twist(table, prm[17:18], prm[18:19]).astype(bf16)
+        keep(table_ref, h, table)
+        keep(out_ref, h, twist(table, prm[17:18], prm[18:19]))
 
     def falling(h):
-        down_ref[h] = ladder(prm_ref[h], -1).astype(bf16)
+        keep(down_ref, h, ladder(prm_ref[h], -1))
 
     def taps(h):
         wrow = jnp.broadcast_to(prm_ref[h, 16:17, :], (16, 2 * NSTATE))
-        mat_ref[h] = toeplitz(dot2(split(wrow), table_ref[h], 1)[0:1])
+        keep(mat_ref, h, toeplitz(dot2(split(wrow), table_ref[h], 1)[0:1]))
 
     def local(h):
         prm = prm_ref[h, 16:24, :]
@@ -156,7 +156,7 @@
 
 def ssm_forward(ends, prm, x, nck, nch):
     vm = pl.BlockSpec(memory_space=pltpu.VMEM)
-    table = jax.ShapeDtypeStruct((nch, CH, 2 * NSTATE), bf16)
+    table = jax.ShapeDtypeStruct((nch, 2, CH, 2 * NSTATE), bf16)
     return pl.pallas_call(
         partial(fwd_body, nck, nch, x.shape[0] // nck),
         out_shape=(jax.ShapeDtypeStruct((nck * nch, CH), f32), jax.ShapeDtypeStruct((nck * nch, 2 * NSTATE), f32)) + (table,) * 4,
@@ -241,7 +241,7 @@
 
     def carried(h):
         dgt = dot3(masked(split(g_ref[at_channel(h), :]), low_ref, DOCS), split(prior_ref[at_channel(h), :]), 0, 0)
-        table = table_ref[h].astype(f32)
+        table = table_ref[h, 0].astype(f32) + table_ref[h, 1].astype(f32)
         same, cross = dgt * table, dgt * swap(table)
         put(2, h, same)
         put(3, h, cross)
@@ -252,7 +252,7 @@
         prm = prm_ref[h, 16:24, :]
         u = split(x_ref[pl.ds(h, nck, stride=apart), :] * prm[3:4] + prm[4:5])
         ddown = dot3(masked(u, low_ref, DOCS + 1), split(adj_ref[at_channel(h), :]), 0, 0) * ((CH - 1) - late)
-        down = down_ref[h].astype(f32)
+        down = down_ref[h, 0].astype(f32) + down_ref[h, 1].astype(f32)
         put(6, h, ddown * down)
         put(7, h, ddown * swap(down))
 
@@ -788,8 +788,6 @@
     modes, modes_pull = jax.vjp(mixing, few[2], many[0], many[1], many[2], many[3])
     prm = mode_rows(*modes, few[0], few[1], few[3])
     outs, prior, *tables = ssm_forward(ends, prm, hats, nck, nch)
-    if direct():
-        outs, plane = lax.optimization_barrier((outs, plane))
     response = lax.all_to_all(outs.reshape(seq, -1, nch, CH), "seq", 0, 0).reshape(-1, CH)
     if direct():
         far = [hop(plane[0], 2), hop(plane[1], 1)]

time: 283 us -> 277 us (0.979)
  waiting for transfers between devices: 87.1 us -> 76.9 us
  Pallas kernels: 54.8 us -> 60.9 us
    all_to_all x1, waiting for transfers between devices: 25.8 us -> 11.9 us  [per_device(): lax.all_to_all(outs.reshape(seq, -1, nch, CH), 'seq', 0, 0).reshape(-1, CH)]
    ppermute x24, waiting for transfers between devices: 43.6 us -> 47.7 us  [hop(): return lax.ppermute(v, 'seq', [(i, i ^ step) for i in range(16)])]
    pallas_call x1, Pallas kernels: 11.7 us -> 14.8 us  [ssm_forward(): pl.pallas_call(partial(fwd_body, nck, nch, x.shape[0] // nck), out_shape=...]
    all_to_all x1, starting transfers between devices: 7.72 us -> 4.66 us  [per_device(): lax.all_to_all(d_response.reshape(seq, -1, nch, CH), 'seq', 0, 0)]
  transfers between devices with their start and end apart: 46 -> 46, of which waited for: 19 -> 21; matrix products, arithmetic and copies ran while one was open for 14% -> 17% of each run, Pallas kernels for 11% -> 13%
where the time goes in v6:
time: 277 us; the launch traced here: 275 us
  starting transfers between devices  78.7 us (28%)
  waiting for transfers between devices  76.9 us (28%)
  Pallas kernels  60.9 us (22%)
  other arithmetic  30 us (11%)
  local copies, waits for them, and re-layouts  24.1 us (9%)
  between operations  4.79 us (2%)
    ppermute x24, waiting for transfers between devices, hop(): return lax.ppermute(v, 'seq', [(i, i ^ step) for i in range(16)])  47.7 us
    ppermute x24, starting transfers between devices, hop(): return lax.ppermute(v, 'seq', [(i, i ^ step) for i in range(16)])  31.5 us
    pallas_call x1, Pallas kernels, ssm_backward(): pl.pallas_call(partial(bwd_body, nck, nch, x.shape[0] // nck), out_shape=...  22.3 us
    ppermute x4, starting transfers between devices, scatter_modes(): come = lax.ppermute(blocks[1], 'seq', [(i, i + step) for i in range(step)])  15.4 us
    pallas_call x1, Pallas kernels, ssm_forward(): pl.pallas_call(partial(fwd_body, nck, nch, x.shape[0] // nck), out_shape=...  14.8 us
    pallas_call x1, Pallas kernels, mlp_kernel(): pl.pallas_call(partial(mlp_body, share, devices, nseq, streams), out_shap...  14.8 us
    all_to_all x1, waiting for transfers between devices, per_device(): lax.all_to_all(outs.reshape(seq, -1, nch, CH), 'seq', 0, 0).reshape(-1, CH)  11.9 us
    pallas_call x1, Pallas kernels, pack_kernel(): pl.pallas_call(partial(pack_body, tuple((s[:3] for s in streams)), tiles,...  9 us
  transfers between devices with their start and end apart: 46, of which 21 were waited for; matrix products, arithmetic and copies ran while one was open for 17% of the time, Pallas kernels for 13%

profile of v6, /device:TPU:0, one launch (start us, length us, event | category | flops | bytes accessed | tf_op | source)
XLA Modules:
  0.0 275.4 jit_solution(15253834549016262580)
XLA Ops:
  1.2 3.7 %dynamic_update_slice.3 = f32[88064]{0:T(1024)S(1)} dynamic-update-slice(f32[88064]{0:T(1024)S(1)} %broadcast_in_dim.11, f32[86224]{0:T(1024)} %param.24, s32[]{:T(128)S(6)} %select_n.74) | dynamic-update-slice | bytes 689796 | tf_op jit(solution)/shard_map/dynamic_update_slice | solution.py:623
  12.9 7.2 %all-to-all-start = ((f32[16,2,32,128]{3,1,2,0:T(2,128)}), f32[16,2,32,128]{3,1,2,0:T(2,128)S(1)}, u32[]{:S(2)}, u32[]{:S(2)}) async-start(f32[16,2,32,128]{3,1,2,0:T(2,128)} %multiply_bitcast_fusion), calls=%async_computation | async-start | bytes 1048576 | tf_op jit(solution)/shard_map/all_to_all | solution.py:749
  23.2 3.8 %collective-permute-start.8 = (f32[2,2,2,65,128]{4,3,0,1,2:T(8,128)S(1)}, f32[2,2,2,65,128]{4,3,0,1,2:T(8,128)S(1)}, u32[]{:S(2)}, u32[]{:S(2)}) collective-permute-start(f32[2,2,2,65,128]{4,3,0,1,2:T(8,128)S(1)} %slice_bitcast_fusion.2), channel_id=1, source_target_pairs={{0,2},{1,3}} | collective-permute-start | bytes 798728 | tf_op jit(solution)/shard_map/ppermute | solution.py:709
  27.8 9.7 %collective-permute-done.1 = f32[688,128]{1,0:T(8,128)S(1)} collective-permute-done((f32[688,128]{1,0:T(8,128)S(1)}, f32[688,128]{1,0:T(8,128)S(1)}, u32[]{:S(2)}, u32[]{:S(2)}) %collective-permute-start.1) | collective-permute-done | bytes 352288 | tf_op jit(solution)/shard_map/ppermute | solution.py:596
  43.8 7.4 %collective-permute-start.10 = (f32[2,65,128]{2,1,0:T(8,128)S(1)}, f32[2,65,128]{2,1,0:T(8,128)S(1)}, u32[]{:S(2)}, u32[]{:S(2)}) collective-permute-start(f32[2,65,128]{2,1,0:T(8,128)S(1)} %slice_bitcast_fusion.18), channel_id=1, source_target_pairs={{0,8},{2,10},{4,12},{6,14},{1,9},{3,11},{5,13},{7,15}} | collective-permute-start | bytes 199688 | tf_op jit(solution)/shard_map/ppermute | solution.py:709
  60.9 6.8 %collective-permute-done.5 = f32[1376,128]{1,0:T(8,128)S(1)} collective-permute-done((f32[1376,128]{1,0:T(8,128)S(1)}, f32[1376,128]{1,0:T(8,128)S(1)}, u32[]{:S(2)}, u32[]{:S(2)}) %collective-permute-start.5) | collective-permute-done | bytes 704544 | tf_op jit(solution)/shard_map/ppermute | solution.py:596
  74.5 14.8 %state_forward.1 = (f32[1024,128]{1,0:T(8,128)}, f32[1024,128]{1,0:T(8,128)}, bf16[32,2,128,128]{3,2,1,0:T(8,128)(2,1)}, bf16[32,2,128,128]{3,2,1,0:T(8,128)(2,1...) custom-call(s32[4]{0:T(128)} %bitcast.350, f32[32,24,128]{2,1,0:T(8,128)} %concatenate.102.prm_ref, ...), custom_call_target="tpu_custom_call" | custom-call | flops 20000000000 | bytes 3145728 | tf_op jit(solution)/shard_map/state_forward/pallas_call | solution.py:160
  89.3 6.6 %all-to-all-start.1 = ((f32[16,2,32,128]{3,2,1,0:T(8,128)}), f32[16,2,32,128]{3,2,1,0:T(8,128)S(1)}, u32[]{:S(2)}, u32[]{:S(2)}) async-start(f32[16,2,32,128]{3,2,1,0:T(8,128)} %bitcast.340), calls=%async_computation.1 | async-start | bytes 1048576 | tf_op jit(solution)/shard_map/all_to_all | solution.py:791
  96.5 11.9 %all-to-all-done.1 = f32[16,2,32,128]{3,2,1,0:T(8,128)S(1)} async-done(((f32[16,2,32,128]{3,2,1,0:T(8,128)}), f32[16,2,32,128]{3,2,1,0:T(8,128)S(1)}, u32[]{:S(2)}, u32[]{:S(2)}) %all-to-all-start.1) | async-done | bytes 524320 | tf_op jit(solution)/shard_map/all_to_all | solution.py:791
  113.9 14.8 %feed_forward.1 = (bf16[256,512]{1,0:T(8,128)(2,1)}, f32[256,512]{1,0:T(8,128)}, f32[1024,128]{1,0:T(8,128)}, f32[40,128]{1,0:T(8,128)}, f32[1040,128]{1,0:T(8,1...) custom-call(s32[5]{0:T(128)} %pad_add_fusion.place_ref, ...), custom_call_target="tpu_custom_call" | custom-call | flops 10000000000 | bytes 20971520 | tf_op jit(solution)/shard_map/feed_forward/pallas_call | solution.py:510
  128.7 9.0 %weight_gradients.1 = (f32[4352,128]{1,0:T(8,128)}, f32[4352,128]{1,0:T(8,128)}, f32[4352,128]{1,0:T(8,128)}, f32[4352,128]{1,0:T(8,128)}, f32[2304,128]{1,0:T(8,128)}, /*index=5*/f32[2304,128]{1,0:T(8,128)}) custom-call(s32[96]{0:T(128)} %fusion.52.refs_0_, bf16[256,512]{1,0:T(8,128)(2,1)} %get-tuple-element.61.refs_1_, ...), custom_call_target="tpu_custom_call" | custom-call | flops 8000000000 | bytes 16777216 | tf_op jit(solution)/shard_map/weight_gradients/pallas_call | solution.py:580
  138.7 4.7 %all-to-all-start.2 = ((f32[16,2,32,128]{3,2,1,0:T(8,128)}), f32[16,2,32,128]{3,2,1,0:T(8,128)}, u32[]{:S(2)}, u32[]{:S(2)}) async-start(f32[16,2,32,128]{3,2,1,0:T(8,128)} %bitcast.43), calls=%async_computation.2 | async-start | bytes 1048576 | tf_op jit(solution)/shard_map/all_to_all | solution.py:797
  148.2 3.0 %slice_add_fusion = (f32[2176,128]{1,0:T(8,128)}, f32[2176,128]{1,0:T(8,128)S(1)}) fusion(f32[4352,128]{1,0:T(8,128)} %copy-done.8, f32[4352,128]{1,0:T(8,128)S(1)} %copy-done.7), kind=kLoop, calls=%fused_computation | loop fusion | flops 557056 | bytes 6684672 | tf_op jit(solution)/shard_map/add | solution.py:676
  151.2 2.9 %slice_add_fusion.2 = (f32[2176,128]{1,0:T(8,128)}, f32[2176,128]{1,0:T(8,128)S(1)}) fusion(f32[4352,128]{1,0:T(8,128)} %collective-permute-done.16, f32[4352,128]{1,0:T(8,128)S(1)} %copy-done.6), kind=kLoop, calls=%fused_computation.2 | loop fusion | flops 557056 | bytes 6684672 | tf_op jit(solution)/shard_map/add | solution.py:676
  154.1 4.8 %all-to-all-done.2 = f32[16,2,32,128]{3,2,1,0:T(8,128)} async-done(((f32[16,2,32,128]{3,2,1,0:T(8,128)}), f32[16,2,32,128]{3,2,1,0:T(8,128)}, u32[]{:S(2)}, u32[]{:S(2)}) %all-to-all-start.2) | async-done | bytes 524320 | tf_op jit(solution)/shard_map/all_to_all | solution.py:797
  161.3 22.3 %state_backward.1 = (f32[1024,128]{1,0:T(8,128)}, f32[16,32,128]{2,1,0:T(8,128)}) custom-call(s32[4]{0:T(128)} %bitcast.351, f32[32,24,128]{2,1,0:T(8,128)} %concatenate.102.prm_ref, f32[1024,128]{1,0:T(8,128)} %bitcast.337, f32[1024,128]{1,0:T(8,128)} %bitcast.44.g_ref, f32[1024,128]{1,0:T(8,128)} %get-tuple-element.75.prior_ref, ...), custom_call_target="tpu_custom_call" | custom-call | flops 35000000512 | bytes 4194304 | tf_op jit(solution)/shard_map/state_backward/pallas_call | solution.py:264
  198.1 5.7 %all-to-all-start.3 = ((f32[16,2,32,128]{3,1,2,0:T(2,128)}), f32[16,2,32,128]{3,1,2,0:T(2,128)S(1)}, u32[]{:S(2)}, u32[]{:S(2)}) async-start(f32[16,2,32,128]{3,1,2,0:T(2,128)} %copy.59), calls=%async_computation.3 | async-start | bytes 1048576 | tf_op jit(solution)/shard_map/all_to_all | solution.py:754
  207.2 8.4 %collective-permute-done.23 = f32[1088,128]{1,0:T(8,128)} collective-permute-done((f32[1088,128]{1,0:T(8,128)}, f32[1088,128]{1,0:T(8,128)}, u32[]{:S(2)}, u32[]{:S(2)}) %collective-permute-start.23) | collective-permute-done | bytes 557088 | tf_op jit(solution)/shard_map/ppermute | solution.py:596
  221.3 3.6 %collective-permute-start.27 = (f32[544,128]{1,0:T(8,128)S(1)}, f32[544,128]{1,0:T(8,128)S(1)}, u32[]{:S(2)}, u32[]{:S(2)}) collective-permute-start(f32[544,128]{1,0:T(8,128)S(1)} %pad_maximum_fusion.5), channel_id=1, source_target_pairs={{0,16},{2,18},{4,20},{6,22},{8,24},{10,26},{12,28},{14,30},{16,0},... | collective-permute-start | bytes 835592 | tf_op jit(solution)/shard_map/ppermute | solution.py:596
  227.1 3.0 %collective-permute-done.29 = f32[288,128]{1,0:T(8,128)S(1)} collective-permute-done((f32[288,128]{1,0:T(8,128)S(1)}, f32[288,128]{1,0:T(8,128)S(1)}, u32[]{:S(2)}, u32[]{:S(2)}) %collective-permute-start.29) | collective-permute-done | bytes 147488 | tf_op jit(solution)/shard_map/ppermute | solution.py:596
  235.5 8.9 %collective-permute-done.27 = f32[544,128]{1,0:T(8,128)S(1)} collective-permute-done((f32[544,128]{1,0:T(8,128)S(1)}, f32[544,128]{1,0:T(8,128)S(1)}, u32[]{:S(2)}, u32[]{:S(2)}) %collective-permute-start.27) | collective-permute-done | bytes 278560 | tf_op jit(solution)/shard_map/ppermute | solution.py:596
  253.4 2.9 %collective-permute-done.38 = f32[8,128]{1,0:T(8,128)S(1)} collective-permute-done((f32[8,128]{1,0:T(8,128)S(1)}, f32[8,128]{1,0:T(8,128)S(1)}, u32[]{:S(2)}, u32[]{:S(2)}) %collective-permute-start.38) | collective-permute-done | bytes 4128 | tf_op jit(solution)/shard_map/ppermute | solution.py:596
  256.4 3.0 %collective-permute-start.39 = (f32[8,128]{1,0:T(8,128)S(1)}, f32[8,128]{1,0:T(8,128)S(1)}, u32[]{:S(2)}, u32[]{:S(2)}) collective-permute-start(f32[8,128]{1,0:T(8,128)S(1)} %add_add_fusion.3), channel_id=1, source_target_pairs={{0,8},{2,10},{4,12},{6,14},{8,0},{10,2},{12,4},{14,6},{16,24},{18,... | collective-permute-start | bytes 12296 | tf_op jit(solution)/shard_map/ppermute | solution.py:596
  266.4 3.8 %collective-permute-done.34 = f32[520,128]{1,0:T(8,128)S(1)} collective-permute-done((f32[520,128]{1,0:T(8,128)S(1)}, f32[520,128]{1,0:T(8,128)S(1)}, u32[]{:S(2)}, u32[]{:S(2)}) %collective-permute-start.34) | collective-permute-done | bytes 266272 | tf_op jit(solution)/shard_map/ppermute | solution.py:724
  (264 shorter events, 98.0 us)
Async XLA Ops:
  0.6 21.0 %collective-permute-start.7 = (f32[86224]{0:T(1024)}, f32[86224]{0:T(1024)}, u32[]{:S(2)}, u32[]{:S(2)}) collective-permute-start(f32[86224]{0:T(1024)} %param.24), channel_id=1, source_target_pairs={{0,1},{1,0},{2,3},{3,2},{4,5},{5,4},{6,7},{7,6},{8,9},{9,8},{10,11... | collective-permute-start | bytes 1034696 | tf_op jit(solution)/shard_map/ppermute | solution.py:600
  4.9 22.1 %collective-permute-start = (f32[688,128]{1,0:T(8,128)S(1)}, f32[688,128]{1,0:T(8,128)S(1)}, u32[]{:S(2)}, u32[]{:S(2)}) collective-permute-start(f32[688,128]{1,0:T(8,128)S(1)} %bitcast.315), channel_id=1, source_target_pairs={{0,8},{2,10},{4,12},{6,14},{8,0},{10,2},{12,4},{14,6},{16,24},{18,... | collective-permute-start | bytes 1056776 | tf_op jit(solution)/shard_map/ppermute | solution.py:596
  7.6 30.0 %collective-permute-start.1 = (f32[688,128]{1,0:T(8,128)S(1)}, f32[688,128]{1,0:T(8,128)S(1)}, u32[]{:S(2)}, u32[]{:S(2)}) collective-permute-start(f32[688,128]{1,0:T(8,128)S(1)} %bitcast.316), channel_id=1, source_target_pairs={{0,16},{2,18},{4,20},{6,22},{8,24},{10,26},{12,28},{14,30},{16,0},... | collective-permute-start | bytes 1056776 | tf_op jit(solution)/shard_map/ppermute | solution.py:596
  10.2 31.0 %collective-permute-start.2 = (f32[688,128]{1,0:T(8,128)S(1)}, f32[688,128]{1,0:T(8,128)S(1)}, u32[]{:S(2)}, u32[]{:S(2)}) collective-permute-start(f32[688,128]{1,0:T(8,128)S(1)} %bitcast.317), channel_id=1, source_target_pairs={{0,24},{2,26},{4,28},{6,30},{8,16},{10,18},{12,20},{14,22},{16,8},... | collective-permute-start | bytes 1056776 | tf_op jit(solution)/shard_map/ppermute | solution.py:596
  12.9 47.1 %all-to-all-start = ((f32[16,2,32,128]{3,1,2,0:T(2,128)}), f32[16,2,32,128]{3,1,2,0:T(2,128)S(1)}, u32[]{:S(2)}, u32[]{:S(2)}) async-start(f32[16,2,32,128]{3,1,2,0:T(2,128)} %multiply_bitcast_fusion), calls=%async_computation | async-start | bytes 1048576 | tf_op jit(solution)/shard_map/all_to_all | solution.py:749
  23.2 15.2 %collective-permute-start.8 = (f32[2,2,2,65,128]{4,3,0,1,2:T(8,128)S(1)}, f32[2,2,2,65,128]{4,3,0,1,2:T(8,128)S(1)}, u32[]{:S(2)}, u32[]{:S(2)}) collective-permute-start(f32[2,2,2,65,128]{4,3,0,1,2:T(8,128)S(1)} %slice_bitcast_fusion.2), channel_id=1, source_target_pairs={{0,2},{1,3}} | collective-permute-start | bytes 798728 | tf_op jit(solution)/shard_map/ppermute | solution.py:709
  51.3 16.4 %collective-permute-start.5 = (f32[1376,128]{1,0:T(8,128)S(1)}, f32[1376,128]{1,0:T(8,128)S(1)}, u32[]{:S(2)}, u32[]{:S(2)}) collective-permute-start(f32[1376,128]{1,0:T(8,128)S(1)} %pad_maximum_fusion.1), channel_id=1, source_target_pairs={{0,4},{2,6},{4,0},{6,2},{8,12},{10,14},{12,8},{14,10},{16,20},{18,... | collective-permute-start | bytes 2113544 | tf_op jit(solution)/shard_map/ppermute | solution.py:596
  54.6 17.0 %collective-permute-start.3 = (f32[1376,128]{1,0:T(8,128)S(1)}, f32[1376,128]{1,0:T(8,128)}, u32[]{:S(2)}, u32[]{:S(2)}) collective-permute-start(f32[1376,128]{1,0:T(8,128)S(1)} %pad_maximum_fusion), channel_id=1, source_target_pairs={{0,2},{2,0},{4,6},{6,4},{8,10},{10,8},{12,14},{14,12},{16,18},{18,... | collective-permute-start | bytes 2113544 | tf_op jit(solution)/shard_map/ppermute | solution.py:596
  68.6 39.7 %collective-permute-start.13 = (f32[2752,128]{1,0:T(8,128)}, f32[2752,128]{1,0:T(8,128)}, u32[]{:S(2)}, u32[]{:S(2)}) collective-permute-start(f32[2752,128]{1,0:T(8,128)} %constant_dynamic-update-slice_fusion.5.refs_2_), channel_id=1, source_target_pairs={{0,2},{2,0},{4,6},{6,4},{8,10},{10,8},{12,14},{14,12},{16,18},{18,... | collective-permute-start | bytes 4227080 | tf_op jit(solution)/shard_map/ppermute | solution.py:596
  73.6 34.7 %collective-permute-start.12 = (f32[2752,128]{1,0:T(8,128)}, f32[2752,128]{1,0:T(8,128)}, u32[]{:S(2)}, u32[]{:S(2)}) collective-permute-start(f32[2752,128]{1,0:T(8,128)} %constant_dynamic-update-slice_fusion.refs_0_), channel_id=1, source_target_pairs={{0,4},{2,6},{4,0},{6,2},{8,12},{10,14},{12,8},{14,10},{16,20},{18,... | collective-permute-start | bytes 4227080 | tf_op jit(solution)/shard_map/ppermute | solution.py:596
  89.3 19.0 %all-to-all-start.1 = ((f32[16,2,32,128]{3,2,1,0:T(8,128)}), f32[16,2,32,128]{3,2,1,0:T(8,128)S(1)}, u32[]{:S(2)}, u32[]{:S(2)}) async-start(f32[16,2,32,128]{3,2,1,0:T(8,128)} %bitcast.340), calls=%async_computation.1 | async-start | bytes 1048576 | tf_op jit(solution)/shard_map/all_to_all | solution.py:791
  95.9 14.8 %collective-permute-start.6 = (f32[2752,128]{1,0:T(8,128)S(1)}, f32[2752,128]{1,0:T(8,128)}, u32[]{:S(2)}, u32[]{:S(2)}) collective-permute-start(f32[2752,128]{1,0:T(8,128)S(1)} %copy-done.18), channel_id=1, source_target_pairs={{0,1},{1,0},{2,3},{3,2},{4,5},{5,4},{6,7},{7,6},{8,9},{9,8},{10,11... | collective-permute-start | bytes 4227080 | tf_op jit(solution)/shard_map/ppermute | solution.py:600
  96.0 14.8 %collective-permute-start.4 = (f32[2752,128]{1,0:T(8,128)}, f32[2752,128]{1,0:T(8,128)}, u32[]{:S(2)}, u32[]{:S(2)}) collective-permute-start(f32[2752,128]{1,0:T(8,128)} %constant_dynamic-update-slice_fusion.refs_0_), channel_id=1, source_target_pairs={{0,1},{1,0},{2,3},{3,2},{4,5},{5,4},{6,7},{7,6},{8,9},{9,8},{10,11... | collective-permute-start | bytes 4227080 | tf_op jit(solution)/shard_map/ppermute | solution.py:600
  138.7 20.2 %all-to-all-start.2 = ((f32[16,2,32,128]{3,2,1,0:T(8,128)}), f32[16,2,32,128]{3,2,1,0:T(8,128)}, u32[]{:S(2)}, u32[]{:S(2)}) async-start(f32[16,2,32,128]{3,2,1,0:T(8,128)} %bitcast.43), calls=%async_computation.2 | async-start | bytes 1048576 | tf_op jit(solution)/shard_map/all_to_all | solution.py:797
  158.9 26.7 %collective-permute-start.21 = (f32[1152,128]{1,0:T(8,128)}, f32[1152,128]{1,0:T(8,128)}, u32[]{:S(2)}, u32[]{:S(2)}) collective-permute-start(f32[1152,128]{1,0:T(8,128)} %get-tuple-element.87), channel_id=1, source_target_pairs={{0,16},{2,18},{4,20},{6,22},{8,24},{10,26},{12,28},{14,30},{16,0},... | collective-permute-start | bytes 1769480 | tf_op jit(solution)/shard_map/ppermute | solution.py:596
  159.8 27.0 %collective-permute-start.20 = (f32[2176,128]{1,0:T(8,128)}, f32[2176,128]{1,0:T(8,128)}, u32[]{:S(2)}, u32[]{:S(2)}) collective-permute-start(f32[2176,128]{1,0:T(8,128)} %get-tuple-element.85), channel_id=1, source_target_pairs={{0,4},{2,6},{4,0},{6,2},{8,12},{10,14},{12,8},{14,10},{16,20},{18,... | collective-permute-start | bytes 3342344 | tf_op jit(solution)/shard_map/ppermute | solution.py:596
  160.6 27.8 %collective-permute-start.19 = (f32[2176,128]{1,0:T(8,128)}, f32[2176,128]{1,0:T(8,128)}, u32[]{:S(2)}, u32[]{:S(2)}) collective-permute-start(f32[2176,128]{1,0:T(8,128)} %get-tuple-element.83), channel_id=1, source_target_pairs={{0,2},{2,0},{4,6},{6,4},{8,10},{10,8},{12,14},{14,12},{16,18},{18,... | collective-permute-start | bytes 3342344 | tf_op jit(solution)/shard_map/ppermute | solution.py:596
  192.1 14.0 %collective-permute-start.24 = (f32[1088,128]{1,0:T(8,128)}, f32[1088,128]{1,0:T(8,128)}, u32[]{:S(2)}, u32[]{:S(2)}) collective-permute-start(f32[1088,128]{1,0:T(8,128)} %slice_bitcast_fusion), channel_id=1, source_target_pairs={{0,2},{2,0},{4,6},{6,4},{8,10},{10,8},{12,14},{14,12},{16,18},{18,... | collective-permute-start | bytes 1671176 | tf_op jit(solution)/shard_map/ppermute | solution.py:596
  196.1 19.5 %collective-permute-start.23 = (f32[1088,128]{1,0:T(8,128)}, f32[1088,128]{1,0:T(8,128)}, u32[]{:S(2)}, u32[]{:S(2)}) collective-permute-start(f32[1088,128]{1,0:T(8,128)} %slice_bitcast_fusion.1), channel_id=1, source_target_pairs={{0,4},{2,6},{4,0},{6,2},{8,12},{10,14},{12,8},{14,10},{16,20},{18,... | collective-permute-start | bytes 1671176 | tf_op jit(solution)/shard_map/ppermute | solution.py:596
  198.1 46.4 %all-to-all-start.3 = ((f32[16,2,32,128]{3,1,2,0:T(2,128)}), f32[16,2,32,128]{3,1,2,0:T(2,128)S(1)}, u32[]{:S(2)}, u32[]{:S(2)}) async-start(f32[16,2,32,128]{3,1,2,0:T(2,128)} %copy.59), calls=%async_computation.3 | async-start | bytes 1048576 | tf_op jit(solution)/shard_map/all_to_all | solution.py:754
  218.8 16.7 %collective-permute-start.26 = (f32[544,128]{1,0:T(8,128)S(1)}, f32[544,128]{1,0:T(8,128)S(1)}, u32[]{:S(2)}, u32[]{:S(2)}) collective-permute-start(f32[544,128]{1,0:T(8,128)S(1)} %pad_maximum_fusion.4), channel_id=1, source_target_pairs={{0,8},{2,10},{4,12},{6,14},{8,0},{10,2},{12,4},{14,6},{16,24},{18,... | collective-permute-start | bytes 835592 | tf_op jit(solution)/shard_map/ppermute | solution.py:596
  221.3 23.1 %collective-permute-start.27 = (f32[544,128]{1,0:T(8,128)S(1)}, f32[544,128]{1,0:T(8,128)S(1)}, u32[]{:S(2)}, u32[]{:S(2)}) collective-permute-start(f32[544,128]{1,0:T(8,128)S(1)} %pad_maximum_fusion.5), channel_id=1, source_target_pairs={{0,16},{2,18},{4,20},{6,22},{8,24},{10,26},{12,28},{14,30},{16,0},... | collective-permute-start | bytes 835592 | tf_op jit(solution)/shard_map/ppermute | solution.py:596
  225.1 19.3 %collective-permute-start.28 = (f32[544,128]{1,0:T(8,128)S(1)}, f32[544,128]{1,0:T(8,128)S(1)}, u32[]{:S(2)}, u32[]{:S(2)}) collective-permute-start(f32[544,128]{1,0:T(8,128)S(1)} %pad_maximum_fusion.6), channel_id=1, source_target_pairs={{0,24},{2,26},{4,28},{6,30},{8,16},{10,18},{12,20},{14,22},{16,8},... | collective-permute-start | bytes 835592 | tf_op jit(solution)/shard_map/ppermute | solution.py:596
  244.6 17.3 %collective-permute-start.33 = (f32[260,128]{1,0:T(8,128)S(1)}, f32[260,128]{1,0:T(8,128)S(1)}, u32[]{:S(2)}, u32[]{:S(2)}) collective-permute-start(f32[260,128]{1,0:T(8,128)S(1)} %pad_maximum_fusion.9), channel_id=1, source_target_pairs={{4,0},{6,2},{5,1},{7,3}} | collective-permute-start | bytes 399368 | tf_op jit(solution)/shard_map/ppermute | solution.py:724
  (50 other events, 526.2 us)

commit v7 on v6

--- a/solution.py
+++ b/solution.py
@@ -394,9 +394,12 @@
     return jnp.sum(v, axis=0, keepdims=True)
 
 
-def mlp_body(share, devices, nseq, streams, place_ref, ids, *refs):
+def mlp_body(share, devices, nseq, streams, plan, place_ref, ids, slots, *refs):
     boxes = refs[:len(streams)]
-    resp_ref, x_ref, cot_ref, out_ref, dmid_ref, dresp_ref, small_ref, lead_ref, hidden_ref, active_ref, normed_ref, back_ref, dopen_ref, dlift_ref, flat, side, gate, expand, reduce, acc, dnorm, sems = refs[len(streams):]
+    resp_ref, x_ref, cot_ref, out_ref, dmid_ref, dresp_ref, lead_ref = refs[len(streams):len(streams) + 7]
+    ways = 2 if len(plan) > 1 else 1
+    outs = refs[len(streams) + 7:len(streams) + 7 + ways * len(plan)]
+    small_ref, hidden_ref, active_ref, normed_ref, back_ref, dopen_ref, dlift_ref, flat, side, gate, expand, reduce, acc, dnorm, sems, out_sems = refs[len(streams) + 7 + len(outs):]
     base, box, _ = lay(share, devices)
     nch = D // nseq
     group = x_ref.shape[0]
@@ -501,30 +504,72 @@
         for d in range(nseq):
             dresp_ref[pl.ds((d * parts + k) * nch, nch), :] = back_turned[d * nch:(d + 1) * nch]
 
-
-def mlp_kernel(place, streams, ids, boxes, response, rows, cotangent, share, devices, nseq):
+    flat[:MODE_TILES * 8, :] = jnp.zeros((MODE_TILES * 8, CH), f32)
+    for k, tile in enumerate(SMALL_AT):
+        flat[tile * 8:(tile + 1) * 8, :] = small_ref[k * 8:(k + 1) * 8, :]
+    flat[(SMALL_AT[-1] + 1) * 8:, :] = jnp.zeros((flat.shape[0] - (SMALL_AT[-1] + 1) * 8, CH), f32)
+    sent = 0
+    for first, left, right, per, until in (
+        (GATE_AT, hidden_ref, dopen_ref, G // CH, EXPAND_AT),
+        (EXPAND_AT, normed_ref, dlift_ref, FF // CH, REDUCE_AT),
+        (REDUCE_AT, active_ref, back_ref, D // CH, flat.shape[0]),
+    ):
+        flip = left[...].T
+        for k in range(left.shape[1] // CH):
+            v = product(flip[k * CH:(k + 1) * CH], right[...], 1, 0)
+            for c in range(per):
+                flat[pl.ds(first * 8 + k * CH * per + c, CH, stride=per), :] = v[:, c * CH:(c + 1) * CH]
+        ready = sum((j * share) // TILE + box <= until for j in range(devices))
+        for k, (low, high) in enumerate(plan):
+            rows = (high - low) * 8
+
+            def send(j, _, k=k, low=low, rows=rows):
+                slot = slots[k * devices + j]
+                block = flat.at[pl.ds(pl.multiple_of((start_of(j) + low) * 8, 8), rows), :]
+                for o in range(ways):
+                    at = slot - o * (devices // ways)
+
+                    @pl.when((at >= 0) & (at < devices // ways))
+                    def _():
+                        target = outs[k * ways + o].at[pl.ds(pl.multiple_of(at * rows, 8), rows), :]
+                        pltpu.make_async_copy(block, target, out_sems.at[k * ways + o]).start()
+
+                return 0
+
+            lax.fori_loop(sent, ready, send, 0)
+        sent = ready
+    for k, out in enumerate(outs):
+        pltpu.make_async_copy(out, out, out_sems.at[k]).wait()
+
+
+def mlp_kernel(place, streams, ids, boxes, plan, slots, response, rows, cotangent, share, devices, nseq):
     base, box, tiles = lay(share, devices)
     group = rows.shape[0]
     vm = pl.BlockSpec(memory_space=pltpu.VMEM)
+    hbm = pl.BlockSpec(memory_space=pl.ANY)
+    smem = pl.BlockSpec(memory_space=pltpu.SMEM)
     shape = lambda r, c, t: jax.ShapeDtypeStruct((r, c), t)
+    count = 2 if len(plan) > 1 else 1
+    packed = [shape(devices // count * (high - low) * 8, CH, f32) for low, high in plan for _ in range(count)]
     return pl.pallas_call(
-        partial(mlp_body, share, devices, nseq, streams),
+        partial(mlp_body, share, devices, nseq, streams, plan),
         out_shape=(
             shape(group, D, bf16),
             shape(group, D, f32),
             jax.ShapeDtypeStruct(response.shape, f32),
-            shape(len(SMALL_AT) * 8, CH, f32),
             shape(MODE_TILES * 8, CH, f32),
-            shape(group, D, bf16),
-            shape(group, FF, bf16),
-            shape(group, D, bf16),
-            shape(group, D, bf16),
-            shape(group, G, bf16),
-            shape(group, FF, bf16),
+            *packed,
         ),
-        in_specs=[pl.BlockSpec(memory_space=pltpu.SMEM)] * 2 + [pl.BlockSpec(memory_space=pl.ANY)] * len(boxes) + [vm] * 3,
-        out_specs=(vm,) * 11,
+        in_specs=[smem] * 3 + [hbm] * len(boxes) + [vm] * 3,
+        out_specs=(vm,) * 4 + (hbm,) * len(packed),
         scratch_shapes=[
+            pltpu.VMEM((len(SMALL_AT) * 8, CH), f32),
+            pltpu.VMEM((group, D), bf16),
+            pltpu.VMEM((group, FF), bf16),
+            pltpu.VMEM((group, D), bf16),
+            pltpu.VMEM((group, D), bf16),
+            pltpu.VMEM((group, G), bf16),
+            pltpu.VMEM((group, FF), bf16),
             pltpu.VMEM((tiles * 8, CH), f32),
             pltpu.VMEM((3, devices * 8 + 8, CH), f32),
             pltpu.VMEM((D, G), bf16),
@@ -533,59 +578,11 @@
             pltpu.VMEM((group, D), f32),
             pltpu.VMEM((group, D), f32),
             pltpu.SemaphoreType.DMA((2,)),
+            pltpu.SemaphoreType.DMA((len(packed),)),
         ],
-        cost_estimate=pl.CostEstimate(flops=int(1.0e10), bytes_accessed=20 * 2**20, transcendentals=0),
+        cost_estimate=pl.CostEstimate(flops=int(2.0e10), bytes_accessed=30 * 2**20, transcendentals=0),
         name="feed_forward",
-    )(place, ids, *boxes, response, rows, cotangent)
-
-
-def pack_body(streams, tiles, has_lead, *refs):
-    n = len(streams)
-    dest, hidden, active, normed, back, dopen, dlift, small_ref = refs[:8]
-    outs = refs[8 + has_lead:8 + has_lead + n]
-    flat, sem = refs[8 + has_lead + n:]
-    if has_lead:
-        flat[:MODE_TILES * 8, :] = refs[8][...]
-    else:
-        flat[:MODE_TILES * 8, :] = jnp.zeros((MODE_TILES * 8, CH), f32)
-    for k, tile in enumerate(SMALL_AT):
-        flat[tile * 8:(tile + 1) * 8, :] = small_ref[k * 8:(k + 1) * 8, :]
-    flat[(SMALL_AT[-1] + 1) * 8:, :] = jnp.zeros(((tiles - SMALL_AT[-1] - 1) * 8, CH), f32)
-    for first, left, right, per in ((GATE_AT, hidden, dopen, G // CH), (EXPAND_AT, normed, dlift, FF // CH), (REDUCE_AT, active, back, D // CH)):
-        wide = 128
-        flip = left[...].T
-
-        for k in range(left.shape[1] // wide):
-            v = product(flip[k * wide:(k + 1) * wide], right[...], 1, 0)
-            for c in range(per):
-                flat[pl.ds(first * 8 + k * wide * per + c, wide, stride=per), :] = v[:, c * CH:(c + 1) * CH]
-    for k, (first, last, order) in enumerate(streams):
-        rows = (last - first) * 8
-
-        def send(b, _, k=k, first=first, rows=rows, order=order):
-            at = pl.multiple_of(dest[order + b], 8)
-            pltpu.make_async_copy(flat.at[pl.ds(at + first * 8, rows), :], outs[k].at[pl.ds(pl.multiple_of(b * rows, 8), rows), :], sem.at[k]).start()
-            return 0
-
-        lax.fori_loop(0, outs[k].shape[0] // rows, send, 0)
-    for k, out in enumerate(outs):
-        pltpu.make_async_copy(out, out, sem.at[k]).wait()
-
-
-def pack_kernel(streams, dest, values, small, lead, share, devices):
-    _, _, tiles = lay(share, devices)
-    hbm = pl.BlockSpec(memory_space=pl.ANY)
-    vm = pl.BlockSpec(memory_space=pltpu.VMEM)
-    has = int(lead is not None)
-    return pl.pallas_call(
-        partial(pack_body, tuple(s[:3] for s in streams), tiles, has),
-        out_shape=tuple(jax.ShapeDtypeStruct((blocks * (last - first) * 8, CH), f32) for first, last, _, blocks in streams),
-        in_specs=[pl.BlockSpec(memory_space=pltpu.SMEM)] + [vm] * (7 + has),
-        out_specs=(hbm,) * len(streams),
-        scratch_shapes=[pltpu.VMEM((tiles * 8, CH), f32), pltpu.SemaphoreType.DMA((len(streams),))],
-        cost_estimate=pl.CostEstimate(flops=int(0.8e10), bytes_accessed=16 * 2**20, transcendentals=0),
-        name="weight_gradients",
-    )(dest, *values, small, *((lead,) if has else ()))
+    )(place, ids, slots, *boxes, response, rows, cotangent)
 
 
 AXES = ("seq", "batch")
@@ -648,17 +645,17 @@
 def scatter_plan(share, devices):
     _, tiles, _ = lay(share, devices)
     if not direct():
-        return ((0, tiles, 0, devices),), jnp.arange(devices, dtype=jnp.int32) * share // TILE * 8
+        return ((0, tiles),), jnp.arange(devices, dtype=jnp.int32)
     one, two = cuts_of(tiles)
-    streams, ids = [], []
-    for first, last, bits in ((0, one, (1, 2, 8, 4)), (one, two, (2, 1, 8, 4)), (two, tiles, (8, 4, 2, 1))):
-        steps = [0]
-        for bit in bits[::-1]:
-            steps = steps + [bit + step for step in steps]
-        for other in range(2):
-            streams.append((first, last, 16 * len(ids), 16))
-            ids.append(places_of(steps, other))
-    return tuple(streams), (jnp.concatenate(ids) * share // TILE * 8).astype(jnp.int32)
+    index = np.arange(devices, dtype=np.int32)
+    step, other = index // 2 ^ lax.axis_index("seq"), index % 2 ^ lax.axis_index("batch")
+    slots = []
+    for bits in ((1, 2, 8, 4), (2, 1, 8, 4), (8, 4, 2, 1)):
+        at = 16 * other
+        for k, bit in enumerate(bits[::-1]):
+            at = at + jnp.where(step & bit != 0, 1 << k, 0)
+        slots.append(at)
+    return ((0, one), (one, two), (two, tiles)), jnp.concatenate(slots).astype(jnp.int32)
 
 
 def pieces(v, count):
@@ -735,11 +732,8 @@
 def total_of(v):
     if not direct():
         return lax.psum(v, AXES)
-    v = jnp.broadcast_to(v, (8, CH))
-    v = v + swap_cores(v)
-    v = v + (hop(v, 1) + hop(v, 2) + hop(v, 3))
-    v = v + (hop(v, 4) + hop(v, 8) + hop(v, 12))
-    return v[0, 0]
+    terms = lax.all_to_all(jnp.broadcast_to(v, (32, 8, CH)), AXES, 0, 0)
+    return jnp.sum(terms[:, 0, 0])
 
 
 def to_channels(rows):
@@ -773,8 +767,10 @@
     first_hat, first_scale = normalize(rows)
     hats = to_channels(first_hat)
 
+    plan, slots = scatter_plan(share, devices)
+
     def feed_forward(response):
-        return mlp_kernel(place, streams, ids, boxes, response, inputs[0], cotangent[0], share, devices, seq)
+        return mlp_kernel(place, streams, ids, boxes, plan, slots, response, inputs[0], cotangent[0], share, devices, seq)
 
     if direct():
         few, many = read_modes(scatter_modes(master))
@@ -793,11 +789,10 @@
         far = [hop(plane[0], 2), hop(plane[1], 1)]
         response, far = lax.optimization_barrier((response, far))
         streams, ids, boxes = gather_cores(plane, far, box.shape[0] // 8)
-    output, d_mid, d_response, small, lead, *values = feed_forward(response)
+    output, d_mid, d_response, lead, *packed = feed_forward(response)
     d_outs = lax.all_to_all(d_response.reshape(seq, -1, nch, CH), "seq", 0, 0).reshape(-1, CH)
-    plan, places = scatter_plan(share, devices)
     if direct():
-        packed = join_cores(pack_kernel(plan, places, values, small, None, share, devices))
+        packed = join_cores(packed)
         d_outs, packed = lax.optimization_barrier((d_outs, packed))
     d_signals, sums = ssm_backward(ends, prm, hats, d_outs, prior, tables, nck, nch)
     if direct():
@@ -808,32 +803,30 @@
     d_modes = modes_pull(mode_grads(sums, *modes))
     few = jnp.stack([lane_sums[1], lane_sums[2], d_modes[0], lane_sums[0]])
     many = jnp.stack(d_modes[1:])
-    if not direct():
-
-        def spread(v):
-            whole = jnp.zeros((v.shape[0], D) + v.shape[2:], f32)
-            return lax.dynamic_update_slice_in_dim(whole, v, lax.axis_index("seq") * nch, 1)
-
-        lead = jnp.concatenate([spread(few).reshape(-1), spread(many).reshape(-1)]).reshape(-1, CH)
-        packed = pack_kernel(plan, places, values, small, lead, share, devices)
     me = device_index()
     if direct():
         own = jnp.concatenate([few.reshape(1, CH), many.reshape(64, CH)])
         own, packed = lax.optimization_barrier((own + swap_cores(own), join_second(packed)))
-        box, block, d_signal = lax.optimization_barrier((join_last(packed), gather_modes(own, (8, 4)), d_signal))
+        box, block, d_signal = lax.optimization_barrier((join_last(packed), gather_modes(own, (8, 4, 2)), d_signal))
     else:
         box = lax.psum_scatter(packed[0].reshape(devices, -1, CH), AXES, scatter_dimension=0)
     d_rows = d_mid + norm_back(d_signal * norm_gain, first_hat, first_scale)
     shard = lax.dynamic_slice(box.reshape(-1), (me * share % TILE,), (share,))
+    mark = me * share + jnp.arange(share, dtype=jnp.int32) < MODE_TILES * TILE
+    squares = jnp.sum(jnp.where(mark, 0.0, shard * shard))
     if direct():
-        lead = mode_vector(gather_modes(block, (2, 1)))
-        lead = jnp.pad(lead, (0, 2 * share - lead.shape[0]))
-        mark = me * share + jnp.arange(share, dtype=jnp.int32) < MODE_TILES * TILE
-        squares = jnp.sum(jnp.where(mark, 0.0, shard * shard))
         squares = squares + 0.5 * jnp.sum(own * own)
-        shard = jnp.where(mark, lax.dynamic_slice(lead, (jnp.minimum(me, 1) * share,), (share,)), shard)
+        lead = mode_vector(gather_modes(block, (1,)))
     else:
-        squares = jnp.sum(shard * shard)
+
+        def spread(v):
+            whole = jnp.zeros((v.shape[0], D) + v.shape[2:], f32)
+            return lax.dynamic_update_slice_in_dim(whole, v, lax.axis_index("seq") * nch, 1)
+
+        lead = lax.psum(jnp.concatenate([spread(few).reshape(-1), spread(many).reshape(-1)]), AXES)
+        squares = squares + jnp.sum(lead * lead) / devices
+    lead = lax.dynamic_slice(jnp.pad(lead, (0, share)), (jnp.minimum(me * share, MODE_TILES * TILE),), (share,))
+    shard = jnp.where(mark, lead, shard)
     total = total_of(squares)
     grad_norm = jnp.sqrt(total)
     factor = jnp.minimum(1.0, 1.0 / (grad_norm + 1e-06))

time: 277 us -> 266 us (0.960)
  starting transfers between devices: 78.7 us -> 74.8 us
  waiting for transfers between devices: 76.9 us -> 73 us
  Pallas kernels: 60.9 us -> 57.4 us
    ppermute x24 -> x18, waiting for transfers between devices: 47.7 us -> 36.1 us  [hop(): return lax.ppermute(v, 'seq', [(i, i ^ step) for i in range(16)])]
    ppermute x24 -> x18, starting transfers between devices: 31.5 us -> 21.9 us  [hop(): return lax.ppermute(v, 'seq', [(i, i ^ step) for i in range(16)])]
    all_to_all x0 -> x1, waiting for transfers between devices: none -> 6.69 us  [total_of(): terms = lax.all_to_all(jnp.broadcast_to(v, (32, 8, CH)), AXES, 0, 0)]
    all_to_all x0 -> x1, starting transfers between devices: none -> 5.75 us  [total_of(): terms = lax.all_to_all(jnp.broadcast_to(v, (32, 8, CH)), AXES, 0, 0)]
    pallas_call x2 -> x1, Pallas kernels: 23.8 us -> 20.2 us  [mlp_kernel(): pl.pallas_call(partial(mlp_body, share, devices, nseq, streams, plan), ou...]
  transfers between devices with their start and end apart: 46 -> 40, of which waited for: 21 -> 17; matrix products, arithmetic and copies ran while one was open for 17% -> 18% of each run, Pallas kernels for 13% -> 14%
where the time goes in v7:
time: 266 us; the launch traced here: 264 us
  starting transfers between devices  74.8 us (28%)
  waiting for transfers between devices  73 us (27%)
  Pallas kernels  57.4 us (22%)
  other arithmetic  30.8 us (12%)
  local copies, waits for them, and re-layouts  23.5 us (9%)
  between operations  4.78 us (2%)
    ppermute x18, waiting for transfers between devices, hop(): return lax.ppermute(v, 'seq', [(i, i ^ step) for i in range(16)])  36.1 us
    pallas_call x1, Pallas kernels, ssm_backward(): pl.pallas_call(partial(bwd_body, nck, nch, x.shape[0] // nck), out_shape=...  22.3 us
    ppermute x18, starting transfers between devices, hop(): return lax.ppermute(v, 'seq', [(i, i ^ step) for i in range(16)])  21.9 us
    pallas_call x1, Pallas kernels, mlp_kernel(): pl.pallas_call(partial(mlp_body, share, devices, nseq, streams, plan), ou...  20.2 us
    ppermute x4, starting transfers between devices, scatter_modes(): come = lax.ppermute(blocks[1], 'seq', [(i, i + step) for i in range(step)])  15.3 us
    pallas_call x1, Pallas kernels, ssm_forward(): pl.pallas_call(partial(fwd_body, nck, nch, x.shape[0] // nck), out_shape=...  14.9 us
    all_to_all x1, waiting for transfers between devices, per_device(): lax.all_to_all(outs.reshape(seq, -1, nch, CH), 'seq', 0, 0).reshape(-1, CH)  11.8 us
    add x3, other arithmetic, join_cores(): sums.append([own[k] + far[k] for k in range(2)])  8.59 us
  transfers between devices with their start and end apart: 40, of which 17 were waited for; matrix products, arithmetic and copies ran while one was open for 18% of the time, Pallas kernels for 14%

profile of v7, /device:TPU:0, one launch (start us, length us, event | category | flops | bytes accessed | tf_op | source)
XLA Modules:
  0.0 264.4 jit_solution(16124388360394968987)
XLA Ops:
  1.2 3.7 %dynamic_update_slice.3 = f32[88064]{0:T(1024)S(1)} dynamic-update-slice(f32[88064]{0:T(1024)S(1)} %broadcast_in_dim.60, f32[86224]{0:T(1024)} %param.20, s32[]{:T(128)S(6)} %select_n.112) | dynamic-update-slice | bytes 689796 | tf_op jit(solution)/shard_map/dynamic_update_slice | solution.py:620
  12.9 7.2 %all-to-all-start = ((f32[16,2,32,128]{3,1,2,0:T(2,128)}), f32[16,2,32,128]{3,1,2,0:T(2,128)S(1)}, u32[]{:S(2)}, u32[]{:S(2)}) async-start(f32[16,2,32,128]{3,1,2,0:T(2,128)} %multiply_bitcast_fusion), calls=%async_computation | async-start | bytes 1048576 | tf_op jit(solution)/shard_map/all_to_all | solution.py:743
  23.2 3.8 %collective-permute-start.8 = (f32[2,2,2,65,128]{4,3,0,1,2:T(8,128)S(1)}, f32[2,2,2,65,128]{4,3,0,1,2:T(8,128)S(1)}, u32[]{:S(2)}, u32[]{:S(2)}) collective-permute-start(f32[2,2,2,65,128]{4,3,0,1,2:T(8,128)S(1)} %slice_bitcast_fusion.2), channel_id=1, source_target_pairs={{0,2},{1,3}} | collective-permute-start | bytes 798728 | tf_op jit(solution)/shard_map/ppermute | solution.py:706
  27.8 9.7 %collective-permute-done.1 = f32[688,128]{1,0:T(8,128)S(1)} collective-permute-done((f32[688,128]{1,0:T(8,128)S(1)}, f32[688,128]{1,0:T(8,128)S(1)}, u32[]{:S(2)}, u32[]{:S(2)}) %collective-permute-start.1) | collective-permute-done | bytes 352288 | tf_op jit(solution)/shard_map/ppermute | solution.py:593
  38.4 2.7 %collective-permute-start.9 = (f32[2,2,65,128]{3,2,0,1:T(8,128)S(1)}, f32[2,2,65,128]{3,2,0,1:T(8,128)S(1)}, u32[]{:S(2)}, u32[]{:S(2)}) collective-permute-start(f32[2,2,65,128]{3,2,0,1:T(8,128)S(1)} %slice_bitcast_fusion.7), channel_id=1, source_target_pairs={{0,4},{2,6},{1,5},{3,7}} | collective-permute-start | bytes 399368 | tf_op jit(solution)/shard_map/ppermute | solution.py:706
  43.8 7.4 %collective-permute-start.10 = (f32[2,65,128]{2,1,0:T(8,128)S(1)}, f32[2,65,128]{2,1,0:T(8,128)S(1)}, u32[]{:S(2)}, u32[]{:S(2)}) collective-permute-start(f32[2,65,128]{2,1,0:T(8,128)S(1)} %slice_bitcast_fusion.18), channel_id=1, source_target_pairs={{0,8},{2,10},{4,12},{6,14},{1,9},{3,11},{5,13},{7,15}} | collective-permute-start | bytes 199688 | tf_op jit(solution)/shard_map/ppermute | solution.py:706
  60.9 6.8 %collective-permute-done.5 = f32[1376,128]{1,0:T(8,128)S(1)} collective-permute-done((f32[1376,128]{1,0:T(8,128)S(1)}, f32[1376,128]{1,0:T(8,128)S(1)}, u32[]{:S(2)}, u32[]{:S(2)}) %collective-permute-start.5) | collective-permute-done | bytes 704544 | tf_op jit(solution)/shard_map/ppermute | solution.py:593
  74.4 14.9 %state_forward.1 = (f32[1024,128]{1,0:T(8,128)}, f32[1024,128]{1,0:T(8,128)}, bf16[32,2,128,128]{3,2,1,0:T(8,128)(2,1)}, bf16[32,2,128,128]{3,2,1,0:T(8,128)(2,1...) custom-call(s32[4]{0:T(128)} %bitcast.350, f32[32,24,128]{2,1,0:T(8,128)} %concatenate.103.prm_ref, ...), custom_call_target="tpu_custom_call" | custom-call | flops 20000000000 | bytes 3145728 | tf_op jit(solution)/shard_map/state_forward/pallas_call | solution.py:160
  89.3 6.6 %all-to-all-start.1 = ((f32[16,2,32,128]{3,2,1,0:T(8,128)}), f32[16,2,32,128]{3,2,1,0:T(8,128)S(1)}, u32[]{:S(2)}, u32[]{:S(2)}) async-start(f32[16,2,32,128]{3,2,1,0:T(8,128)} %bitcast.340), calls=%async_computation.1 | async-start | bytes 1048576 | tf_op jit(solution)/shard_map/all_to_all | solution.py:787
  96.5 11.8 %all-to-all-done.1 = f32[16,2,32,128]{3,2,1,0:T(8,128)S(1)} async-done(((f32[16,2,32,128]{3,2,1,0:T(8,128)}), f32[16,2,32,128]{3,2,1,0:T(8,128)S(1)}, u32[]{:S(2)}, u32[]{:S(2)}) %all-to-all-start.1) | async-done | bytes 524320 | tf_op jit(solution)/shard_map/all_to_all | solution.py:787
  113.9 20.2 %feed_forward.1 = (bf16[256,512]{1,0:T(8,128)(2,1)}, f32[256,512]{1,0:T(8,128)}, f32[1024,128]{1,0:T(8,128)}, f32[1040,128]{1,0:T(8,128)}, f32[4352,128]{1,0:T(8...) custom-call(s32[5]{0:T(128)} %pad_add_fusion.place_ref, ...), custom_call_target="tpu_custom_call" | custom-call | flops 20000000000 | bytes 31457280 | tf_op jit(solution)/shard_map/feed_forward/pallas_call | solution.py:554
  135.1 4.7 %all-to-all-start.2 = ((f32[16,2,32,128]{3,2,1,0:T(8,128)}), f32[16,2,32,128]{3,2,1,0:T(8,128)}, u32[]{:S(2)}, u32[]{:S(2)}) async-start(f32[16,2,32,128]{3,2,1,0:T(8,128)} %bitcast.339), calls=%async_computation.2 | async-start | bytes 1048576 | tf_op jit(solution)/shard_map/all_to_all | solution.py:793
  144.6 3.0 %slice_add_fusion = (f32[2176,128]{1,0:T(8,128)}, f32[2176,128]{1,0:T(8,128)S(1)}) fusion(f32[4352,128]{1,0:T(8,128)} %copy-done.8, f32[4352,128]{1,0:T(8,128)S(1)} %copy-done.7), kind=kLoop, calls=%fused_computation | loop fusion | flops 557056 | bytes 6684672 | tf_op jit(solution)/shard_map/add | solution.py:673
  147.6 2.9 %slice_add_fusion.2 = (f32[2176,128]{1,0:T(8,128)}, f32[2176,128]{1,0:T(8,128)S(1)}) fusion(f32[4352,128]{1,0:T(8,128)} %collective-permute-done.16, f32[4352,128]{1,0:T(8,128)S(1)} %copy-done.6), kind=kLoop, calls=%fused_computation.2 | loop fusion | flops 557056 | bytes 6684672 | tf_op jit(solution)/shard_map/add | solution.py:673
  150.5 4.8 %all-to-all-done.2 = f32[16,2,32,128]{3,2,1,0:T(8,128)} async-done(((f32[16,2,32,128]{3,2,1,0:T(8,128)}), f32[16,2,32,128]{3,2,1,0:T(8,128)}, u32[]{:S(2)}, u32[]{:S(2)}) %all-to-all-start.2) | async-done | bytes 524320 | tf_op jit(solution)/shard_map/all_to_all | solution.py:793
  157.7 22.3 %state_backward.1 = (f32[1024,128]{1,0:T(8,128)}, f32[16,32,128]{2,1,0:T(8,128)}) custom-call(s32[4]{0:T(128)} %bitcast.351, f32[32,24,128]{2,1,0:T(8,128)} %concatenate.103.prm_ref, f32[1024,128]{1,0:T(8,128)} %bitcast.336, f32[1024,128]{1,0:T(8,128)} %bitcast.44.g_ref, f32[1024,128]{1,0:T(8,128)} %get-tuple-element.61.prior_ref, ...), custom_call_target="tpu_custom_call" | custom-call | flops 35000000512 | bytes 4194304 | tf_op jit(solution)/shard_map/state_backward/pallas_call | solution.py:264
  194.6 5.6 %all-to-all-start.3 = ((f32[16,2,32,128]{3,1,2,0:T(2,128)}), f32[16,2,32,128]{3,1,2,0:T(2,128)S(1)}, u32[]{:S(2)}, u32[]{:S(2)}) async-start(f32[16,2,32,128]{3,1,2,0:T(2,128)} %copy.89), calls=%async_computation.3 | async-start | bytes 1048576 | tf_op jit(solution)/shard_map/all_to_all | solution.py:748
  203.7 8.4 %collective-permute-done.23 = f32[1088,128]{1,0:T(8,128)} collective-permute-done((f32[1088,128]{1,0:T(8,128)}, f32[1088,128]{1,0:T(8,128)}, u32[]{:S(2)}, u32[]{:S(2)}) %collective-permute-start.23) | collective-permute-done | bytes 557088 | tf_op jit(solution)/shard_map/ppermute | solution.py:593
  217.7 3.6 %collective-permute-start.27 = (f32[544,128]{1,0:T(8,128)S(1)}, f32[544,128]{1,0:T(8,128)S(1)}, u32[]{:S(2)}, u32[]{:S(2)}) collective-permute-start(f32[544,128]{1,0:T(8,128)S(1)} %pad_maximum_fusion.6), channel_id=1, source_target_pairs={{0,16},{2,18},{4,20},{6,22},{8,24},{10,26},{12,28},{14,30},{16,0},... | collective-permute-start | bytes 835592 | tf_op jit(solution)/shard_map/ppermute | solution.py:593
  223.6 3.0 %collective-permute-done.29 = f32[288,128]{1,0:T(8,128)S(1)} collective-permute-done((f32[288,128]{1,0:T(8,128)S(1)}, f32[288,128]{1,0:T(8,128)S(1)}, u32[]{:S(2)}, u32[]{:S(2)}) %collective-permute-start.29) | collective-permute-done | bytes 147488 | tf_op jit(solution)/shard_map/ppermute | solution.py:593
  232.2 5.6 %collective-permute-done.33 = f32[260,128]{1,0:T(8,128)S(1)} collective-permute-done((f32[260,128]{1,0:T(8,128)S(1)}, f32[260,128]{1,0:T(8,128)S(1)}, u32[]{:S(2)}, u32[]{:S(2)}) %collective-permute-start.33) | collective-permute-done | bytes 133152 | tf_op jit(solution)/shard_map/ppermute | solution.py:721
  237.8 3.1 %collective-permute-done.27 = f32[544,128]{1,0:T(8,128)S(1)} collective-permute-done((f32[544,128]{1,0:T(8,128)S(1)}, f32[544,128]{1,0:T(8,128)S(1)}, u32[]{:S(2)}, u32[]{:S(2)}) %collective-permute-start.27) | collective-permute-done | bytes 278560 | tf_op jit(solution)/shard_map/ppermute | solution.py:593
  244.6 5.8 %all-to-all-start.4 = ((f32[32,8,128]{2,1,0:T(8,128)}), f32[32,8,128]{2,1,0:T(8,128)S(1)}, u32[]{:S(2)}, u32[]{:S(2)}) async-start(f32[32,8,128]{2,1,0:T(8,128)} %broadcast_in_dim.64), calls=%async_computation.4 | async-start | bytes 262144 | tf_op jit(solution)/shard_map/all_to_all | solution.py:735
  251.9 6.7 %all-to-all-done.4 = f32[32,8,128]{2,1,0:T(8,128)S(1)} async-done(((f32[32,8,128]{2,1,0:T(8,128)}), f32[32,8,128]{2,1,0:T(8,128)S(1)}, u32[]{:S(2)}, u32[]{:S(2)}) %all-to-all-start.4) | async-done | bytes 131104 | tf_op jit(solution)/shard_map/all_to_all | solution.py:735
  (247 shorter events, 85.3 us)
Async XLA Ops:
  0.6 21.0 %collective-permute-start.7 = (f32[86224]{0:T(1024)}, f32[86224]{0:T(1024)}, u32[]{:S(2)}, u32[]{:S(2)}) collective-permute-start(f32[86224]{0:T(1024)} %param.20), channel_id=1, source_target_pairs={{0,1},{1,0},{2,3},{3,2},{4,5},{5,4},{6,7},{7,6},{8,9},{9,8},{10,11... | collective-permute-start | bytes 1034696 | tf_op jit(solution)/shard_map/ppermute | solution.py:597
  4.9 22.1 %collective-permute-start = (f32[688,128]{1,0:T(8,128)S(1)}, f32[688,128]{1,0:T(8,128)S(1)}, u32[]{:S(2)}, u32[]{:S(2)}) collective-permute-start(f32[688,128]{1,0:T(8,128)S(1)} %bitcast.314), channel_id=1, source_target_pairs={{0,8},{2,10},{4,12},{6,14},{8,0},{10,2},{12,4},{14,6},{16,24},{18,... | collective-permute-start | bytes 1056776 | tf_op jit(solution)/shard_map/ppermute | solution.py:593
  7.6 30.0 %collective-permute-start.1 = (f32[688,128]{1,0:T(8,128)S(1)}, f32[688,128]{1,0:T(8,128)S(1)}, u32[]{:S(2)}, u32[]{:S(2)}) collective-permute-start(f32[688,128]{1,0:T(8,128)S(1)} %bitcast.315), channel_id=1, source_target_pairs={{0,16},{2,18},{4,20},{6,22},{8,24},{10,26},{12,28},{14,30},{16,0},... | collective-permute-start | bytes 1056776 | tf_op jit(solution)/shard_map/ppermute | solution.py:593
  10.2 31.0 %collective-permute-start.2 = (f32[688,128]{1,0:T(8,128)S(1)}, f32[688,128]{1,0:T(8,128)S(1)}, u32[]{:S(2)}, u32[]{:S(2)}) collective-permute-start(f32[688,128]{1,0:T(8,128)S(1)} %bitcast.316), channel_id=1, source_target_pairs={{0,24},{2,26},{4,28},{6,30},{8,16},{10,18},{12,20},{14,22},{16,8},... | collective-permute-start | bytes 1056776 | tf_op jit(solution)/shard_map/ppermute | solution.py:593
  12.9 47.1 %all-to-all-start = ((f32[16,2,32,128]{3,1,2,0:T(2,128)}), f32[16,2,32,128]{3,1,2,0:T(2,128)S(1)}, u32[]{:S(2)}, u32[]{:S(2)}) async-start(f32[16,2,32,128]{3,1,2,0:T(2,128)} %multiply_bitcast_fusion), calls=%async_computation | async-start | bytes 1048576 | tf_op jit(solution)/shard_map/all_to_all | solution.py:743
  23.2 15.2 %collective-permute-start.8 = (f32[2,2,2,65,128]{4,3,0,1,2:T(8,128)S(1)}, f32[2,2,2,65,128]{4,3,0,1,2:T(8,128)S(1)}, u32[]{:S(2)}, u32[]{:S(2)}) collective-permute-start(f32[2,2,2,65,128]{4,3,0,1,2:T(8,128)S(1)} %slice_bitcast_fusion.2), channel_id=1, source_target_pairs={{0,2},{1,3}} | collective-permute-start | bytes 798728 | tf_op jit(solution)/shard_map/ppermute | solution.py:706
  51.3 16.4 %collective-permute-start.5 = (f32[1376,128]{1,0:T(8,128)S(1)}, f32[1376,128]{1,0:T(8,128)S(1)}, u32[]{:S(2)}, u32[]{:S(2)}) collective-permute-start(f32[1376,128]{1,0:T(8,128)S(1)} %pad_maximum_fusion.1), channel_id=1, source_target_pairs={{0,4},{2,6},{4,0},{6,2},{8,12},{10,14},{12,8},{14,10},{16,20},{18,... | collective-permute-start | bytes 2113544 | tf_op jit(solution)/shard_map/ppermute | solution.py:593
  54.7 16.9 %collective-permute-start.3 = (f32[1376,128]{1,0:T(8,128)S(1)}, f32[1376,128]{1,0:T(8,128)}, u32[]{:S(2)}, u32[]{:S(2)}) collective-permute-start(f32[1376,128]{1,0:T(8,128)S(1)} %pad_maximum_fusion), channel_id=1, source_target_pairs={{0,2},{2,0},{4,6},{6,4},{8,10},{10,8},{12,14},{14,12},{16,18},{18,... | collective-permute-start | bytes 2113544 | tf_op jit(solution)/shard_map/ppermute | solution.py:593
  68.7 39.6 %collective-permute-start.13 = (f32[2752,128]{1,0:T(8,128)}, f32[2752,128]{1,0:T(8,128)}, u32[]{:S(2)}, u32[]{:S(2)}) collective-permute-start(f32[2752,128]{1,0:T(8,128)} %constant_dynamic-update-slice_fusion.5.refs_2_), channel_id=1, source_target_pairs={{0,2},{2,0},{4,6},{6,4},{8,10},{10,8},{12,14},{14,12},{16,18},{18,... | collective-permute-start | bytes 4227080 | tf_op jit(solution)/shard_map/ppermute | solution.py:593
  73.6 34.7 %collective-permute-start.12 = (f32[2752,128]{1,0:T(8,128)}, f32[2752,128]{1,0:T(8,128)}, u32[]{:S(2)}, u32[]{:S(2)}) collective-permute-start(f32[2752,128]{1,0:T(8,128)} %constant_dynamic-update-slice_fusion.refs_0_), channel_id=1, source_target_pairs={{0,4},{2,6},{4,0},{6,2},{8,12},{10,14},{12,8},{14,10},{16,20},{18,... | collective-permute-start | bytes 4227080 | tf_op jit(solution)/shard_map/ppermute | solution.py:593
  89.3 19.0 %all-to-all-start.1 = ((f32[16,2,32,128]{3,2,1,0:T(8,128)}), f32[16,2,32,128]{3,2,1,0:T(8,128)S(1)}, u32[]{:S(2)}, u32[]{:S(2)}) async-start(f32[16,2,32,128]{3,2,1,0:T(8,128)} %bitcast.340), calls=%async_computation.1 | async-start | bytes 1048576 | tf_op jit(solution)/shard_map/all_to_all | solution.py:787
  95.9 14.9 %collective-permute-start.6 = (f32[2752,128]{1,0:T(8,128)S(1)}, f32[2752,128]{1,0:T(8,128)}, u32[]{:S(2)}, u32[]{:S(2)}) collective-permute-start(f32[2752,128]{1,0:T(8,128)S(1)} %copy-done.18), channel_id=1, source_target_pairs={{0,1},{1,0},{2,3},{3,2},{4,5},{5,4},{6,7},{7,6},{8,9},{9,8},{10,11... | collective-permute-start | bytes 4227080 | tf_op jit(solution)/shard_map/ppermute | solution.py:597
  96.0 14.8 %collective-permute-start.4 = (f32[2752,128]{1,0:T(8,128)}, f32[2752,128]{1,0:T(8,128)}, u32[]{:S(2)}, u32[]{:S(2)}) collective-permute-start(f32[2752,128]{1,0:T(8,128)} %constant_dynamic-update-slice_fusion.refs_0_), channel_id=1, source_target_pairs={{0,1},{1,0},{2,3},{3,2},{4,5},{5,4},{6,7},{7,6},{8,9},{9,8},{10,11... | collective-permute-start | bytes 4227080 | tf_op jit(solution)/shard_map/ppermute | solution.py:597
  135.1 20.2 %all-to-all-start.2 = ((f32[16,2,32,128]{3,2,1,0:T(8,128)}), f32[16,2,32,128]{3,2,1,0:T(8,128)}, u32[]{:S(2)}, u32[]{:S(2)}) async-start(f32[16,2,32,128]{3,2,1,0:T(8,128)} %bitcast.339), calls=%async_computation.2 | async-start | bytes 1048576 | tf_op jit(solution)/shard_map/all_to_all | solution.py:793
  155.4 26.7 %collective-permute-start.21 = (f32[1152,128]{1,0:T(8,128)}, f32[1152,128]{1,0:T(8,128)}, u32[]{:S(2)}, u32[]{:S(2)}) collective-permute-start(f32[1152,128]{1,0:T(8,128)} %get-tuple-element.73), channel_id=1, source_target_pairs={{0,16},{2,18},{4,20},{6,22},{8,24},{10,26},{12,28},{14,30},{16,0},... | collective-permute-start | bytes 1769480 | tf_op jit(solution)/shard_map/ppermute | solution.py:593
  156.3 27.0 %collective-permute-start.20 = (f32[2176,128]{1,0:T(8,128)}, f32[2176,128]{1,0:T(8,128)}, u32[]{:S(2)}, u32[]{:S(2)}) collective-permute-start(f32[2176,128]{1,0:T(8,128)} %get-tuple-element.71), channel_id=1, source_target_pairs={{0,4},{2,6},{4,0},{6,2},{8,12},{10,14},{12,8},{14,10},{16,20},{18,... | collective-permute-start | bytes 3342344 | tf_op jit(solution)/shard_map/ppermute | solution.py:593
  157.0 27.8 %collective-permute-start.19 = (f32[2176,128]{1,0:T(8,128)}, f32[2176,128]{1,0:T(8,128)}, u32[]{:S(2)}, u32[]{:S(2)}) collective-permute-start(f32[2176,128]{1,0:T(8,128)} %get-tuple-element.69), channel_id=1, source_target_pairs={{0,2},{2,0},{4,6},{6,4},{8,10},{10,8},{12,14},{14,12},{16,18},{18,... | collective-permute-start | bytes 3342344 | tf_op jit(solution)/shard_map/ppermute | solution.py:593
  188.6 14.0 %collective-permute-start.24 = (f32[1088,128]{1,0:T(8,128)}, f32[1088,128]{1,0:T(8,128)}, u32[]{:S(2)}, u32[]{:S(2)}) collective-permute-start(f32[1088,128]{1,0:T(8,128)} %slice_bitcast_fusion), channel_id=1, source_target_pairs={{0,2},{2,0},{4,6},{6,4},{8,10},{10,8},{12,14},{14,12},{16,18},{18,... | collective-permute-start | bytes 1671176 | tf_op jit(solution)/shard_map/ppermute | solution.py:593
  192.6 19.5 %collective-permute-start.23 = (f32[1088,128]{1,0:T(8,128)}, f32[1088,128]{1,0:T(8,128)}, u32[]{:S(2)}, u32[]{:S(2)}) collective-permute-start(f32[1088,128]{1,0:T(8,128)} %slice_bitcast_fusion.1), channel_id=1, source_target_pairs={{0,4},{2,6},{4,0},{6,2},{8,12},{10,14},{12,8},{14,10},{16,20},{18,... | collective-permute-start | bytes 1671176 | tf_op jit(solution)/shard_map/ppermute | solution.py:593
  194.6 46.4 %all-to-all-start.3 = ((f32[16,2,32,128]{3,1,2,0:T(2,128)}), f32[16,2,32,128]{3,1,2,0:T(2,128)S(1)}, u32[]{:S(2)}, u32[]{:S(2)}) async-start(f32[16,2,32,128]{3,1,2,0:T(2,128)} %copy.89), calls=%async_computation.3 | async-start | bytes 1048576 | tf_op jit(solution)/shard_map/all_to_all | solution.py:748
  215.2 22.5 %collective-permute-start.26 = (f32[544,128]{1,0:T(8,128)S(1)}, f32[544,128]{1,0:T(8,128)S(1)}, u32[]{:S(2)}, u32[]{:S(2)}) collective-permute-start(f32[544,128]{1,0:T(8,128)S(1)} %pad_maximum_fusion.5), channel_id=1, source_target_pairs={{0,8},{2,10},{4,12},{6,14},{8,0},{10,2},{12,4},{14,6},{16,24},{18,... | collective-permute-start | bytes 835592 | tf_op jit(solution)/shard_map/ppermute | solution.py:593
  217.7 23.1 %collective-permute-start.27 = (f32[544,128]{1,0:T(8,128)S(1)}, f32[544,128]{1,0:T(8,128)S(1)}, u32[]{:S(2)}, u32[]{:S(2)}) collective-permute-start(f32[544,128]{1,0:T(8,128)S(1)} %pad_maximum_fusion.6), channel_id=1, source_target_pairs={{0,16},{2,18},{4,20},{6,22},{8,24},{10,26},{12,28},{14,30},{16,0},... | collective-permute-start | bytes 835592 | tf_op jit(solution)/shard_map/ppermute | solution.py:593
  221.5 19.3 %collective-permute-start.28 = (f32[544,128]{1,0:T(8,128)S(1)}, f32[544,128]{1,0:T(8,128)S(1)}, u32[]{:S(2)}, u32[]{:S(2)}) collective-permute-start(f32[544,128]{1,0:T(8,128)S(1)} %pad_maximum_fusion.7), channel_id=1, source_target_pairs={{0,24},{2,26},{4,28},{6,30},{8,16},{10,18},{12,20},{14,22},{16,8},... | collective-permute-start | bytes 835592 | tf_op jit(solution)/shard_map/ppermute | solution.py:593
  241.0 18.9 %collective-permute-start.34 = (f32[520,128]{1,0:T(8,128)S(1)}, f32[520,128]{1,0:T(8,128)S(1)}, u32[]{:S(2)}, u32[]{:S(2)}) collective-permute-start(f32[520,128]{1,0:T(8,128)S(1)} %pad_maximum_fusion.8), channel_id=1, source_target_pairs={{2,0},{3,1}} | collective-permute-start | bytes 798728 | tf_op jit(solution)/shard_map/ppermute | solution.py:721
  (44 other events, 506.5 us)

commit v8 on v7

--- a/solution.py
+++ b/solution.py
@@ -171,7 +171,7 @@
         name="state_forward",
     )(ends, prm, x)
 
-def bwd_body(nck, nch, apart, ends_ref, prm_ref, x_ref, g_ref, prior_ref, table_ref, down_ref, out_ref, mat_ref, dx_ref, rows_ref, masks_ref, low_ref, lead_ref, adj_ref, taps_ref):
+def bwd_body(nck, nch, apart, ends_ref, prm_ref, x_ref, g_ref, prior_ref, table_ref, down_ref, out_ref, mat_ref, coef_ref, dx_ref, grad_ref, rows_ref, masks_ref, low_ref, lead_ref, adj_ref, taps_ref):
     make_masks(ends_ref, masks_ref, low_ref, nck)
     at_channel = lambda h: pl.ds(h, nck, stride=nch)
 
@@ -198,8 +198,6 @@
     _, same, cross = lax.fori_loop(0, nck, step, (zero, zero, zero))
     rows_ref[8] = same
     rows_ref[9] = cross
-    for k in range(13, 16):
-        rows_ref[k] = zero
     row = lax.broadcasted_iota(jnp.int32, (CH, CH), 0)
     col = lax.broadcasted_iota(jnp.int32, (CH, CH), 1)
     flip = (row + col == CH - 1).astype(f32).astype(bf16)
@@ -258,15 +256,26 @@
 
     for body in (signal, taps, kernel, carried, ending):
         for_channels(nch, body)
-
-def ssm_backward(ends, prm, x, g, prior, tables, nck, nch):
+    rows = [rows_ref[k] for k in range(13)]
+    total = lambda v: jnp.sum(v, axis=1, keepdims=True)
+    d_step, d_decay, d_frequency, d_real, d_imag = mode_grads(rows, [coef_ref[k] for k in range(14)])
+    grad_ref[0] = jnp.concatenate([d_decay, d_frequency], axis=1)
+    grad_ref[1] = jnp.concatenate([d_real, d_imag], axis=1)
+    lane = lax.broadcasted_iota(jnp.int32, (nch, CH), 1)
+    few = jnp.zeros((nch, CH), f32)
+    for k, v in enumerate((total(rows[11]), total(rows[12]), total(d_step), total(rows[10]))):
+        few = jnp.where(lane == k, v, few)
+    grad_ref[2] = few
+
+def ssm_backward(ends, prm, x, g, prior, tables, coefs, nck, nch):
     vm = pl.BlockSpec(memory_space=pltpu.VMEM)
     return pl.pallas_call(
         partial(bwd_body, nck, nch, x.shape[0] // nck),
-        out_shape=(jax.ShapeDtypeStruct((nck * nch, CH), f32), jax.ShapeDtypeStruct((16, nch, 2 * NSTATE), f32)),
-        in_specs=[pl.BlockSpec(memory_space=pltpu.SMEM)] + [vm] * 8,
+        out_shape=(jax.ShapeDtypeStruct((nck * nch, CH), f32), jax.ShapeDtypeStruct((3, nch, 2 * NSTATE), f32)),
+        in_specs=[pl.BlockSpec(memory_space=pltpu.SMEM)] + [vm] * 9,
         out_specs=(vm, vm),
         scratch_shapes=[
+            pltpu.VMEM((13, nch, 2 * NSTATE), f32),
             pltpu.VMEM((DOCS + 2, nck, CH), f32),
             pltpu.VMEM((2 * DOCS + 2, nck, CH), bf16),
             pltpu.VMEM((nck * nch, 2 * NSTATE), f32),
@@ -275,21 +284,24 @@
         ],
         cost_estimate=pl.CostEstimate(flops=int(3.5e10), bytes_accessed=4 * 2**20, transcendentals=0),
         name="state_backward",
-    )(ends, prm, x, g, prior, *tables)
+    )(ends, prm, x, g, prior, *tables, coefs)
 
 def mixing(step_log, decay_log, frequency, out_real, out_imag):
     delta = jnp.exp(step_log)[:, None]
     rate_re = -jnp.exp(decay_log)
     arg_re, arg_im = delta * rate_re, delta * frequency
     magnitude = jnp.exp(arg_re)
-    pole_re = magnitude * jnp.cos(arg_im) - 1.0
-    pole_im = magnitude * jnp.sin(arg_im)
-    denom = rate_re * rate_re + frequency * frequency
-    ratio_re = (pole_re * rate_re + pole_im * frequency) / denom
-    ratio_im = (pole_im * rate_re - pole_re * frequency) / denom
+    p_re, p_im = magnitude * jnp.cos(arg_im), magnitude * jnp.sin(arg_im)
+    inverse = 1.0 / (rate_re * rate_re + frequency * frequency)
+    ratio_re = ((p_re - 1.0) * rate_re + p_im * frequency) * inverse
+    ratio_im = (p_im * rate_re - (p_re - 1.0) * frequency) * inverse
     mix_re = out_real * ratio_re - out_imag * ratio_im
     mix_im = out_real * ratio_im + out_imag * ratio_re
-    return arg_re, arg_im, mix_re, mix_im
+    magnitude = jnp.exp(arg_re * CH)
+    f_re, f_im = magnitude * jnp.cos(arg_im * CH), magnitude * jnp.sin(arg_im * CH)
+    wide = jnp.broadcast_to(delta, arg_re.shape)
+    coefs = jnp.stack([p_re, p_im, f_re, f_im, mix_re, mix_im, out_real, out_imag, ratio_re, ratio_im, rate_re, frequency, inverse, wide])
+    return (arg_re, arg_im, mix_re, mix_im), coefs
 
 def pair(left, right):
     return jnp.concatenate([left, right], axis=-1)
@@ -307,27 +319,31 @@
     rest = jnp.stack([pair(mix_re, -mix_im), pair(c_re, -c_re), pair(-c_im, -c_im), flat(gain), flat(bias), flat(skip), flat(0 * gain), flat(0 * gain)], axis=1)
     return jnp.concatenate([powers, rest], axis=1)
 
-def mode_grads(rows, arg_re, arg_im, mix_re, mix_im):
-    lo, hi = rows[:, :, :NSTATE], rows[:, :, NSTATE:]
-    magnitude = jnp.exp(arg_re)
-    p_re, p_im = magnitude * jnp.cos(arg_im), magnitude * jnp.sin(arg_im)
-    magnitude = jnp.exp(arg_re * CH)
-    f_re, f_im = magnitude * jnp.cos(arg_im * CH), magnitude * jnp.sin(arg_im * CH)
+def mode_grads(rows, coefs):
+    p_re, p_im, f_re, f_im, mix_re, mix_im, out_real, out_imag, ratio_re, ratio_im, rate, freq, inverse, delta = coefs
+    lo = [v[:, :NSTATE] for v in rows]
+    hi = [v[:, NSTATE:] for v in rows]
     a_re, a_im = lo[2] - hi[2], -(hi[3] + lo[3])
-    b_re, b_im = lo[4] - hi[4], -(hi[5] + lo[5])
-    b_re, b_im = b_re + a_re, b_im + a_im
+    b_re, b_im = lo[4] - hi[4] + a_re, a_im - (hi[5] + lo[5])
     w_re = lo[0] + p_re * a_re + p_im * a_im
     w_im = -hi[0] + p_re * a_im - p_im * a_re
     v_re = lo[1] + p_re * b_re + p_im * b_im
     v_im = -hi[1] + p_re * b_im - p_im * b_re
-    g_re = mix_re * v_re + mix_im * v_im
-    g_im = mix_re * v_im - mix_im * v_re
-    g_re = g_re + lo[6] + hi[6]
-    g_im = g_im + hi[7] - lo[7]
     d_re, d_im = lo[8] + hi[8], hi[9] - lo[9]
-    g_re = g_re + CH * (f_re * d_re + f_im * d_im)
-    g_im = g_im + CH * (f_re * d_im - f_im * d_re)
-    return g_re, g_im, w_re, w_im
+    g_re = mix_re * v_re + mix_im * v_im + lo[6] + hi[6] + CH * (f_re * d_re + f_im * d_im)
+    g_im = mix_re * v_im - mix_im * v_re + hi[7] - lo[7] + CH * (f_re * d_im - f_im * d_re)
+    d_real, d_imag = w_re * ratio_re + w_im * ratio_im, w_im * ratio_re - w_re * ratio_im
+    r_re = (w_re * out_real + w_im * out_imag) * inverse
+    r_im = (w_im * out_real - w_re * out_imag) * inverse
+    fall = 2.0 * (r_re * ratio_re + r_im * ratio_im)
+    pole_re = r_re * rate - r_im * freq
+    pole_im = r_re * freq + r_im * rate
+    d_rate = r_re * (p_re - 1.0) + r_im * p_im - fall * rate
+    d_freq = r_re * p_im - r_im * (p_re - 1.0) - fall * freq
+    g_re = g_re + pole_re * p_re + pole_im * p_im
+    g_im = g_im + pole_im * p_re - pole_re * p_im
+    d_step = delta * (rate * g_re + freq * g_im)
+    return d_step, (d_rate + delta * g_re) * rate, d_freq + delta * g_im, d_real, d_imag
 
 
 def gelu(values):
@@ -723,10 +739,9 @@
 
 
 def mode_vector(block):
-    blocks = block.reshape(2, 2, 2, 2, MODE_ROWS, CH).transpose(3, 2, 1, 0, 4, 5).reshape(16, MODE_ROWS, CH)
-    lead = blocks[:, 0].reshape(16, 4, 32).transpose(1, 0, 2).reshape(-1)
-    tail = blocks[:, 1:].reshape(16, 4, 16, CH).transpose(1, 0, 2, 3).reshape(-1)
-    return jnp.concatenate([lead, tail])
+    blocks = block.reshape(2, 2, 2, 2, 3, -1, CH).transpose(4, 3, 2, 1, 0, 5, 6).reshape(3, D, CH)
+    few = blocks[2, :, :4].T
+    return jnp.concatenate([v.reshape(-1) for v in (few, blocks[0, :, :NSTATE], blocks[0, :, NSTATE:], blocks[1, :, :NSTATE], blocks[1, :, NSTATE:])])
 
 
 def total_of(v):
@@ -781,7 +796,7 @@
         many = mine(lead[4 * D:MODE_TILES * TILE].reshape(4, D, NSTATE))
     if direct():
         plane = gather_plane(near)
-    modes, modes_pull = jax.vjp(mixing, few[2], many[0], many[1], many[2], many[3])
+    modes, coefs = mixing(few[2], many[0], many[1], many[2], many[3])
     prm = mode_rows(*modes, few[0], few[1], few[3])
     outs, prior, *tables = ssm_forward(ends, prm, hats, nck, nch)
     response = lax.all_to_all(outs.reshape(seq, -1, nch, CH), "seq", 0, 0).reshape(-1, CH)
@@ -794,18 +809,14 @@
     if direct():
         packed = join_cores(packed)
         d_outs, packed = lax.optimization_barrier((d_outs, packed))
-    d_signals, sums = ssm_backward(ends, prm, hats, d_outs, prior, tables, nck, nch)
+    d_signals, sums = ssm_backward(ends, prm, hats, d_outs, prior, tables, coefs, nck, nch)
     if direct():
         d_signals, sums, packed = lax.optimization_barrier((d_signals, sums, join_first(packed)))
     d_signal = to_tokens(d_signals, group)
     norm_gain = lead[:D // CH].reshape(D)
-    lane_sums = jnp.sum(sums[10:13], axis=-1)
-    d_modes = modes_pull(mode_grads(sums, *modes))
-    few = jnp.stack([lane_sums[1], lane_sums[2], d_modes[0], lane_sums[0]])
-    many = jnp.stack(d_modes[1:])
     me = device_index()
     if direct():
-        own = jnp.concatenate([few.reshape(1, CH), many.reshape(64, CH)])
+        own = sums.reshape(-1, CH)
         own, packed = lax.optimization_barrier((own + swap_cores(own), join_second(packed)))
         box, block, d_signal = lax.optimization_barrier((join_last(packed), gather_modes(own, (8, 4, 2)), d_signal))
     else:
@@ -823,6 +834,8 @@
             whole = jnp.zeros((v.shape[0], D) + v.shape[2:], f32)
             return lax.dynamic_update_slice_in_dim(whole, v, lax.axis_index("seq") * nch, 1)
 
+        few = sums[2, :, :4].T
+        many = jnp.stack([sums[0, :, :NSTATE], sums[0, :, NSTATE:], sums[1, :, :NSTATE], sums[1, :, NSTATE:]])
         lead = lax.psum(jnp.concatenate([spread(few).reshape(-1), spread(many).reshape(-1)]), AXES)
         squares = squares + jnp.sum(lead * lead) / devices
     lead = lax.dynamic_slice(jnp.pad(lead, (0, share)), (jnp.minimum(me * share, MODE_TILES * TILE),), (share,))

time: 266 us -> 263 us (0.989)
    ppermute x18, waiting for transfers between devices: 36.1 us -> 40.2 us  [hop(): return lax.ppermute(v, 'seq', [(i, i ^ step) for i in range(16)])]
    ppermute x4, waiting for transfers between devices: 8.28 us -> 4.34 us  [gather_modes(): block = jnp.concatenate([block, lax.ppermute(block, 'seq', pairs)])]
  transfers between devices with their start and end apart: 40 -> 40, of which waited for: 17 -> 16; matrix products, arithmetic and copies ran while one was open for 18% -> 18% of each run, Pallas kernels for 14% -> 14%
where the time goes in v8:
time: 263 us; the launch traced here: 262 us
  starting transfers between devices  74.5 us (28%)
  waiting for transfers between devices  72.2 us (27%)
  Pallas kernels  57.7 us (22%)
  other arithmetic  29.4 us (11%)
  local copies, waits for them, and re-layouts  23.2 us (9%)
  between operations  4.84 us (2%)
    ppermute x18, waiting for transfers between devices, hop(): return lax.ppermute(v, 'seq', [(i, i ^ step) for i in range(16)])  40.2 us
    pallas_call x1, Pallas kernels, ssm_backward(): pl.pallas_call(partial(bwd_body, nck, nch, x.shape[0] // nck), out_shape=...  22.6 us
    ppermute x18, starting transfers between devices, hop(): return lax.ppermute(v, 'seq', [(i, i ^ step) for i in range(16)])  21.6 us
    pallas_call x1, Pallas kernels, mlp_kernel(): pl.pallas_call(partial(mlp_body, share, devices, nseq, streams, plan), ou...  20.2 us
    ppermute x4, starting transfers between devices, scatter_modes(): come = lax.ppermute(blocks[1], 'seq', [(i, i + step) for i in range(step)])  15.3 us
    pallas_call x1, Pallas kernels, ssm_forward(): pl.pallas_call(partial(fwd_body, nck, nch, x.shape[0] // nck), out_shape=...  14.9 us
    all_to_all x1, waiting for transfers between devices, per_device(): lax.all_to_all(outs.reshape(seq, -1, nch, CH), 'seq', 0, 0).reshape(-1, CH)  10.6 us
    add x3, other arithmetic, join_cores(): sums.append([own[k] + far[k] for k in range(2)])  8.59 us
  transfers between devices with their start and end apart: 40, of which 16 were waited for; matrix products, arithmetic and copies ran while one was open for 18% of the time, Pallas kernels for 14%

profile of v8, /device:TPU:0, one launch (start us, length us, event | category | flops | bytes accessed | tf_op | source)
XLA Modules:
  0.0 261.9 jit_solution(9169333492467608768)
XLA Ops:
  1.2 3.7 %dynamic_update_slice.3 = f32[88064]{0:T(1024)S(1)} dynamic-update-slice(f32[88064]{0:T(1024)S(1)} %broadcast_in_dim.60, f32[86224]{0:T(1024)} %param.20, s32[]{:T(128)S(6)} %select_n.112) | dynamic-update-slice | bytes 689796 | tf_op jit(solution)/shard_map/dynamic_update_slice | solution.py:636
  12.9 7.2 %all-to-all-start = ((f32[16,2,32,128]{3,1,2,0:T(2,128)}), f32[16,2,32,128]{3,1,2,0:T(2,128)S(1)}, u32[]{:S(2)}, u32[]{:S(2)}) async-start(f32[16,2,32,128]{3,1,2,0:T(2,128)} %multiply_bitcast_fusion), calls=%async_computation | async-start | bytes 1048576 | tf_op jit(solution)/shard_map/all_to_all | solution.py:758
  23.2 3.8 %collective-permute-start.8 = (f32[2,2,2,65,128]{4,3,0,1,2:T(8,128)S(1)}, f32[2,2,2,65,128]{4,3,0,1,2:T(8,128)S(1)}, u32[]{:S(2)}, u32[]{:S(2)}) collective-permute-start(f32[2,2,2,65,128]{4,3,0,1,2:T(8,128)S(1)} %slice_bitcast_fusion.2), channel_id=1, source_target_pairs={{0,2},{1,3}} | collective-permute-start | bytes 798728 | tf_op jit(solution)/shard_map/ppermute | solution.py:722
  27.9 9.7 %collective-permute-done.1 = f32[688,128]{1,0:T(8,128)S(1)} collective-permute-done((f32[688,128]{1,0:T(8,128)S(1)}, f32[688,128]{1,0:T(8,128)S(1)}, u32[]{:S(2)}, u32[]{:S(2)}) %collective-permute-start.1) | collective-permute-done | bytes 352288 | tf_op jit(solution)/shard_map/ppermute | solution.py:609
  43.8 7.4 %collective-permute-start.10 = (f32[2,65,128]{2,1,0:T(8,128)S(1)}, f32[2,65,128]{2,1,0:T(8,128)S(1)}, u32[]{:S(2)}, u32[]{:S(2)}) collective-permute-start(f32[2,65,128]{2,1,0:T(8,128)S(1)} %slice_bitcast_fusion.19), channel_id=1, source_target_pairs={{0,8},{2,10},{4,12},{6,14},{1,9},{3,11},{5,13},{7,15}} | collective-permute-start | bytes 199688 | tf_op jit(solution)/shard_map/ppermute | solution.py:722
  60.8 6.9 %collective-permute-done.5 = f32[1376,128]{1,0:T(8,128)S(1)} collective-permute-done((f32[1376,128]{1,0:T(8,128)S(1)}, f32[1376,128]{1,0:T(8,128)S(1)}, u32[]{:S(2)}, u32[]{:S(2)}) %collective-permute-start.5) | collective-permute-done | bytes 704544 | tf_op jit(solution)/shard_map/ppermute | solution.py:609
  74.5 14.9 %state_forward.1 = (f32[1024,128]{1,0:T(8,128)}, f32[1024,128]{1,0:T(8,128)}, bf16[32,2,128,128]{3,2,1,0:T(8,128)(2,1)}, bf16[32,2,128,128]{3,2,1,0:T(8,128)(2,1...) custom-call(s32[4]{0:T(128)} %bitcast.213, f32[32,24,128]{2,1,0:T(8,128)} %concatenate.100.prm_ref, ...), custom_call_target="tpu_custom_call" | custom-call | flops 20000000000 | bytes 3145728 | tf_op jit(solution)/shard_map/state_forward/pallas_call | solution.py:160
  89.4 6.6 %all-to-all-start.1 = ((f32[16,2,32,128]{3,2,1,0:T(8,128)}), f32[16,2,32,128]{3,2,1,0:T(8,128)S(1)}, u32[]{:S(2)}, u32[]{:S(2)}) async-start(f32[16,2,32,128]{3,2,1,0:T(8,128)} %bitcast.200), calls=%async_computation.1 | async-start | bytes 1048576 | tf_op jit(solution)/shard_map/all_to_all | solution.py:802
  97.7 10.6 %all-to-all-done.1 = f32[16,2,32,128]{3,2,1,0:T(8,128)S(1)} async-done(((f32[16,2,32,128]{3,2,1,0:T(8,128)}), f32[16,2,32,128]{3,2,1,0:T(8,128)S(1)}, u32[]{:S(2)}, u32[]{:S(2)}) %all-to-all-start.1) | async-done | bytes 524320 | tf_op jit(solution)/shard_map/all_to_all | solution.py:802
  113.9 20.2 %feed_forward.1 = (bf16[256,512]{1,0:T(8,128)(2,1)}, f32[256,512]{1,0:T(8,128)}, f32[1024,128]{1,0:T(8,128)}, f32[1040,128]{1,0:T(8,128)}, f32[4352,128]{1,0:T(8...) custom-call(s32[5]{0:T(128)} %pad_add_fusion.place_ref, ...), custom_call_target="tpu_custom_call" | custom-call | flops 20000000000 | bytes 31457280 | tf_op jit(solution)/shard_map/feed_forward/pallas_call | solution.py:570
  135.3 4.6 %all-to-all-start.2 = ((f32[16,2,32,128]{3,2,1,0:T(8,128)}), f32[16,2,32,128]{3,2,1,0:T(8,128)}, u32[]{:S(2)}, u32[]{:S(2)}) async-start(f32[16,2,32,128]{3,2,1,0:T(8,128)} %bitcast.199), calls=%async_computation.2 | async-start | bytes 1048576 | tf_op jit(solution)/shard_map/all_to_all | solution.py:808
  144.7 3.0 %slice_add_fusion = (f32[2176,128]{1,0:T(8,128)}, f32[2176,128]{1,0:T(8,128)S(1)}) fusion(f32[4352,128]{1,0:T(8,128)} %copy-done.8, f32[4352,128]{1,0:T(8,128)S(1)} %copy-done.7), kind=kLoop, calls=%fused_computation | loop fusion | flops 557056 | bytes 6684672 | tf_op jit(solution)/shard_map/add | solution.py:689
  147.7 2.9 %slice_add_fusion.2 = (f32[2176,128]{1,0:T(8,128)}, f32[2176,128]{1,0:T(8,128)S(1)}) fusion(f32[4352,128]{1,0:T(8,128)} %collective-permute-done.16, f32[4352,128]{1,0:T(8,128)S(1)} %copy-done.6), kind=kLoop, calls=%fused_computation.2 | loop fusion | flops 557056 | bytes 6684672 | tf_op jit(solution)/shard_map/add | solution.py:689
  150.7 4.8 %all-to-all-done.2 = f32[16,2,32,128]{3,2,1,0:T(8,128)} async-done(((f32[16,2,32,128]{3,2,1,0:T(8,128)}), f32[16,2,32,128]{3,2,1,0:T(8,128)}, u32[]{:S(2)}, u32[]{:S(2)}) %all-to-all-start.2) | async-done | bytes 524320 | tf_op jit(solution)/shard_map/all_to_all | solution.py:808
  157.8 22.6 %state_backward.1 = (f32[1024,128]{1,0:T(8,128)}, f32[3,32,128]{2,1,0:T(8,128)}) custom-call(s32[4]{0:T(128)} %bitcast.214, f32[32,24,128]{2,1,0:T(8,128)} %concatenate.100.prm_ref, f32[1024,128]{1,0:T(8,128)} %bitcast.197, f32[1024,128]{1,0:T(8,128)} %bitcast.44.g_ref, f32[1024,128]{1,0:T(8,128)} %get-tuple-element.61.prior_ref, ...), custom_call_target="tpu_custom_call" | custom-call | flops 35000000512 | bytes 4194304 | tf_op jit(solution)/shard_map/state_backward/pallas_call | solution.py:272
  192.2 5.7 %all-to-all-start.3 = ((f32[16,2,32,128]{3,1,2,0:T(2,128)}), f32[16,2,32,128]{3,1,2,0:T(2,128)S(1)}, u32[]{:S(2)}, u32[]{:S(2)}) async-start(f32[16,2,32,128]{3,1,2,0:T(2,128)} %copy.85), calls=%async_computation.3 | async-start | bytes 1048576 | tf_op jit(solution)/shard_map/all_to_all | solution.py:763
  198.9 4.2 %collective-permute-done.24 = f32[1088,128]{1,0:T(8,128)} collective-permute-done((f32[1088,128]{1,0:T(8,128)}, f32[1088,128]{1,0:T(8,128)}, u32[]{:S(2)}, u32[]{:S(2)}) %collective-permute-start.24) | collective-permute-done | bytes 557088 | tf_op jit(solution)/shard_map/ppermute | solution.py:609
  204.2 5.8 %collective-permute-done.23 = f32[1088,128]{1,0:T(8,128)} collective-permute-done((f32[1088,128]{1,0:T(8,128)}, f32[1088,128]{1,0:T(8,128)}, u32[]{:S(2)}, u32[]{:S(2)}) %collective-permute-start.23) | collective-permute-done | bytes 557088 | tf_op jit(solution)/shard_map/ppermute | solution.py:609
  215.4 3.6 %collective-permute-start.27 = (f32[544,128]{1,0:T(8,128)S(1)}, f32[544,128]{1,0:T(8,128)S(1)}, u32[]{:S(2)}, u32[]{:S(2)}) collective-permute-start(f32[544,128]{1,0:T(8,128)S(1)} %pad_maximum_fusion.7), channel_id=1, source_target_pairs={{0,16},{2,18},{4,20},{6,22},{8,24},{10,26},{12,28},{14,30},{16,0},... | collective-permute-start | bytes 835592 | tf_op jit(solution)/shard_map/ppermute | solution.py:609
  221.2 3.0 %collective-permute-done.29 = f32[288,128]{1,0:T(8,128)S(1)} collective-permute-done((f32[288,128]{1,0:T(8,128)S(1)}, f32[288,128]{1,0:T(8,128)S(1)}, u32[]{:S(2)}, u32[]{:S(2)}) %collective-permute-start.29) | collective-permute-done | bytes 147488 | tf_op jit(solution)/shard_map/ppermute | solution.py:609
  225.8 4.3 %collective-permute-done.32 = f32[192,128]{1,0:T(8,128)S(1)} collective-permute-done((f32[192,128]{1,0:T(8,128)S(1)}, f32[192,128]{1,0:T(8,128)S(1)}, u32[]{:S(2)}, u32[]{:S(2)}) %collective-permute-start.32) | collective-permute-done | bytes 98336 | tf_op jit(solution)/shard_map/ppermute | solution.py:737
  231.5 7.0 %collective-permute-done.27 = f32[544,128]{1,0:T(8,128)S(1)} collective-permute-done((f32[544,128]{1,0:T(8,128)S(1)}, f32[544,128]{1,0:T(8,128)S(1)}, u32[]{:S(2)}, u32[]{:S(2)}) %collective-permute-start.27) | collective-permute-done | bytes 278560 | tf_op jit(solution)/shard_map/ppermute | solution.py:609
  242.3 5.8 %all-to-all-start.4 = ((f32[32,8,128]{2,1,0:T(8,128)}), f32[32,8,128]{2,1,0:T(8,128)S(1)}, u32[]{:S(2)}, u32[]{:S(2)}) async-start(f32[32,8,128]{2,1,0:T(8,128)} %broadcast_in_dim.64), calls=%async_computation.4 | async-start | bytes 262144 | tf_op jit(solution)/shard_map/all_to_all | solution.py:750
  249.6 6.7 %all-to-all-done.4 = f32[32,8,128]{2,1,0:T(8,128)S(1)} async-done(((f32[32,8,128]{2,1,0:T(8,128)}), f32[32,8,128]{2,1,0:T(8,128)S(1)}, u32[]{:S(2)}, u32[]{:S(2)}) %all-to-all-start.4) | async-done | bytes 131104 | tf_op jit(solution)/shard_map/all_to_all | solution.py:750
  (253 shorter events, 82.1 us)
Async XLA Ops:
  0.6 21.0 %collective-permute-start.7 = (f32[86224]{0:T(1024)}, f32[86224]{0:T(1024)}, u32[]{:S(2)}, u32[]{:S(2)}) collective-permute-start(f32[86224]{0:T(1024)} %param.20), channel_id=1, source_target_pairs={{0,1},{1,0},{2,3},{3,2},{4,5},{5,4},{6,7},{7,6},{8,9},{9,8},{10,11... | collective-permute-start | bytes 1034696 | tf_op jit(solution)/shard_map/ppermute | solution.py:613
  4.9 22.2 %collective-permute-start = (f32[688,128]{1,0:T(8,128)S(1)}, f32[688,128]{1,0:T(8,128)S(1)}, u32[]{:S(2)}, u32[]{:S(2)}) collective-permute-start(f32[688,128]{1,0:T(8,128)S(1)} %bitcast.179), channel_id=1, source_target_pairs={{0,8},{2,10},{4,12},{6,14},{8,0},{10,2},{12,4},{14,6},{16,24},{18,... | collective-permute-start | bytes 1056776 | tf_op jit(solution)/shard_map/ppermute | solution.py:609
  7.6 30.0 %collective-permute-start.1 = (f32[688,128]{1,0:T(8,128)S(1)}, f32[688,128]{1,0:T(8,128)S(1)}, u32[]{:S(2)}, u32[]{:S(2)}) collective-permute-start(f32[688,128]{1,0:T(8,128)S(1)} %bitcast.180), channel_id=1, source_target_pairs={{0,16},{2,18},{4,20},{6,22},{8,24},{10,26},{12,28},{14,30},{16,0},... | collective-permute-start | bytes 1056776 | tf_op jit(solution)/shard_map/ppermute | solution.py:609
  10.2 31.0 %collective-permute-start.2 = (f32[688,128]{1,0:T(8,128)S(1)}, f32[688,128]{1,0:T(8,128)S(1)}, u32[]{:S(2)}, u32[]{:S(2)}) collective-permute-start(f32[688,128]{1,0:T(8,128)S(1)} %bitcast.181), channel_id=1, source_target_pairs={{0,24},{2,26},{4,28},{6,30},{8,16},{10,18},{12,20},{14,22},{16,8},... | collective-permute-start | bytes 1056776 | tf_op jit(solution)/shard_map/ppermute | solution.py:609
  12.9 47.0 %all-to-all-start = ((f32[16,2,32,128]{3,1,2,0:T(2,128)}), f32[16,2,32,128]{3,1,2,0:T(2,128)S(1)}, u32[]{:S(2)}, u32[]{:S(2)}) async-start(f32[16,2,32,128]{3,1,2,0:T(2,128)} %multiply_bitcast_fusion), calls=%async_computation | async-start | bytes 1048576 | tf_op jit(solution)/shard_map/all_to_all | solution.py:758
  23.2 15.1 %collective-permute-start.8 = (f32[2,2,2,65,128]{4,3,0,1,2:T(8,128)S(1)}, f32[2,2,2,65,128]{4,3,0,1,2:T(8,128)S(1)}, u32[]{:S(2)}, u32[]{:S(2)}) collective-permute-start(f32[2,2,2,65,128]{4,3,0,1,2:T(8,128)S(1)} %slice_bitcast_fusion.2), channel_id=1, source_target_pairs={{0,2},{1,3}} | collective-permute-start | bytes 798728 | tf_op jit(solution)/shard_map/ppermute | solution.py:722
  51.3 16.4 %collective-permute-start.5 = (f32[1376,128]{1,0:T(8,128)S(1)}, f32[1376,128]{1,0:T(8,128)S(1)}, u32[]{:S(2)}, u32[]{:S(2)}) collective-permute-start(f32[1376,128]{1,0:T(8,128)S(1)} %pad_maximum_fusion.2), channel_id=1, source_target_pairs={{0,4},{2,6},{4,0},{6,2},{8,12},{10,14},{12,8},{14,10},{16,20},{18,... | collective-permute-start | bytes 2113544 | tf_op jit(solution)/shard_map/ppermute | solution.py:609
  54.6 17.0 %collective-permute-start.3 = (f32[1376,128]{1,0:T(8,128)S(1)}, f32[1376,128]{1,0:T(8,128)}, u32[]{:S(2)}, u32[]{:S(2)}) collective-permute-start(f32[1376,128]{1,0:T(8,128)S(1)} %pad_maximum_fusion.1), channel_id=1, source_target_pairs={{0,2},{2,0},{4,6},{6,4},{8,10},{10,8},{12,14},{14,12},{16,18},{18,... | collective-permute-start | bytes 2113544 | tf_op jit(solution)/shard_map/ppermute | solution.py:609
  68.6 39.7 %collective-permute-start.13 = (f32[2752,128]{1,0:T(8,128)}, f32[2752,128]{1,0:T(8,128)}, u32[]{:S(2)}, u32[]{:S(2)}) collective-permute-start(f32[2752,128]{1,0:T(8,128)} %constant_dynamic-update-slice_fusion.5.refs_2_), channel_id=1, source_target_pairs={{0,2},{2,0},{4,6},{6,4},{8,10},{10,8},{12,14},{14,12},{16,18},{18,... | collective-permute-start | bytes 4227080 | tf_op jit(solution)/shard_map/ppermute | solution.py:609
  73.7 34.7 %collective-permute-start.12 = (f32[2752,128]{1,0:T(8,128)}, f32[2752,128]{1,0:T(8,128)}, u32[]{:S(2)}, u32[]{:S(2)}) collective-permute-start(f32[2752,128]{1,0:T(8,128)} %constant_dynamic-update-slice_fusion.refs_0_), channel_id=1, source_target_pairs={{0,4},{2,6},{4,0},{6,2},{8,12},{10,14},{12,8},{14,10},{16,20},{18,... | collective-permute-start | bytes 4227080 | tf_op jit(solution)/shard_map/ppermute | solution.py:609
  89.4 18.9 %all-to-all-start.1 = ((f32[16,2,32,128]{3,2,1,0:T(8,128)}), f32[16,2,32,128]{3,2,1,0:T(8,128)S(1)}, u32[]{:S(2)}, u32[]{:S(2)}) async-start(f32[16,2,32,128]{3,2,1,0:T(8,128)} %bitcast.200), calls=%async_computation.1 | async-start | bytes 1048576 | tf_op jit(solution)/shard_map/all_to_all | solution.py:802
  97.2 13.3 %collective-permute-start.4 = (f32[2752,128]{1,0:T(8,128)}, f32[2752,128]{1,0:T(8,128)}, u32[]{:S(2)}, u32[]{:S(2)}) collective-permute-start(f32[2752,128]{1,0:T(8,128)} %constant_dynamic-update-slice_fusion.refs_0_), channel_id=1, source_target_pairs={{0,1},{1,0},{2,3},{3,2},{4,5},{5,4},{6,7},{7,6},{8,9},{9,8},{10,11... | collective-permute-start | bytes 4227080 | tf_op jit(solution)/shard_map/ppermute | solution.py:613
  135.3 20.1 %all-to-all-start.2 = ((f32[16,2,32,128]{3,2,1,0:T(8,128)}), f32[16,2,32,128]{3,2,1,0:T(8,128)}, u32[]{:S(2)}, u32[]{:S(2)}) async-start(f32[16,2,32,128]{3,2,1,0:T(8,128)} %bitcast.199), calls=%async_computation.2 | async-start | bytes 1048576 | tf_op jit(solution)/shard_map/all_to_all | solution.py:808
  155.4 26.7 %collective-permute-start.21 = (f32[1152,128]{1,0:T(8,128)}, f32[1152,128]{1,0:T(8,128)}, u32[]{:S(2)}, u32[]{:S(2)}) collective-permute-start(f32[1152,128]{1,0:T(8,128)} %get-tuple-element.73), channel_id=1, source_target_pairs={{0,16},{2,18},{4,20},{6,22},{8,24},{10,26},{12,28},{14,30},{16,0},... | collective-permute-start | bytes 1769480 | tf_op jit(solution)/shard_map/ppermute | solution.py:609
  156.3 27.0 %collective-permute-start.20 = (f32[2176,128]{1,0:T(8,128)}, f32[2176,128]{1,0:T(8,128)}, u32[]{:S(2)}, u32[]{:S(2)}) collective-permute-start(f32[2176,128]{1,0:T(8,128)} %get-tuple-element.71), channel_id=1, source_target_pairs={{0,4},{2,6},{4,0},{6,2},{8,12},{10,14},{12,8},{14,10},{16,20},{18,... | collective-permute-start | bytes 3342344 | tf_op jit(solution)/shard_map/ppermute | solution.py:609
  157.1 27.8 %collective-permute-start.19 = (f32[2176,128]{1,0:T(8,128)}, f32[2176,128]{1,0:T(8,128)}, u32[]{:S(2)}, u32[]{:S(2)}) collective-permute-start(f32[2176,128]{1,0:T(8,128)} %get-tuple-element.69), channel_id=1, source_target_pairs={{0,2},{2,0},{4,6},{6,4},{8,10},{10,8},{12,14},{14,12},{16,18},{18,... | collective-permute-start | bytes 3342344 | tf_op jit(solution)/shard_map/ppermute | solution.py:609
  188.1 15.0 %collective-permute-start.24 = (f32[1088,128]{1,0:T(8,128)}, f32[1088,128]{1,0:T(8,128)}, u32[]{:S(2)}, u32[]{:S(2)}) collective-permute-start(f32[1088,128]{1,0:T(8,128)} %slice_bitcast_fusion), channel_id=1, source_target_pairs={{0,2},{2,0},{4,6},{6,4},{8,10},{10,8},{12,14},{14,12},{16,18},{18,... | collective-permute-start | bytes 1671176 | tf_op jit(solution)/shard_map/ppermute | solution.py:609
  190.5 19.6 %collective-permute-start.23 = (f32[1088,128]{1,0:T(8,128)}, f32[1088,128]{1,0:T(8,128)}, u32[]{:S(2)}, u32[]{:S(2)}) collective-permute-start(f32[1088,128]{1,0:T(8,128)} %slice_bitcast_fusion.1), channel_id=1, source_target_pairs={{0,4},{2,6},{4,0},{6,2},{8,12},{10,14},{12,8},{14,10},{16,20},{18,... | collective-permute-start | bytes 1671176 | tf_op jit(solution)/shard_map/ppermute | solution.py:609
  192.2 46.5 %all-to-all-start.3 = ((f32[16,2,32,128]{3,1,2,0:T(2,128)}), f32[16,2,32,128]{3,1,2,0:T(2,128)S(1)}, u32[]{:S(2)}, u32[]{:S(2)}) async-start(f32[16,2,32,128]{3,1,2,0:T(2,128)} %copy.85), calls=%async_computation.3 | async-start | bytes 1048576 | tf_op jit(solution)/shard_map/all_to_all | solution.py:763
  213.2 18.3 %collective-permute-start.26 = (f32[544,128]{1,0:T(8,128)S(1)}, f32[544,128]{1,0:T(8,128)S(1)}, u32[]{:S(2)}, u32[]{:S(2)}) collective-permute-start(f32[544,128]{1,0:T(8,128)S(1)} %pad_maximum_fusion.6), channel_id=1, source_target_pairs={{0,8},{2,10},{4,12},{6,14},{8,0},{10,2},{12,4},{14,6},{16,24},{18,... | collective-permute-start | bytes 835592 | tf_op jit(solution)/shard_map/ppermute | solution.py:609
  215.4 23.1 %collective-permute-start.27 = (f32[544,128]{1,0:T(8,128)S(1)}, f32[544,128]{1,0:T(8,128)S(1)}, u32[]{:S(2)}, u32[]{:S(2)}) collective-permute-start(f32[544,128]{1,0:T(8,128)S(1)} %pad_maximum_fusion.7), channel_id=1, source_target_pairs={{0,16},{2,18},{4,20},{6,22},{8,24},{10,26},{12,28},{14,30},{16,0},... | collective-permute-start | bytes 835592 | tf_op jit(solution)/shard_map/ppermute | solution.py:609
  219.2 19.3 %collective-permute-start.28 = (f32[544,128]{1,0:T(8,128)S(1)}, f32[544,128]{1,0:T(8,128)S(1)}, u32[]{:S(2)}, u32[]{:S(2)}) collective-permute-start(f32[544,128]{1,0:T(8,128)S(1)} %pad_maximum_fusion.8), channel_id=1, source_target_pairs={{0,24},{2,26},{4,28},{6,30},{8,16},{10,18},{12,20},{14,22},{16,8},... | collective-permute-start | bytes 835592 | tf_op jit(solution)/shard_map/ppermute | solution.py:609
  238.8 18.9 %collective-permute-start.34 = (f32[768,128]{1,0:T(8,128)S(1)}, f32[768,128]{1,0:T(8,128)S(1)}, u32[]{:S(2)}, u32[]{:S(2)}) collective-permute-start(f32[768,128]{1,0:T(8,128)S(1)} %pad_maximum_fusion.4), channel_id=1, source_target_pairs={{2,0},{3,1}} | collective-permute-start | bytes 1179656 | tf_op jit(solution)/shard_map/ppermute | solution.py:737
  242.3 14.0 %all-to-all-start.4 = ((f32[32,8,128]{2,1,0:T(8,128)}), f32[32,8,128]{2,1,0:T(8,128)S(1)}, u32[]{:S(2)}, u32[]{:S(2)}) async-start(f32[32,8,128]{2,1,0:T(8,128)} %broadcast_in_dim.64), calls=%async_computation.4 | async-start | bytes 262144 | tf_op jit(solution)/shard_map/all_to_all | solution.py:750
  (43 other events, 444.3 us)

commit v9 on v8

--- a/solution.py
+++ b/solution.py
@@ -747,8 +747,8 @@
 def total_of(v):
     if not direct():
         return lax.psum(v, AXES)
-    terms = lax.all_to_all(jnp.broadcast_to(v, (32, 8, CH)), AXES, 0, 0)
-    return jnp.sum(terms[:, 0, 0])
+    terms = lax.all_to_all(jnp.broadcast_to(v, (32, CH)), AXES, 0, 0)
+    return jnp.sum(terms[:, 0])
 
 
 def to_channels(rows):

time: 263 us -> 262 us (level)
  no operation moved by 1% of the time
where the time goes in v9:
time: 262 us; the launch traced here: 261 us
  starting transfers between devices  74.5 us (28%)
  waiting for transfers between devices  71.1 us (27%)
  Pallas kernels  57.7 us (22%)
  other arithmetic  29.3 us (11%)
  local copies, waits for them, and re-layouts  23.2 us (9%)
  between operations  4.84 us (2%)
    ppermute x18, waiting for transfers between devices, hop(): return lax.ppermute(v, 'seq', [(i, i ^ step) for i in range(16)])  40.2 us
    pallas_call x1, Pallas kernels, ssm_backward(): pl.pallas_call(partial(bwd_body, nck, nch, x.shape[0] // nck), out_shape=...  22.6 us
    ppermute x18, starting transfers between devices, hop(): return lax.ppermute(v, 'seq', [(i, i ^ step) for i in range(16)])  21.6 us
    pallas_call x1, Pallas kernels, mlp_kernel(): pl.pallas_call(partial(mlp_body, share, devices, nseq, streams, plan), ou...  20.2 us
    ppermute x4, starting transfers between devices, scatter_modes(): come = lax.ppermute(blocks[1], 'seq', [(i, i + step) for i in range(step)])  15.3 us
    pallas_call x1, Pallas kernels, ssm_forward(): pl.pallas_call(partial(fwd_body, nck, nch, x.shape[0] // nck), out_shape=...  14.9 us
    all_to_all x1, waiting for transfers between devices, per_device(): lax.all_to_all(outs.reshape(seq, -1, nch, CH), 'seq', 0, 0).reshape(-1, CH)  10.6 us
    add x3, other arithmetic, join_cores(): sums.append([own[k] + far[k] for k in range(2)])  8.59 us
  transfers between devices with their start and end apart: 40, of which 16 were waited for; matrix products, arithmetic and copies ran while one was open for 18% of the time, Pallas kernels for 14%

profile of v9, /device:TPU:0, one launch (start us, length us, event | category | flops | bytes accessed | tf_op | source)
XLA Modules:
  0.0 260.6 jit_solution(13002361922785346978)
XLA Ops:
  1.2 3.7 %dynamic_update_slice.3 = f32[88064]{0:T(1024)S(1)} dynamic-update-slice(f32[88064]{0:T(1024)S(1)} %broadcast_in_dim.60, f32[86224]{0:T(1024)} %param.20, s32[]{:T(128)S(6)} %select_n.112) | dynamic-update-slice | bytes 689796 | tf_op jit(solution)/shard_map/dynamic_update_slice | solution.py:636
  12.9 7.2 %all-to-all-start = ((f32[16,2,32,128]{3,1,2,0:T(2,128)}), f32[16,2,32,128]{3,1,2,0:T(2,128)S(1)}, u32[]{:S(2)}, u32[]{:S(2)}) async-start(f32[16,2,32,128]{3,1,2,0:T(2,128)} %multiply_bitcast_fusion), calls=%async_computation | async-start | bytes 1048576 | tf_op jit(solution)/shard_map/all_to_all | solution.py:758
  23.2 3.8 %collective-permute-start.8 = (f32[2,2,2,65,128]{4,3,0,1,2:T(8,128)S(1)}, f32[2,2,2,65,128]{4,3,0,1,2:T(8,128)S(1)}, u32[]{:S(2)}, u32[]{:S(2)}) collective-permute-start(f32[2,2,2,65,128]{4,3,0,1,2:T(8,128)S(1)} %slice_bitcast_fusion.2), channel_id=1, source_target_pairs={{0,2},{1,3}} | collective-permute-start | bytes 798728 | tf_op jit(solution)/shard_map/ppermute | solution.py:722
  27.9 9.7 %collective-permute-done.1 = f32[688,128]{1,0:T(8,128)S(1)} collective-permute-done((f32[688,128]{1,0:T(8,128)S(1)}, f32[688,128]{1,0:T(8,128)S(1)}, u32[]{:S(2)}, u32[]{:S(2)}) %collective-permute-start.1) | collective-permute-done | bytes 352288 | tf_op jit(solution)/shard_map/ppermute | solution.py:609
  43.8 7.4 %collective-permute-start.10 = (f32[2,65,128]{2,1,0:T(8,128)S(1)}, f32[2,65,128]{2,1,0:T(8,128)S(1)}, u32[]{:S(2)}, u32[]{:S(2)}) collective-permute-start(f32[2,65,128]{2,1,0:T(8,128)S(1)} %slice_bitcast_fusion.19), channel_id=1, source_target_pairs={{0,8},{2,10},{4,12},{6,14},{1,9},{3,11},{5,13},{7,15}} | collective-permute-start | bytes 199688 | tf_op jit(solution)/shard_map/ppermute | solution.py:722
  60.8 6.9 %collective-permute-done.5 = f32[1376,128]{1,0:T(8,128)S(1)} collective-permute-done((f32[1376,128]{1,0:T(8,128)S(1)}, f32[1376,128]{1,0:T(8,128)S(1)}, u32[]{:S(2)}, u32[]{:S(2)}) %collective-permute-start.5) | collective-permute-done | bytes 704544 | tf_op jit(solution)/shard_map/ppermute | solution.py:609
  74.5 14.9 %state_forward.1 = (f32[1024,128]{1,0:T(8,128)}, f32[1024,128]{1,0:T(8,128)}, bf16[32,2,128,128]{3,2,1,0:T(8,128)(2,1)}, bf16[32,2,128,128]{3,2,1,0:T(8,128)(2,1...) custom-call(s32[4]{0:T(128)} %bitcast.215, f32[32,24,128]{2,1,0:T(8,128)} %concatenate.100.prm_ref, ...), custom_call_target="tpu_custom_call" | custom-call | flops 20000000000 | bytes 3145728 | tf_op jit(solution)/shard_map/state_forward/pallas_call | solution.py:160
  89.4 6.6 %all-to-all-start.1 = ((f32[16,2,32,128]{3,2,1,0:T(8,128)}), f32[16,2,32,128]{3,2,1,0:T(8,128)S(1)}, u32[]{:S(2)}, u32[]{:S(2)}) async-start(f32[16,2,32,128]{3,2,1,0:T(8,128)} %bitcast.201), calls=%async_computation.1 | async-start | bytes 1048576 | tf_op jit(solution)/shard_map/all_to_all | solution.py:802
  97.7 10.6 %all-to-all-done.1 = f32[16,2,32,128]{3,2,1,0:T(8,128)S(1)} async-done(((f32[16,2,32,128]{3,2,1,0:T(8,128)}), f32[16,2,32,128]{3,2,1,0:T(8,128)S(1)}, u32[]{:S(2)}, u32[]{:S(2)}) %all-to-all-start.1) | async-done | bytes 524320 | tf_op jit(solution)/shard_map/all_to_all | solution.py:802
  113.9 20.2 %feed_forward.1 = (bf16[256,512]{1,0:T(8,128)(2,1)}, f32[256,512]{1,0:T(8,128)}, f32[1024,128]{1,0:T(8,128)}, f32[1040,128]{1,0:T(8,128)}, f32[4352,128]{1,0:T(8...) custom-call(s32[5]{0:T(128)} %pad_add_fusion.place_ref, ...), custom_call_target="tpu_custom_call" | custom-call | flops 20000000000 | bytes 31457280 | tf_op jit(solution)/shard_map/feed_forward/pallas_call | solution.py:570
  135.3 4.6 %all-to-all-start.2 = ((f32[16,2,32,128]{3,2,1,0:T(8,128)}), f32[16,2,32,128]{3,2,1,0:T(8,128)}, u32[]{:S(2)}, u32[]{:S(2)}) async-start(f32[16,2,32,128]{3,2,1,0:T(8,128)} %bitcast.200), calls=%async_computation.2 | async-start | bytes 1048576 | tf_op jit(solution)/shard_map/all_to_all | solution.py:808
  144.7 3.0 %slice_add_fusion = (f32[2176,128]{1,0:T(8,128)}, f32[2176,128]{1,0:T(8,128)S(1)}) fusion(f32[4352,128]{1,0:T(8,128)} %copy-done.8, f32[4352,128]{1,0:T(8,128)S(1)} %copy-done.7), kind=kLoop, calls=%fused_computation | loop fusion | flops 557056 | bytes 6684672 | tf_op jit(solution)/shard_map/add | solution.py:689
  147.7 2.9 %slice_add_fusion.2 = (f32[2176,128]{1,0:T(8,128)}, f32[2176,128]{1,0:T(8,128)S(1)}) fusion(f32[4352,128]{1,0:T(8,128)} %collective-permute-done.16, f32[4352,128]{1,0:T(8,128)S(1)} %copy-done.6), kind=kLoop, calls=%fused_computation.2 | loop fusion | flops 557056 | bytes 6684672 | tf_op jit(solution)/shard_map/add | solution.py:689
  150.7 4.8 %all-to-all-done.2 = f32[16,2,32,128]{3,2,1,0:T(8,128)} async-done(((f32[16,2,32,128]{3,2,1,0:T(8,128)}), f32[16,2,32,128]{3,2,1,0:T(8,128)}, u32[]{:S(2)}, u32[]{:S(2)}) %all-to-all-start.2) | async-done | bytes 524320 | tf_op jit(solution)/shard_map/all_to_all | solution.py:808
  157.8 22.6 %state_backward.1 = (f32[1024,128]{1,0:T(8,128)}, f32[3,32,128]{2,1,0:T(8,128)}) custom-call(s32[4]{0:T(128)} %bitcast.216, f32[32,24,128]{2,1,0:T(8,128)} %concatenate.100.prm_ref, f32[1024,128]{1,0:T(8,128)} %bitcast.198, f32[1024,128]{1,0:T(8,128)} %bitcast.44.g_ref, f32[1024,128]{1,0:T(8,128)} %get-tuple-element.61.prior_ref, ...), custom_call_target="tpu_custom_call" | custom-call | flops 35000000512 | bytes 4194304 | tf_op jit(solution)/shard_map/state_backward/pallas_call | solution.py:272
  192.2 5.7 %all-to-all-start.3 = ((f32[16,2,32,128]{3,1,2,0:T(2,128)}), f32[16,2,32,128]{3,1,2,0:T(2,128)S(1)}, u32[]{:S(2)}, u32[]{:S(2)}) async-start(f32[16,2,32,128]{3,1,2,0:T(2,128)} %copy.85), calls=%async_computation.3 | async-start | bytes 1048576 | tf_op jit(solution)/shard_map/all_to_all | solution.py:763
  198.9 4.2 %collective-permute-done.24 = f32[1088,128]{1,0:T(8,128)} collective-permute-done((f32[1088,128]{1,0:T(8,128)}, f32[1088,128]{1,0:T(8,128)}, u32[]{:S(2)}, u32[]{:S(2)}) %collective-permute-start.24) | collective-permute-done | bytes 557088 | tf_op jit(solution)/shard_map/ppermute | solution.py:609
  204.2 5.8 %collective-permute-done.23 = f32[1088,128]{1,0:T(8,128)} collective-permute-done((f32[1088,128]{1,0:T(8,128)}, f32[1088,128]{1,0:T(8,128)}, u32[]{:S(2)}, u32[]{:S(2)}) %collective-permute-start.23) | collective-permute-done | bytes 557088 | tf_op jit(solution)/shard_map/ppermute | solution.py:609
  215.4 3.6 %collective-permute-start.27 = (f32[544,128]{1,0:T(8,128)S(1)}, f32[544,128]{1,0:T(8,128)S(1)}, u32[]{:S(2)}, u32[]{:S(2)}) collective-permute-start(f32[544,128]{1,0:T(8,128)S(1)} %pad_maximum_fusion.7), channel_id=1, source_target_pairs={{0,16},{2,18},{4,20},{6,22},{8,24},{10,26},{12,28},{14,30},{16,0},... | collective-permute-start | bytes 835592 | tf_op jit(solution)/shard_map/ppermute | solution.py:609
  221.2 3.0 %collective-permute-done.29 = f32[288,128]{1,0:T(8,128)S(1)} collective-permute-done((f32[288,128]{1,0:T(8,128)S(1)}, f32[288,128]{1,0:T(8,128)S(1)}, u32[]{:S(2)}, u32[]{:S(2)}) %collective-permute-start.29) | collective-permute-done | bytes 147488 | tf_op jit(solution)/shard_map/ppermute | solution.py:609
  225.8 4.3 %collective-permute-done.32 = f32[192,128]{1,0:T(8,128)S(1)} collective-permute-done((f32[192,128]{1,0:T(8,128)S(1)}, f32[192,128]{1,0:T(8,128)S(1)}, u32[]{:S(2)}, u32[]{:S(2)}) %collective-permute-start.32) | collective-permute-done | bytes 98336 | tf_op jit(solution)/shard_map/ppermute | solution.py:737
  231.5 7.0 %collective-permute-done.27 = f32[544,128]{1,0:T(8,128)S(1)} collective-permute-done((f32[544,128]{1,0:T(8,128)S(1)}, f32[544,128]{1,0:T(8,128)S(1)}, u32[]{:S(2)}, u32[]{:S(2)}) %collective-permute-start.27) | collective-permute-done | bytes 278560 | tf_op jit(solution)/shard_map/ppermute | solution.py:609
  242.2 5.8 %all-to-all-start.4 = ((f32[32,1,128]{2,1,0:T(1,128)}), f32[32,1,128]{2,1,0:T(1,128)S(1)}, u32[]{:S(2)}, u32[]{:S(2)}) async-start(f32[32,1,128]{2,1,0:T(1,128)} %broadcast_in_dim.64), calls=%async_computation.4 | async-start | bytes 32768 | tf_op jit(solution)/shard_map/all_to_all | solution.py:750
  249.5 5.5 %all-to-all-done.4 = f32[32,1,128]{2,1,0:T(1,128)S(1)} async-done(((f32[32,1,128]{2,1,0:T(1,128)}), f32[32,1,128]{2,1,0:T(1,128)S(1)}, u32[]{:S(2)}, u32[]{:S(2)}) %all-to-all-start.4) | async-done | bytes 16416 | tf_op jit(solution)/shard_map/all_to_all | solution.py:750
  (253 shorter events, 82.0 us)
Async XLA Ops:
  0.6 21.0 %collective-permute-start.7 = (f32[86224]{0:T(1024)}, f32[86224]{0:T(1024)}, u32[]{:S(2)}, u32[]{:S(2)}) collective-permute-start(f32[86224]{0:T(1024)} %param.20), channel_id=1, source_target_pairs={{0,1},{1,0},{2,3},{3,2},{4,5},{5,4},{6,7},{7,6},{8,9},{9,8},{10,11... | collective-permute-start | bytes 1034696 | tf_op jit(solution)/shard_map/ppermute | solution.py:613
  4.9 22.2 %collective-permute-start = (f32[688,128]{1,0:T(8,128)S(1)}, f32[688,128]{1,0:T(8,128)S(1)}, u32[]{:S(2)}, u32[]{:S(2)}) collective-permute-start(f32[688,128]{1,0:T(8,128)S(1)} %bitcast.180), channel_id=1, source_target_pairs={{0,8},{2,10},{4,12},{6,14},{8,0},{10,2},{12,4},{14,6},{16,24},{18,... | collective-permute-start | bytes 1056776 | tf_op jit(solution)/shard_map/ppermute | solution.py:609
  7.6 30.0 %collective-permute-start.1 = (f32[688,128]{1,0:T(8,128)S(1)}, f32[688,128]{1,0:T(8,128)S(1)}, u32[]{:S(2)}, u32[]{:S(2)}) collective-permute-start(f32[688,128]{1,0:T(8,128)S(1)} %bitcast.181), channel_id=1, source_target_pairs={{0,16},{2,18},{4,20},{6,22},{8,24},{10,26},{12,28},{14,30},{16,0},... | collective-permute-start | bytes 1056776 | tf_op jit(solution)/shard_map/ppermute | solution.py:609
  10.2 31.0 %collective-permute-start.2 = (f32[688,128]{1,0:T(8,128)S(1)}, f32[688,128]{1,0:T(8,128)S(1)}, u32[]{:S(2)}, u32[]{:S(2)}) collective-permute-start(f32[688,128]{1,0:T(8,128)S(1)} %bitcast.182), channel_id=1, source_target_pairs={{0,24},{2,26},{4,28},{6,30},{8,16},{10,18},{12,20},{14,22},{16,8},... | collective-permute-start | bytes 1056776 | tf_op jit(solution)/shard_map/ppermute | solution.py:609
  12.9 47.0 %all-to-all-start = ((f32[16,2,32,128]{3,1,2,0:T(2,128)}), f32[16,2,32,128]{3,1,2,0:T(2,128)S(1)}, u32[]{:S(2)}, u32[]{:S(2)}) async-start(f32[16,2,32,128]{3,1,2,0:T(2,128)} %multiply_bitcast_fusion), calls=%async_computation | async-start | bytes 1048576 | tf_op jit(solution)/shard_map/all_to_all | solution.py:758
  23.2 15.1 %collective-permute-start.8 = (f32[2,2,2,65,128]{4,3,0,1,2:T(8,128)S(1)}, f32[2,2,2,65,128]{4,3,0,1,2:T(8,128)S(1)}, u32[]{:S(2)}, u32[]{:S(2)}) collective-permute-start(f32[2,2,2,65,128]{4,3,0,1,2:T(8,128)S(1)} %slice_bitcast_fusion.2), channel_id=1, source_target_pairs={{0,2},{1,3}} | collective-permute-start | bytes 798728 | tf_op jit(solution)/shard_map/ppermute | solution.py:722
  51.3 16.4 %collective-permute-start.5 = (f32[1376,128]{1,0:T(8,128)S(1)}, f32[1376,128]{1,0:T(8,128)S(1)}, u32[]{:S(2)}, u32[]{:S(2)}) collective-permute-start(f32[1376,128]{1,0:T(8,128)S(1)} %pad_maximum_fusion.2), channel_id=1, source_target_pairs={{0,4},{2,6},{4,0},{6,2},{8,12},{10,14},{12,8},{14,10},{16,20},{18,... | collective-permute-start | bytes 2113544 | tf_op jit(solution)/shard_map/ppermute | solution.py:609
  54.6 17.0 %collective-permute-start.3 = (f32[1376,128]{1,0:T(8,128)S(1)}, f32[1376,128]{1,0:T(8,128)}, u32[]{:S(2)}, u32[]{:S(2)}) collective-permute-start(f32[1376,128]{1,0:T(8,128)S(1)} %pad_maximum_fusion.1), channel_id=1, source_target_pairs={{0,2},{2,0},{4,6},{6,4},{8,10},{10,8},{12,14},{14,12},{16,18},{18,... | collective-permute-start | bytes 2113544 | tf_op jit(solution)/shard_map/ppermute | solution.py:609
  68.6 39.7 %collective-permute-start.13 = (f32[2752,128]{1,0:T(8,128)}, f32[2752,128]{1,0:T(8,128)}, u32[]{:S(2)}, u32[]{:S(2)}) collective-permute-start(f32[2752,128]{1,0:T(8,128)} %constant_dynamic-update-slice_fusion.5.refs_2_), channel_id=1, source_target_pairs={{0,2},{2,0},{4,6},{6,4},{8,10},{10,8},{12,14},{14,12},{16,18},{18,... | collective-permute-start | bytes 4227080 | tf_op jit(solution)/shard_map/ppermute | solution.py:609
  73.7 34.7 %collective-permute-start.12 = (f32[2752,128]{1,0:T(8,128)}, f32[2752,128]{1,0:T(8,128)}, u32[]{:S(2)}, u32[]{:S(2)}) collective-permute-start(f32[2752,128]{1,0:T(8,128)} %constant_dynamic-update-slice_fusion.refs_0_), channel_id=1, source_target_pairs={{0,4},{2,6},{4,0},{6,2},{8,12},{10,14},{12,8},{14,10},{16,20},{18,... | collective-permute-start | bytes 4227080 | tf_op jit(solution)/shard_map/ppermute | solution.py:609
  89.4 18.9 %all-to-all-start.1 = ((f32[16,2,32,128]{3,2,1,0:T(8,128)}), f32[16,2,32,128]{3,2,1,0:T(8,128)S(1)}, u32[]{:S(2)}, u32[]{:S(2)}) async-start(f32[16,2,32,128]{3,2,1,0:T(8,128)} %bitcast.201), calls=%async_computation.1 | async-start | bytes 1048576 | tf_op jit(solution)/shard_map/all_to_all | solution.py:802
  97.2 13.2 %collective-permute-start.6 = (f32[2752,128]{1,0:T(8,128)S(1)}, f32[2752,128]{1,0:T(8,128)}, u32[]{:S(2)}, u32[]{:S(2)}) collective-permute-start(f32[2752,128]{1,0:T(8,128)S(1)} %copy-done.16), channel_id=1, source_target_pairs={{0,1},{1,0},{2,3},{3,2},{4,5},{5,4},{6,7},{7,6},{8,9},{9,8},{10,11... | collective-permute-start | bytes 4227080 | tf_op jit(solution)/shard_map/ppermute | solution.py:613
  97.2 13.3 %collective-permute-start.4 = (f32[2752,128]{1,0:T(8,128)}, f32[2752,128]{1,0:T(8,128)}, u32[]{:S(2)}, u32[]{:S(2)}) collective-permute-start(f32[2752,128]{1,0:T(8,128)} %constant_dynamic-update-slice_fusion.refs_0_), channel_id=1, source_target_pairs={{0,1},{1,0},{2,3},{3,2},{4,5},{5,4},{6,7},{7,6},{8,9},{9,8},{10,11... | collective-permute-start | bytes 4227080 | tf_op jit(solution)/shard_map/ppermute | solution.py:613
  135.3 20.1 %all-to-all-start.2 = ((f32[16,2,32,128]{3,2,1,0:T(8,128)}), f32[16,2,32,128]{3,2,1,0:T(8,128)}, u32[]{:S(2)}, u32[]{:S(2)}) async-start(f32[16,2,32,128]{3,2,1,0:T(8,128)} %bitcast.200), calls=%async_computation.2 | async-start | bytes 1048576 | tf_op jit(solution)/shard_map/all_to_all | solution.py:808
  155.4 26.7 %collective-permute-start.21 = (f32[1152,128]{1,0:T(8,128)}, f32[1152,128]{1,0:T(8,128)}, u32[]{:S(2)}, u32[]{:S(2)}) collective-permute-start(f32[1152,128]{1,0:T(8,128)} %get-tuple-element.73), channel_id=1, source_target_pairs={{0,16},{2,18},{4,20},{6,22},{8,24},{10,26},{12,28},{14,30},{16,0},... | collective-permute-start | bytes 1769480 | tf_op jit(solution)/shard_map/ppermute | solution.py:609
  156.3 27.0 %collective-permute-start.20 = (f32[2176,128]{1,0:T(8,128)}, f32[2176,128]{1,0:T(8,128)}, u32[]{:S(2)}, u32[]{:S(2)}) collective-permute-start(f32[2176,128]{1,0:T(8,128)} %get-tuple-element.71), channel_id=1, source_target_pairs={{0,4},{2,6},{4,0},{6,2},{8,12},{10,14},{12,8},{14,10},{16,20},{18,... | collective-permute-start | bytes 3342344 | tf_op jit(solution)/shard_map/ppermute | solution.py:609
  157.1 27.8 %collective-permute-start.19 = (f32[2176,128]{1,0:T(8,128)}, f32[2176,128]{1,0:T(8,128)}, u32[]{:S(2)}, u32[]{:S(2)}) collective-permute-start(f32[2176,128]{1,0:T(8,128)} %get-tuple-element.69), channel_id=1, source_target_pairs={{0,2},{2,0},{4,6},{6,4},{8,10},{10,8},{12,14},{14,12},{16,18},{18,... | collective-permute-start | bytes 3342344 | tf_op jit(solution)/shard_map/ppermute | solution.py:609
  188.1 15.0 %collective-permute-start.24 = (f32[1088,128]{1,0:T(8,128)}, f32[1088,128]{1,0:T(8,128)}, u32[]{:S(2)}, u32[]{:S(2)}) collective-permute-start(f32[1088,128]{1,0:T(8,128)} %slice_bitcast_fusion), channel_id=1, source_target_pairs={{0,2},{2,0},{4,6},{6,4},{8,10},{10,8},{12,14},{14,12},{16,18},{18,... | collective-permute-start | bytes 1671176 | tf_op jit(solution)/shard_map/ppermute | solution.py:609
  190.5 19.6 %collective-permute-start.23 = (f32[1088,128]{1,0:T(8,128)}, f32[1088,128]{1,0:T(8,128)}, u32[]{:S(2)}, u32[]{:S(2)}) collective-permute-start(f32[1088,128]{1,0:T(8,128)} %slice_bitcast_fusion.1), channel_id=1, source_target_pairs={{0,4},{2,6},{4,0},{6,2},{8,12},{10,14},{12,8},{14,10},{16,20},{18,... | collective-permute-start | bytes 1671176 | tf_op jit(solution)/shard_map/ppermute | solution.py:609
  192.2 46.5 %all-to-all-start.3 = ((f32[16,2,32,128]{3,1,2,0:T(2,128)}), f32[16,2,32,128]{3,1,2,0:T(2,128)S(1)}, u32[]{:S(2)}, u32[]{:S(2)}) async-start(f32[16,2,32,128]{3,1,2,0:T(2,128)} %copy.85), calls=%async_computation.3 | async-start | bytes 1048576 | tf_op jit(solution)/shard_map/all_to_all | solution.py:763
  213.2 18.3 %collective-permute-start.26 = (f32[544,128]{1,0:T(8,128)S(1)}, f32[544,128]{1,0:T(8,128)S(1)}, u32[]{:S(2)}, u32[]{:S(2)}) collective-permute-start(f32[544,128]{1,0:T(8,128)S(1)} %pad_maximum_fusion.6), channel_id=1, source_target_pairs={{0,8},{2,10},{4,12},{6,14},{8,0},{10,2},{12,4},{14,6},{16,24},{18,... | collective-permute-start | bytes 835592 | tf_op jit(solution)/shard_map/ppermute | solution.py:609
  215.4 23.1 %collective-permute-start.27 = (f32[544,128]{1,0:T(8,128)S(1)}, f32[544,128]{1,0:T(8,128)S(1)}, u32[]{:S(2)}, u32[]{:S(2)}) collective-permute-start(f32[544,128]{1,0:T(8,128)S(1)} %pad_maximum_fusion.7), channel_id=1, source_target_pairs={{0,16},{2,18},{4,20},{6,22},{8,24},{10,26},{12,28},{14,30},{16,0},... | collective-permute-start | bytes 835592 | tf_op jit(solution)/shard_map/ppermute | solution.py:609
  219.2 19.3 %collective-permute-start.28 = (f32[544,128]{1,0:T(8,128)S(1)}, f32[544,128]{1,0:T(8,128)S(1)}, u32[]{:S(2)}, u32[]{:S(2)}) collective-permute-start(f32[544,128]{1,0:T(8,128)S(1)} %pad_maximum_fusion.8), channel_id=1, source_target_pairs={{0,24},{2,26},{4,28},{6,30},{8,16},{10,18},{12,20},{14,22},{16,8},... | collective-permute-start | bytes 835592 | tf_op jit(solution)/shard_map/ppermute | solution.py:609
  238.8 17.6 %collective-permute-start.34 = (f32[768,128]{1,0:T(8,128)S(1)}, f32[768,128]{1,0:T(8,128)S(1)}, u32[]{:S(2)}, u32[]{:S(2)}) collective-permute-start(f32[768,128]{1,0:T(8,128)S(1)} %pad_maximum_fusion.4), channel_id=1, source_target_pairs={{2,0},{3,1}} | collective-permute-start | bytes 1179656 | tf_op jit(solution)/shard_map/ppermute | solution.py:737
  (43 other events, 443.8 us)

commit v10 on v9

--- a/solution.py
+++ b/solution.py
@@ -437,7 +437,7 @@
             ).start()
             return 0
 
-        lax.fori_loop(0, count, copy_box, 0)
+        lax.fori_loop(0, count, copy_box, 0, unroll=8)
         inside += (hi - lo) * count
     parts = group // CH
     turned = [
@@ -469,11 +469,11 @@
         flat[pl.ds(pl.multiple_of((at + step) * 8, 8), 8), :] = jnp.where(far, two, one) + then
         return 0
 
-    lax.fori_loop(0, devices, join, 0)
+    lax.fori_loop(0, devices, join, 0, unroll=8)
 
     some = flat.at[pl.ds(0, inside * 8), :]
     pltpu.make_async_copy(some, some, sems.at[0]).wait()
-    lead_ref[...] = flat[:MODE_TILES * 8, :]
+    lead_ref[...] = flat[:8, :]
     narrow(flat, gate, GATE_AT, D, G // CH)
     gate_bias = small_row(flat, SMALL_AT[0], 0, G)
     second_gain = small_row(flat, SMALL_AT[1], 0, D)
@@ -573,7 +573,7 @@
             shape(group, D, bf16),
             shape(group, D, f32),
             jax.ShapeDtypeStruct(response.shape, f32),
-            shape(MODE_TILES * 8, CH, f32),
+            shape(8, CH, f32),
             *packed,
         ),
         in_specs=[smem] * 3 + [hbm] * len(boxes) + [vm] * 3,

time: 262 us -> 262 us (level)
  transfers between devices with their start and end apart: 40 -> 40, of which waited for: 16 -> 17; matrix products, arithmetic and copies ran while one was open for 18% -> 17% of each run, Pallas kernels for 14% -> 14%
where the time goes in v10:
time: 262 us; the launch traced here: 260 us
  starting transfers between devices  74.5 us (28%)
  waiting for transfers between devices  71.7 us (27%)
  Pallas kernels  57.3 us (22%)
  other arithmetic  29.3 us (11%)
  local copies, waits for them, and re-layouts  22.5 us (9%)
  between operations  4.86 us (2%)
    ppermute x18, waiting for transfers between devices, hop(): return lax.ppermute(v, 'seq', [(i, i ^ step) for i in range(16)])  40.2 us
    pallas_call x1, Pallas kernels, ssm_backward(): pl.pallas_call(partial(bwd_body, nck, nch, x.shape[0] // nck), out_shape=...  22.6 us
    ppermute x18, starting transfers between devices, hop(): return lax.ppermute(v, 'seq', [(i, i ^ step) for i in range(16)])  21.6 us
    pallas_call x1, Pallas kernels, mlp_kernel(): pl.pallas_call(partial(mlp_body, share, devices, nseq, streams, plan), ou...  19.9 us
    ppermute x4, starting transfers between devices, scatter_modes(): come = lax.ppermute(blocks[1], 'seq', [(i, i + step) for i in range(step)])  15.3 us
    pallas_call x1, Pallas kernels, ssm_forward(): pl.pallas_call(partial(fwd_body, nck, nch, x.shape[0] // nck), out_shape=...  14.9 us
    all_to_all x1, waiting for transfers between devices, per_device(): lax.all_to_all(outs.reshape(seq, -1, nch, CH), 'seq', 0, 0).reshape(-1, CH)  10.6 us
    add x3, other arithmetic, join_cores(): sums.append([own[k] + far[k] for k in range(2)])  8.59 us
  transfers between devices with their start and end apart: 40, of which 17 were waited for; matrix products, arithmetic and copies ran while one was open for 17% of the time, Pallas kernels for 14%

profile of v10, /device:TPU:0, one launch (start us, length us, event | category | flops | bytes accessed | tf_op | source)
XLA Modules:
  0.0 260.3 jit_solution(2285428737043302902)
XLA Ops:
  1.2 3.7 %dynamic_update_slice.3 = f32[88064]{0:T(1024)S(1)} dynamic-update-slice(f32[88064]{0:T(1024)S(1)} %broadcast_in_dim.60, f32[86224]{0:T(1024)} %param.20, s32[]{:T(128)S(6)} %select_n.112) | dynamic-update-slice | bytes 689796 | tf_op jit(solution)/shard_map/dynamic_update_slice | solution.py:636
  12.9 7.2 %all-to-all-start = ((f32[16,2,32,128]{3,1,2,0:T(2,128)}), f32[16,2,32,128]{3,1,2,0:T(2,128)S(1)}, u32[]{:S(2)}, u32[]{:S(2)}) async-start(f32[16,2,32,128]{3,1,2,0:T(2,128)} %multiply_bitcast_fusion), calls=%async_computation | async-start | bytes 1048576 | tf_op jit(solution)/shard_map/all_to_all | solution.py:758
  23.2 3.8 %collective-permute-start.8 = (f32[2,2,2,65,128]{4,3,0,1,2:T(8,128)S(1)}, f32[2,2,2,65,128]{4,3,0,1,2:T(8,128)S(1)}, u32[]{:S(2)}, u32[]{:S(2)}) collective-permute-start(f32[2,2,2,65,128]{4,3,0,1,2:T(8,128)S(1)} %slice_bitcast_fusion.2), channel_id=1, source_target_pairs={{0,2},{1,3}} | collective-permute-start | bytes 798728 | tf_op jit(solution)/shard_map/ppermute | solution.py:722
  27.9 9.7 %collective-permute-done.1 = f32[688,128]{1,0:T(8,128)S(1)} collective-permute-done((f32[688,128]{1,0:T(8,128)S(1)}, f32[688,128]{1,0:T(8,128)S(1)}, u32[]{:S(2)}, u32[]{:S(2)}) %collective-permute-start.1) | collective-permute-done | bytes 352288 | tf_op jit(solution)/shard_map/ppermute | solution.py:609
  43.8 7.3 %collective-permute-start.10 = (f32[2,65,128]{2,1,0:T(8,128)S(1)}, f32[2,65,128]{2,1,0:T(8,128)S(1)}, u32[]{:S(2)}, u32[]{:S(2)}) collective-permute-start(f32[2,65,128]{2,1,0:T(8,128)S(1)} %slice_bitcast_fusion.19), channel_id=1, source_target_pairs={{0,8},{2,10},{4,12},{6,14},{1,9},{3,11},{5,13},{7,15}} | collective-permute-start | bytes 199688 | tf_op jit(solution)/shard_map/ppermute | solution.py:722
  60.8 6.9 %collective-permute-done.5 = f32[1376,128]{1,0:T(8,128)S(1)} collective-permute-done((f32[1376,128]{1,0:T(8,128)S(1)}, f32[1376,128]{1,0:T(8,128)S(1)}, u32[]{:S(2)}, u32[]{:S(2)}) %collective-permute-start.5) | collective-permute-done | bytes 704544 | tf_op jit(solution)/shard_map/ppermute | solution.py:609
  74.5 14.9 %state_forward.1 = (f32[1024,128]{1,0:T(8,128)}, f32[1024,128]{1,0:T(8,128)}, bf16[32,2,128,128]{3,2,1,0:T(8,128)(2,1)}, bf16[32,2,128,128]{3,2,1,0:T(8,128)(2,1...) custom-call(s32[4]{0:T(128)} %bitcast.215, f32[32,24,128]{2,1,0:T(8,128)} %concatenate.100.prm_ref, ...), custom_call_target="tpu_custom_call" | custom-call | flops 20000000000 | bytes 3145728 | tf_op jit(solution)/shard_map/state_forward/pallas_call | solution.py:160
  89.3 6.6 %all-to-all-start.1 = ((f32[16,2,32,128]{3,2,1,0:T(8,128)}), f32[16,2,32,128]{3,2,1,0:T(8,128)S(1)}, u32[]{:S(2)}, u32[]{:S(2)}) async-start(f32[16,2,32,128]{3,2,1,0:T(8,128)} %bitcast.201), calls=%async_computation.1 | async-start | bytes 1048576 | tf_op jit(solution)/shard_map/all_to_all | solution.py:802
  97.7 10.6 %all-to-all-done.1 = f32[16,2,32,128]{3,2,1,0:T(8,128)S(1)} async-done(((f32[16,2,32,128]{3,2,1,0:T(8,128)}), f32[16,2,32,128]{3,2,1,0:T(8,128)S(1)}, u32[]{:S(2)}, u32[]{:S(2)}) %all-to-all-start.1) | async-done | bytes 524320 | tf_op jit(solution)/shard_map/all_to_all | solution.py:802
  113.9 19.9 %feed_forward.1 = (bf16[256,512]{1,0:T(8,128)(2,1)}, f32[256,512]{1,0:T(8,128)}, f32[1024,128]{1,0:T(8,128)}, f32[8,128]{1,0:T(8,128)}, f32[4352,128]{1,0:T(8,12...) custom-call(s32[5]{0:T(128)} %pad_add_fusion.place_ref, ...), custom_call_target="tpu_custom_call" | custom-call | flops 20000000000 | bytes 31457280 | tf_op jit(solution)/shard_map/feed_forward/pallas_call | solution.py:570
  134.9 4.7 %all-to-all-start.2 = ((f32[16,2,32,128]{3,2,1,0:T(8,128)}), f32[16,2,32,128]{3,2,1,0:T(8,128)}, u32[]{:S(2)}, u32[]{:S(2)}) async-start(f32[16,2,32,128]{3,2,1,0:T(8,128)} %bitcast.200), calls=%async_computation.2 | async-start | bytes 1048576 | tf_op jit(solution)/shard_map/all_to_all | solution.py:808
  144.4 3.0 %slice_add_fusion = (f32[2176,128]{1,0:T(8,128)}, f32[2176,128]{1,0:T(8,128)S(1)}) fusion(f32[4352,128]{1,0:T(8,128)} %copy-done.8, f32[4352,128]{1,0:T(8,128)S(1)} %copy-done.7), kind=kLoop, calls=%fused_computation | loop fusion | flops 557056 | bytes 6684672 | tf_op jit(solution)/shard_map/add | solution.py:689
  147.4 2.9 %slice_add_fusion.2 = (f32[2176,128]{1,0:T(8,128)}, f32[2176,128]{1,0:T(8,128)S(1)}) fusion(f32[4352,128]{1,0:T(8,128)} %collective-permute-done.16, f32[4352,128]{1,0:T(8,128)S(1)} %copy-done.6), kind=kLoop, calls=%fused_computation.2 | loop fusion | flops 557056 | bytes 6684672 | tf_op jit(solution)/shard_map/add | solution.py:689
  150.3 4.8 %all-to-all-done.2 = f32[16,2,32,128]{3,2,1,0:T(8,128)} async-done(((f32[16,2,32,128]{3,2,1,0:T(8,128)}), f32[16,2,32,128]{3,2,1,0:T(8,128)}, u32[]{:S(2)}, u32[]{:S(2)}) %all-to-all-start.2) | async-done | bytes 524320 | tf_op jit(solution)/shard_map/all_to_all | solution.py:808
  157.4 22.6 %state_backward.1 = (f32[1024,128]{1,0:T(8,128)}, f32[3,32,128]{2,1,0:T(8,128)}) custom-call(s32[4]{0:T(128)} %bitcast.216, f32[32,24,128]{2,1,0:T(8,128)} %concatenate.100.prm_ref, f32[1024,128]{1,0:T(8,128)} %bitcast.198, f32[1024,128]{1,0:T(8,128)} %bitcast.44.g_ref, f32[1024,128]{1,0:T(8,128)} %get-tuple-element.61.prior_ref, ...), custom_call_target="tpu_custom_call" | custom-call | flops 35000000512 | bytes 4194304 | tf_op jit(solution)/shard_map/state_backward/pallas_call | solution.py:272
  191.9 5.6 %all-to-all-start.3 = ((f32[16,2,32,128]{3,1,2,0:T(2,128)}), f32[16,2,32,128]{3,1,2,0:T(2,128)S(1)}, u32[]{:S(2)}, u32[]{:S(2)}) async-start(f32[16,2,32,128]{3,1,2,0:T(2,128)} %copy.85), calls=%async_computation.3 | async-start | bytes 1048576 | tf_op jit(solution)/shard_map/all_to_all | solution.py:763
  198.6 4.2 %collective-permute-done.24 = f32[1088,128]{1,0:T(8,128)} collective-permute-done((f32[1088,128]{1,0:T(8,128)}, f32[1088,128]{1,0:T(8,128)}, u32[]{:S(2)}, u32[]{:S(2)}) %collective-permute-start.24) | collective-permute-done | bytes 557088 | tf_op jit(solution)/shard_map/ppermute | solution.py:609
  203.9 5.8 %collective-permute-done.23 = f32[1088,128]{1,0:T(8,128)} collective-permute-done((f32[1088,128]{1,0:T(8,128)}, f32[1088,128]{1,0:T(8,128)}, u32[]{:S(2)}, u32[]{:S(2)}) %collective-permute-start.23) | collective-permute-done | bytes 557088 | tf_op jit(solution)/shard_map/ppermute | solution.py:609
  215.0 3.6 %collective-permute-start.27 = (f32[544,128]{1,0:T(8,128)S(1)}, f32[544,128]{1,0:T(8,128)S(1)}, u32[]{:S(2)}, u32[]{:S(2)}) collective-permute-start(f32[544,128]{1,0:T(8,128)S(1)} %pad_maximum_fusion.7), channel_id=1, source_target_pairs={{0,16},{2,18},{4,20},{6,22},{8,24},{10,26},{12,28},{14,30},{16,0},... | collective-permute-start | bytes 835592 | tf_op jit(solution)/shard_map/ppermute | solution.py:609
  220.9 3.0 %collective-permute-done.29 = f32[288,128]{1,0:T(8,128)S(1)} collective-permute-done((f32[288,128]{1,0:T(8,128)S(1)}, f32[288,128]{1,0:T(8,128)S(1)}, u32[]{:S(2)}, u32[]{:S(2)}) %collective-permute-start.29) | collective-permute-done | bytes 147488 | tf_op jit(solution)/shard_map/ppermute | solution.py:609
  225.4 4.3 %collective-permute-done.32 = f32[192,128]{1,0:T(8,128)S(1)} collective-permute-done((f32[192,128]{1,0:T(8,128)S(1)}, f32[192,128]{1,0:T(8,128)S(1)}, u32[]{:S(2)}, u32[]{:S(2)}) %collective-permute-start.32) | collective-permute-done | bytes 98336 | tf_op jit(solution)/shard_map/ppermute | solution.py:737
  231.1 7.0 %collective-permute-done.27 = f32[544,128]{1,0:T(8,128)S(1)} collective-permute-done((f32[544,128]{1,0:T(8,128)S(1)}, f32[544,128]{1,0:T(8,128)S(1)}, u32[]{:S(2)}, u32[]{:S(2)}) %collective-permute-start.27) | collective-permute-done | bytes 278560 | tf_op jit(solution)/shard_map/ppermute | solution.py:609
  241.9 5.8 %all-to-all-start.4 = ((f32[32,1,128]{2,1,0:T(1,128)}), f32[32,1,128]{2,1,0:T(1,128)S(1)}, u32[]{:S(2)}, u32[]{:S(2)}) async-start(f32[32,1,128]{2,1,0:T(1,128)} %broadcast_in_dim.64), calls=%async_computation.4 | async-start | bytes 32768 | tf_op jit(solution)/shard_map/all_to_all | solution.py:750
  249.2 5.5 %all-to-all-done.4 = f32[32,1,128]{2,1,0:T(1,128)S(1)} async-done(((f32[32,1,128]{2,1,0:T(1,128)}), f32[32,1,128]{2,1,0:T(1,128)S(1)}, u32[]{:S(2)}, u32[]{:S(2)}) %all-to-all-start.4) | async-done | bytes 16416 | tf_op jit(solution)/shard_map/all_to_all | solution.py:750
  (255 shorter events, 82.0 us)
Async XLA Ops:
  0.6 21.0 %collective-permute-start.7 = (f32[86224]{0:T(1024)}, f32[86224]{0:T(1024)}, u32[]{:S(2)}, u32[]{:S(2)}) collective-permute-start(f32[86224]{0:T(1024)} %param.20), channel_id=1, source_target_pairs={{0,1},{1,0},{2,3},{3,2},{4,5},{5,4},{6,7},{7,6},{8,9},{9,8},{10,11... | collective-permute-start | bytes 1034696 | tf_op jit(solution)/shard_map/ppermute | solution.py:613
  4.9 22.1 %collective-permute-start = (f32[688,128]{1,0:T(8,128)S(1)}, f32[688,128]{1,0:T(8,128)S(1)}, u32[]{:S(2)}, u32[]{:S(2)}) collective-permute-start(f32[688,128]{1,0:T(8,128)S(1)} %bitcast.180), channel_id=1, source_target_pairs={{0,8},{2,10},{4,12},{6,14},{8,0},{10,2},{12,4},{14,6},{16,24},{18,... | collective-permute-start | bytes 1056776 | tf_op jit(solution)/shard_map/ppermute | solution.py:609
  7.6 30.0 %collective-permute-start.1 = (f32[688,128]{1,0:T(8,128)S(1)}, f32[688,128]{1,0:T(8,128)S(1)}, u32[]{:S(2)}, u32[]{:S(2)}) collective-permute-start(f32[688,128]{1,0:T(8,128)S(1)} %bitcast.181), channel_id=1, source_target_pairs={{0,16},{2,18},{4,20},{6,22},{8,24},{10,26},{12,28},{14,30},{16,0},... | collective-permute-start | bytes 1056776 | tf_op jit(solution)/shard_map/ppermute | solution.py:609
  10.2 31.0 %collective-permute-start.2 = (f32[688,128]{1,0:T(8,128)S(1)}, f32[688,128]{1,0:T(8,128)S(1)}, u32[]{:S(2)}, u32[]{:S(2)}) collective-permute-start(f32[688,128]{1,0:T(8,128)S(1)} %bitcast.182), channel_id=1, source_target_pairs={{0,24},{2,26},{4,28},{6,30},{8,16},{10,18},{12,20},{14,22},{16,8},... | collective-permute-start | bytes 1056776 | tf_op jit(solution)/shard_map/ppermute | solution.py:609
  12.9 47.0 %all-to-all-start = ((f32[16,2,32,128]{3,1,2,0:T(2,128)}), f32[16,2,32,128]{3,1,2,0:T(2,128)S(1)}, u32[]{:S(2)}, u32[]{:S(2)}) async-start(f32[16,2,32,128]{3,1,2,0:T(2,128)} %multiply_bitcast_fusion), calls=%async_computation | async-start | bytes 1048576 | tf_op jit(solution)/shard_map/all_to_all | solution.py:758
  23.2 15.2 %collective-permute-start.8 = (f32[2,2,2,65,128]{4,3,0,1,2:T(8,128)S(1)}, f32[2,2,2,65,128]{4,3,0,1,2:T(8,128)S(1)}, u32[]{:S(2)}, u32[]{:S(2)}) collective-permute-start(f32[2,2,2,65,128]{4,3,0,1,2:T(8,128)S(1)} %slice_bitcast_fusion.2), channel_id=1, source_target_pairs={{0,2},{1,3}} | collective-permute-start | bytes 798728 | tf_op jit(solution)/shard_map/ppermute | solution.py:722
  51.3 16.4 %collective-permute-start.5 = (f32[1376,128]{1,0:T(8,128)S(1)}, f32[1376,128]{1,0:T(8,128)S(1)}, u32[]{:S(2)}, u32[]{:S(2)}) collective-permute-start(f32[1376,128]{1,0:T(8,128)S(1)} %pad_maximum_fusion.2), channel_id=1, source_target_pairs={{0,4},{2,6},{4,0},{6,2},{8,12},{10,14},{12,8},{14,10},{16,20},{18,... | collective-permute-start | bytes 2113544 | tf_op jit(solution)/shard_map/ppermute | solution.py:609
  54.6 17.0 %collective-permute-start.3 = (f32[1376,128]{1,0:T(8,128)S(1)}, f32[1376,128]{1,0:T(8,128)}, u32[]{:S(2)}, u32[]{:S(2)}) collective-permute-start(f32[1376,128]{1,0:T(8,128)S(1)} %pad_maximum_fusion.1), channel_id=1, source_target_pairs={{0,2},{2,0},{4,6},{6,4},{8,10},{10,8},{12,14},{14,12},{16,18},{18,... | collective-permute-start | bytes 2113544 | tf_op jit(solution)/shard_map/ppermute | solution.py:609
  68.6 39.7 %collective-permute-start.13 = (f32[2752,128]{1,0:T(8,128)}, f32[2752,128]{1,0:T(8,128)}, u32[]{:S(2)}, u32[]{:S(2)}) collective-permute-start(f32[2752,128]{1,0:T(8,128)} %constant_dynamic-update-slice_fusion.5.refs_2_), channel_id=1, source_target_pairs={{0,2},{2,0},{4,6},{6,4},{8,10},{10,8},{12,14},{14,12},{16,18},{18,... | collective-permute-start | bytes 4227080 | tf_op jit(solution)/shard_map/ppermute | solution.py:609
  73.6 34.7 %collective-permute-start.12 = (f32[2752,128]{1,0:T(8,128)}, f32[2752,128]{1,0:T(8,128)}, u32[]{:S(2)}, u32[]{:S(2)}) collective-permute-start(f32[2752,128]{1,0:T(8,128)} %constant_dynamic-update-slice_fusion.refs_0_), channel_id=1, source_target_pairs={{0,4},{2,6},{4,0},{6,2},{8,12},{10,14},{12,8},{14,10},{16,20},{18,... | collective-permute-start | bytes 4227080 | tf_op jit(solution)/shard_map/ppermute | solution.py:609
  89.3 19.0 %all-to-all-start.1 = ((f32[16,2,32,128]{3,2,1,0:T(8,128)}), f32[16,2,32,128]{3,2,1,0:T(8,128)S(1)}, u32[]{:S(2)}, u32[]{:S(2)}) async-start(f32[16,2,32,128]{3,2,1,0:T(8,128)} %bitcast.201), calls=%async_computation.1 | async-start | bytes 1048576 | tf_op jit(solution)/shard_map/all_to_all | solution.py:802
  97.2 13.3 %collective-permute-start.6 = (f32[2752,128]{1,0:T(8,128)S(1)}, f32[2752,128]{1,0:T(8,128)}, u32[]{:S(2)}, u32[]{:S(2)}) collective-permute-start(f32[2752,128]{1,0:T(8,128)S(1)} %copy-done.16), channel_id=1, source_target_pairs={{0,1},{1,0},{2,3},{3,2},{4,5},{5,4},{6,7},{7,6},{8,9},{9,8},{10,11... | collective-permute-start | bytes 4227080 | tf_op jit(solution)/shard_map/ppermute | solution.py:613
  97.2 13.3 %collective-permute-start.4 = (f32[2752,128]{1,0:T(8,128)}, f32[2752,128]{1,0:T(8,128)}, u32[]{:S(2)}, u32[]{:S(2)}) collective-permute-start(f32[2752,128]{1,0:T(8,128)} %constant_dynamic-update-slice_fusion.refs_0_), channel_id=1, source_target_pairs={{0,1},{1,0},{2,3},{3,2},{4,5},{5,4},{6,7},{7,6},{8,9},{9,8},{10,11... | collective-permute-start | bytes 4227080 | tf_op jit(solution)/shard_map/ppermute | solution.py:613
  134.9 20.2 %all-to-all-start.2 = ((f32[16,2,32,128]{3,2,1,0:T(8,128)}), f32[16,2,32,128]{3,2,1,0:T(8,128)}, u32[]{:S(2)}, u32[]{:S(2)}) async-start(f32[16,2,32,128]{3,2,1,0:T(8,128)} %bitcast.200), calls=%async_computation.2 | async-start | bytes 1048576 | tf_op jit(solution)/shard_map/all_to_all | solution.py:808
  155.1 26.7 %collective-permute-start.21 = (f32[1152,128]{1,0:T(8,128)}, f32[1152,128]{1,0:T(8,128)}, u32[]{:S(2)}, u32[]{:S(2)}) collective-permute-start(f32[1152,128]{1,0:T(8,128)} %get-tuple-element.73), channel_id=1, source_target_pairs={{0,16},{2,18},{4,20},{6,22},{8,24},{10,26},{12,28},{14,30},{16,0},... | collective-permute-start | bytes 1769480 | tf_op jit(solution)/shard_map/ppermute | solution.py:609
  156.0 27.0 %collective-permute-start.20 = (f32[2176,128]{1,0:T(8,128)}, f32[2176,128]{1,0:T(8,128)}, u32[]{:S(2)}, u32[]{:S(2)}) collective-permute-start(f32[2176,128]{1,0:T(8,128)} %get-tuple-element.71), channel_id=1, source_target_pairs={{0,4},{2,6},{4,0},{6,2},{8,12},{10,14},{12,8},{14,10},{16,20},{18,... | collective-permute-start | bytes 3342344 | tf_op jit(solution)/shard_map/ppermute | solution.py:609
  156.7 27.8 %collective-permute-start.19 = (f32[2176,128]{1,0:T(8,128)}, f32[2176,128]{1,0:T(8,128)}, u32[]{:S(2)}, u32[]{:S(2)}) collective-permute-start(f32[2176,128]{1,0:T(8,128)} %get-tuple-element.69), channel_id=1, source_target_pairs={{0,2},{2,0},{4,6},{6,4},{8,10},{10,8},{12,14},{14,12},{16,18},{18,... | collective-permute-start | bytes 3342344 | tf_op jit(solution)/shard_map/ppermute | solution.py:609
  187.8 15.0 %collective-permute-start.24 = (f32[1088,128]{1,0:T(8,128)}, f32[1088,128]{1,0:T(8,128)}, u32[]{:S(2)}, u32[]{:S(2)}) collective-permute-start(f32[1088,128]{1,0:T(8,128)} %slice_bitcast_fusion), channel_id=1, source_target_pairs={{0,2},{2,0},{4,6},{6,4},{8,10},{10,8},{12,14},{14,12},{16,18},{18,... | collective-permute-start | bytes 1671176 | tf_op jit(solution)/shard_map/ppermute | solution.py:609
  190.1 19.6 %collective-permute-start.23 = (f32[1088,128]{1,0:T(8,128)}, f32[1088,128]{1,0:T(8,128)}, u32[]{:S(2)}, u32[]{:S(2)}) collective-permute-start(f32[1088,128]{1,0:T(8,128)} %slice_bitcast_fusion.1), channel_id=1, source_target_pairs={{0,4},{2,6},{4,0},{6,2},{8,12},{10,14},{12,8},{14,10},{16,20},{18,... | collective-permute-start | bytes 1671176 | tf_op jit(solution)/shard_map/ppermute | solution.py:609
  191.9 46.5 %all-to-all-start.3 = ((f32[16,2,32,128]{3,1,2,0:T(2,128)}), f32[16,2,32,128]{3,1,2,0:T(2,128)S(1)}, u32[]{:S(2)}, u32[]{:S(2)}) async-start(f32[16,2,32,128]{3,1,2,0:T(2,128)} %copy.85), calls=%async_computation.3 | async-start | bytes 1048576 | tf_op jit(solution)/shard_map/all_to_all | solution.py:763
  212.8 18.3 %collective-permute-start.26 = (f32[544,128]{1,0:T(8,128)S(1)}, f32[544,128]{1,0:T(8,128)S(1)}, u32[]{:S(2)}, u32[]{:S(2)}) collective-permute-start(f32[544,128]{1,0:T(8,128)S(1)} %pad_maximum_fusion.6), channel_id=1, source_target_pairs={{0,8},{2,10},{4,12},{6,14},{8,0},{10,2},{12,4},{14,6},{16,24},{18,... | collective-permute-start | bytes 835592 | tf_op jit(solution)/shard_map/ppermute | solution.py:609
  215.0 23.1 %collective-permute-start.27 = (f32[544,128]{1,0:T(8,128)S(1)}, f32[544,128]{1,0:T(8,128)S(1)}, u32[]{:S(2)}, u32[]{:S(2)}) collective-permute-start(f32[544,128]{1,0:T(8,128)S(1)} %pad_maximum_fusion.7), channel_id=1, source_target_pairs={{0,16},{2,18},{4,20},{6,22},{8,24},{10,26},{12,28},{14,30},{16,0},... | collective-permute-start | bytes 835592 | tf_op jit(solution)/shard_map/ppermute | solution.py:609
  218.8 19.3 %collective-permute-start.28 = (f32[544,128]{1,0:T(8,128)S(1)}, f32[544,128]{1,0:T(8,128)S(1)}, u32[]{:S(2)}, u32[]{:S(2)}) collective-permute-start(f32[544,128]{1,0:T(8,128)S(1)} %pad_maximum_fusion.8), channel_id=1, source_target_pairs={{0,24},{2,26},{4,28},{6,30},{8,16},{10,18},{12,20},{14,22},{16,8},... | collective-permute-start | bytes 835592 | tf_op jit(solution)/shard_map/ppermute | solution.py:609
  238.4 17.7 %collective-permute-start.34 = (f32[768,128]{1,0:T(8,128)S(1)}, f32[768,128]{1,0:T(8,128)S(1)}, u32[]{:S(2)}, u32[]{:S(2)}) collective-permute-start(f32[768,128]{1,0:T(8,128)S(1)} %pad_maximum_fusion.4), channel_id=1, source_target_pairs={{2,0},{3,1}} | collective-permute-start | bytes 1179656 | tf_op jit(solution)/shard_map/ppermute | solution.py:737
  (44 other events, 449.7 us)
